TPU v7x, 32 devices: a whole 2x2x4 slice. The times are simulated.
32 devices in a mesh: feat: 4 (over y, x), ex: 8 (over z, core).
Axes of the slice: x: 2, y: 2, z: 4, core: 2. Of those that a mesh axis runs over, the one named last changes fastest.
Arguments:
- x_values: bfloat16 [8192, 8192], P('ex', 'feat'), may hold values from -6 to 9, as said below
- tile_live: int32 [64, 64], P('ex', 'feat'), may hold values from 0 to 1
- labels: int32 [8192], P('ex'), may hold values from 0 to 127
- margins: bfloat16 [8192, 128], P('ex'), may hold values from -6 to 240, as said below
- coef: float32 [2, 4096, 128], P(None, ('feat', 'ex')), may hold values from -1.2 to 1.2
- order: int32 [3, 4], P(None, 'feat'), may hold values from 0 to 1
Outputs:
- margins_out: float32 [8192, 128], P('ex')
- coef_out: float32 [2, 4096, 128], P(None, ('feat', 'ex'))
Inputs may be any that keep to these rules, and one draw needn't show every extreme that they name: `x_values`: feature values lie within this range. `margins`: start scores lie within this range.
All inputs are finite; a program needn't handle non-finite values.
Results may differ from a plain program's by a relative error of at most 0.0015.
Values may be sent and summed in bfloat16 or wider, within the bound.
No kernel may reach another device: no remote copies, remote signals or barrier semaphores. Data moves between devices by JAX's collectives and lax.ppermute only.
A program may use at most 64 MiB of HBM per device.

v0:
```python
import jax
import jax.numpy as jnp
from jax import lax
from jax.sharding import PartitionSpec as P

C = 128
BLOCK = 1024
STEPS = 3


ridge = 0.002
lasso = 0.005


def soft_parts(score, onehot):
    row_max = jnp.max(score, axis=1, keepdims=True)
    expo = jnp.exp(score - row_max)
    prob = expo / jnp.sum(expo, axis=1, keepdims=True)
    residual = (prob - onehot).astype(jnp.bfloat16)
    spread = (1.0 - jnp.sum(prob * prob, axis=1)).astype(jnp.bfloat16)
    return (residual, spread)


def proximal(old_rows, grad_sum, curv_sum, count):
    curv = curv_sum / count + ridge
    shifted = old_rows - grad_sum / count / curv[:, None]
    limit = (lasso / curv)[:, None]
    return shifted - jnp.clip(shifted, -limit, limit)


def local(x_values, tile_live, labels, margins, coef, order):
    rows_here = x_values.shape[0]
    count = rows_here * lax.axis_size("ex")
    rows_own = coef.shape[1]
    tiles = BLOCK // 128
    classes = jnp.arange(C, dtype=jnp.int32)
    onehot = (labels[:, None] == classes[None, :]).astype(jnp.float32)
    score = margins.astype(jnp.float32)
    for step in range(STEPS):
        residual, spread = soft_parts(score, onehot)
        chosen = order[step, 0]
        block_x = lax.dynamic_slice_in_dim(x_values, chosen * BLOCK, BLOCK, 1)
        live_tiles = lax.dynamic_slice_in_dim(tile_live, chosen * tiles, tiles, 1).astype(
            jnp.bfloat16
        )
        block_x = (
            block_x.reshape(rows_here // 128, 128, tiles, 128) * live_tiles[:, None, :, None]
        ).reshape(rows_here, BLOCK)
        squares = block_x * block_x
        grad_part = lax.dot_general(
            block_x, residual, (((0,), (0,)), ((), ())), preferred_element_type=jnp.float32
        )
        curv_part = jnp.dot(spread, squares, preferred_element_type=jnp.float32)
        old_rows = lax.dynamic_index_in_dim(coef, chosen, 0, keepdims=False)
        grad_sum, curv_sum = lax.psum((grad_part, curv_part), "ex")
        old_block = lax.all_gather(old_rows, "ex", axis=0, tiled=True)
        new_block = proximal(old_block, grad_sum, curv_sum, count)
        step_delta = (new_block - old_block).astype(jnp.bfloat16)
        own_start = lax.axis_index("ex") * rows_own
        new_rows = lax.dynamic_slice_in_dim(new_block, own_start, rows_own, 0)
        coef = lax.dynamic_update_index_in_dim(coef, new_rows, chosen, 0)
        contrib = jnp.dot(block_x, step_delta, preferred_element_type=jnp.float32)
        score = score + lax.psum(contrib, "feat")
    return (score, coef)


def solution(mesh):
    return jax.shard_map(
        local,
        mesh=mesh,
        in_specs=(
            P("ex", "feat"),
            P("ex", "feat"),
            P("ex"),
            P("ex", None),
            P(None, ("feat", "ex"), None),
            P(None, "feat"),
        ),
        out_specs=(P("ex", None), P(None, ("feat", "ex"), None)),
        check_vma=False,
    )
```

profile of v0, /device:TPU:0, one launch (start us, length us, event | category | flops | bytes accessed | tf_op | source)
XLA Modules:
  0.0 367.0 jit_solution(16654294411127184689)
XLA Ops:
  7.2 0.0 all-reduce.7.cloned.1.call-start
  7.2 0.9 copy.24
  8.1 1.3 fusion.45
  13.1 1.1 reduce_max.32
  14.3 1.3 fusion.8
  15.6 0.9 dynamic-slice_convert_fusion
  16.5 0.3 mul.76
  16.8 0.0 copy-start.3
  16.8 0.3 mul.83
  17.2 0.3 mul.91
  17.5 1.5 copy-done.3
  19.0 4.4 %bitcast_multiply_fusion = (bf16[1024,1024]{1,0:T(8,128)(2,1)S(1)}, bf16[1024,1024]{1,0:T(8,128)(2,1)S(1)}, bf16[1024,1024]{1,0:T(8,128)(2,1)}) fusion(bf16[128,8,8,128]{3,2,1,0:T(8,128)(2,1)S(1)} %bitcast.59, bf16[1024,2048]{1,0:T(8,128)(2,1)S(1)} %copy-done.3, s32[]{:T(128)S(6)} %select_n.44, bf16[128,8,8,128]{3,2,1,0:T(8,128)(2,1)S(1)} %bitcast.57, ...), kind=kLoop, calls=%fused_computation | loop fusion | flops 12582912 | bytes 18874380 | tf_op jit(solution)/shard_map/mul | solution.py:47
  23.4 1.3 copy-done.1
  24.7 0.0 copy-done.2
  24.7 0.0 copy-done.9
  24.7 2.1 fusion.19
  26.8 0.0 all-reduce.7.cloned.1.call-update
  26.8 0.0 all-reduce.9.cloned.1.call-start
  26.9 0.5 multiply_reduce_fusion.2
  28.0 2.0 fusion.4
  30.0 18.1 %psum.64 = f32[1024]{0:T(1024)S(1)} all-reduce(f32[1024]{0:T(1024)S(1)} %bitcast.60), channel_id=1, replica_groups=mesh['feat'=4,'ex'=8] {'ex'}, use_global_device_ids=true, to_apply=%region_4.5 | all-reduce | flops 1024 | bytes 8192 | tf_op jit(solution)/shard_map/psum | solution.py:55
  49.5 15.0 %all-gather = f32[1,1024,128]{2,1,0:T(8,128)S(1)} all-gather(f32[1,128,128]{2,1,0:T(8,128)S(1)} %constant_dynamic-slice_fusion.2), channel_id=2, replica_groups=mesh['feat'=4,'ex'=8] {'ex'}, dimensions={1}, use_global_device_ids=true | all-gather | bytes 589824 | tf_op jit(solution)/shard_map/all_gather | solution.py:56
  64.4 21.9 %all-reduce.7.cloned.1.call-done = f32[1024,128]{1,0:T(8,128)} async-done(((f32[1024,128]{1,0:T(8,128)}), f32[1024,128]{1,0:T(8,128)}) %all-reduce.7.cloned.1.call-update) | async-done | bytes 524304 | tf_op jit(solution)/shard_map/psum | solution.py:55
  86.3 1.5 minimum_subtract_fusion.2
  87.9 3.1 fusion.21
  91.0 0.0 all-reduce.9.cloned.1.call-update
  91.0 0.0 all-reduce.11.cloned.1.call-start
  92.7 14.8 %all-gather.1 = f32[1,1024,128]{2,1,0:T(8,128)S(1)} all-gather(f32[1,128,128]{2,1,0:T(8,128)S(1)} %constant_dynamic-slice_fusion), channel_id=3, replica_groups=mesh['feat'=4,'ex'=8] {'ex'}, dimensions={1}, use_global_device_ids=true | all-gather | bytes 589824 | tf_op jit(solution)/shard_map/all_gather | solution.py:56
  107.6 27.9 %all-reduce.9.cloned.1.call-done = f32[1024,128]{1,0:T(8,128)} async-done(((f32[1024,128]{1,0:T(8,128)}), f32[1024,128]{1,0:T(8,128)}) %all-reduce.9.cloned.1.call-update) | async-done | bytes 524304 | tf_op jit(solution)/shard_map/psum | solution.py:63
  135.5 1.4 fusion.37
  136.9 1.4 fusion.16
  138.3 1.5 multiply_reduce_fusion.1
  139.8 0.0 copy-done
  139.9 3.1 fusion.29
  143.0 0.0 all-reduce.11.cloned.1.call-update
  143.0 0.0 all-reduce.13.cloned.1.call-start
  143.0 2.0 fusion.2
  145.0 16.3 %psum.67 = f32[1024]{0:T(1024)S(1)} all-reduce(f32[1024]{0:T(1024)S(1)} %bitcast.61), channel_id=1, replica_groups=mesh['feat'=4,'ex'=8] {'ex'}, use_global_device_ids=true, to_apply=%region_10.11 | all-reduce | flops 1024 | bytes 8192 | tf_op jit(solution)/shard_map/psum | solution.py:55
  161.3 38.0 %all-reduce.11.cloned.1.call-done = f32[1024,128]{1,0:T(8,128)} async-done(((f32[1024,128]{1,0:T(8,128)}), f32[1024,128]{1,0:T(8,128)}) %all-reduce.11.cloned.1.call-update) | async-done | bytes 524304 | tf_op jit(solution)/shard_map/psum | solution.py:55
  199.3 1.5 minimum_subtract_fusion.1
  200.8 0.8 copy-done.6
  201.6 3.2 fusion.23
  204.8 0.0 all-reduce.13.cloned.1.call-update
  204.8 0.0 all-reduce.15.cloned.1.call-start
  206.8 0.9 bitcast_dynamic-update-slice_fusion.1
  207.7 15.9 %all-gather.2 = f32[1,1024,128]{2,1,0:T(8,128)} all-gather(f32[1,128,128]{2,1,0:T(8,128)S(1)} %constant_dynamic-slice_fusion.1), channel_id=4, replica_groups=mesh['feat'=4,'ex'=8] {'ex'}, dimensions={1}, use_global_device_ids=true | all-gather | bytes 589824 | tf_op jit(solution)/shard_map/all_gather | solution.py:56
  223.6 25.7 %all-reduce.13.cloned.1.call-done = f32[1024,128]{1,0:T(8,128)} async-done(((f32[1024,128]{1,0:T(8,128)}), f32[1024,128]{1,0:T(8,128)}) %all-reduce.13.cloned.1.call-update) | async-done | bytes 524304 | tf_op jit(solution)/shard_map/psum | solution.py:63
  249.3 0.0 copy-done.4
  249.3 1.3 fusion.43
  250.5 0.4 fusion.18
  250.9 0.5 multiply_reduce_fusion
  251.4 2.1 fusion.27
  253.5 0.0 all-reduce.15.cloned.1.call-update
  253.5 0.0 all-reduce.17.cloned.1.call-start
  253.6 0.4 fusion
  254.0 16.2 %psum.70 = f32[1024]{0:T(1024)S(1)} all-reduce(f32[1024]{0:T(1024)S(1)} %bitcast.62), channel_id=1, replica_groups=mesh['feat'=4,'ex'=8] {'ex'}, use_global_device_ids=true, to_apply=%region_16.17 | all-reduce | flops 1024 | bytes 8192 | tf_op jit(solution)/shard_map/psum | solution.py:55
  270.1 39.7 %all-reduce.15.cloned.1.call-done = f32[1024,128]{1,0:T(8,128)} async-done(((f32[1024,128]{1,0:T(8,128)}), f32[1024,128]{1,0:T(8,128)}) %all-reduce.15.cloned.1.call-update) | async-done | bytes 524304 | tf_op jit(solution)/shard_map/psum | solution.py:55
  309.9 1.5 minimum_subtract_fusion
  311.4 0.8 copy-done.7
  312.2 1.5 fusion.25
  313.7 0.0 all-reduce.17.cloned.1.call-update
  313.7 0.9 bitcast_dynamic-update-slice_fusion
  314.6 43.6 %all-reduce.17.cloned.1.call-done = f32[1024,128]{1,0:T(8,128)} async-done(((f32[1024,128]{1,0:T(8,128)}), f32[1024,128]{1,0:T(8,128)}) %all-reduce.17.cloned.1.call-update) | async-done | bytes 524304 | tf_op jit(solution)/shard_map/psum | solution.py:63
  358.2 1.9 add.88
  (25 shorter events, 0.1 us)
Async XLA Ops:
  7.2 79.2 %all-reduce.7.cloned.1.call-start = ((), (), s32[]{:S(2)}) async-start(), calls=%async_computation | async-start | bytes 1048576 | tf_op jit(solution)/shard_map/psum | solution.py:55
  16.8 2.2 copy-start.3
  19.0 5.7 %copy-start.2 = (bf16[1024,128]{1,0:T(8,128)(2,1)S(1)}, bf16[1024,128]{1,0:T(8,128)(2,1)}, u32[]{:S(2)}) copy-start(bf16[1024,128]{1,0:T(8,128)(2,1)} %param.9) | copy-start | bytes 786436
  19.0 5.7 %copy-start.9 = (s32[1024]{0:T(1024)S(1)}, s32[1024]{0:T(1024)}, u32[]{:S(2)}) copy-start(s32[1024]{0:T(1024)} %param.8) | copy-start | bytes 12292
  23.4 1.3 copy-start.1
  26.8 108.6 %all-reduce.9.cloned.1.call-start = ((), (), s32[]{:S(2)}) async-start(), calls=%async_computation.1 | async-start | bytes 1048576 | tf_op jit(solution)/shard_map/psum | solution.py:63
  91.0 108.3 %all-reduce.11.cloned.1.call-start = ((), (), s32[]{:S(2)}) async-start(), calls=%async_computation.2 | async-start | bytes 1048576 | tf_op jit(solution)/shard_map/psum | solution.py:55
  135.5 4.4 %copy-start = (bf16[1024,1024]{1,0:T(8,128)(2,1)S(1)}, bf16[1024,1024]{1,0:T(8,128)(2,1)}, u32[]{:S(2)}) copy-start(bf16[1024,1024]{1,0:T(8,128)(2,1)} %get-tuple-element.6) | copy-start | bytes 6291460
  143.0 106.3 %all-reduce.13.cloned.1.call-start = ((), (), s32[]{:S(2)}) async-start(), calls=%async_computation.3 | async-start | bytes 1048576 | tf_op jit(solution)/shard_map/psum | solution.py:63
  200.8 0.8 copy-start.6
  201.6 47.6 %copy-start.4 = (f32[1024,128]{1,0:T(8,128)S(1)}, f32[1024,128]{1,0:T(8,128)}, u32[]{:S(2)}) copy-start(f32[1024,128]{1,0:T(8,128)} %all-reduce.9.cloned.1.call-done) | copy-start | bytes 1572868
  204.8 105.1 %all-reduce.15.cloned.1.call-start = ((), (), s32[]{:S(2)}) async-start(), calls=%async_computation.4 | async-start | bytes 1048576 | tf_op jit(solution)/shard_map/psum | solution.py:55
  253.5 56.4 %copy-start.5 = (f32[1,1024,128]{2,1,0:T(8,128)S(1)}, f32[1,1024,128]{2,1,0:T(8,128)}, u32[]{:S(2)}) copy-start(f32[1,1024,128]{2,1,0:T(8,128)} %all-gather.2) | copy-start | bytes 1572868
  253.5 104.7 %all-reduce.17.cloned.1.call-start = ((), (), s32[]{:S(2)}) async-start(), calls=%async_computation.5 | async-start | bytes 1048576 | tf_op jit(solution)/shard_map/psum | solution.py:63
  311.4 0.8 copy-start.7
  314.6 45.5 %copy-start.8 = (f32[2,128,128]{2,1,0:T(8,128)}, f32[2,128,128]{2,1,0:T(8,128)S(1)}, u32[]{:S(2)}) copy-start(f32[2,128,128]{2,1,0:T(8,128)S(1)} %bitcast_dynamic-update-slice_fusion) | copy-start | bytes 393220
Sparse Core Ops, SparseCore 0:
  26.9 59.3 all-reduce.6
  91.1 44.3 all-reduce.8
  143.1 56.1 all-reduce.10
  204.9 44.2 all-reduce.12
  253.7 56.1 all-reduce.14
  313.9 44.3 all-reduce.16
where the time goes:
time: 368 us; the launch traced here: 367 us
  waiting for transfers between devices  197 us (54%)
  blocking collectives  96.3 us (26%)
  between operations  23.5 us (6%)
  other arithmetic  21.1 us (6%)
  matrix products  19.3 us (5%)
  local copies, waits for them, and re-layouts  9.45 us (3%)
    psum x3, waiting for transfers between devices, local(): grad_sum, curv_sum = lax.psum((grad_part, curv_part), 'ex')  99.7 us
    psum x3, waiting for transfers between devices, local(): score = score + lax.psum(contrib, 'feat')  97.2 us
    psum x3, blocking collectives, local(): grad_sum, curv_sum = lax.psum((grad_part, curv_part), 'ex')  50.6 us
    all_gather x3, blocking collectives, local(): old_block = lax.all_gather(old_rows, 'ex', axis=0, tiled=True)  45.7 us
    dot_general x3, matrix products, local(): contrib = jnp.dot(block_x, step_delta, preferred_element_type=jnp.float32)  7.76 us
  transfers between devices with their start and end apart: 6, of which 6 were waited for; matrix products, arithmetic and copies ran while one was open for 2% of the time, Pallas kernels for 0%

commit v1 on v0

v1 whole, which is shorter than its diff:
```python
import functools

import jax
import jax.numpy as jnp
from jax import lax
from jax.experimental import pallas as pl
from jax.experimental.pallas import tpu as pltpu
from jax.sharding import PartitionSpec as P

C = 128
BLOCK = 1024
STEPS = 3
HALF = BLOCK // 2
TILE = 128
NB = HALF // TILE
ROWS = C + 8

ridge = 0.002
lasso = 0.005

F32 = jnp.float32
BF16 = jnp.bfloat16


def vmem(n):
    return [pl.BlockSpec(memory_space=pltpu.VMEM)] * n


def smem(n):
    return [pl.BlockSpec(memory_space=pltpu.SMEM)] * n


def call(body, outs, in_specs, name, flops=0, nbytes=0, **kw):
    return pl.pallas_call(
        body,
        out_shape=outs,
        in_specs=in_specs,
        out_specs=jax.tree.map(lambda _: pl.BlockSpec(memory_space=pltpu.VMEM), outs),
        name=name,
        cost_estimate=pl.CostEstimate(flops=flops, bytes_accessed=nbytes, transcendentals=0),
        **kw,
    )


def sds(shape, dtype):
    return jax.ShapeDtypeStruct(shape, dtype)


def prep_body(info_ref, live_ref, x_ref, out_ref, buf, sems):
    chosen, core = info_ref[0], info_ref[1]
    rows = out_ref.shape[0]
    tiles = BLOCK // TILE

    def copy(r):
        return pltpu.make_async_copy(
            x_ref.at[pl.ds(r * TILE, TILE), pl.ds(pl.multiple_of(chosen * BLOCK, BLOCK), BLOCK)],
            buf.at[pl.ds(r * TILE, TILE)],
            sems.at[r],
        )

    for r in range(rows // TILE):
        copy(r).start()
    for r in range(rows // TILE):
        copy(r).wait()
        here = pl.ds(r * TILE, TILE)
        for k in range(tiles):
            col = 2 * (k % NB) + (core if k < NB else 1 - core)
            live = live_ref[r, chosen * tiles + col].astype(F32)
            tile = buf[here, pl.ds(pl.multiple_of(col * TILE, TILE), TILE)]
            out_ref[here, k * TILE : (k + 1) * TILE] = (tile.astype(F32) * live).astype(BF16)


def prep(x_values, tile_live, chosen, core):
    rows = x_values.shape[0]
    info = jnp.stack([chosen, core])
    return call(
        prep_body,
        sds((rows, BLOCK), BF16),
        smem(2) + [pl.BlockSpec(memory_space=pl.ANY)],
        "prep",
        nbytes=4 * rows * BLOCK,
        scratch_shapes=[
            pltpu.VMEM((rows, BLOCK), BF16),
            pltpu.SemaphoreType.DMA((rows // TILE,)),
        ],
    )(info, tile_live, x_values)


def prep_general(x_values, tile_live, chosen, core, own):
    rows = x_values.shape[0]
    tiles = BLOCK // TILE
    x = lax.dynamic_slice_in_dim(x_values, chosen * BLOCK, BLOCK, 1)
    live = lax.dynamic_slice_in_dim(tile_live, chosen * tiles, tiles, 1).astype(BF16)
    x = x.reshape(rows // TILE, TILE, tiles, TILE) * live[:, None, :, None]
    x = x.reshape(rows, HALF // own, 2, own)
    mine = lax.dynamic_index_in_dim(x, core, 2, keepdims=False)
    other = lax.dynamic_index_in_dim(x, 1 - core, 2, keepdims=False)
    return jnp.concatenate([mine.reshape(rows, HALF), other.reshape(rows, HALF)], axis=1)


def half_sums(res_t, spread_ref, x_ref, first, g_ref):
    rows = x_ref.shape[0]
    grad = jnp.dot(res_t, x_ref[:, first : first + HALF], preferred_element_type=F32)
    row = lax.broadcasted_iota(jnp.int32, (8, TILE), 0)
    for k in range(NB):
        lanes = slice(first + k * TILE, first + (k + 1) * TILE)
        acc = jnp.zeros((8, TILE), F32)
        for r in range(rows // TILE):
            here = slice(r * TILE, (r + 1) * TILE)
            x = x_ref[here, lanes].astype(F32)
            term = x * x * spread_ref[here, :]
            acc = acc + jnp.sum(term.reshape(TILE // 8, 8, TILE), axis=0)
        total = jnp.sum(acc, axis=0, keepdims=True)
        g_ref[k, 0:C, :] = grad[:, k * TILE : (k + 1) * TILE]
        g_ref[k, C:ROWS, :] = jnp.where(row == 0, total, 0.0)


def soft_tile(score, labels):
    top = jnp.max(score, axis=1, keepdims=True)
    expo = jnp.exp(score - top)
    prob = expo / jnp.sum(expo, axis=1, keepdims=True)
    label_col = jnp.broadcast_to(labels.astype(F32), (TILE, TILE)).T
    classes = lax.broadcasted_iota(jnp.int32, (TILE, C), 1).astype(F32)
    residual = prob - jnp.where(label_col == classes, 1.0, 0.0)
    spread = (1.0 - jnp.sum(prob * prob, axis=1, keepdims=True)).astype(BF16).astype(F32)
    return residual.T.astype(BF16), jnp.broadcast_to(spread, (TILE, TILE))


def first_body(margins_ref, lab_ref, x_ref, res_ref, spread_ref, g_ref):
    for r in range(margins_ref.shape[0] // TILE):
        here = slice(r * TILE, (r + 1) * TILE)
        res_t, spread = soft_tile(margins_ref[here, :].astype(F32), lab_ref[r : r + 1, :])
        res_ref[:, here] = res_t
        spread_ref[here, :] = spread
    half_sums(res_ref[...], spread_ref, x_ref, HALF, g_ref)


def next_body(score_ref, a_ref, ra_ref, b_ref, rb_ref, lab_ref, x_ref, new_ref, res_ref, spread_ref, g_ref):
    rows = score_ref.shape[0]
    for r in range(rows // TILE):
        here = slice(r * TILE, (r + 1) * TILE)
        if 2 * r * TILE < rows:
            part, got, at = a_ref, ra_ref, here
        else:
            part, got = b_ref, rb_ref
            at = slice(r * TILE - rows // 2, (r + 1) * TILE - rows // 2)
        change = part[at, :].astype(F32) + got[at, :].astype(F32)
        score = score_ref[here, :].astype(F32) + change
        new_ref[here, :] = score
        res_t, spread = soft_tile(score, lab_ref[r : r + 1, :])
        res_ref[:, here] = res_t
        spread_ref[here, :] = spread
    half_sums(res_ref[...], spread_ref, x_ref, HALF, g_ref)


def own_body(res_ref, spread_ref, x_ref, g_ref):
    half_sums(res_ref[...], spread_ref, x_ref, 0, g_ref)


def encode(k, grad, curv, out_ref):
    out_ref[k, 0:C, :] = grad.astype(BF16)
    high = curv.astype(BF16).astype(F32)
    low = curv - high
    row = lax.broadcasted_iota(jnp.int32, (8, TILE), 0)
    tail = jnp.where(row == 0, high, jnp.where(row == 1, low, 0.0))
    out_ref[k, C:ROWS, :] = tail.astype(BF16)


def pair_body(own_ref, got_ref, out_ref):
    for k in range(NB):
        total = own_ref[k] + got_ref[k]
        encode(k, total[0:C], total[C : C + 1], out_ref)


def decode_sum(k, mine_ref, got_ref):
    total = mine_ref[k].astype(F32) + got_ref[k].astype(F32)
    return total[0:C], total[C : C + 1] + total[C + 1 : C + 2]


def hop_body(mine_ref, got_ref, out_ref):
    for k in range(NB):
        encode(k, *decode_sum(k, mine_ref, got_ref), out_ref)


def prox_body(count, info_ref, mine_ref, got_ref, old_ref, new_ref, delta_ref):
    chosen, place = info_ref[0], info_ref[1]
    new_ref[1 - chosen] = old_ref[1 - chosen]
    for j in range(NB):
        k = jnp.bitwise_xor(place, j)
        grad, curv = decode_sum(k, mine_ref, got_ref)
        curv = curv / count + ridge
        old = old_ref[chosen, j]
        shifted = old - grad / count / curv
        limit = lasso / curv
        new = shifted - jnp.clip(shifted, -limit, limit)
        new_ref[chosen, j] = new
        delta_ref[k] = (new - old).astype(BF16)


def contrib_dot(x_ref, mine_ref, got_ref):
    delta = [mine_ref[k] for k in range(NB)] + [got_ref[k] for k in range(NB)]
    delta = jnp.concatenate(delta, axis=1)
    return lax.dot_general(
        x_ref[...], delta, (((1,), (1,)), ((), ())), preferred_element_type=F32
    )


def change_first_body(x_ref, mine_ref, got_ref, total_ref, a_ref, b_ref):
    part = contrib_dot(x_ref, mine_ref, got_ref)
    half = part.shape[0] // 2
    total_ref[...] = part
    a_ref[...] = part[:half].astype(BF16)
    b_ref[...] = part[half:].astype(BF16)


def change_next_body(x_ref, mine_ref, got_ref, before_ref, total_ref, a_ref, b_ref):
    part = contrib_dot(x_ref, mine_ref, got_ref)
    half = part.shape[0] // 2
    total_ref[...] = before_ref[...] + part
    a_ref[...] = part[:half].astype(BF16)
    b_ref[...] = part[half:].astype(BF16)


def change_last_body(x_ref, mine_ref, got_ref, before_ref, a_ref, b_ref):
    part = before_ref[...] + contrib_dot(x_ref, mine_ref, got_ref)
    half = part.shape[0] // 2
    a_ref[...] = part[:half]
    b_ref[...] = part[half:]


def flip(x, axis, bit):
    n = lax.axis_size(axis)
    return lax.ppermute(x, axis, [(i, i ^ bit) for i in range(n)])


def bits(n):
    return [1 << i for i in range(n.bit_length() - 1)]


def add_as(x, y, dtype):
    return (x.astype(F32) + y.astype(F32)).astype(dtype)


def spread_over_feat(a, b):
    order = bits(lax.axis_size("feat"))
    for n, (bit_a, bit_b) in enumerate(zip(order, reversed(order))):
        got_a, got_b = flip(a, "feat", bit_a), flip(b, "feat", bit_b)
        if n == len(order) - 1:
            return a, got_a, b, got_b
        a, b = add_as(a, got_a, a.dtype), add_as(b, got_b, b.dtype)


def local(x_values, tile_live, labels, margins, coef, order):
    rows = x_values.shape[0]
    n_ex = lax.axis_size("ex")
    count = float(rows * n_ex)
    own = coef.shape[1]
    me = lax.axis_index("ex")
    core, place = me % 2, me // 2
    aligned = own == TILE
    labels = labels.reshape(rows // TILE, TILE)
    z_bits = [2 * b for b in bits(n_ex // 2)]

    mine = jnp.swapaxes(coef, 1, 2)[:, None]
    if aligned:
        far = mine.astype(BF16)
        for bit in z_bits:
            far = jnp.concatenate([far, flip(far, "ex", bit)], axis=1)
        old = jnp.concatenate([mine, far[:, 1:].astype(F32)], axis=1)
    else:
        far = mine
        for bit in z_bits:
            far = jnp.concatenate([far, flip(far, "ex", bit)], axis=1)
        far = jnp.take(far, jnp.bitwise_xor(jnp.arange(n_ex // 2), place), axis=1)
        old = far.transpose(0, 2, 1, 3).reshape(2, C, NB, TILE).transpose(0, 2, 1, 3)

    g_shape = sds((NB, ROWS, TILE), F32)
    m_shape = sds((NB, ROWS, TILE), BF16)
    soft_shapes = (sds((C, rows), BF16), sds((rows, TILE), F32), g_shape)
    half_shape = (rows // 2, C)
    half_flops = 2 * rows * HALF * C
    score, total = margins, None
    for step in range(STEPS):
        chosen = order[step, 0]
        if aligned:
            x = prep(x_values, tile_live, chosen, core)
        else:
            x = prep_general(x_values, tile_live, chosen, core, own)
        if step == 0:
            res_t, spread, g_other = call(
                first_body, soft_shapes, vmem(3), "soft_first", half_flops, 1 << 20
            )(margins, labels, x)
        else:
            score, res_t, spread, g_other = call(
                next_body, (sds((rows, C), F32),) + soft_shapes, vmem(7), "soft_next", half_flops, 1 << 20
            )(score, a, got_a, b, got_b, labels, x)
        got = flip(g_other, "ex", 1)
        g_own = call(own_body, g_shape, vmem(3), "own", half_flops, 1 << 20)(res_t, spread, x)
        message = call(pair_body, m_shape, vmem(2), "pair")(g_own, got)
        for bit in z_bits[:-1]:
            got = flip(message, "ex", bit)
            message = call(hop_body, m_shape, vmem(2), "hop")(message, got)
        got = flip(message, "ex", z_bits[-1])
        info = jnp.stack([chosen, place if aligned else jnp.int32(0)])
        old, delta = call(
            functools.partial(prox_body, count),
            (sds(old.shape, F32), sds((NB, C, TILE), BF16)),
            smem(1) + vmem(3),
            "prox",
        )(info, message, got, old)
        got = flip(delta, "ex", 1)
        if step == 0:
            total, a, b = call(
                change_first_body,
                (sds((rows, C), F32), sds(half_shape, BF16), sds(half_shape, BF16)),
                vmem(3), "change_first", 2 * half_flops, 1 << 20,
            )(x, delta, got)
        elif step < STEPS - 1:
            total, a, b = call(
                change_next_body,
                (sds((rows, C), F32), sds(half_shape, BF16), sds(half_shape, BF16)),
                vmem(4), "change_next", 2 * half_flops, 1 << 20,
            )(x, delta, got, total)
        else:
            a, b = call(
                change_last_body,
                (sds(half_shape, F32), sds(half_shape, F32)),
                vmem(4), "change_last", 2 * half_flops, 1 << 20,
            )(x, delta, got, total)
        a, got_a, b, got_b = spread_over_feat(a, b)
    score = margins.astype(F32) + jnp.concatenate([a + got_a, b + got_b])
    if aligned:
        coef = old[:, 0]
    else:
        old = old.transpose(0, 2, 1, 3).reshape(2, C, HALF)
        coef = lax.dynamic_slice_in_dim(old, place * own, own, 2)
    return score, jnp.swapaxes(coef, 1, 2)


def solution(mesh):
    return jax.shard_map(
        local,
        mesh=mesh,
        in_specs=(
            P("ex", "feat"),
            P("ex", "feat"),
            P("ex"),
            P("ex", None),
            P(None, ("feat", "ex"), None),
            P(None, "feat"),
        ),
        out_specs=(P("ex", None), P(None, ("feat", "ex"), None)),
        check_vma=False,
    )
```

time: 368 us -> 173 us (0.47)
  waiting for transfers between devices: 197 us -> 61.7 us
  blocking collectives: 96.3 us -> 0 us
  Pallas kernels: 0 us -> 60.1 us
  between operations: 23.5 us -> 0.9 us
  starting transfers between devices: 0.25 us -> 21.2 us
  matrix products: 19.3 us -> 0 us
  other arithmetic: 21.1 us -> 15 us
  local copies, waits for them, and re-layouts: 9.45 us -> 13.2 us
    psum x6 -> x0, waiting for transfers between devices: 197 us -> none  [the longest x3 99.7 us: local(): grad_sum, curv_sum = lax.psum((grad_part, curv_part), 'ex')]
    ppermute x0 -> x26, waiting for transfers between devices: none -> 61.7 us  [flip(): return lax.ppermute(x, axis, [(i, i ^ bit) for i in range(n)])]
    pallas_call x0 -> x21, Pallas kernels: none -> 60.1 us  [the longest x3 11.2 us: prep(): call(prep_body, sds((rows, BLOCK), BF16), smem(2) + [pl.BlockSpec(memory_...]
    psum x3 -> x0, blocking collectives: 50.6 us -> none  [local(): grad_sum, curv_sum = lax.psum((grad_part, curv_part), 'ex')]
    all_gather x3 -> x0, blocking collectives: 45.7 us -> none  [local(): old_block = lax.all_gather(old_rows, 'ex', axis=0, tiled=True)]
    ppermute x0 -> x26, starting transfers between devices: none -> 21.2 us  [flip(): return lax.ppermute(x, axis, [(i, i ^ bit) for i in range(n)])]
    dot_general x9 -> x0, matrix products: 19.3 us -> none  [the longest x3 7.76 us: local(): contrib = jnp.dot(block_x, step_delta, preferred_element_type=jnp.float32)]
    another operation x0 -> x6, other arithmetic: none -> 7.48 us  [the longest x3 3.78 us: local(): info = jnp.stack([chosen, place if aligned else jnp.int32(0)])]
  transfers between devices with their start and end apart: 6 -> 26, of which waited for: 6 -> 14; matrix products, arithmetic and copies ran while one was open for 2% -> 9% of each run, Pallas kernels for 0% -> 12%
where the time goes in v1:
time: 173 us; the launch traced here: 172 us
  waiting for transfers between devices  61.7 us (36%)
  Pallas kernels  60.1 us (35%)
  starting transfers between devices  21.2 us (12%)
  other arithmetic  15 us (9%)
  local copies, waits for them, and re-layouts  13.2 us (8%)
    ppermute x26, waiting for transfers between devices, flip(): return lax.ppermute(x, axis, [(i, i ^ bit) for i in range(n)])  61.7 us
    ppermute x26, starting transfers between devices, flip(): return lax.ppermute(x, axis, [(i, i ^ bit) for i in range(n)])  21.2 us
    pallas_call x3, Pallas kernels, prep(): call(prep_body, sds((rows, BLOCK), BF16), smem(2) + [pl.BlockSpec(memory_...  11.2 us
    unnamed x46, local copies, waits for them, and re-layouts  10.8 us
    pallas_call x3, Pallas kernels, local(): call(own_body, g_shape, vmem(3), 'own', half_flops, 1 << 20)  9.25 us
    pallas_call x2, Pallas kernels, local(): call(next_body, (sds((rows, C), F32),) + soft_shapes, vmem(7), 'soft_next...  9.05 us
    pallas_call x3, Pallas kernels, local(): call(functools.partial(prox_body, count), (sds(old.shape, F32), sds((NB,...  6.41 us
    pallas_call x3, Pallas kernels, local(): message = call(pair_body, m_shape, vmem(2), 'pair')(g_own, got)  5.18 us
  transfers between devices with their start and end apart: 26, of which 14 were waited for; matrix products, arithmetic and copies ran while one was open for 9% of the time, Pallas kernels for 12%

profile of v1, /device:TPU:0, one launch (start us, length us, event | category | flops | bytes accessed | tf_op | source)
XLA Modules:
  0.0 172.2 jit_solution(3452628085543402818)
XLA Ops:
  0.6 1.4 fusion.1
  2.1 1.2 pad_add_fusion.3.info_ref
  3.3 3.7 %prep.4.x_ref = bf16[1024,1024]{1,0:T(8,128)(2,1)} custom-call(s32[2]{0:T(128)} %pad_add_fusion.3.info_ref, s32[8,16]{1,0:T(8,128)} %live_ref.5, bf16[1024,2048]{1,0:T(8,128)(2,1)} %x_ref.5), custom_call_target="tpu_custom_call" | custom-call | bytes 4194304 | tf_op jit(solution)/shard_map/prep/pallas_call | solution.py:76
  7.0 4.3 %soft_first.1 = (bf16[128,1024]{1,0:T(8,128)(2,1)}, f32[1024,128]{1,0:T(8,128)}, f32[4,136,128]{2,1,0:T(8,128)}) custom-call(bf16[1024,128]{1,0:T(8,128)(2,1)} %score_ref.1, s32[8,128]{1,0:T(8,128)} %bitcast.21, bf16[1024,1024]{1,0:T(8,128)(2,1)} %prep.4.x_ref), custom_call_target="tpu_custom_call" | custom-call | flops 134217728 | bytes 1048576 | tf_op jit(solution)/shard_map/soft_first/pallas_call | solution.py:290
  11.9 2.6 %collective-permute-start.3 = (bf16[2,1,128,128]{3,2,1,0:T(8,128)(2,1)S(1)}, bf16[2,1,128,128]{3,2,1,0:T(8,128)(2,1)S(1)}, u32[]{:S(2)}, u32[]{:S(2)}) collective-permute-start(bf16[2,1,128,128]{3,2,1,0:T(8,128)(2,1)S(1)} %fusion), channel_id=1, source_target_pairs={{0,2},{1,3},{2,0},{3,1},{4,6},{5,7},{6,4},{7,5},{8,10},{9,11},{10,... | collective-permute-start | bytes 196616 | tf_op jit(solution)/shard_map/ppermute | solution.py:233
  14.6 3.1 %own.3.own_ref = f32[4,136,128]{2,1,0:T(8,128)} custom-call(bf16[128,1024]{1,0:T(8,128)(2,1)} %get-tuple-element.26.res_ref, f32[1024,128]{1,0:T(8,128)} %get-tuple-element.27.spread_ref, bf16[1024,1024]{1,0:T(8,128)(2,1)} %prep.4.x_ref), custom_call_target="tpu_custom_call" | custom-call | flops 134217728 | bytes 1048576 | tf_op jit(solution)/shard_map/own/pallas_call | solution.py:298
  17.6 0.7 copy-done.5
  18.3 1.7 %pair.3.mine_ref = bf16[4,136,128]{2,1,0:T(8,128)(2,1)} custom-call(f32[4,136,128]{2,1,0:T(8,128)} %own.3.own_ref, f32[4,136,128]{2,1,0:T(8,128)} %copy-done.5), custom_call_target="tpu_custom_call" | custom-call | tf_op jit(solution)/shard_map/pair/pallas_call | solution.py:299
  20.1 3.1 %collective-permute-start.4 = (bf16[2,2,128,128]{3,2,1,0:T(8,128)(2,1)S(1)}, bf16[2,2,128,128]{3,2,1,0:T(8,128)(2,1)S(1)}, u32[]{:S(2)}, u32[]{:S(2)}) collective-permute-start(bf16[2,2,128,128]{3,2,1,0:T(8,128)(2,1)S(1)} %pad_maximum_fusion.1), channel_id=1, source_target_pairs={{0,4},{1,5},{2,6},{3,7},{4,0},{5,1},{6,2},{7,3},{8,12},{9,13},{10,... | collective-permute-start | bytes 393224 | tf_op jit(solution)/shard_map/ppermute | solution.py:233
  23.2 1.3 pad_add_fusion.2.info_ref
  24.5 4.4 %collective-permute-done.1.got_ref = bf16[4,136,128]{2,1,0:T(8,128)(2,1)S(1)} collective-permute-done((bf16[4,136,128]{2,1,0:T(8,128)(2,1)}, bf16[4,136,128]{2,1,0:T(8,128)(2,1)S(1)}, u32[]{:S(2)}, u32[]{:S(2)}) %collective-permute-start.1) | collective-permute-done | bytes 139296 | tf_op jit(solution)/shard_map/ppermute | solution.py:233
  29.6 1.7 hop.3.mine_ref
  31.8 0.8 pad_maximum_fusion.old_ref
  32.6 6.8 %collective-permute-done.2.got_ref = bf16[4,136,128]{2,1,0:T(8,128)(2,1)S(1)} collective-permute-done((bf16[4,136,128]{2,1,0:T(8,128)(2,1)}, bf16[4,136,128]{2,1,0:T(8,128)(2,1)S(1)}, u32[]{:S(2)}, u32[]{:S(2)}) %collective-permute-start.2) | collective-permute-done | bytes 139296 | tf_op jit(solution)/shard_map/ppermute | solution.py:233
  40.1 2.1 %prox.3 = (f32[2,4,128,128]{3,2,1,0:T(8,128)}, bf16[4,128,128]{2,1,0:T(8,128)(2,1)}) custom-call(s32[2]{0:T(128)} %pad_add_fusion.2.info_ref, bf16[4,136,128]{2,1,0:T(8,128)(2,1)} %hop.3.mine_ref, bf16[4,136,128]{2,1,0:T(8,128)(2,1)} %copy-done.9, f32[2,4,128,128]{3,2,1,0:T(8,128)} %pad_maximum_fusion.old_ref), custom_call_target="tpu_custom_call" | custom-call | tf_op jit(solution)/shard_map/prox/pallas_call | solution.py:305
  42.2 1.5 collective-permute-done.5.got_ref
  44.4 3.2 %change_first.1 = (f32[1024,128]{1,0:T(8,128)}, bf16[512,128]{1,0:T(8,128)(2,1)}, bf16[512,128]{1,0:T(8,128)(2,1)}) custom-call(bf16[1024,1024]{1,0:T(8,128)(2,1)} %prep.4.x_ref, bf16[4,128,128]{2,1,0:T(8,128)(2,1)} %get-tuple-element.29.mine_ref, bf16[4,128,128]{2,1,0:T(8,128)(2,1)} %copy-done.20), custom_call_target="tpu_custom_call" | custom-call | flops 268435456 | bytes 1048576 | tf_op jit(solution)/shard_map/change_first/pallas_call | solution.py:313
  47.6 1.5 collective-permute-start.8
  49.1 1.5 collective-permute-start.6
  50.6 2.8 %collective-permute-done.8 = bf16[512,128]{1,0:T(8,128)(2,1)S(1)} collective-permute-done((bf16[512,128]{1,0:T(8,128)(2,1)}, bf16[512,128]{1,0:T(8,128)(2,1)S(1)}, u32[]{:S(2)}, u32[]{:S(2)}) %collective-permute-start.8) | collective-permute-done | bytes 131104 | tf_op jit(solution)/shard_map/ppermute | solution.py:233
  53.4 0.9 add_convert_fusion.2.b_ref
  54.3 1.6 collective-permute-start.9
  55.9 0.9 add_convert_fusion.3.a_ref
  56.8 1.6 collective-permute-start.7
  58.4 1.2 pad_add_fusion.5.info_ref
  59.6 3.7 %prep.5.x_ref = bf16[1024,1024]{1,0:T(8,128)(2,1)} custom-call(s32[2]{0:T(128)} %pad_add_fusion.5.info_ref, s32[8,16]{1,0:T(8,128)} %live_ref.5, bf16[1024,2048]{1,0:T(8,128)(2,1)} %x_ref.5), custom_call_target="tpu_custom_call" | custom-call | bytes 4194304 | tf_op jit(solution)/shard_map/prep/pallas_call | solution.py:76
  64.7 4.5 %soft_next.2 = (f32[1024,128]{1,0:T(8,128)}, bf16[128,1024]{1,0:T(8,128)(2,1)}, f32[1024,128]{1,0:T(8,128)}, f32[4,136,128]{2,1,0:T(8,128)}) custom-call(bf16[1024,128]{1,0:T(8,128)(2,1)} %score_ref.1, bf16[512,128]{1,0:T(8,128)(2,1)} %copy-done.4, bf16[512,128]{1,0:T(8,128)(2,1)} %copy-done.17, bf16[512,128]{1,0:T(8,128)(2,1)} %copy-done.2, ...), custom_call_target="tpu_custom_call" | custom-call | flops 134217728 | bytes 1048576 | tf_op jit(solution)/shard_map/soft_next/pallas_call | solution.py:294
  69.2 3.1 %own.4.own_ref = f32[4,136,128]{2,1,0:T(8,128)} custom-call(bf16[128,1024]{1,0:T(8,128)(2,1)} %get-tuple-element.33.res_ref, f32[1024,128]{1,0:T(8,128)} %get-tuple-element.34.spread_ref, bf16[1024,1024]{1,0:T(8,128)(2,1)} %prep.5.x_ref), custom_call_target="tpu_custom_call" | custom-call | flops 134217728 | bytes 1048576 | tf_op jit(solution)/shard_map/own/pallas_call | solution.py:298
  73.0 1.7 %pair.4.mine_ref = bf16[4,136,128]{2,1,0:T(8,128)(2,1)} custom-call(f32[4,136,128]{2,1,0:T(8,128)} %own.4.own_ref, f32[4,136,128]{2,1,0:T(8,128)} %copy-done.7), custom_call_target="tpu_custom_call" | custom-call | tf_op jit(solution)/shard_map/pair/pallas_call | solution.py:299
  74.7 6.3 %collective-permute-done.11.got_ref = bf16[4,136,128]{2,1,0:T(8,128)(2,1)S(1)} collective-permute-done((bf16[4,136,128]{2,1,0:T(8,128)(2,1)}, bf16[4,136,128]{2,1,0:T(8,128)(2,1)S(1)}, u32[]{:S(2)}, u32[]{:S(2)}) %collective-permute-start.11) | collective-permute-done | bytes 139296 | tf_op jit(solution)/shard_map/ppermute | solution.py:233
  81.7 1.7 hop.4.mine_ref
  83.3 1.2 pad_add_fusion.4.info_ref
  84.5 8.1 %collective-permute-done.12.got_ref = bf16[4,136,128]{2,1,0:T(8,128)(2,1)S(1)} collective-permute-done((bf16[4,136,128]{2,1,0:T(8,128)(2,1)}, bf16[4,136,128]{2,1,0:T(8,128)(2,1)S(1)}, u32[]{:S(2)}, u32[]{:S(2)}) %collective-permute-start.12) | collective-permute-done | bytes 139296 | tf_op jit(solution)/shard_map/ppermute | solution.py:233
  93.3 2.1 %prox.4 = (f32[2,4,128,128]{3,2,1,0:T(8,128)}, bf16[4,128,128]{2,1,0:T(8,128)(2,1)}) custom-call(s32[2]{0:T(128)} %pad_add_fusion.4.info_ref, bf16[4,136,128]{2,1,0:T(8,128)(2,1)} %hop.4.mine_ref, bf16[4,136,128]{2,1,0:T(8,128)(2,1)} %copy-done.11, f32[2,4,128,128]{3,2,1,0:T(8,128)} %get-tuple-element.36.old_ref), custom_call_target="tpu_custom_call" | custom-call | tf_op jit(solution)/shard_map/prox/pallas_call | solution.py:305
  95.5 1.5 collective-permute-done.13.got_ref
  97.7 3.3 %change_next.1 = (f32[1024,128]{1,0:T(8,128)}, bf16[512,128]{1,0:T(8,128)(2,1)}, bf16[512,128]{1,0:T(8,128)(2,1)}) custom-call(bf16[1024,1024]{1,0:T(8,128)(2,1)} %prep.5.x_ref, bf16[4,128,128]{2,1,0:T(8,128)(2,1)} %get-tuple-element.37.mine_ref, bf16[4,128,128]{2,1,0:T(8,128)(2,1)} %copy-done.18, f32[1024,128]{1,0:T(8,128)} %get-tuple-element.38.before_ref), custom_call_target="tpu_custom_call" | custom-call | flops 268435456 | bytes 1048576 | tf_op jit(solution)/shard_map/change_next/pallas_call | solution.py:319
  102.0 4.7 %collective-permute-done.16 = bf16[512,128]{1,0:T(8,128)(2,1)S(1)} collective-permute-done((bf16[512,128]{1,0:T(8,128)(2,1)}, bf16[512,128]{1,0:T(8,128)(2,1)S(1)}, u32[]{:S(2)}, u32[]{:S(2)}) %collective-permute-start.16) | collective-permute-done | bytes 131104 | tf_op jit(solution)/shard_map/ppermute | solution.py:233
  106.8 0.9 add_convert_fusion.b_ref
  108.3 0.9 add_convert_fusion.1.a_ref
  109.9 1.3 pad_add_fusion.1.info_ref
  111.1 3.7 %prep.3.x_ref = bf16[1024,1024]{1,0:T(8,128)(2,1)} custom-call(s32[2]{0:T(128)} %pad_add_fusion.1.info_ref, s32[8,16]{1,0:T(8,128)} %live_ref.5, bf16[1024,2048]{1,0:T(8,128)(2,1)} %x_ref.5), custom_call_target="tpu_custom_call" | custom-call | bytes 4194304 | tf_op jit(solution)/shard_map/prep/pallas_call | solution.py:76
  115.6 4.6 %soft_next.3 = (f32[1024,128]{1,0:T(8,128)}, bf16[128,1024]{1,0:T(8,128)(2,1)}, f32[1024,128]{1,0:T(8,128)}, f32[4,136,128]{2,1,0:T(8,128)}) custom-call(f32[1024,128]{1,0:T(8,128)} %get-tuple-element.32.score_ref, bf16[512,128]{1,0:T(8,128)(2,1)} %copy-done.3, bf16[512,128]{1,0:T(8,128)(2,1)} %copy-done.16, bf16[512,128]{1,0:T(8,128)(2,1)} %copy-done.1, ...), custom_call_target="tpu_custom_call" | custom-call | flops 134217728 | bytes 1048576 | tf_op jit(solution)/shard_map/soft_next/pallas_call | solution.py:294
  120.2 3.1 %own.5.own_ref = f32[4,136,128]{2,1,0:T(8,128)} custom-call(bf16[128,1024]{1,0:T(8,128)(2,1)} %get-tuple-element.41.res_ref, f32[1024,128]{1,0:T(8,128)} %get-tuple-element.42.spread_ref, bf16[1024,1024]{1,0:T(8,128)(2,1)} %prep.3.x_ref), custom_call_target="tpu_custom_call" | custom-call | flops 134217728 | bytes 1048576 | tf_op jit(solution)/shard_map/own/pallas_call | solution.py:298
  123.2 0.7 copy-done.6
  123.9 1.7 %pair.5.mine_ref = bf16[4,136,128]{2,1,0:T(8,128)(2,1)} custom-call(f32[4,136,128]{2,1,0:T(8,128)} %own.5.own_ref, f32[4,136,128]{2,1,0:T(8,128)} %copy-done.6), custom_call_target="tpu_custom_call" | custom-call | tf_op jit(solution)/shard_map/pair/pallas_call | solution.py:299
  125.7 6.3 %collective-permute-done.19.got_ref = bf16[4,136,128]{2,1,0:T(8,128)(2,1)S(1)} collective-permute-done((bf16[4,136,128]{2,1,0:T(8,128)(2,1)}, bf16[4,136,128]{2,1,0:T(8,128)(2,1)S(1)}, u32[]{:S(2)}, u32[]{:S(2)}) %collective-permute-start.19) | collective-permute-done | bytes 139296 | tf_op jit(solution)/shard_map/ppermute | solution.py:233
  132.6 1.7 hop.5.mine_ref
  134.3 1.3 pad_add_fusion.info_ref
  135.6 8.0 %collective-permute-done.20.got_ref = bf16[4,136,128]{2,1,0:T(8,128)(2,1)S(1)} collective-permute-done((bf16[4,136,128]{2,1,0:T(8,128)(2,1)}, bf16[4,136,128]{2,1,0:T(8,128)(2,1)S(1)}, u32[]{:S(2)}, u32[]{:S(2)}) %collective-permute-start.20) | collective-permute-done | bytes 139296 | tf_op jit(solution)/shard_map/ppermute | solution.py:233
  144.3 2.1 %prox.5 = (f32[2,4,128,128]{3,2,1,0:T(8,128)}, bf16[4,128,128]{2,1,0:T(8,128)(2,1)}) custom-call(s32[2]{0:T(128)} %pad_add_fusion.info_ref, bf16[4,136,128]{2,1,0:T(8,128)(2,1)} %hop.5.mine_ref, bf16[4,136,128]{2,1,0:T(8,128)(2,1)} %copy-done.10, f32[2,4,128,128]{3,2,1,0:T(8,128)} %get-tuple-element.44.old_ref), custom_call_target="tpu_custom_call" | custom-call | tf_op jit(solution)/shard_map/prox/pallas_call | solution.py:305
  146.4 1.5 collective-permute-done.21.got_ref
  148.6 3.2 %change_last.1 = (f32[512,128]{1,0:T(8,128)}, f32[512,128]{1,0:T(8,128)}) custom-call(bf16[1024,1024]{1,0:T(8,128)(2,1)} %prep.3.x_ref, bf16[4,128,128]{2,1,0:T(8,128)(2,1)} %get-tuple-element.45.mine_ref, bf16[4,128,128]{2,1,0:T(8,128)(2,1)} %copy-done.19, f32[1024,128]{1,0:T(8,128)} %get-tuple-element.46.before_ref), custom_call_target="tpu_custom_call" | custom-call | flops 268435456 | bytes 1048576 | tf_op jit(solution)/shard_map/change_last/pallas_call | solution.py:325
  151.8 1.5 collective-permute-start.22
  153.3 1.5 collective-permute-start.24
  154.8 5.6 %collective-permute-done.22 = f32[512,128]{1,0:T(8,128)S(1)} collective-permute-done((f32[512,128]{1,0:T(8,128)}, f32[512,128]{1,0:T(8,128)S(1)}, u32[]{:S(2)}, u32[]{:S(2)}) %collective-permute-start.22) | collective-permute-done | bytes 262176 | tf_op jit(solution)/shard_map/ppermute | solution.py:233
  160.4 1.0 add.37
  161.4 1.6 collective-permute-start.23
  163.0 1.0 add.39
  163.9 1.6 collective-permute-start.25
  165.5 0.9 slice_bitcast_fusion
  166.4 0.8 copy.10
  167.2 1.8 %collective-permute-done.23 = f32[512,128]{1,0:T(8,128)S(1)} collective-permute-done((f32[512,128]{1,0:T(8,128)S(1)}, f32[512,128]{1,0:T(8,128)S(1)}, u32[]{:S(2)}, u32[]{:S(2)}) %collective-permute-start.23) | collective-permute-done | bytes 262176 | tf_op jit(solution)/shard_map/ppermute | solution.py:233
  169.0 2.2 %collective-permute-done.25 = f32[512,128]{1,0:T(8,128)S(1)} collective-permute-done((f32[512,128]{1,0:T(8,128)S(1)}, f32[512,128]{1,0:T(8,128)S(1)}, u32[]{:S(2)}, u32[]{:S(2)}) %collective-permute-start.25) | collective-permute-done | bytes 262176 | tf_op jit(solution)/shard_map/ppermute | solution.py:233
  171.3 0.8 maximum_add_fusion
  (76 shorter events, 12.0 us)
Async XLA Ops:
  7.0 4.8 %copy-start.21 = (f32[2,128,128]{2,1,0:T(8,128)S(1)}, f32[2,128,128]{2,1,0:T(8,128)}, u32[]{:S(2)}) copy-start(f32[2,128,128]{2,1,0:T(8,128)} %param.10) | copy-start | bytes 393220
  11.3 6.3 %collective-permute-start = (f32[4,136,128]{2,1,0:T(8,128)}, f32[4,136,128]{2,1,0:T(8,128)S(1)}, u32[]{:S(2)}, u32[]{:S(2)}) collective-permute-start(f32[4,136,128]{2,1,0:T(8,128)} %get-tuple-element.28), channel_id=1, source_target_pairs={{0,1},{1,0},{2,3},{3,2},{4,5},{5,4},{6,7},{7,6},{8,9},{9,8},{10,11... | collective-permute-start | bytes 835592 | tf_op jit(solution)/shard_map/ppermute | solution.py:233
  11.9 8.2 %collective-permute-start.3 = (bf16[2,1,128,128]{3,2,1,0:T(8,128)(2,1)S(1)}, bf16[2,1,128,128]{3,2,1,0:T(8,128)(2,1)S(1)}, u32[]{:S(2)}, u32[]{:S(2)}) collective-permute-start(bf16[2,1,128,128]{3,2,1,0:T(8,128)(2,1)S(1)} %fusion), channel_id=1, source_target_pairs={{0,2},{1,3},{2,0},{3,1},{4,6},{5,7},{6,4},{7,5},{8,10},{9,11},{10,... | collective-permute-start | bytes 196616 | tf_op jit(solution)/shard_map/ppermute | solution.py:233
  17.6 0.7 copy-start.5
  20.1 8.8 %collective-permute-start.1 = (bf16[4,136,128]{2,1,0:T(8,128)(2,1)}, bf16[4,136,128]{2,1,0:T(8,128)(2,1)S(1)}, u32[]{:S(2)}, u32[]{:S(2)}) collective-permute-start(bf16[4,136,128]{2,1,0:T(8,128)(2,1)} %pair.3.mine_ref), channel_id=1, source_target_pairs={{0,2},{1,3},{2,0},{3,1},{4,6},{5,7},{6,4},{7,5},{8,10},{9,11},{10,... | collective-permute-start | bytes 417800 | tf_op jit(solution)/shard_map/ppermute | solution.py:233
  20.1 11.6 %collective-permute-start.4 = (bf16[2,2,128,128]{3,2,1,0:T(8,128)(2,1)S(1)}, bf16[2,2,128,128]{3,2,1,0:T(8,128)(2,1)S(1)}, u32[]{:S(2)}, u32[]{:S(2)}) collective-permute-start(bf16[2,2,128,128]{3,2,1,0:T(8,128)(2,1)S(1)} %pad_maximum_fusion.1), channel_id=1, source_target_pairs={{0,4},{1,5},{2,6},{3,7},{4,0},{5,1},{6,2},{7,3},{8,12},{9,13},{10,... | collective-permute-start | bytes 393224 | tf_op jit(solution)/shard_map/ppermute | solution.py:233
  28.9 0.7 copy-start.8
  31.2 8.2 %collective-permute-start.2 = (bf16[4,136,128]{2,1,0:T(8,128)(2,1)}, bf16[4,136,128]{2,1,0:T(8,128)(2,1)S(1)}, u32[]{:S(2)}, u32[]{:S(2)}) collective-permute-start(bf16[4,136,128]{2,1,0:T(8,128)(2,1)} %hop.3.mine_ref), channel_id=1, source_target_pairs={{0,4},{1,5},{2,6},{3,7},{4,0},{5,1},{6,2},{7,3},{8,12},{9,13},{10,... | collective-permute-start | bytes 417800 | tf_op jit(solution)/shard_map/ppermute | solution.py:233
  39.4 0.7 copy-start.9
  42.2 1.6 collective-permute-start.5
  43.8 0.6 copy-start.20
  47.6 5.8 %collective-permute-start.8 = (bf16[512,128]{1,0:T(8,128)(2,1)}, bf16[512,128]{1,0:T(8,128)(2,1)S(1)}, u32[]{:S(2)}, u32[]{:S(2)}) collective-permute-start(bf16[512,128]{1,0:T(8,128)(2,1)} %get-tuple-element.31), channel_id=1, source_target_pairs={{0,16},{8,24},{16,0},{24,8},{1,17},{9,25},{17,1},{25,9},{2,18},{10... | collective-permute-start | bytes 393224 | tf_op jit(solution)/shard_map/ppermute | solution.py:233
  49.1 6.8 %collective-permute-start.6 = (bf16[512,128]{1,0:T(8,128)(2,1)}, bf16[512,128]{1,0:T(8,128)(2,1)S(1)}, u32[]{:S(2)}, u32[]{:S(2)}) collective-permute-start(bf16[512,128]{1,0:T(8,128)(2,1)} %get-tuple-element.30), channel_id=1, source_target_pairs={{0,8},{8,0},{16,24},{24,16},{1,9},{9,1},{17,25},{25,17},{2,10},{10... | collective-permute-start | bytes 393224 | tf_op jit(solution)/shard_map/ppermute | solution.py:233
  54.3 9.0 %copy-start.2 = (bf16[512,128]{1,0:T(8,128)(2,1)}, bf16[512,128]{1,0:T(8,128)(2,1)S(1)}, u32[]{:S(2)}) copy-start(bf16[512,128]{1,0:T(8,128)(2,1)S(1)} %add_convert_fusion.2.b_ref) | copy-start | bytes 393220
  54.3 9.1 %collective-permute-start.9 = (bf16[512,128]{1,0:T(8,128)(2,1)S(1)}, bf16[512,128]{1,0:T(8,128)(2,1)S(1)}, u32[]{:S(2)}, u32[]{:S(2)}) collective-permute-start(bf16[512,128]{1,0:T(8,128)(2,1)S(1)} %add_convert_fusion.2.b_ref), channel_id=1, source_target_pairs={{0,8},{8,0},{16,24},{24,16},{1,9},{9,1},{17,25},{25,17},{2,10},{10... | collective-permute-start | bytes 393224 | tf_op jit(solution)/shard_map/ppermute | solution.py:233
  56.8 6.5 %copy-start.4 = (bf16[512,128]{1,0:T(8,128)(2,1)}, bf16[512,128]{1,0:T(8,128)(2,1)S(1)}, u32[]{:S(2)}) copy-start(bf16[512,128]{1,0:T(8,128)(2,1)S(1)} %add_convert_fusion.3.a_ref) | copy-start | bytes 393220
  56.8 6.6 %collective-permute-start.7 = (bf16[512,128]{1,0:T(8,128)(2,1)S(1)}, bf16[512,128]{1,0:T(8,128)(2,1)S(1)}, u32[]{:S(2)}, u32[]{:S(2)}) collective-permute-start(bf16[512,128]{1,0:T(8,128)(2,1)S(1)} %add_convert_fusion.3.a_ref), channel_id=1, source_target_pairs={{0,16},{8,24},{16,0},{24,8},{1,17},{9,25},{17,1},{25,9},{2,18},{10... | collective-permute-start | bytes 393224 | tf_op jit(solution)/shard_map/ppermute | solution.py:233
  63.4 0.6 copy-start.15
  64.0 0.7 copy-start.17
  69.2 3.1 %collective-permute-start.10 = (f32[4,136,128]{2,1,0:T(8,128)}, f32[4,136,128]{2,1,0:T(8,128)S(1)}, u32[]{:S(2)}, u32[]{:S(2)}) collective-permute-start(f32[4,136,128]{2,1,0:T(8,128)} %get-tuple-element.35), channel_id=1, source_target_pairs={{0,1},{1,0},{2,3},{3,2},{4,5},{5,4},{6,7},{7,6},{8,9},{9,8},{10,11... | collective-permute-start | bytes 835592 | tf_op jit(solution)/shard_map/ppermute | solution.py:233
  72.3 0.7 copy-start.7
  74.7 6.3 %collective-permute-start.11 = (bf16[4,136,128]{2,1,0:T(8,128)(2,1)}, bf16[4,136,128]{2,1,0:T(8,128)(2,1)S(1)}, u32[]{:S(2)}, u32[]{:S(2)}) collective-permute-start(bf16[4,136,128]{2,1,0:T(8,128)(2,1)} %pair.4.mine_ref), channel_id=1, source_target_pairs={{0,2},{1,3},{2,0},{3,1},{4,6},{5,7},{6,4},{7,5},{8,10},{9,11},{10,... | collective-permute-start | bytes 417800 | tf_op jit(solution)/shard_map/ppermute | solution.py:233
  81.0 0.7 copy-start.12
  83.3 9.3 %collective-permute-start.12 = (bf16[4,136,128]{2,1,0:T(8,128)(2,1)}, bf16[4,136,128]{2,1,0:T(8,128)(2,1)S(1)}, u32[]{:S(2)}, u32[]{:S(2)}) collective-permute-start(bf16[4,136,128]{2,1,0:T(8,128)(2,1)} %hop.4.mine_ref), channel_id=1, source_target_pairs={{0,4},{1,5},{2,6},{3,7},{4,0},{5,1},{6,2},{7,3},{8,12},{9,13},{10,... | collective-permute-start | bytes 417800 | tf_op jit(solution)/shard_map/ppermute | solution.py:233
  92.7 0.7 copy-start.11
  95.5 1.6 collective-permute-start.13
  97.0 0.7 copy-start.18
  101.0 5.8 %collective-permute-start.16 = (bf16[512,128]{1,0:T(8,128)(2,1)}, bf16[512,128]{1,0:T(8,128)(2,1)S(1)}, u32[]{:S(2)}, u32[]{:S(2)}) collective-permute-start(bf16[512,128]{1,0:T(8,128)(2,1)} %get-tuple-element.40), channel_id=1, source_target_pairs={{0,16},{8,24},{16,0},{24,8},{1,17},{9,25},{17,1},{25,9},{2,18},{10... | collective-permute-start | bytes 393224 | tf_op jit(solution)/shard_map/ppermute | solution.py:233
  101.5 6.8 %collective-permute-start.14 = (bf16[512,128]{1,0:T(8,128)(2,1)}, bf16[512,128]{1,0:T(8,128)(2,1)S(1)}, u32[]{:S(2)}, u32[]{:S(2)}) collective-permute-start(bf16[512,128]{1,0:T(8,128)(2,1)} %get-tuple-element.39), channel_id=1, source_target_pairs={{0,8},{8,0},{16,24},{24,16},{1,9},{9,1},{17,25},{25,17},{2,10},{10... | collective-permute-start | bytes 393224 | tf_op jit(solution)/shard_map/ppermute | solution.py:233
  107.7 7.1 %copy-start.1 = (bf16[512,128]{1,0:T(8,128)(2,1)}, bf16[512,128]{1,0:T(8,128)(2,1)S(1)}, u32[]{:S(2)}) copy-start(bf16[512,128]{1,0:T(8,128)(2,1)S(1)} %add_convert_fusion.b_ref) | copy-start | bytes 393220
  107.7 7.2 %collective-permute-start.17 = (bf16[512,128]{1,0:T(8,128)(2,1)S(1)}, bf16[512,128]{1,0:T(8,128)(2,1)S(1)}, u32[]{:S(2)}, u32[]{:S(2)}) collective-permute-start(bf16[512,128]{1,0:T(8,128)(2,1)S(1)} %add_convert_fusion.b_ref), channel_id=1, source_target_pairs={{0,8},{8,0},{16,24},{24,16},{1,9},{9,1},{17,25},{25,17},{2,10},{10... | collective-permute-start | bytes 393224 | tf_op jit(solution)/shard_map/ppermute | solution.py:233
  109.3 5.6 %copy-start.3 = (bf16[512,128]{1,0:T(8,128)(2,1)}, bf16[512,128]{1,0:T(8,128)(2,1)S(1)}, u32[]{:S(2)}) copy-start(bf16[512,128]{1,0:T(8,128)(2,1)S(1)} %add_convert_fusion.1.a_ref) | copy-start | bytes 393220
  109.3 5.6 %collective-permute-start.15 = (bf16[512,128]{1,0:T(8,128)(2,1)S(1)}, bf16[512,128]{1,0:T(8,128)(2,1)S(1)}, u32[]{:S(2)}, u32[]{:S(2)}) collective-permute-start(bf16[512,128]{1,0:T(8,128)(2,1)S(1)} %add_convert_fusion.1.a_ref), channel_id=1, source_target_pairs={{0,16},{8,24},{16,0},{24,8},{1,17},{9,25},{17,1},{25,9},{2,18},{10... | collective-permute-start | bytes 393224 | tf_op jit(solution)/shard_map/ppermute | solution.py:233
  114.9 0.7 copy-start.14
  114.9 0.7 copy-start.16
  120.2 3.1 %collective-permute-start.18 = (f32[4,136,128]{2,1,0:T(8,128)}, f32[4,136,128]{2,1,0:T(8,128)S(1)}, u32[]{:S(2)}, u32[]{:S(2)}) collective-permute-start(f32[4,136,128]{2,1,0:T(8,128)} %get-tuple-element.43), channel_id=1, source_target_pairs={{0,1},{1,0},{2,3},{3,2},{4,5},{5,4},{6,7},{7,6},{8,9},{9,8},{10,11... | collective-permute-start | bytes 835592 | tf_op jit(solution)/shard_map/ppermute | solution.py:233
  123.2 0.7 copy-start.6
  125.7 6.3 %collective-permute-start.19 = (bf16[4,136,128]{2,1,0:T(8,128)(2,1)}, bf16[4,136,128]{2,1,0:T(8,128)(2,1)S(1)}, u32[]{:S(2)}, u32[]{:S(2)}) collective-permute-start(bf16[4,136,128]{2,1,0:T(8,128)(2,1)} %pair.5.mine_ref), channel_id=1, source_target_pairs={{0,2},{1,3},{2,0},{3,1},{4,6},{5,7},{6,4},{7,5},{8,10},{9,11},{10,... | collective-permute-start | bytes 417800 | tf_op jit(solution)/shard_map/ppermute | solution.py:233
  132.0 0.7 copy-start.13
  134.3 9.3 %collective-permute-start.20 = (bf16[4,136,128]{2,1,0:T(8,128)(2,1)}, bf16[4,136,128]{2,1,0:T(8,128)(2,1)S(1)}, u32[]{:S(2)}, u32[]{:S(2)}) collective-permute-start(bf16[4,136,128]{2,1,0:T(8,128)(2,1)} %hop.5.mine_ref), channel_id=1, source_target_pairs={{0,4},{1,5},{2,6},{3,7},{4,0},{5,1},{6,2},{7,3},{8,12},{9,13},{10,... | collective-permute-start | bytes 417800 | tf_op jit(solution)/shard_map/ppermute | solution.py:233
  143.6 0.7 copy-start.10
  146.4 1.6 collective-permute-start.21
  148.0 0.6 copy-start.19
  151.8 19.5 %copy-start = (bf16[1024,128]{1,0:T(8,128)(2,1)S(1)}, bf16[1024,128]{1,0:T(8,128)(2,1)}, u32[]{:S(2)}) copy-start(bf16[1024,128]{1,0:T(8,128)(2,1)} %score_ref.1) | copy-start | bytes 786436
  151.8 8.6 %collective-permute-start.22 = (f32[512,128]{1,0:T(8,128)}, f32[512,128]{1,0:T(8,128)S(1)}, u32[]{:S(2)}, u32[]{:S(2)}) collective-permute-start(f32[512,128]{1,0:T(8,128)} %get-tuple-element.47), channel_id=1, source_target_pairs={{0,8},{8,0},{16,24},{24,16},{1,9},{9,1},{17,25},{25,17},{2,10},{10... | collective-permute-start | bytes 786440 | tf_op jit(solution)/shard_map/ppermute | solution.py:233
  153.3 9.7 %collective-permute-start.24 = (f32[512,128]{1,0:T(8,128)}, f32[512,128]{1,0:T(8,128)S(1)}, u32[]{:S(2)}, u32[]{:S(2)}) collective-permute-start(f32[512,128]{1,0:T(8,128)} %get-tuple-element.48), channel_id=1, source_target_pairs={{0,16},{8,24},{16,0},{24,8},{1,17},{9,25},{17,1},{25,9},{2,18},{10... | collective-permute-start | bytes 786440 | tf_op jit(solution)/shard_map/ppermute | solution.py:233
  161.4 7.6 %collective-permute-start.23 = (f32[512,128]{1,0:T(8,128)S(1)}, f32[512,128]{1,0:T(8,128)S(1)}, u32[]{:S(2)}, u32[]{:S(2)}) collective-permute-start(f32[512,128]{1,0:T(8,128)S(1)} %add.37), channel_id=1, source_target_pairs={{0,16},{8,24},{16,0},{24,8},{1,17},{9,25},{17,1},{25,9},{2,18},{10... | collective-permute-start | bytes 786440 | tf_op jit(solution)/shard_map/ppermute | solution.py:233
  163.9 7.3 %collective-permute-start.25 = (f32[512,128]{1,0:T(8,128)S(1)}, f32[512,128]{1,0:T(8,128)S(1)}, u32[]{:S(2)}, u32[]{:S(2)}) collective-permute-start(f32[512,128]{1,0:T(8,128)S(1)} %add.39), channel_id=1, source_target_pairs={{0,8},{8,0},{16,24},{24,16},{1,9},{9,1},{17,25},{25,17},{2,10},{10... | collective-permute-start | bytes 786440 | tf_op jit(solution)/shard_map/ppermute | solution.py:233

commit v2 on v1

--- a/solution.py
+++ b/solution.py
@@ -31,23 +31,36 @@
 
 
 def call(body, outs, in_specs, name, flops=0, nbytes=0, **kw):
-    return pl.pallas_call(
+    f = pl.pallas_call(
         body,
         out_shape=outs,
         in_specs=in_specs,
         out_specs=jax.tree.map(lambda _: pl.BlockSpec(memory_space=pltpu.VMEM), outs),
         name=name,
         cost_estimate=pl.CostEstimate(flops=flops, bytes_accessed=nbytes, transcendentals=0),
+        compiler_params=pltpu.CompilerParams(vmem_limit_bytes=16 << 20),
         **kw,
     )
 
+    def run(*args):
+        return f(
+            *(
+                pltpu.with_memory_space_constraint(x, pltpu.VMEM)
+                if spec.memory_space == pltpu.VMEM
+                else x
+                for spec, x in zip(in_specs, args, strict=True)
+            )
+        )
+
+    return run
+
 
 def sds(shape, dtype):
-    return jax.ShapeDtypeStruct(shape, dtype)
-
-
-def prep_body(info_ref, live_ref, x_ref, out_ref, buf, sems):
-    chosen, core = info_ref[0], info_ref[1]
+    return pltpu.VMEM(shape, dtype)
+
+
+def prep_body(step, order_ref, live_ref, x_ref, out_ref, buf, sems):
+    chosen, core = order_ref[step, 0], lax.axis_index("ex") % 2
     rows = out_ref.shape[0]
     tiles = BLOCK // TILE
 
@@ -70,11 +83,10 @@
             out_ref[here, k * TILE : (k + 1) * TILE] = (tile.astype(F32) * live).astype(BF16)
 
 
-def prep(x_values, tile_live, chosen, core):
+def prep(x_values, tile_live, order, step):
     rows = x_values.shape[0]
-    info = jnp.stack([chosen, core])
     return call(
-        prep_body,
+        functools.partial(prep_body, step),
         sds((rows, BLOCK), BF16),
         smem(2) + [pl.BlockSpec(memory_space=pl.ANY)],
         "prep",
@@ -83,7 +95,7 @@
             pltpu.VMEM((rows, BLOCK), BF16),
             pltpu.SemaphoreType.DMA((rows // TILE,)),
         ],
-    )(info, tile_live, x_values)
+    )(order, tile_live, x_values)
 
 
 def prep_general(x_values, tile_live, chosen, core, own):
@@ -182,11 +194,12 @@
         encode(k, *decode_sum(k, mine_ref, got_ref), out_ref)
 
 
-def prox_body(count, info_ref, mine_ref, got_ref, old_ref, new_ref, delta_ref):
-    chosen, place = info_ref[0], info_ref[1]
+def prox_body(count, step, aligned, order_ref, mine_ref, got_ref, old_ref, new_ref, delta_ref):
+    chosen = order_ref[step, 0]
+    place = lax.axis_index("ex") // 2 if aligned else 0
     new_ref[1 - chosen] = old_ref[1 - chosen]
     for j in range(NB):
-        k = jnp.bitwise_xor(place, j)
+        k = jnp.bitwise_xor(place, j) if aligned else j
         grad, curv = decode_sum(k, mine_ref, got_ref)
         curv = curv / count + ridge
         old = old_ref[chosen, j]
@@ -283,7 +296,7 @@
     for step in range(STEPS):
         chosen = order[step, 0]
         if aligned:
-            x = prep(x_values, tile_live, chosen, core)
+            x = prep(x_values, tile_live, order, step)
         else:
             x = prep_general(x_values, tile_live, chosen, core, own)
         if step == 0:
@@ -301,13 +314,12 @@
             got = flip(message, "ex", bit)
             message = call(hop_body, m_shape, vmem(2), "hop")(message, got)
         got = flip(message, "ex", z_bits[-1])
-        info = jnp.stack([chosen, place if aligned else jnp.int32(0)])
         old, delta = call(
-            functools.partial(prox_body, count),
+            functools.partial(prox_body, count, step, aligned),
             (sds(old.shape, F32), sds((NB, C, TILE), BF16)),
             smem(1) + vmem(3),
             "prox",
-        )(info, message, got, old)
+        )(order, message, got, old)
         got = flip(delta, "ex", 1)
         if step == 0:
             total, a, b = call(

time: 173 us -> 119 us (0.69)
  Pallas kernels: 60.1 us -> 16.6 us
  other arithmetic: 15 us -> 2.11 us
  starting transfers between devices: 21.2 us -> 29.6 us
  local copies, waits for them, and re-layouts: 13.2 us -> 6.06 us
    pallas_call x21, Pallas kernels: 60.1 us -> 16.6 us  [run(): f(*(pltpu.with_memory_space_constraint(x, pltpu.VMEM) if spec.memory_spac...]
    ppermute x26, starting transfers between devices: 21.2 us -> 29.6 us  [flip(): return lax.ppermute(x, axis, [(i, i ^ bit) for i in range(n)])]
    another operation x6 -> x0, other arithmetic: 7.48 us -> none  [the longest x3 3.78 us: local(): info = jnp.stack([chosen, place if aligned else jnp.int32(0)])]
    unnamed x46 -> x17, local copies, waits for them, and re-layouts: 10.8 us -> 6.05 us
    convert_element_type x4, other arithmetic: 3.78 us -> 0.15 us  [add_as(): return (x.astype(F32) + y.astype(F32)).astype(dtype)]
    add x2, other arithmetic: 1.98 us -> 0.06 us  [add_as(): return (x.astype(F32) + y.astype(F32)).astype(dtype)]
  transfers between devices with their start and end apart: 26 -> 26, of which waited for: 14 -> 22; matrix products, arithmetic and copies ran while one was open for 9% -> 3% of each run, Pallas kernels for 12% -> 4%
where the time goes in v2:
time: 119 us; the launch traced here: 118 us
  waiting for transfers between devices  63 us (53%)
  starting transfers between devices  29.6 us (25%)
  Pallas kernels  16.6 us (14%)
  local copies, waits for them, and re-layouts  6.06 us (5%)
  other arithmetic  2.11 us (2%)
    ppermute x26, waiting for transfers between devices, flip(): return lax.ppermute(x, axis, [(i, i ^ bit) for i in range(n)])  63 us
    ppermute x26, starting transfers between devices, flip(): return lax.ppermute(x, axis, [(i, i ^ bit) for i in range(n)])  29.6 us
    pallas_call x21, Pallas kernels, run(): f(*(pltpu.with_memory_space_constraint(x, pltpu.VMEM) if spec.memory_spac...  16.6 us
    unnamed x17, local copies, waits for them, and re-layouts  6.05 us
  transfers between devices with their start and end apart: 26, of which 22 were waited for; matrix products, arithmetic and copies ran while one was open for 3% of the time, Pallas kernels for 4%

profile of v2, /device:TPU:0, one launch (start us, length us, event | category | flops | bytes accessed | tf_op | source)
XLA Modules:
  0.0 118.3 jit_solution(13860261235698238076)
XLA Ops:
  0.6 0.7 copy.8.order_ref
  1.4 2.2 %copy-done = bf16[1024,2048]{1,0:T(8,128)(2,1)S(1)} copy-done((bf16[1024,2048]{1,0:T(8,128)(2,1)S(1)}, bf16[1024,2048]{1,0:T(8,128)(2,1)}, u32[]{:S(2)}) %copy-start) | copy-done | bytes 4194328
  3.6 0.7 copy-done.3
  4.3 1.5 %prep.4.x_ref = bf16[1024,1024]{1,0:T(8,128)(2,1)S(1)} custom-call(s32[3,1]{1,0:T(4,128)S(1)} %copy.8.order_ref, s32[8,16]{1,0:T(8,128)S(1)} %copy-done.3, bf16[1024,2048]{1,0:T(8,128)(2,1)S(1)} %copy-done), custom_call_target="tpu_custom_call" | custom-call | bytes 4194304 | tf_op jit(solution)/shard_map/prep/pallas_call | solution.py:46
  5.7 2.5 %soft_first.1 = (bf16[128,1024]{1,0:T(8,128)(2,1)S(1)}, f32[1024,128]{1,0:T(8,128)S(1)}, f32[4,136,128]{2,1,0:T(8,128)}) custom-call(bf16[1024,128]{1,0:T(8,128)(2,1)S(1)} %copy-done.2, s32[8,128]{1,0:T(8,128)S(1)} %bitcast.15, bf16[1024,1024]{1,0:T(8,128)(2,1)S(1)} %prep.4.x_ref), custom_call_target="tpu_custom_call" | custom-call | flops 134217728 | bytes 1048576 | tf_op jit(solution)/shard_map/soft_first/pallas_call | solution.py:46
  8.2 0.5 collective-permute-start
  8.7 1.7 %copy.10 = f32[2,128,128]{1,2,0:T(8,128)} copy(f32[2,128,128]{2,1,0:T(8,128)} %param.10) | data formatting | bytes 262144 | tf_op args[4]
  10.3 0.9 fusion
  11.2 2.6 %collective-permute-start.3 = (bf16[2,1,128,128]{3,2,1,0:T(8,128)(2,1)S(1)}, bf16[2,1,128,128]{3,2,1,0:T(8,128)(2,1)S(1)}, u32[]{:S(2)}, u32[]{:S(2)}) collective-permute-start(bf16[2,1,128,128]{3,2,1,0:T(8,128)(2,1)S(1)} %fusion), channel_id=1, source_target_pairs={{0,2},{1,3},{2,0},{3,1},{4,6},{5,7},{6,4},{7,5},{8,10},{9,11},{10,... | collective-permute-start | bytes 196616 | tf_op jit(solution)/shard_map/ppermute | solution.py:246
  13.9 0.5 own.3.own_ref
  14.5 2.1 %collective-permute-done.3 = bf16[2,1,128,128]{3,2,1,0:T(8,128)(2,1)S(1)} collective-permute-done((bf16[2,1,128,128]{3,2,1,0:T(8,128)(2,1)S(1)}, bf16[2,1,128,128]{3,2,1,0:T(8,128)(2,1)S(1)}, u32[]{:S(2)}, u32[]{:S(2)}) %collective-permute-start.3) | collective-permute-done | bytes 65568 | tf_op jit(solution)/shard_map/ppermute | solution.py:246
  16.7 2.8 %collective-permute-start.4 = (bf16[2,2,128,128]{3,2,1,0:T(8,128)(2,1)S(1)}, bf16[2,2,128,128]{3,2,1,0:T(8,128)(2,1)S(1)}, u32[]{:S(2)}, u32[]{:S(2)}) collective-permute-start(bf16[2,2,128,128]{3,2,1,0:T(8,128)(2,1)S(1)} %pad_maximum_fusion.1), channel_id=1, source_target_pairs={{0,4},{1,5},{2,6},{3,7},{4,0},{5,1},{6,2},{7,3},{8,12},{9,13},{10,... | collective-permute-start | bytes 393224 | tf_op jit(solution)/shard_map/ppermute | solution.py:246
  19.5 2.4 %collective-permute-done.1.got_ref = bf16[4,136,128]{2,1,0:T(8,128)(2,1)S(1)} collective-permute-done((bf16[4,136,128]{2,1,0:T(8,128)(2,1)S(1)}, bf16[4,136,128]{2,1,0:T(8,128)(2,1)S(1)}, u32[]{:S(2)}, u32[]{:S(2)}) %collective-permute-start.1) | collective-permute-done | bytes 139296 | tf_op jit(solution)/shard_map/ppermute | solution.py:246
  22.0 1.8 %collective-permute-start.2 = (bf16[4,136,128]{2,1,0:T(8,128)(2,1)S(1)}, bf16[4,136,128]{2,1,0:T(8,128)(2,1)S(1)}, u32[]{:S(2)}, u32[]{:S(2)}) collective-permute-start(bf16[4,136,128]{2,1,0:T(8,128)(2,1)S(1)} %hop.3.mine_ref), channel_id=1, source_target_pairs={{0,4},{1,5},{2,6},{3,7},{4,0},{5,1},{6,2},{7,3},{8,12},{9,13},{10,... | collective-permute-start | bytes 417800 | tf_op jit(solution)/shard_map/ppermute | solution.py:246
  23.7 5.5 %collective-permute-done.4 = bf16[2,2,128,128]{3,2,1,0:T(8,128)(2,1)S(1)} collective-permute-done((bf16[2,2,128,128]{3,2,1,0:T(8,128)(2,1)S(1)}, bf16[2,2,128,128]{3,2,1,0:T(8,128)(2,1)S(1)}, u32[]{:S(2)}, u32[]{:S(2)}) %collective-permute-start.4) | collective-permute-done | bytes 131104 | tf_op jit(solution)/shard_map/ppermute | solution.py:246
  29.4 2.4 %collective-permute-done.2.got_ref = bf16[4,136,128]{2,1,0:T(8,128)(2,1)S(1)} collective-permute-done((bf16[4,136,128]{2,1,0:T(8,128)(2,1)S(1)}, bf16[4,136,128]{2,1,0:T(8,128)(2,1)S(1)}, u32[]{:S(2)}, u32[]{:S(2)}) %collective-permute-start.2) | collective-permute-done | bytes 139296 | tf_op jit(solution)/shard_map/ppermute | solution.py:246
  31.8 0.7 prox.3
  32.6 1.3 %collective-permute-done.5.got_ref = bf16[4,128,128]{2,1,0:T(8,128)(2,1)S(1)} collective-permute-done((bf16[4,128,128]{2,1,0:T(8,128)(2,1)S(1)}, bf16[4,128,128]{2,1,0:T(8,128)(2,1)S(1)}, u32[]{:S(2)}, u32[]{:S(2)}) %collective-permute-start.5) | collective-permute-done | bytes 131104 | tf_op jit(solution)/shard_map/ppermute | solution.py:246
  33.9 0.7 change_first.1
  34.6 1.5 %collective-permute-start.8 = (bf16[512,128]{1,0:T(8,128)(2,1)S(1)}, bf16[512,128]{1,0:T(8,128)(2,1)S(1)}, u32[]{:S(2)}, u32[]{:S(2)}) collective-permute-start(bf16[512,128]{1,0:T(8,128)(2,1)S(1)} %get-tuple-element.31), channel_id=1, source_target_pairs={{0,16},{8,24},{16,0},{24,8},{1,17},{9,25},{17,1},{25,9},{2,18},{10... | collective-permute-start | bytes 393224 | tf_op jit(solution)/shard_map/ppermute | solution.py:246
  36.2 1.5 %collective-permute-start.6 = (bf16[512,128]{1,0:T(8,128)(2,1)S(1)}, bf16[512,128]{1,0:T(8,128)(2,1)S(1)}, u32[]{:S(2)}, u32[]{:S(2)}) collective-permute-start(bf16[512,128]{1,0:T(8,128)(2,1)S(1)} %get-tuple-element.30), channel_id=1, source_target_pairs={{0,8},{8,0},{16,24},{24,16},{1,9},{9,1},{17,25},{25,17},{2,10},{10... | collective-permute-start | bytes 393224 | tf_op jit(solution)/shard_map/ppermute | solution.py:246
  37.6 2.6 %collective-permute-done.8 = bf16[512,128]{1,0:T(8,128)(2,1)S(1)} collective-permute-done((bf16[512,128]{1,0:T(8,128)(2,1)S(1)}, bf16[512,128]{1,0:T(8,128)(2,1)S(1)}, u32[]{:S(2)}, u32[]{:S(2)}) %collective-permute-start.8) | collective-permute-done | bytes 131104 | tf_op jit(solution)/shard_map/ppermute | solution.py:246
  40.3 1.5 %collective-permute-start.9 = (bf16[512,128]{1,0:T(8,128)(2,1)S(1)}, bf16[512,128]{1,0:T(8,128)(2,1)S(1)}, u32[]{:S(2)}, u32[]{:S(2)}) collective-permute-start(bf16[512,128]{1,0:T(8,128)(2,1)S(1)} %add_convert_fusion.2.b_ref), channel_id=1, source_target_pairs={{0,8},{8,0},{16,24},{24,16},{1,9},{9,1},{17,25},{25,17},{2,10},{10... | collective-permute-start | bytes 393224 | tf_op jit(solution)/shard_map/ppermute | solution.py:246
  41.8 1.6 %collective-permute-start.7 = (bf16[512,128]{1,0:T(8,128)(2,1)S(1)}, bf16[512,128]{1,0:T(8,128)(2,1)S(1)}, u32[]{:S(2)}, u32[]{:S(2)}) collective-permute-start(bf16[512,128]{1,0:T(8,128)(2,1)S(1)} %add_convert_fusion.3.a_ref), channel_id=1, source_target_pairs={{0,16},{8,24},{16,0},{24,8},{1,17},{9,25},{17,1},{25,9},{2,18},{10... | collective-permute-start | bytes 393224 | tf_op jit(solution)/shard_map/ppermute | solution.py:246
  43.4 1.5 %prep.5.x_ref = bf16[1024,1024]{1,0:T(8,128)(2,1)S(1)} custom-call(s32[3,1]{1,0:T(4,128)S(1)} %copy.8.order_ref, s32[8,16]{1,0:T(8,128)S(1)} %copy-done.4, bf16[1024,2048]{1,0:T(8,128)(2,1)S(1)} %copy-done.1), custom_call_target="tpu_custom_call" | custom-call | bytes 4194304 | tf_op jit(solution)/shard_map/prep/pallas_call | solution.py:46
  44.9 0.4 collective-permute-done.9.rb_ref
  45.3 1.6 %collective-permute-done.7.ra_ref = bf16[512,128]{1,0:T(8,128)(2,1)S(1)} collective-permute-done((bf16[512,128]{1,0:T(8,128)(2,1)S(1)}, bf16[512,128]{1,0:T(8,128)(2,1)S(1)}, u32[]{:S(2)}, u32[]{:S(2)}) %collective-permute-start.7) | collective-permute-done | bytes 131104 | tf_op jit(solution)/shard_map/ppermute | solution.py:246
  46.9 1.7 %soft_next.2 = (f32[1024,128]{1,0:T(8,128)S(1)}, bf16[128,1024]{1,0:T(8,128)(2,1)S(1)}, f32[1024,128]{1,0:T(8,128)S(1)}, f32[4,136,128]{2,1,0:T(8,128)S(1)}) custom-call(bf16[1024,128]{1,0:T(8,128)(2,1)S(1)} %copy-done.2, bf16[512,128]{1,0:T(8,128)(2,1)S(1)} %add_convert_fusion.3.a_ref, bf16[512,128]{1,0:T(8,128)(2,1)S(1)} %collective-permute-done.7.ra_ref, ...), custom_call_target="tpu_custom_call" | custom-call | flops 134217728 | bytes 1048576 | tf_op jit(solution)/shard_map/soft_next/pallas_call | solution.py:46
  48.7 0.5 own.4.own_ref
  49.2 1.0 collective-permute-done.10.got_ref
  50.2 0.7 collective-permute-start.11
  50.9 5.1 %collective-permute-done.11.got_ref = bf16[4,136,128]{2,1,0:T(8,128)(2,1)S(1)} collective-permute-done((bf16[4,136,128]{2,1,0:T(8,128)(2,1)S(1)}, bf16[4,136,128]{2,1,0:T(8,128)(2,1)S(1)}, u32[]{:S(2)}, u32[]{:S(2)}) %collective-permute-start.11) | collective-permute-done | bytes 139296 | tf_op jit(solution)/shard_map/ppermute | solution.py:246
  56.1 2.3 %collective-permute-start.12 = (bf16[4,136,128]{2,1,0:T(8,128)(2,1)S(1)}, bf16[4,136,128]{2,1,0:T(8,128)(2,1)S(1)}, u32[]{:S(2)}, u32[]{:S(2)}) collective-permute-start(bf16[4,136,128]{2,1,0:T(8,128)(2,1)S(1)} %hop.4.mine_ref), channel_id=1, source_target_pairs={{0,4},{1,5},{2,6},{3,7},{4,0},{5,1},{6,2},{7,3},{8,12},{9,13},{10,... | collective-permute-start | bytes 417800 | tf_op jit(solution)/shard_map/ppermute | solution.py:246
  58.4 6.5 %collective-permute-done.12.got_ref = bf16[4,136,128]{2,1,0:T(8,128)(2,1)S(1)} collective-permute-done((bf16[4,136,128]{2,1,0:T(8,128)(2,1)S(1)}, bf16[4,136,128]{2,1,0:T(8,128)(2,1)S(1)}, u32[]{:S(2)}, u32[]{:S(2)}) %collective-permute-start.12) | collective-permute-done | bytes 139296 | tf_op jit(solution)/shard_map/ppermute | solution.py:246
  64.9 0.7 prox.4
  65.7 1.3 %collective-permute-done.13.got_ref = bf16[4,128,128]{2,1,0:T(8,128)(2,1)S(1)} collective-permute-done((bf16[4,128,128]{2,1,0:T(8,128)(2,1)S(1)}, bf16[4,128,128]{2,1,0:T(8,128)(2,1)S(1)}, u32[]{:S(2)}, u32[]{:S(2)}) %collective-permute-start.13) | collective-permute-done | bytes 131104 | tf_op jit(solution)/shard_map/ppermute | solution.py:246
  67.0 0.7 change_next.1
  67.7 1.6 %collective-permute-start.16 = (bf16[512,128]{1,0:T(8,128)(2,1)S(1)}, bf16[512,128]{1,0:T(8,128)(2,1)S(1)}, u32[]{:S(2)}, u32[]{:S(2)}) collective-permute-start(bf16[512,128]{1,0:T(8,128)(2,1)S(1)} %get-tuple-element.40), channel_id=1, source_target_pairs={{0,16},{8,24},{16,0},{24,8},{1,17},{9,25},{17,1},{25,9},{2,18},{10... | collective-permute-start | bytes 393224 | tf_op jit(solution)/shard_map/ppermute | solution.py:246
  69.3 0.5 collective-permute-start.14
  69.9 3.5 %collective-permute-done.16 = bf16[512,128]{1,0:T(8,128)(2,1)S(1)} collective-permute-done((bf16[512,128]{1,0:T(8,128)(2,1)S(1)}, bf16[512,128]{1,0:T(8,128)(2,1)S(1)}, u32[]{:S(2)}, u32[]{:S(2)}) %collective-permute-start.16) | collective-permute-done | bytes 131104 | tf_op jit(solution)/shard_map/ppermute | solution.py:246
  73.4 1.2 %collective-permute-start.17 = (bf16[512,128]{1,0:T(8,128)(2,1)S(1)}, bf16[512,128]{1,0:T(8,128)(2,1)S(1)}, u32[]{:S(2)}, u32[]{:S(2)}) collective-permute-start(bf16[512,128]{1,0:T(8,128)(2,1)S(1)} %add_convert_fusion.b_ref), channel_id=1, source_target_pairs={{0,8},{8,0},{16,24},{24,16},{1,9},{9,1},{17,25},{25,17},{2,10},{10... | collective-permute-start | bytes 393224 | tf_op jit(solution)/shard_map/ppermute | solution.py:246
  74.6 1.0 collective-permute-start.15
  75.6 1.6 %prep.3.x_ref = bf16[1024,1024]{1,0:T(8,128)(2,1)S(1)} custom-call(s32[3,1]{1,0:T(4,128)S(1)} %copy.8.order_ref, s32[8,16]{1,0:T(8,128)S(1)} %copy-done.4, bf16[1024,2048]{1,0:T(8,128)(2,1)S(1)} %copy-done.1), custom_call_target="tpu_custom_call" | custom-call | bytes 4194304 | tf_op jit(solution)/shard_map/prep/pallas_call | solution.py:46
  77.3 1.2 collective-permute-done.17.rb_ref
  78.4 1.2 %collective-permute-done.15.ra_ref = bf16[512,128]{1,0:T(8,128)(2,1)S(1)} collective-permute-done((bf16[512,128]{1,0:T(8,128)(2,1)S(1)}, bf16[512,128]{1,0:T(8,128)(2,1)S(1)}, u32[]{:S(2)}, u32[]{:S(2)}) %collective-permute-start.15) | collective-permute-done | bytes 131104 | tf_op jit(solution)/shard_map/ppermute | solution.py:246
  79.7 1.8 %soft_next.3 = (f32[1024,128]{1,0:T(8,128)}, bf16[128,1024]{1,0:T(8,128)(2,1)S(1)}, f32[1024,128]{1,0:T(8,128)S(1)}, f32[4,136,128]{2,1,0:T(8,128)S(1)}) custom-call(f32[1024,128]{1,0:T(8,128)S(1)} %get-tuple-element.32.score_ref, bf16[512,128]{1,0:T(8,128)(2,1)S(1)} %add_convert_fusion.1.a_ref, bf16[512,128]{1,0:T(8,128)(2,1)S(1)} %collective-permute-done.15.ra_ref, ...), custom_call_target="tpu_custom_call" | custom-call | flops 134217728 | bytes 1048576 | tf_op jit(solution)/shard_map/soft_next/pallas_call | solution.py:46
  81.5 0.6 own.5.own_ref
  82.1 1.0 collective-permute-done.18.got_ref
  83.1 0.7 collective-permute-start.19
  83.8 5.1 %collective-permute-done.19.got_ref = bf16[4,136,128]{2,1,0:T(8,128)(2,1)S(1)} collective-permute-done((bf16[4,136,128]{2,1,0:T(8,128)(2,1)S(1)}, bf16[4,136,128]{2,1,0:T(8,128)(2,1)S(1)}, u32[]{:S(2)}, u32[]{:S(2)}) %collective-permute-start.19) | collective-permute-done | bytes 139296 | tf_op jit(solution)/shard_map/ppermute | solution.py:246
  88.9 2.3 %collective-permute-start.20 = (bf16[4,136,128]{2,1,0:T(8,128)(2,1)S(1)}, bf16[4,136,128]{2,1,0:T(8,128)(2,1)S(1)}, u32[]{:S(2)}, u32[]{:S(2)}) collective-permute-start(bf16[4,136,128]{2,1,0:T(8,128)(2,1)S(1)} %hop.5.mine_ref), channel_id=1, source_target_pairs={{0,4},{1,5},{2,6},{3,7},{4,0},{5,1},{6,2},{7,3},{8,12},{9,13},{10,... | collective-permute-start | bytes 417800 | tf_op jit(solution)/shard_map/ppermute | solution.py:246
  91.3 6.5 %collective-permute-done.20.got_ref = bf16[4,136,128]{2,1,0:T(8,128)(2,1)S(1)} collective-permute-done((bf16[4,136,128]{2,1,0:T(8,128)(2,1)S(1)}, bf16[4,136,128]{2,1,0:T(8,128)(2,1)S(1)}, u32[]{:S(2)}, u32[]{:S(2)}) %collective-permute-start.20) | collective-permute-done | bytes 139296 | tf_op jit(solution)/shard_map/ppermute | solution.py:246
  97.8 0.7 prox.5
  98.6 1.3 %collective-permute-done.21.got_ref = bf16[4,128,128]{2,1,0:T(8,128)(2,1)S(1)} collective-permute-done((bf16[4,128,128]{2,1,0:T(8,128)(2,1)S(1)}, bf16[4,128,128]{2,1,0:T(8,128)(2,1)S(1)}, u32[]{:S(2)}, u32[]{:S(2)}) %collective-permute-start.21) | collective-permute-done | bytes 131104 | tf_op jit(solution)/shard_map/ppermute | solution.py:246
  99.9 0.7 change_last.1
  100.6 1.0 collective-permute-start.22
  101.6 1.5 %collective-permute-start.24 = (f32[512,128]{1,0:T(8,128)S(1)}, f32[512,128]{1,0:T(8,128)S(1)}, u32[]{:S(2)}, u32[]{:S(2)}) collective-permute-start(f32[512,128]{1,0:T(8,128)S(1)} %get-tuple-element.48), channel_id=1, source_target_pairs={{0,16},{8,24},{16,0},{24,8},{1,17},{9,25},{17,1},{25,9},{2,18},{10... | collective-permute-start | bytes 786440 | tf_op jit(solution)/shard_map/ppermute | solution.py:246
  103.1 5.9 %collective-permute-done.22 = f32[512,128]{1,0:T(8,128)S(1)} collective-permute-done((f32[512,128]{1,0:T(8,128)S(1)}, f32[512,128]{1,0:T(8,128)S(1)}, u32[]{:S(2)}, u32[]{:S(2)}) %collective-permute-start.22) | collective-permute-done | bytes 262176 | tf_op jit(solution)/shard_map/ppermute | solution.py:246
  109.1 1.0 collective-permute-start.23
  110.1 1.6 %collective-permute-start.25 = (f32[512,128]{1,0:T(8,128)S(1)}, f32[512,128]{1,0:T(8,128)S(1)}, u32[]{:S(2)}, u32[]{:S(2)}) collective-permute-start(f32[512,128]{1,0:T(8,128)S(1)} %add.33), channel_id=1, source_target_pairs={{0,8},{8,0},{16,24},{24,16},{1,9},{9,1},{17,25},{25,17},{2,10},{10... | collective-permute-start | bytes 786440 | tf_op jit(solution)/shard_map/ppermute | solution.py:246
  111.7 0.8 copy.16
  112.4 4.2 %collective-permute-done.23 = f32[512,128]{1,0:T(8,128)S(1)} collective-permute-done((f32[512,128]{1,0:T(8,128)S(1)}, f32[512,128]{1,0:T(8,128)S(1)}, u32[]{:S(2)}, u32[]{:S(2)}) %collective-permute-start.23) | collective-permute-done | bytes 262176 | tf_op jit(solution)/shard_map/ppermute | solution.py:246
  116.7 0.7 collective-permute-done.25
  117.4 0.9 maximum_add_fusion
  (40 shorter events, 1.1 us)
Async XLA Ops:
  1.4 2.2 %copy-start = (bf16[1024,2048]{1,0:T(8,128)(2,1)S(1)}, bf16[1024,2048]{1,0:T(8,128)(2,1)}, u32[]{:S(2)}) copy-start(bf16[1024,2048]{1,0:T(8,128)(2,1)} %x_ref.5) | copy-start | bytes 12582916
  3.6 0.7 copy-start.3
  4.2 1.5 %copy-start.2 = (bf16[1024,128]{1,0:T(8,128)(2,1)S(1)}, bf16[1024,128]{1,0:T(8,128)(2,1)}, u32[]{:S(2)}) copy-start(bf16[1024,128]{1,0:T(8,128)(2,1)} %score_ref.1) | copy-start | bytes 786436
  4.2 1.5 %copy-start.5 = (s32[1024]{0:T(1024)S(1)}, s32[1024]{0:T(1024)}, u32[]{:S(2)}) copy-start(s32[1024]{0:T(1024)} %param.8) | copy-start | bytes 12292
  8.2 6.2 %collective-permute-start = (f32[4,136,128]{2,1,0:T(8,128)}, f32[4,136,128]{2,1,0:T(8,128)S(1)}, u32[]{:S(2)}, u32[]{:S(2)}) collective-permute-start(f32[4,136,128]{2,1,0:T(8,128)} %get-tuple-element.28), channel_id=1, source_target_pairs={{0,1},{1,0},{2,3},{3,2},{4,5},{5,4},{6,7},{7,6},{8,9},{9,8},{10,11... | collective-permute-start | bytes 835592 | tf_op jit(solution)/shard_map/ppermute | solution.py:246
  11.2 5.4 %collective-permute-start.3 = (bf16[2,1,128,128]{3,2,1,0:T(8,128)(2,1)S(1)}, bf16[2,1,128,128]{3,2,1,0:T(8,128)(2,1)S(1)}, u32[]{:S(2)}, u32[]{:S(2)}) collective-permute-start(bf16[2,1,128,128]{3,2,1,0:T(8,128)(2,1)S(1)} %fusion), channel_id=1, source_target_pairs={{0,2},{1,3},{2,0},{3,1},{4,6},{5,7},{6,4},{7,5},{8,10},{9,11},{10,... | collective-permute-start | bytes 196616 | tf_op jit(solution)/shard_map/ppermute | solution.py:246
  13.9 15.4 %copy-start.6 = (f32[2,128,128]{1,2,0:T(8,128)S(1)}, f32[2,128,128]{1,2,0:T(8,128)}, u32[]{:S(2)}) copy-start(f32[2,128,128]{1,2,0:T(8,128)} %copy.10) | copy-start | bytes 393220
  14.5 7.5 %collective-permute-start.1 = (bf16[4,136,128]{2,1,0:T(8,128)(2,1)S(1)}, bf16[4,136,128]{2,1,0:T(8,128)(2,1)S(1)}, u32[]{:S(2)}, u32[]{:S(2)}) collective-permute-start(bf16[4,136,128]{2,1,0:T(8,128)(2,1)S(1)} %pair.3.mine_ref), channel_id=1, source_target_pairs={{0,2},{1,3},{2,0},{3,1},{4,6},{5,7},{6,4},{7,5},{8,10},{9,11},{10,... | collective-permute-start | bytes 417800 | tf_op jit(solution)/shard_map/ppermute | solution.py:246
  16.7 12.6 %collective-permute-start.4 = (bf16[2,2,128,128]{3,2,1,0:T(8,128)(2,1)S(1)}, bf16[2,2,128,128]{3,2,1,0:T(8,128)(2,1)S(1)}, u32[]{:S(2)}, u32[]{:S(2)}) collective-permute-start(bf16[2,2,128,128]{3,2,1,0:T(8,128)(2,1)S(1)} %pad_maximum_fusion.1), channel_id=1, source_target_pairs={{0,4},{1,5},{2,6},{3,7},{4,0},{5,1},{6,2},{7,3},{8,12},{9,13},{10,... | collective-permute-start | bytes 393224 | tf_op jit(solution)/shard_map/ppermute | solution.py:246
  22.0 9.8 %collective-permute-start.2 = (bf16[4,136,128]{2,1,0:T(8,128)(2,1)S(1)}, bf16[4,136,128]{2,1,0:T(8,128)(2,1)S(1)}, u32[]{:S(2)}, u32[]{:S(2)}) collective-permute-start(bf16[4,136,128]{2,1,0:T(8,128)(2,1)S(1)} %hop.3.mine_ref), channel_id=1, source_target_pairs={{0,4},{1,5},{2,6},{3,7},{4,0},{5,1},{6,2},{7,3},{8,12},{9,13},{10,... | collective-permute-start | bytes 417800 | tf_op jit(solution)/shard_map/ppermute | solution.py:246
  29.3 14.1 %copy-start.1 = (bf16[1024,2048]{1,0:T(8,128)(2,1)S(1)}, bf16[1024,2048]{1,0:T(8,128)(2,1)}, u32[]{:S(2)}) copy-start(bf16[1024,2048]{1,0:T(8,128)(2,1)} %x_ref.5) | copy-start | bytes 12582916
  29.4 14.1 %copy-start.4 = (s32[8,16]{1,0:T(8,128)S(1)}, s32[8,16]{1,0:T(8,128)}, u32[]{:S(2)}) copy-start(s32[8,16]{1,0:T(8,128)} %live_ref.5) | copy-start | bytes 1540
  32.5 1.4 %collective-permute-start.5 = (bf16[4,128,128]{2,1,0:T(8,128)(2,1)S(1)}, bf16[4,128,128]{2,1,0:T(8,128)(2,1)S(1)}, u32[]{:S(2)}, u32[]{:S(2)}) collective-permute-start(bf16[4,128,128]{2,1,0:T(8,128)(2,1)S(1)} %get-tuple-element.29.mine_ref), channel_id=1, source_target_pairs={{0,1},{1,0},{2,3},{3,2},{4,5},{5,4},{6,7},{7,6},{8,9},{9,8},{10,11... | collective-permute-start | bytes 393224 | tf_op jit(solution)/shard_map/ppermute | solution.py:246
  34.6 5.6 %collective-permute-start.8 = (bf16[512,128]{1,0:T(8,128)(2,1)S(1)}, bf16[512,128]{1,0:T(8,128)(2,1)S(1)}, u32[]{:S(2)}, u32[]{:S(2)}) collective-permute-start(bf16[512,128]{1,0:T(8,128)(2,1)S(1)} %get-tuple-element.31), channel_id=1, source_target_pairs={{0,16},{8,24},{16,0},{24,8},{1,17},{9,25},{17,1},{25,9},{2,18},{10... | collective-permute-start | bytes 393224 | tf_op jit(solution)/shard_map/ppermute | solution.py:246
  36.2 5.6 %collective-permute-start.6 = (bf16[512,128]{1,0:T(8,128)(2,1)S(1)}, bf16[512,128]{1,0:T(8,128)(2,1)S(1)}, u32[]{:S(2)}, u32[]{:S(2)}) collective-permute-start(bf16[512,128]{1,0:T(8,128)(2,1)S(1)} %get-tuple-element.30), channel_id=1, source_target_pairs={{0,8},{8,0},{16,24},{24,16},{1,9},{9,1},{17,25},{25,17},{2,10},{10... | collective-permute-start | bytes 393224 | tf_op jit(solution)/shard_map/ppermute | solution.py:246
  40.3 5.0 %collective-permute-start.9 = (bf16[512,128]{1,0:T(8,128)(2,1)S(1)}, bf16[512,128]{1,0:T(8,128)(2,1)S(1)}, u32[]{:S(2)}, u32[]{:S(2)}) collective-permute-start(bf16[512,128]{1,0:T(8,128)(2,1)S(1)} %add_convert_fusion.2.b_ref), channel_id=1, source_target_pairs={{0,8},{8,0},{16,24},{24,16},{1,9},{9,1},{17,25},{25,17},{2,10},{10... | collective-permute-start | bytes 393224 | tf_op jit(solution)/shard_map/ppermute | solution.py:246
  41.8 5.0 %collective-permute-start.7 = (bf16[512,128]{1,0:T(8,128)(2,1)S(1)}, bf16[512,128]{1,0:T(8,128)(2,1)S(1)}, u32[]{:S(2)}, u32[]{:S(2)}) collective-permute-start(bf16[512,128]{1,0:T(8,128)(2,1)S(1)} %add_convert_fusion.3.a_ref), channel_id=1, source_target_pairs={{0,16},{8,24},{16,0},{24,8},{1,17},{9,25},{17,1},{25,9},{2,18},{10... | collective-permute-start | bytes 393224 | tf_op jit(solution)/shard_map/ppermute | solution.py:246
  48.6 1.6 %collective-permute-start.10 = (f32[4,136,128]{2,1,0:T(8,128)S(1)}, f32[4,136,128]{2,1,0:T(8,128)S(1)}, u32[]{:S(2)}, u32[]{:S(2)}) collective-permute-start(f32[4,136,128]{2,1,0:T(8,128)S(1)} %get-tuple-element.35), channel_id=1, source_target_pairs={{0,1},{1,0},{2,3},{3,2},{4,5},{5,4},{6,7},{7,6},{8,9},{9,8},{10,11... | collective-permute-start | bytes 835592 | tf_op jit(solution)/shard_map/ppermute | solution.py:246
  50.2 5.8 %collective-permute-start.11 = (bf16[4,136,128]{2,1,0:T(8,128)(2,1)S(1)}, bf16[4,136,128]{2,1,0:T(8,128)(2,1)S(1)}, u32[]{:S(2)}, u32[]{:S(2)}) collective-permute-start(bf16[4,136,128]{2,1,0:T(8,128)(2,1)S(1)} %pair.4.mine_ref), channel_id=1, source_target_pairs={{0,2},{1,3},{2,0},{3,1},{4,6},{5,7},{6,4},{7,5},{8,10},{9,11},{10,... | collective-permute-start | bytes 417800 | tf_op jit(solution)/shard_map/ppermute | solution.py:246
  56.1 8.8 %collective-permute-start.12 = (bf16[4,136,128]{2,1,0:T(8,128)(2,1)S(1)}, bf16[4,136,128]{2,1,0:T(8,128)(2,1)S(1)}, u32[]{:S(2)}, u32[]{:S(2)}) collective-permute-start(bf16[4,136,128]{2,1,0:T(8,128)(2,1)S(1)} %hop.4.mine_ref), channel_id=1, source_target_pairs={{0,4},{1,5},{2,6},{3,7},{4,0},{5,1},{6,2},{7,3},{8,12},{9,13},{10,... | collective-permute-start | bytes 417800 | tf_op jit(solution)/shard_map/ppermute | solution.py:246
  65.6 1.4 %collective-permute-start.13 = (bf16[4,128,128]{2,1,0:T(8,128)(2,1)S(1)}, bf16[4,128,128]{2,1,0:T(8,128)(2,1)S(1)}, u32[]{:S(2)}, u32[]{:S(2)}) collective-permute-start(bf16[4,128,128]{2,1,0:T(8,128)(2,1)S(1)} %get-tuple-element.37.mine_ref), channel_id=1, source_target_pairs={{0,1},{1,0},{2,3},{3,2},{4,5},{5,4},{6,7},{7,6},{8,9},{9,8},{10,11... | collective-permute-start | bytes 393224 | tf_op jit(solution)/shard_map/ppermute | solution.py:246
  67.7 5.6 %collective-permute-start.16 = (bf16[512,128]{1,0:T(8,128)(2,1)S(1)}, bf16[512,128]{1,0:T(8,128)(2,1)S(1)}, u32[]{:S(2)}, u32[]{:S(2)}) collective-permute-start(bf16[512,128]{1,0:T(8,128)(2,1)S(1)} %get-tuple-element.40), channel_id=1, source_target_pairs={{0,16},{8,24},{16,0},{24,8},{1,17},{9,25},{17,1},{25,9},{2,18},{10... | collective-permute-start | bytes 393224 | tf_op jit(solution)/shard_map/ppermute | solution.py:246
  69.3 5.3 %collective-permute-start.14 = (bf16[512,128]{1,0:T(8,128)(2,1)S(1)}, bf16[512,128]{1,0:T(8,128)(2,1)S(1)}, u32[]{:S(2)}, u32[]{:S(2)}) collective-permute-start(bf16[512,128]{1,0:T(8,128)(2,1)S(1)} %get-tuple-element.39), channel_id=1, source_target_pairs={{0,8},{8,0},{16,24},{24,16},{1,9},{9,1},{17,25},{25,17},{2,10},{10... | collective-permute-start | bytes 393224 | tf_op jit(solution)/shard_map/ppermute | solution.py:246
  73.4 5.0 %collective-permute-start.17 = (bf16[512,128]{1,0:T(8,128)(2,1)S(1)}, bf16[512,128]{1,0:T(8,128)(2,1)S(1)}, u32[]{:S(2)}, u32[]{:S(2)}) collective-permute-start(bf16[512,128]{1,0:T(8,128)(2,1)S(1)} %add_convert_fusion.b_ref), channel_id=1, source_target_pairs={{0,8},{8,0},{16,24},{24,16},{1,9},{9,1},{17,25},{25,17},{2,10},{10... | collective-permute-start | bytes 393224 | tf_op jit(solution)/shard_map/ppermute | solution.py:246
  74.6 5.0 %collective-permute-start.15 = (bf16[512,128]{1,0:T(8,128)(2,1)S(1)}, bf16[512,128]{1,0:T(8,128)(2,1)S(1)}, u32[]{:S(2)}, u32[]{:S(2)}) collective-permute-start(bf16[512,128]{1,0:T(8,128)(2,1)S(1)} %add_convert_fusion.1.a_ref), channel_id=1, source_target_pairs={{0,16},{8,24},{16,0},{24,8},{1,17},{9,25},{17,1},{25,9},{2,18},{10... | collective-permute-start | bytes 393224 | tf_op jit(solution)/shard_map/ppermute | solution.py:246
  81.4 1.6 %collective-permute-start.18 = (f32[4,136,128]{2,1,0:T(8,128)S(1)}, f32[4,136,128]{2,1,0:T(8,128)S(1)}, u32[]{:S(2)}, u32[]{:S(2)}) collective-permute-start(f32[4,136,128]{2,1,0:T(8,128)S(1)} %get-tuple-element.43), channel_id=1, source_target_pairs={{0,1},{1,0},{2,3},{3,2},{4,5},{5,4},{6,7},{7,6},{8,9},{9,8},{10,11... | collective-permute-start | bytes 835592 | tf_op jit(solution)/shard_map/ppermute | solution.py:246
  83.1 5.8 %collective-permute-start.19 = (bf16[4,136,128]{2,1,0:T(8,128)(2,1)S(1)}, bf16[4,136,128]{2,1,0:T(8,128)(2,1)S(1)}, u32[]{:S(2)}, u32[]{:S(2)}) collective-permute-start(bf16[4,136,128]{2,1,0:T(8,128)(2,1)S(1)} %pair.5.mine_ref), channel_id=1, source_target_pairs={{0,2},{1,3},{2,0},{3,1},{4,6},{5,7},{6,4},{7,5},{8,10},{9,11},{10,... | collective-permute-start | bytes 417800 | tf_op jit(solution)/shard_map/ppermute | solution.py:246
  88.9 8.8 %collective-permute-start.20 = (bf16[4,136,128]{2,1,0:T(8,128)(2,1)S(1)}, bf16[4,136,128]{2,1,0:T(8,128)(2,1)S(1)}, u32[]{:S(2)}, u32[]{:S(2)}) collective-permute-start(bf16[4,136,128]{2,1,0:T(8,128)(2,1)S(1)} %hop.5.mine_ref), channel_id=1, source_target_pairs={{0,4},{1,5},{2,6},{3,7},{4,0},{5,1},{6,2},{7,3},{8,12},{9,13},{10,... | collective-permute-start | bytes 417800 | tf_op jit(solution)/shard_map/ppermute | solution.py:246
  98.5 1.4 %collective-permute-start.21 = (bf16[4,128,128]{2,1,0:T(8,128)(2,1)S(1)}, bf16[4,128,128]{2,1,0:T(8,128)(2,1)S(1)}, u32[]{:S(2)}, u32[]{:S(2)}) collective-permute-start(bf16[4,128,128]{2,1,0:T(8,128)(2,1)S(1)} %get-tuple-element.45.mine_ref), channel_id=1, source_target_pairs={{0,1},{1,0},{2,3},{3,2},{4,5},{5,4},{6,7},{7,6},{8,9},{9,8},{10,11... | collective-permute-start | bytes 393224 | tf_op jit(solution)/shard_map/ppermute | solution.py:246
  100.6 8.4 %collective-permute-start.22 = (f32[512,128]{1,0:T(8,128)S(1)}, f32[512,128]{1,0:T(8,128)S(1)}, u32[]{:S(2)}, u32[]{:S(2)}) collective-permute-start(f32[512,128]{1,0:T(8,128)S(1)} %get-tuple-element.47), channel_id=1, source_target_pairs={{0,8},{8,0},{16,24},{24,16},{1,9},{9,1},{17,25},{25,17},{2,10},{10... | collective-permute-start | bytes 786440 | tf_op jit(solution)/shard_map/ppermute | solution.py:246
  101.6 8.5 %collective-permute-start.24 = (f32[512,128]{1,0:T(8,128)S(1)}, f32[512,128]{1,0:T(8,128)S(1)}, u32[]{:S(2)}, u32[]{:S(2)}) collective-permute-start(f32[512,128]{1,0:T(8,128)S(1)} %get-tuple-element.48), channel_id=1, source_target_pairs={{0,16},{8,24},{16,0},{24,8},{1,17},{9,25},{17,1},{25,9},{2,18},{10... | collective-permute-start | bytes 786440 | tf_op jit(solution)/shard_map/ppermute | solution.py:246
  109.1 7.6 %collective-permute-start.23 = (f32[512,128]{1,0:T(8,128)S(1)}, f32[512,128]{1,0:T(8,128)S(1)}, u32[]{:S(2)}, u32[]{:S(2)}) collective-permute-start(f32[512,128]{1,0:T(8,128)S(1)} %add.31), channel_id=1, source_target_pairs={{0,16},{8,24},{16,0},{24,8},{1,17},{9,25},{17,1},{25,9},{2,18},{10... | collective-permute-start | bytes 786440 | tf_op jit(solution)/shard_map/ppermute | solution.py:246
  110.1 7.3 %collective-permute-start.25 = (f32[512,128]{1,0:T(8,128)S(1)}, f32[512,128]{1,0:T(8,128)S(1)}, u32[]{:S(2)}, u32[]{:S(2)}) collective-permute-start(f32[512,128]{1,0:T(8,128)S(1)} %add.33), channel_id=1, source_target_pairs={{0,8},{8,0},{16,24},{24,16},{1,9},{9,1},{17,25},{25,17},{2,10},{10... | collective-permute-start | bytes 786440 | tf_op jit(solution)/shard_map/ppermute | solution.py:246

commit v3 on v2

v3 whole, which is shorter than its diff:
```python
import functools

import jax
import jax.numpy as jnp
from jax import lax
from jax.experimental import pallas as pl
from jax.experimental.pallas import tpu as pltpu
from jax.sharding import PartitionSpec as P

C = 128
BLOCK = 1024
STEPS = 3
HALF = BLOCK // 2
TILE = 128
NB = HALF // TILE
PB = NB // 2
ROWS = C + 8

ridge = 0.002
lasso = 0.005

F32 = jnp.float32
BF16 = jnp.bfloat16


def vmem(n):
    return [pl.BlockSpec(memory_space=pltpu.VMEM)] * n


def smem(n):
    return [pl.BlockSpec(memory_space=pltpu.SMEM)] * n


def hbm(n):
    return [pl.BlockSpec(memory_space=pltpu.HBM)] * n


def call(body, outs, in_specs, name, flops=0, nbytes=0, **kw):
    f = pl.pallas_call(
        body,
        out_shape=outs,
        in_specs=in_specs,
        out_specs=jax.tree.map(lambda _: pl.BlockSpec(memory_space=pltpu.VMEM), outs),
        name=name,
        cost_estimate=pl.CostEstimate(flops=flops, bytes_accessed=nbytes, transcendentals=0),
        compiler_params=pltpu.CompilerParams(vmem_limit_bytes=16 << 20),
        **kw,
    )

    def run(*args):
        return f(
            *(
                x
                if spec.memory_space == pltpu.SMEM
                else pltpu.with_memory_space_constraint(x, spec.memory_space)
                for spec, x in zip(in_specs, args, strict=True)
            )
        )

    return run


def sds(shape, dtype):
    return pltpu.VMEM(shape, dtype)


def load_block(chosen, x_ref, buf, sems):
    copies = [
        pltpu.make_async_copy(
            x_ref.at[pl.ds(r * TILE, TILE), pl.ds(pl.multiple_of(chosen * BLOCK, BLOCK), BLOCK)],
            buf.at[pl.ds(r * TILE, TILE)],
            sems.at[r],
        )
        for r in range(buf.shape[0] // TILE)
    ]
    for copy in copies:
        copy.start()
    return copies


def mask_tile(r, chosen, core, live_ref, buf, out_ref):
    tiles = BLOCK // TILE
    here = pl.ds(r * TILE, TILE)
    for k in range(tiles):
        col = 2 * (k % NB) + (core if k < NB else 1 - core)
        live = live_ref[r, chosen * tiles + col].astype(F32)
        tile = buf[here, pl.ds(pl.multiple_of(col * TILE, TILE), TILE)]
        out_ref[here, k * TILE : (k + 1) * TILE] = (tile.astype(F32) * live).astype(BF16)


def prep_body(step, order_ref, live_ref, x_ref, out_ref, buf, sems):
    chosen, core = order_ref[0, step], lax.axis_index("ex") % 2
    copies = load_block(chosen, x_ref, buf, sems)
    for r, copy in enumerate(copies):
        copy.wait()
        mask_tile(r, chosen, core, live_ref, buf, out_ref)


def block_scratch(rows):
    return [pltpu.VMEM((rows, BLOCK), BF16), pltpu.SemaphoreType.DMA((rows // TILE,))]


def prep(order, tile_live, x_values, step):
    rows = x_values.shape[0]
    return call(
        functools.partial(prep_body, step),
        sds((rows, BLOCK), BF16),
        smem(2) + hbm(1),
        "prep",
        nbytes=4 * rows * BLOCK,
        scratch_shapes=block_scratch(rows),
    )(order, tile_live, x_values)


def prep_general(x_values, tile_live, chosen, core, own):
    rows = x_values.shape[0]
    tiles = BLOCK // TILE
    x = lax.dynamic_slice_in_dim(x_values, chosen * BLOCK, BLOCK, 1)
    live = lax.dynamic_slice_in_dim(tile_live, chosen * tiles, tiles, 1).astype(BF16)
    x = x.reshape(rows // TILE, TILE, tiles, TILE) * live[:, None, :, None]
    x = x.reshape(rows, HALF // own, 2, own)
    mine = lax.dynamic_index_in_dim(x, core, 2, keepdims=False)
    other = lax.dynamic_index_in_dim(x, 1 - core, 2, keepdims=False)
    return jnp.concatenate([mine.reshape(rows, HALF), other.reshape(rows, HALF)], axis=1)


def half_sums(res_t, spread_ref, x_ref, first, *g_refs):
    rows = x_ref.shape[0]
    row = lax.broadcasted_iota(jnp.int32, (8, TILE), 0)
    for n, g_ref in enumerate(g_refs):
        lane = first + n * PB * TILE
        grad = jnp.dot(res_t, x_ref[:, lane : lane + PB * TILE], preferred_element_type=F32)
        for k in range(PB):
            lanes = slice(lane + k * TILE, lane + (k + 1) * TILE)
            acc = jnp.zeros((8, TILE), F32)
            for r in range(rows // TILE):
                here = slice(r * TILE, (r + 1) * TILE)
                x = x_ref[here, lanes].astype(F32)
                term = x * x * spread_ref[here, :]
                acc = acc + jnp.sum(term.reshape(TILE // 8, 8, TILE), axis=0)
            total = jnp.sum(acc, axis=0, keepdims=True)
            g_ref[k, 0:C, :] = grad[:, k * TILE : (k + 1) * TILE]
            g_ref[k, C:ROWS, :] = jnp.where(row == 0, total, 0.0)


def soft_tile(score, labels):
    top = jnp.max(score, axis=1, keepdims=True)
    expo = jnp.exp(score - top)
    prob = expo / jnp.sum(expo, axis=1, keepdims=True)
    label_col = jnp.broadcast_to(labels.astype(F32), (TILE, TILE)).T
    classes = lax.broadcasted_iota(jnp.int32, (TILE, C), 1).astype(F32)
    residual = prob - jnp.where(label_col == classes, 1.0, 0.0)
    spread = (1.0 - jnp.sum(prob * prob, axis=1, keepdims=True)).astype(BF16).astype(F32)
    return residual.T.astype(BF16), jnp.broadcast_to(spread, (TILE, TILE))


def soft_rows(score, lab_ref, r, res_ref, spread_ref):
    here = slice(r * TILE, (r + 1) * TILE)
    res_t, spread = soft_tile(score, lab_ref[r : r + 1, :])
    res_ref[:, here] = res_t
    spread_ref[here, :] = spread


def first_body(order_ref, live_ref, margins_ref, lab_ref, x_ref, out_ref, res_ref, spread_ref, p_ref, q_ref, buf, sems):
    chosen, core = order_ref[0, 0], lax.axis_index("ex") % 2
    copies = load_block(chosen, x_ref, buf, sems)
    for r in range(len(copies)):
        score = margins_ref[r * TILE : (r + 1) * TILE, :].astype(F32)
        soft_rows(score, lab_ref, r, res_ref, spread_ref)
    for r, copy in enumerate(copies):
        copy.wait()
        mask_tile(r, chosen, core, live_ref, buf, out_ref)
    half_sums(res_ref[...], spread_ref, out_ref, HALF, p_ref, q_ref)


def first_general_body(margins_ref, lab_ref, x_ref, res_ref, spread_ref, p_ref, q_ref):
    for r in range(margins_ref.shape[0] // TILE):
        score = margins_ref[r * TILE : (r + 1) * TILE, :].astype(F32)
        soft_rows(score, lab_ref, r, res_ref, spread_ref)
    half_sums(res_ref[...], spread_ref, x_ref, HALF, p_ref, q_ref)


def next_body(score_ref, a_ref, ra_ref, b_ref, rb_ref, lab_ref, x_ref, new_ref, res_ref, spread_ref, p_ref, q_ref):
    rows = score_ref.shape[0]
    for r in range(rows // TILE):
        here = slice(r * TILE, (r + 1) * TILE)
        if 2 * r * TILE < rows:
            part, got, at = a_ref, ra_ref, here
        else:
            part, got = b_ref, rb_ref
            at = slice(r * TILE - rows // 2, (r + 1) * TILE - rows // 2)
        change = part[at, :].astype(F32) + got[at, :].astype(F32)
        score = score_ref[here, :].astype(F32) + change
        new_ref[here, :] = score
        soft_rows(score, lab_ref, r, res_ref, spread_ref)
    half_sums(res_ref[...], spread_ref, x_ref, HALF, p_ref, q_ref)


def own_body(res_ref, spread_ref, x_ref, p_ref, q_ref):
    half_sums(res_ref[...], spread_ref, x_ref, 0, p_ref, q_ref)


def encode(k, grad, curv, out_ref):
    out_ref[k, 0:C, :] = grad.astype(BF16)
    high = curv.astype(BF16).astype(F32)
    low = curv - high
    row = lax.broadcasted_iota(jnp.int32, (8, TILE), 0)
    tail = jnp.where(row == 0, high, jnp.where(row == 1, low, 0.0))
    out_ref[k, C:ROWS, :] = tail.astype(BF16)


def pair_body(own_ref, got_ref, out_ref):
    for k in range(PB):
        total = own_ref[k] + got_ref[k]
        encode(k, total[0:C], total[C : C + 1], out_ref)


def pair_with_body(slot, order_ref, own_ref, got_ref, coef_ref, out_ref):
    pair_body(own_ref, got_ref, out_ref)
    block = order_ref[0, 0] if slot == 0 else 1 - order_ref[0, 0]
    out_ref[PB, 0:C, :] = coef_ref[block].T.astype(BF16)
    out_ref[PB, C:ROWS, :] = jnp.zeros((ROWS - C, TILE), BF16)


def decode_sum(k, mine_ref, got_ref):
    total = mine_ref[k].astype(F32) + got_ref[k].astype(F32)
    return total[0:C], total[C : C + 1] + total[C + 1 : C + 2]


def hop_body(mine_ref, got_ref, out_ref):
    for k in range(PB):
        encode(k, *decode_sum(k, mine_ref, got_ref), out_ref)


def hop_with_body(mine_ref, got_ref, out_ref):
    hop_body(mine_ref, got_ref, out_ref)
    out_ref[PB] = mine_ref[PB]
    out_ref[PB + 1] = got_ref[PB]


def place_body(slot, order_ref, mine_ref, got_ref, coef_ref, out_ref):
    place = lax.axis_index("ex") // 2
    block = order_ref[0, 0] if slot == 0 else 1 - order_ref[0, 0]
    out_ref[place] = coef_ref[block].T
    out_ref[jnp.bitwise_xor(place, 2)] = mine_ref[PB + 1, 0:C, :].astype(F32)
    out_ref[jnp.bitwise_xor(place, 1)] = got_ref[PB, 0:C, :].astype(F32)
    out_ref[jnp.bitwise_xor(place, 3)] = got_ref[PB + 1, 0:C, :].astype(F32)


def step_coef(count, k, mine_ref, got_ref, old):
    grad, curv = decode_sum(k, mine_ref, got_ref)
    inverse = 1.0 / (curv / count + ridge)
    shifted = old - grad * (inverse / count)
    limit = lasso * inverse
    return shifted - jnp.clip(shifted, -limit, limit)


def prox_first_body(count, first, mine_ref, got_ref, old_ref, new_ref, delta_ref):
    for k in range(PB):
        old = old_ref[first + k]
        new = step_coef(count, k, mine_ref, got_ref, old)
        new_ref[k] = new
        delta_ref[k] = (new - old).astype(BF16)


def prox_body(count, step, first, order_ref, mine_ref, got_ref, old0_ref, old1_ref, new0_ref, new1_ref, delta_ref):
    same = order_ref[0, step] == order_ref[0, 0]
    for k in range(PB):
        old0, old1 = old0_ref[k], old1_ref[first + k]
        old = jnp.where(same, old0, old1)
        new = step_coef(count, k, mine_ref, got_ref, old)
        new0_ref[k] = jnp.where(same, new, old0)
        new1_ref[k] = jnp.where(same, old1, new)
        delta_ref[k] = (new - old).astype(BF16)


def coef_body(order_ref, p0_ref, p1_ref, q0_ref, q1_ref, out_ref):
    place = lax.axis_index("ex") // 2
    block = order_ref[0, 0]

    @pl.when(place < PB)
    def _():
        out_ref[block] = p0_ref[place].T
        out_ref[1 - block] = p1_ref[place].T

    @pl.when(place >= PB)
    def _():
        out_ref[block] = q0_ref[place - PB].T
        out_ref[1 - block] = q1_ref[place - PB].T


def contrib_dot(x_ref, p_ref, q_ref, rp_ref, rq_ref):
    delta = [ref[k] for ref in (p_ref, q_ref, rp_ref, rq_ref) for k in range(PB)]
    delta = jnp.concatenate(delta, axis=1)
    return lax.dot_general(
        x_ref[...], delta, (((1,), (1,)), ((), ())), preferred_element_type=F32
    )


def change_first_body(x_ref, p_ref, q_ref, rp_ref, rq_ref, total_ref, a_ref, b_ref):
    part = contrib_dot(x_ref, p_ref, q_ref, rp_ref, rq_ref)
    half = part.shape[0] // 2
    total_ref[...] = part
    a_ref[...] = part[:half].astype(BF16)
    b_ref[...] = part[half:].astype(BF16)


def change_next_body(x_ref, p_ref, q_ref, rp_ref, rq_ref, before_ref, total_ref, a_ref, b_ref):
    part = contrib_dot(x_ref, p_ref, q_ref, rp_ref, rq_ref)
    half = part.shape[0] // 2
    total_ref[...] = before_ref[...] + part
    a_ref[...] = part[:half].astype(BF16)
    b_ref[...] = part[half:].astype(BF16)


def change_last_body(x_ref, p_ref, q_ref, rp_ref, rq_ref, before_ref, a_ref, b_ref):
    part = before_ref[...] + contrib_dot(x_ref, p_ref, q_ref, rp_ref, rq_ref)
    half = part.shape[0] // 2
    a_ref[...] = part[:half]
    b_ref[...] = part[half:]


def flip(x, axis, bit):
    n = lax.axis_size(axis)
    return lax.ppermute(x, axis, [(i, i ^ bit) for i in range(n)])


def bits(n):
    return [1 << i for i in range(n.bit_length() - 1)]


def add_as(x, y, dtype):
    return (x.astype(F32) + y.astype(F32)).astype(dtype)


def spread_over_feat(a, b):
    order = bits(lax.axis_size("feat"))
    for n, (bit_a, bit_b) in enumerate(zip(order, reversed(order))):
        got_a, got_b = flip(a, "feat", bit_a), flip(b, "feat", bit_b)
        if n == len(order) - 1:
            return a, got_a, b, got_b
        a, b = add_as(a, got_a, a.dtype), add_as(b, got_b, b.dtype)


def gather_blocks(coef, order, z_bits):
    n_z = 1 << len(z_bits)
    far = jnp.swapaxes(coef, 1, 2)[:, None]
    for bit in z_bits:
        far = jnp.concatenate([far, flip(far, "ex", bit)], axis=1)
    place = lax.axis_index("ex") // 2
    far = jnp.take(far, jnp.bitwise_xor(jnp.arange(n_z), place), axis=1)
    old = far.transpose(0, 2, 1, 3).reshape(2, C, NB, TILE).transpose(0, 2, 1, 3)
    block = order[0, 0]
    return [lax.dynamic_index_in_dim(old, i, 0, keepdims=False) for i in (block, 1 - block)]


def own_blocks(olds, order, own):
    place = lax.axis_index("ex") // 2
    rows = []
    for p, q in olds:
        old = jnp.concatenate([p, q]).transpose(1, 0, 2).reshape(C, HALF)
        rows.append(lax.dynamic_slice_in_dim(old, place * own, own, 1))
    first = order[0, 0] == 0
    both = [jnp.where(first, rows[0], rows[1]), jnp.where(first, rows[1], rows[0])]
    return jnp.swapaxes(jnp.stack(both), 1, 2)


def local(x_values, tile_live, labels, margins, coef, order):
    rows = x_values.shape[0]
    n_ex = lax.axis_size("ex")
    count = float(rows * n_ex)
    own = coef.shape[1]
    core = lax.axis_index("ex") % 2
    aligned = own == TILE and n_ex == 2 * NB
    labels = labels.reshape(rows // TILE, TILE)
    order = order.reshape(1, STEPS)
    z_bits = [2 * b for b in bits(n_ex // 2)]
    if not aligned:
        olds = gather_blocks(coef, order, z_bits)

    g_shape = sds((PB, ROWS, TILE), F32)
    x_shape = sds((rows, BLOCK), BF16)
    soft_shapes = (sds((C, rows), BF16), sds((rows, TILE), F32), g_shape, g_shape)
    half_shape = (rows // 2, C)
    old_shape, delta_shape = sds((PB, C, TILE), F32), sds((PB, C, TILE), BF16)
    half_flops = 2 * rows * HALF * C

    def message(n):
        return sds((PB + n, ROWS, TILE), BF16)

    score, total = margins, None
    for step in range(STEPS):
        if not aligned:
            x = prep_general(x_values, tile_live, order[0, step], core, own)
        elif step > 0:
            x = prep(order, tile_live, x_values, step)
        if step > 0:
            score, res_t, spread, other_p, other_q = call(
                next_body, (sds((rows, C), F32),) + soft_shapes, vmem(7), "soft_next", half_flops, 1 << 20
            )(score, a, got_a, b, got_b, labels, x)
        elif aligned:
            x, res_t, spread, other_p, other_q = call(
                first_body, (x_shape,) + soft_shapes, smem(2) + vmem(2) + hbm(1), "soft_first",
                half_flops, 1 << 20, scratch_shapes=block_scratch(rows),
            )(order, tile_live, margins, labels, x_values)
        else:
            res_t, spread, other_p, other_q = call(
                first_general_body, soft_shapes, vmem(3), "soft_first", half_flops, 1 << 20
            )(margins, labels, x)
        got_p, got_q = flip(other_p, "ex", 1), flip(other_q, "ex", 1)
        own_p, own_q = call(
            own_body, (g_shape, g_shape), vmem(3), "own", half_flops, 1 << 20
        )(res_t, spread, x)
        carry = aligned and step < 2
        p = call(pair_body, message(0), vmem(2), "pair_p")(own_p, got_p)
        if carry:
            q = call(
                functools.partial(pair_with_body, step), message(1), smem(1) + vmem(3), "pair_q"
            )(order, own_q, got_q, coef)
        else:
            q = call(pair_body, message(0), vmem(2), "pair_q")(own_q, got_q)
        for n, (bit_p, bit_q) in enumerate(zip(z_bits, reversed(z_bits))):
            got_p, got_q = flip(p, "ex", bit_p), flip(q, "ex", bit_q)
            if n < len(z_bits) - 1:
                p = call(hop_body, message(0), vmem(2), "hop_p")(p, got_p)
                q = call(
                    hop_with_body if carry else hop_body, message(2 if carry else 0), vmem(2), "hop_q"
                )(q, got_q)
        if carry:
            far = call(
                functools.partial(place_body, step), sds((NB, C, TILE), F32), smem(1) + vmem(3), "place"
            )(order, q, got_q, coef)
        elif not aligned and step < 2:
            far = olds[step]
        if step == 0:
            new_p, delta_p = call(
                functools.partial(prox_first_body, count, 0), (old_shape, delta_shape), vmem(3), "prox_p"
            )(p, got_p, far)
            new_q, delta_q = call(
                functools.partial(prox_first_body, count, PB), (old_shape, delta_shape), vmem(3), "prox_q"
            )(q, got_q, far)
        else:
            p1, q1, at = (far, far, PB) if step == 1 else (other_block_p, other_block_q, 0)
            new_p, other_block_p, delta_p = call(
                functools.partial(prox_body, count, step, 0),
                (old_shape, old_shape, delta_shape), smem(1) + vmem(4), "prox_p",
            )(order, p, got_p, new_p, p1)
            new_q, other_block_q, delta_q = call(
                functools.partial(prox_body, count, step, at),
                (old_shape, old_shape, delta_shape), smem(1) + vmem(4), "prox_q",
            )(order, q, got_q, new_q, q1)
        deltas = (delta_p, delta_q, flip(delta_p, "ex", 1), flip(delta_q, "ex", 1))
        if step == 0:
            total, a, b = call(
                change_first_body,
                (sds((rows, C), F32), sds(half_shape, BF16), sds(half_shape, BF16)),
                vmem(5), "change_first", 2 * half_flops, 1 << 20,
            )(x, *deltas)
        elif step < STEPS - 1:
            total, a, b = call(
                change_next_body,
                (sds((rows, C), F32), sds(half_shape, BF16), sds(half_shape, BF16)),
                vmem(6), "change_next", 2 * half_flops, 1 << 20,
            )(x, *deltas, total)
        else:
            a, b = call(
                change_last_body,
                (sds(half_shape, F32), sds(half_shape, F32)),
                vmem(6), "change_last", 2 * half_flops, 1 << 20,
            )(x, *deltas, total)
        a, got_a, b, got_b = spread_over_feat(a, b)
    score = margins.astype(F32) + jnp.concatenate([a + got_a, b + got_b])
    if aligned:
        coef = call(coef_body, sds(coef.shape, F32), smem(1) + vmem(4), "coef_out")(
            order, new_p, other_block_p, new_q, other_block_q
        )
    else:
        coef = own_blocks([(new_p, new_q), (other_block_p, other_block_q)], order, own)
    return score, coef


def solution(mesh):
    return jax.shard_map(
        local,
        mesh=mesh,
        in_specs=(
            P("ex", "feat"),
            P("ex", "feat"),
            P("ex"),
            P("ex", None),
            P(None, ("feat", "ex"), None),
            P(None, "feat"),
        ),
        out_specs=(P("ex", None), P(None, ("feat", "ex"), None)),
        check_vma=False,
    )
```

time: 119 us -> 124 us (1.042)
  starting transfers between devices: 29.6 us -> 45.3 us
  waiting for transfers between devices: 63 us -> 50.3 us
  Pallas kernels: 16.6 us -> 21.9 us
  local copies, waits for them, and re-layouts: 6.06 us -> 3.66 us
    ppermute x26 -> x36, starting transfers between devices: 29.6 us -> 45.3 us  [flip(): return lax.ppermute(x, axis, [(i, i ^ bit) for i in range(n)])]
    ppermute x26 -> x36, waiting for transfers between devices: 63 us -> 50.3 us  [flip(): return lax.ppermute(x, axis, [(i, i ^ bit) for i in range(n)])]
    pallas_call x21 -> x32, Pallas kernels: 16.6 us -> 21.9 us  [run(): f(*(x if spec.memory_space == pltpu.SMEM else pltpu.with_memory_space_con...]
    unnamed x17 -> x19, local copies, waits for them, and re-layouts: 6.05 us -> 3.66 us
  transfers between devices with their start and end apart: 26 -> 36, of which waited for: 22 -> 22; matrix products, arithmetic and copies ran while one was open for 3% -> 1% of each run, Pallas kernels for 4% -> 10%
where the time goes in v3:
time: 124 us; the launch traced here: 123 us
  waiting for transfers between devices  50.3 us (41%)
  starting transfers between devices  45.3 us (37%)
  Pallas kernels  21.9 us (18%)
  local copies, waits for them, and re-layouts  3.66 us (3%)
    ppermute x36, waiting for transfers between devices, flip(): return lax.ppermute(x, axis, [(i, i ^ bit) for i in range(n)])  50.3 us
    ppermute x36, starting transfers between devices, flip(): return lax.ppermute(x, axis, [(i, i ^ bit) for i in range(n)])  45.3 us
    pallas_call x32, Pallas kernels, run(): f(*(x if spec.memory_space == pltpu.SMEM else pltpu.with_memory_space_con...  21.9 us
    unnamed x19, local copies, waits for them, and re-layouts  3.66 us
  transfers between devices with their start and end apart: 36, of which 22 were waited for; matrix products, arithmetic and copies ran while one was open for 1% of the time, Pallas kernels for 10%

profile of v3, /device:TPU:0, one launch (start us, length us, event | category | flops | bytes accessed | tf_op | source)
XLA Modules:
  0.0 123.3 jit_solution(18336375032595110592)
XLA Ops:
  0.6 0.9 copy-done
  1.6 0.7 copy-done.3
  2.2 0.7 copy-done.5
  2.9 0.7 copy-done.7
  3.6 4.3 %soft_first.1 = (bf16[1024,1024]{1,0:T(8,128)(2,1)S(1)}, bf16[128,1024]{1,0:T(8,128)(2,1)S(1)}, f32[1024,128]{1,0:T(8,128)S(1)}, f32[2,136,128]{2,1,0:T(8,128)S(1)}, f32[2,136,128]{2,1,0:T(8,128)S(1)}) custom-call(s32[1,3]{1,0:T(1,128)S(1)} %bitcast.2, s32[8,16]{1,0:T(8,128)S(1)} %copy-done.7, bf16[1024,128]{1,0:T(8,128)(2,1)S(1)} %copy-done, ...), custom_call_target="tpu_custom_call" | custom-call | flops 134217728 | bytes 1048576 | tf_op jit(solution)/shard_map/soft_first/pallas_call | solution.py:51
  9.4 0.6 pair_q.3.mine_ref
  10.1 4.0 %collective-permute-start.4 = (bf16[3,136,128]{2,1,0:T(8,128)(2,1)S(1)}, bf16[3,136,128]{2,1,0:T(8,128)(2,1)S(1)}, u32[]{:S(2)}, u32[]{:S(2)}) collective-permute-start(bf16[3,136,128]{2,1,0:T(8,128)(2,1)S(1)} %pair_q.3.mine_ref), channel_id=1, source_target_pairs={{0,4},{1,5},{2,6},{3,7},{4,0},{5,1},{6,2},{7,3},{8,12},{9,13},{10,... | collective-permute-start | bytes 313352 | tf_op jit(solution)/shard_map/ppermute | solution.py:325
  14.1 5.5 %collective-permute-done.4.got_ref = bf16[3,136,128]{2,1,0:T(8,128)(2,1)S(1)} collective-permute-done((bf16[3,136,128]{2,1,0:T(8,128)(2,1)S(1)}, bf16[3,136,128]{2,1,0:T(8,128)(2,1)S(1)}, u32[]{:S(2)}, u32[]{:S(2)}) %collective-permute-start.4) | collective-permute-done | bytes 104480 | tf_op jit(solution)/shard_map/ppermute | solution.py:325
  19.6 0.8 collective-permute-start.5
  20.4 1.4 %collective-permute-start.1 = (bf16[2,136,128]{2,1,0:T(8,128)(2,1)S(1)}, bf16[2,136,128]{2,1,0:T(8,128)(2,1)S(1)}, u32[]{:S(2)}, u32[]{:S(2)}) collective-permute-start(bf16[2,136,128]{2,1,0:T(8,128)(2,1)S(1)} %pair_p.3.mine_ref), channel_id=1, source_target_pairs={{0,2},{1,3},{2,0},{3,1},{4,6},{5,7},{6,4},{7,5},{8,10},{9,11},{10,... | collective-permute-start | bytes 208904 | tf_op jit(solution)/shard_map/ppermute | solution.py:325
  21.8 4.6 %collective-permute-done.1.got_ref = bf16[2,136,128]{2,1,0:T(8,128)(2,1)S(1)} collective-permute-done((bf16[2,136,128]{2,1,0:T(8,128)(2,1)S(1)}, bf16[2,136,128]{2,1,0:T(8,128)(2,1)S(1)}, u32[]{:S(2)}, u32[]{:S(2)}) %collective-permute-start.1) | collective-permute-done | bytes 69664 | tf_op jit(solution)/shard_map/ppermute | solution.py:325
  26.4 2.8 %collective-permute-start.2 = (bf16[2,136,128]{2,1,0:T(8,128)(2,1)S(1)}, bf16[2,136,128]{2,1,0:T(8,128)(2,1)S(1)}, u32[]{:S(2)}, u32[]{:S(2)}) collective-permute-start(bf16[2,136,128]{2,1,0:T(8,128)(2,1)S(1)} %hop_p.3.mine_ref), channel_id=1, source_target_pairs={{0,4},{1,5},{2,6},{3,7},{4,0},{5,1},{6,2},{7,3},{8,12},{9,13},{10,... | collective-permute-start | bytes 208904 | tf_op jit(solution)/shard_map/ppermute | solution.py:325
  29.2 0.7 place.2.old_ref
  30.0 1.9 %collective-permute-done.2.got_ref = bf16[2,136,128]{2,1,0:T(8,128)(2,1)S(1)} collective-permute-done((bf16[2,136,128]{2,1,0:T(8,128)(2,1)S(1)}, bf16[2,136,128]{2,1,0:T(8,128)(2,1)S(1)}, u32[]{:S(2)}, u32[]{:S(2)}) %collective-permute-start.2) | collective-permute-done | bytes 69664 | tf_op jit(solution)/shard_map/ppermute | solution.py:325
  32.1 1.2 collective-permute-done.6.rp_ref
  33.3 0.7 change_first.1
  34.0 1.6 %collective-permute-start.10 = (bf16[512,128]{1,0:T(8,128)(2,1)S(1)}, bf16[512,128]{1,0:T(8,128)(2,1)S(1)}, u32[]{:S(2)}, u32[]{:S(2)}) collective-permute-start(bf16[512,128]{1,0:T(8,128)(2,1)S(1)} %get-tuple-element.56), channel_id=1, source_target_pairs={{0,16},{8,24},{16,0},{24,8},{1,17},{9,25},{17,1},{25,9},{2,18},{10... | collective-permute-start | bytes 393224 | tf_op jit(solution)/shard_map/ppermute | solution.py:325
  35.6 1.5 %collective-permute-start.8 = (bf16[512,128]{1,0:T(8,128)(2,1)S(1)}, bf16[512,128]{1,0:T(8,128)(2,1)S(1)}, u32[]{:S(2)}, u32[]{:S(2)}) collective-permute-start(bf16[512,128]{1,0:T(8,128)(2,1)S(1)} %get-tuple-element.55), channel_id=1, source_target_pairs={{0,8},{8,0},{16,24},{24,16},{1,9},{9,1},{17,25},{25,17},{2,10},{10... | collective-permute-start | bytes 393224 | tf_op jit(solution)/shard_map/ppermute | solution.py:325
  37.1 2.5 %collective-permute-done.10 = bf16[512,128]{1,0:T(8,128)(2,1)S(1)} collective-permute-done((bf16[512,128]{1,0:T(8,128)(2,1)S(1)}, bf16[512,128]{1,0:T(8,128)(2,1)S(1)}, u32[]{:S(2)}, u32[]{:S(2)}) %collective-permute-start.10) | collective-permute-done | bytes 131104 | tf_op jit(solution)/shard_map/ppermute | solution.py:325
  39.7 1.6 %collective-permute-start.11 = (bf16[512,128]{1,0:T(8,128)(2,1)S(1)}, bf16[512,128]{1,0:T(8,128)(2,1)S(1)}, u32[]{:S(2)}, u32[]{:S(2)}) collective-permute-start(bf16[512,128]{1,0:T(8,128)(2,1)S(1)} %add_convert_fusion.2.b_ref), channel_id=1, source_target_pairs={{0,8},{8,0},{16,24},{24,16},{1,9},{9,1},{17,25},{25,17},{2,10},{10... | collective-permute-start | bytes 393224 | tf_op jit(solution)/shard_map/ppermute | solution.py:325
  41.3 1.6 %collective-permute-start.9 = (bf16[512,128]{1,0:T(8,128)(2,1)S(1)}, bf16[512,128]{1,0:T(8,128)(2,1)S(1)}, u32[]{:S(2)}, u32[]{:S(2)}) collective-permute-start(bf16[512,128]{1,0:T(8,128)(2,1)S(1)} %add_convert_fusion.3.a_ref), channel_id=1, source_target_pairs={{0,16},{8,24},{16,0},{24,8},{1,17},{9,25},{17,1},{25,9},{2,18},{10... | collective-permute-start | bytes 393224 | tf_op jit(solution)/shard_map/ppermute | solution.py:325
  42.9 2.3 %prep.3.x_ref = bf16[1024,1024]{1,0:T(8,128)(2,1)S(1)} custom-call(s32[1,3]{1,0:T(1,128)S(1)} %bitcast.5, s32[8,16]{1,0:T(8,128)S(1)} %copy-done.8, bf16[1024,2048]{1,0:T(8,128)(2,1)} %x_ref.5), custom_call_target="tpu_custom_call" | custom-call | bytes 4194304 | tf_op jit(solution)/shard_map/prep/pallas_call | solution.py:51
  45.1 1.2 collective-permute-done.9.ra_ref
  46.3 1.7 %soft_next.2 = (f32[1024,128]{1,0:T(8,128)S(1)}, bf16[128,1024]{1,0:T(8,128)(2,1)S(1)}, f32[1024,128]{1,0:T(8,128)S(1)}, f32[2,136,128]{2,1,0:T(8,128)S(1)}, f32[2,136,128]{2,1,0:T(8,128)S(1)}) custom-call(bf16[1024,128]{1,0:T(8,128)(2,1)S(1)} %copy-done.1, bf16[512,128]{1,0:T(8,128)(2,1)S(1)} %add_convert_fusion.3.a_ref, ...), custom_call_target="tpu_custom_call" | custom-call | flops 134217728 | bytes 1048576 | tf_op jit(solution)/shard_map/soft_next/pallas_call | solution.py:51
  49.5 0.6 pair_q.4.mine_ref
  50.1 2.6 %collective-permute-start.16 = (bf16[3,136,128]{2,1,0:T(8,128)(2,1)S(1)}, bf16[3,136,128]{2,1,0:T(8,128)(2,1)S(1)}, u32[]{:S(2)}, u32[]{:S(2)}) collective-permute-start(bf16[3,136,128]{2,1,0:T(8,128)(2,1)S(1)} %pair_q.4.mine_ref), channel_id=1, source_target_pairs={{0,4},{1,5},{2,6},{3,7},{4,0},{5,1},{6,2},{7,3},{8,12},{9,13},{10,... | collective-permute-start | bytes 313352 | tf_op jit(solution)/shard_map/ppermute | solution.py:325
  52.7 5.6 %collective-permute-done.16.got_ref = bf16[3,136,128]{2,1,0:T(8,128)(2,1)S(1)} collective-permute-done((bf16[3,136,128]{2,1,0:T(8,128)(2,1)S(1)}, bf16[3,136,128]{2,1,0:T(8,128)(2,1)S(1)}, u32[]{:S(2)}, u32[]{:S(2)}) %collective-permute-start.16) | collective-permute-done | bytes 104480 | tf_op jit(solution)/shard_map/ppermute | solution.py:325
  58.3 0.7 collective-permute-start.17
  59.1 1.5 %collective-permute-start.13 = (bf16[2,136,128]{2,1,0:T(8,128)(2,1)S(1)}, bf16[2,136,128]{2,1,0:T(8,128)(2,1)S(1)}, u32[]{:S(2)}, u32[]{:S(2)}) collective-permute-start(bf16[2,136,128]{2,1,0:T(8,128)(2,1)S(1)} %pair_p.4.mine_ref), channel_id=1, source_target_pairs={{0,2},{1,3},{2,0},{3,1},{4,6},{5,7},{6,4},{7,5},{8,10},{9,11},{10,... | collective-permute-start | bytes 208904 | tf_op jit(solution)/shard_map/ppermute | solution.py:325
  60.5 3.9 %collective-permute-done.13.got_ref = bf16[2,136,128]{2,1,0:T(8,128)(2,1)S(1)} collective-permute-done((bf16[2,136,128]{2,1,0:T(8,128)(2,1)S(1)}, bf16[2,136,128]{2,1,0:T(8,128)(2,1)S(1)}, u32[]{:S(2)}, u32[]{:S(2)}) %collective-permute-start.13) | collective-permute-done | bytes 69664 | tf_op jit(solution)/shard_map/ppermute | solution.py:325
  64.5 3.4 %collective-permute-start.14 = (bf16[2,136,128]{2,1,0:T(8,128)(2,1)S(1)}, bf16[2,136,128]{2,1,0:T(8,128)(2,1)S(1)}, u32[]{:S(2)}, u32[]{:S(2)}) collective-permute-start(bf16[2,136,128]{2,1,0:T(8,128)(2,1)S(1)} %hop_p.4.mine_ref), channel_id=1, source_target_pairs={{0,4},{1,5},{2,6},{3,7},{4,0},{5,1},{6,2},{7,3},{8,12},{9,13},{10,... | collective-permute-start | bytes 208904 | tf_op jit(solution)/shard_map/ppermute | solution.py:325
  67.9 0.7 place.3.old1_ref
  68.5 0.6 prox_q.4
  69.2 1.4 %collective-permute-done.14.got_ref = bf16[2,136,128]{2,1,0:T(8,128)(2,1)S(1)} collective-permute-done((bf16[2,136,128]{2,1,0:T(8,128)(2,1)S(1)}, bf16[2,136,128]{2,1,0:T(8,128)(2,1)S(1)}, u32[]{:S(2)}, u32[]{:S(2)}) %collective-permute-start.14) | collective-permute-done | bytes 69664 | tf_op jit(solution)/shard_map/ppermute | solution.py:325
  70.6 0.6 prox_p.4
  71.3 1.2 collective-permute-done.18.rp_ref
  72.5 0.7 change_next.1
  73.2 1.6 %collective-permute-start.22 = (bf16[512,128]{1,0:T(8,128)(2,1)S(1)}, bf16[512,128]{1,0:T(8,128)(2,1)S(1)}, u32[]{:S(2)}, u32[]{:S(2)}) collective-permute-start(bf16[512,128]{1,0:T(8,128)(2,1)S(1)} %get-tuple-element.70), channel_id=1, source_target_pairs={{0,16},{8,24},{16,0},{24,8},{1,17},{9,25},{17,1},{25,9},{2,18},{10... | collective-permute-start | bytes 393224 | tf_op jit(solution)/shard_map/ppermute | solution.py:325
  74.8 0.5 collective-permute-start.20
  75.3 3.5 %collective-permute-done.22 = bf16[512,128]{1,0:T(8,128)(2,1)S(1)} collective-permute-done((bf16[512,128]{1,0:T(8,128)(2,1)S(1)}, bf16[512,128]{1,0:T(8,128)(2,1)S(1)}, u32[]{:S(2)}, u32[]{:S(2)}) %collective-permute-start.22) | collective-permute-done | bytes 131104 | tf_op jit(solution)/shard_map/ppermute | solution.py:325
  78.9 1.2 collective-permute-start.23
  80.1 1.0 collective-permute-start.21
  81.1 2.3 %prep.2.x_ref = bf16[1024,1024]{1,0:T(8,128)(2,1)S(1)} custom-call(s32[1,3]{1,0:T(1,128)S(1)} %bitcast.10, s32[8,16]{1,0:T(8,128)S(1)} %copy-done.8, bf16[1024,2048]{1,0:T(8,128)(2,1)} %x_ref.5), custom_call_target="tpu_custom_call" | custom-call | bytes 4194304 | tf_op jit(solution)/shard_map/prep/pallas_call | solution.py:51
  83.9 1.3 %collective-permute-done.21.ra_ref = bf16[512,128]{1,0:T(8,128)(2,1)S(1)} collective-permute-done((bf16[512,128]{1,0:T(8,128)(2,1)S(1)}, bf16[512,128]{1,0:T(8,128)(2,1)S(1)}, u32[]{:S(2)}, u32[]{:S(2)}) %collective-permute-start.21) | collective-permute-done | bytes 131104 | tf_op jit(solution)/shard_map/ppermute | solution.py:325
  85.2 1.8 %soft_next.3 = (f32[1024,128]{1,0:T(8,128)}, bf16[128,1024]{1,0:T(8,128)(2,1)S(1)}, f32[1024,128]{1,0:T(8,128)S(1)}, f32[2,136,128]{2,1,0:T(8,128)S(1)}, f32[2,136,128]{2,1,0:T(8,128)S(1)}) custom-call(f32[1024,128]{1,0:T(8,128)S(1)} %get-tuple-element.57.score_ref, bf16[512,128]{1,0:T(8,128)(2,1)S(1)} %add_convert_fusion.1.a_ref, ...), custom_call_target="tpu_custom_call" | custom-call | flops 134217728 | bytes 1048576 | tf_op jit(solution)/shard_map/soft_next/pallas_call | solution.py:51
  88.4 2.6 %collective-permute-start.28 = (bf16[2,136,128]{2,1,0:T(8,128)(2,1)S(1)}, bf16[2,136,128]{2,1,0:T(8,128)(2,1)S(1)}, u32[]{:S(2)}, u32[]{:S(2)}) collective-permute-start(bf16[2,136,128]{2,1,0:T(8,128)(2,1)S(1)} %pair_q.5.mine_ref), channel_id=1, source_target_pairs={{0,4},{1,5},{2,6},{3,7},{4,0},{5,1},{6,2},{7,3},{8,12},{9,13},{10,... | collective-permute-start | bytes 208904 | tf_op jit(solution)/shard_map/ppermute | solution.py:325
  91.0 2.2 %collective-permute-start.25 = (bf16[2,136,128]{2,1,0:T(8,128)(2,1)S(1)}, bf16[2,136,128]{2,1,0:T(8,128)(2,1)S(1)}, u32[]{:S(2)}, u32[]{:S(2)}) collective-permute-start(bf16[2,136,128]{2,1,0:T(8,128)(2,1)S(1)} %pair_p.5.mine_ref), channel_id=1, source_target_pairs={{0,2},{1,3},{2,0},{3,1},{4,6},{5,7},{6,4},{7,5},{8,10},{9,11},{10,... | collective-permute-start | bytes 208904 | tf_op jit(solution)/shard_map/ppermute | solution.py:325
  93.7 2.5 %collective-permute-start.29 = (bf16[2,136,128]{2,1,0:T(8,128)(2,1)S(1)}, bf16[2,136,128]{2,1,0:T(8,128)(2,1)S(1)}, u32[]{:S(2)}, u32[]{:S(2)}) collective-permute-start(bf16[2,136,128]{2,1,0:T(8,128)(2,1)S(1)} %hop_q.5.mine_ref), channel_id=1, source_target_pairs={{0,2},{1,3},{2,0},{3,1},{4,6},{5,7},{6,4},{7,5},{8,10},{9,11},{10,... | collective-permute-start | bytes 208904 | tf_op jit(solution)/shard_map/ppermute | solution.py:325
  96.3 3.1 %collective-permute-start.26 = (bf16[2,136,128]{2,1,0:T(8,128)(2,1)S(1)}, bf16[2,136,128]{2,1,0:T(8,128)(2,1)S(1)}, u32[]{:S(2)}, u32[]{:S(2)}) collective-permute-start(bf16[2,136,128]{2,1,0:T(8,128)(2,1)S(1)} %hop_p.5.mine_ref), channel_id=1, source_target_pairs={{0,4},{1,5},{2,6},{3,7},{4,0},{5,1},{6,2},{7,3},{8,12},{9,13},{10,... | collective-permute-start | bytes 208904 | tf_op jit(solution)/shard_map/ppermute | solution.py:325
  99.4 0.6 prox_q.5
  100.1 2.8 %collective-permute-done.26.got_ref = bf16[2,136,128]{2,1,0:T(8,128)(2,1)S(1)} collective-permute-done((bf16[2,136,128]{2,1,0:T(8,128)(2,1)S(1)}, bf16[2,136,128]{2,1,0:T(8,128)(2,1)S(1)}, u32[]{:S(2)}, u32[]{:S(2)}) %collective-permute-start.26) | collective-permute-done | bytes 69664 | tf_op jit(solution)/shard_map/ppermute | solution.py:325
  102.9 0.6 prox_p.5
  103.6 1.2 collective-permute-done.30.rp_ref
  104.8 0.7 change_last.1
  105.5 1.0 collective-permute-start.32
  106.5 1.5 %collective-permute-start.34 = (f32[512,128]{1,0:T(8,128)S(1)}, f32[512,128]{1,0:T(8,128)S(1)}, u32[]{:S(2)}, u32[]{:S(2)}) collective-permute-start(f32[512,128]{1,0:T(8,128)S(1)} %get-tuple-element.85), channel_id=1, source_target_pairs={{0,16},{8,24},{16,0},{24,8},{1,17},{9,25},{17,1},{25,9},{2,18},{10... | collective-permute-start | bytes 786440 | tf_op jit(solution)/shard_map/ppermute | solution.py:325
  108.0 5.9 %collective-permute-done.32 = f32[512,128]{1,0:T(8,128)S(1)} collective-permute-done((f32[512,128]{1,0:T(8,128)S(1)}, f32[512,128]{1,0:T(8,128)S(1)}, u32[]{:S(2)}, u32[]{:S(2)}) %collective-permute-start.32) | collective-permute-done | bytes 262176 | tf_op jit(solution)/shard_map/ppermute | solution.py:325
  114.0 1.0 collective-permute-start.33
  115.1 1.6 %collective-permute-start.35 = (f32[512,128]{1,0:T(8,128)S(1)}, f32[512,128]{1,0:T(8,128)S(1)}, u32[]{:S(2)}, u32[]{:S(2)}) collective-permute-start(f32[512,128]{1,0:T(8,128)S(1)} %add.33), channel_id=1, source_target_pairs={{0,8},{8,0},{16,24},{24,16},{1,9},{9,1},{17,25},{25,17},{2,10},{10... | collective-permute-start | bytes 786440 | tf_op jit(solution)/shard_map/ppermute | solution.py:325
  116.6 0.7 coef_out.1
  117.3 0.7 copy.8
  117.9 3.7 %collective-permute-done.33 = f32[512,128]{1,0:T(8,128)S(1)} collective-permute-done((f32[512,128]{1,0:T(8,128)S(1)}, f32[512,128]{1,0:T(8,128)S(1)}, u32[]{:S(2)}, u32[]{:S(2)}) %collective-permute-start.33) | collective-permute-done | bytes 262176 | tf_op jit(solution)/shard_map/ppermute | solution.py:325
  121.7 0.7 collective-permute-done.35
  122.4 0.8 maximum_add_fusion
  (68 shorter events, 6.5 us)
Async XLA Ops:
  0.6 1.0 copy-start
  1.6 0.7 copy-start.3
  2.2 0.7 copy-start.5
  2.9 0.7 copy-start.7
  7.9 1.5 %copy-start.2 = (f32[2,128,128]{2,1,0:T(8,128)S(1)}, f32[2,128,128]{2,1,0:T(8,128)}, u32[]{:S(2)}) copy-start(f32[2,128,128]{2,1,0:T(8,128)} %coef_ref.7) | copy-start | bytes 393220
  7.9 1.5 %collective-permute-start.3 = (f32[2,136,128]{2,1,0:T(8,128)S(1)}, f32[2,136,128]{2,1,0:T(8,128)S(1)}, u32[]{:S(2)}, u32[]{:S(2)}) collective-permute-start(f32[2,136,128]{2,1,0:T(8,128)S(1)} %get-tuple-element.52), channel_id=1, source_target_pairs={{0,1},{1,0},{2,3},{3,2},{4,5},{5,4},{6,7},{7,6},{8,9},{9,8},{10,11... | collective-permute-start | bytes 417800 | tf_op jit(solution)/shard_map/ppermute | solution.py:325
  8.4 12.0 %collective-permute-start = (f32[2,136,128]{2,1,0:T(8,128)S(1)}, f32[2,136,128]{2,1,0:T(8,128)S(1)}, u32[]{:S(2)}, u32[]{:S(2)}) collective-permute-start(f32[2,136,128]{2,1,0:T(8,128)S(1)} %get-tuple-element.50), channel_id=1, source_target_pairs={{0,1},{1,0},{2,3},{3,2},{4,5},{5,4},{6,7},{7,6},{8,9},{9,8},{10,11... | collective-permute-start | bytes 417800 | tf_op jit(solution)/shard_map/ppermute | solution.py:325
  8.5 20.7 %copy-start.4 = (s32[3,1]{0,1:T(1,128)S(1)}, s32[3,1]{0,1:T(1,128)}, u32[]{:S(2)}) copy-start(s32[3,1]{0,1:T(1,128)} %param.11) | copy-start | bytes 40
  10.1 9.5 %collective-permute-start.4 = (bf16[3,136,128]{2,1,0:T(8,128)(2,1)S(1)}, bf16[3,136,128]{2,1,0:T(8,128)(2,1)S(1)}, u32[]{:S(2)}, u32[]{:S(2)}) collective-permute-start(bf16[3,136,128]{2,1,0:T(8,128)(2,1)S(1)} %pair_q.3.mine_ref), channel_id=1, source_target_pairs={{0,4},{1,5},{2,6},{3,7},{4,0},{5,1},{6,2},{7,3},{8,12},{9,13},{10,... | collective-permute-start | bytes 313352 | tf_op jit(solution)/shard_map/ppermute | solution.py:325
  19.6 9.6 %collective-permute-start.5 = (bf16[4,136,128]{2,1,0:T(8,128)(2,1)S(1)}, bf16[4,136,128]{2,1,0:T(8,128)(2,1)S(1)}, u32[]{:S(2)}, u32[]{:S(2)}) collective-permute-start(bf16[4,136,128]{2,1,0:T(8,128)(2,1)S(1)} %hop_q.3.mine_ref), channel_id=1, source_target_pairs={{0,2},{1,3},{2,0},{3,1},{4,6},{5,7},{6,4},{7,5},{8,10},{9,11},{10,... | collective-permute-start | bytes 417800 | tf_op jit(solution)/shard_map/ppermute | solution.py:325
  20.4 5.9 %collective-permute-start.1 = (bf16[2,136,128]{2,1,0:T(8,128)(2,1)S(1)}, bf16[2,136,128]{2,1,0:T(8,128)(2,1)S(1)}, u32[]{:S(2)}, u32[]{:S(2)}) collective-permute-start(bf16[2,136,128]{2,1,0:T(8,128)(2,1)S(1)} %pair_p.3.mine_ref), channel_id=1, source_target_pairs={{0,2},{1,3},{2,0},{3,1},{4,6},{5,7},{6,4},{7,5},{8,10},{9,11},{10,... | collective-permute-start | bytes 208904 | tf_op jit(solution)/shard_map/ppermute | solution.py:325
  26.4 5.5 %collective-permute-start.2 = (bf16[2,136,128]{2,1,0:T(8,128)(2,1)S(1)}, bf16[2,136,128]{2,1,0:T(8,128)(2,1)S(1)}, u32[]{:S(2)}, u32[]{:S(2)}) collective-permute-start(bf16[2,136,128]{2,1,0:T(8,128)(2,1)S(1)} %hop_p.3.mine_ref), channel_id=1, source_target_pairs={{0,4},{1,5},{2,6},{3,7},{4,0},{5,1},{6,2},{7,3},{8,12},{9,13},{10,... | collective-permute-start | bytes 208904 | tf_op jit(solution)/shard_map/ppermute | solution.py:325
  29.9 13.0 %copy-start.8 = (s32[8,16]{1,0:T(8,128)S(1)}, s32[8,16]{1,0:T(8,128)}, u32[]{:S(2)}) copy-start(s32[8,16]{1,0:T(8,128)} %live_ref.5) | copy-start | bytes 1540
  29.9 2.1 %collective-permute-start.7 = (bf16[2,128,128]{2,1,0:T(8,128)(2,1)S(1)}, bf16[2,128,128]{2,1,0:T(8,128)(2,1)S(1)}, u32[]{:S(2)}, u32[]{:S(2)}) collective-permute-start(bf16[2,128,128]{2,1,0:T(8,128)(2,1)S(1)} %get-tuple-element.54.q_ref), channel_id=1, source_target_pairs={{0,1},{1,0},{2,3},{3,2},{4,5},{5,4},{6,7},{7,6},{8,9},{9,8},{10,11... | collective-permute-start | bytes 196616 | tf_op jit(solution)/shard_map/ppermute | solution.py:325
  32.0 1.3 %collective-permute-start.6 = (bf16[2,128,128]{2,1,0:T(8,128)(2,1)S(1)}, bf16[2,128,128]{2,1,0:T(8,128)(2,1)S(1)}, u32[]{:S(2)}, u32[]{:S(2)}) collective-permute-start(bf16[2,128,128]{2,1,0:T(8,128)(2,1)S(1)} %get-tuple-element.53.p_ref), channel_id=1, source_target_pairs={{0,1},{1,0},{2,3},{3,2},{4,5},{5,4},{6,7},{7,6},{8,9},{9,8},{10,11... | collective-permute-start | bytes 196616 | tf_op jit(solution)/shard_map/ppermute | solution.py:325
  34.0 5.6 %collective-permute-start.10 = (bf16[512,128]{1,0:T(8,128)(2,1)S(1)}, bf16[512,128]{1,0:T(8,128)(2,1)S(1)}, u32[]{:S(2)}, u32[]{:S(2)}) collective-permute-start(bf16[512,128]{1,0:T(8,128)(2,1)S(1)} %get-tuple-element.56), channel_id=1, source_target_pairs={{0,16},{8,24},{16,0},{24,8},{1,17},{9,25},{17,1},{25,9},{2,18},{10... | collective-permute-start | bytes 393224 | tf_op jit(solution)/shard_map/ppermute | solution.py:325
  35.6 5.6 %collective-permute-start.8 = (bf16[512,128]{1,0:T(8,128)(2,1)S(1)}, bf16[512,128]{1,0:T(8,128)(2,1)S(1)}, u32[]{:S(2)}, u32[]{:S(2)}) collective-permute-start(bf16[512,128]{1,0:T(8,128)(2,1)S(1)} %get-tuple-element.55), channel_id=1, source_target_pairs={{0,8},{8,0},{16,24},{24,16},{1,9},{9,1},{17,25},{25,17},{2,10},{10... | collective-permute-start | bytes 393224 | tf_op jit(solution)/shard_map/ppermute | solution.py:325
  39.7 5.5 %collective-permute-start.11 = (bf16[512,128]{1,0:T(8,128)(2,1)S(1)}, bf16[512,128]{1,0:T(8,128)(2,1)S(1)}, u32[]{:S(2)}, u32[]{:S(2)}) collective-permute-start(bf16[512,128]{1,0:T(8,128)(2,1)S(1)} %add_convert_fusion.2.b_ref), channel_id=1, source_target_pairs={{0,8},{8,0},{16,24},{24,16},{1,9},{9,1},{17,25},{25,17},{2,10},{10... | collective-permute-start | bytes 393224 | tf_op jit(solution)/shard_map/ppermute | solution.py:325
  41.3 5.0 %copy-start.1 = (bf16[1024,128]{1,0:T(8,128)(2,1)S(1)}, bf16[1024,128]{1,0:T(8,128)(2,1)}, u32[]{:S(2)}) copy-start(bf16[1024,128]{1,0:T(8,128)(2,1)} %score_ref.1) | copy-start | bytes 786436
  41.3 5.0 %collective-permute-start.9 = (bf16[512,128]{1,0:T(8,128)(2,1)S(1)}, bf16[512,128]{1,0:T(8,128)(2,1)S(1)}, u32[]{:S(2)}, u32[]{:S(2)}) collective-permute-start(bf16[512,128]{1,0:T(8,128)(2,1)S(1)} %add_convert_fusion.3.a_ref), channel_id=1, source_target_pairs={{0,16},{8,24},{16,0},{24,8},{1,17},{9,25},{17,1},{25,9},{2,18},{10... | collective-permute-start | bytes 393224 | tf_op jit(solution)/shard_map/ppermute | solution.py:325
  48.0 1.4 %collective-permute-start.15 = (f32[2,136,128]{2,1,0:T(8,128)S(1)}, f32[2,136,128]{2,1,0:T(8,128)S(1)}, u32[]{:S(2)}, u32[]{:S(2)}) collective-permute-start(f32[2,136,128]{2,1,0:T(8,128)S(1)} %get-tuple-element.64), channel_id=1, source_target_pairs={{0,1},{1,0},{2,3},{3,2},{4,5},{5,4},{6,7},{7,6},{8,9},{9,8},{10,11... | collective-permute-start | bytes 417800 | tf_op jit(solution)/shard_map/ppermute | solution.py:325
  48.1 10.9 %collective-permute-start.12 = (f32[2,136,128]{2,1,0:T(8,128)S(1)}, f32[2,136,128]{2,1,0:T(8,128)S(1)}, u32[]{:S(2)}, u32[]{:S(2)}) collective-permute-start(f32[2,136,128]{2,1,0:T(8,128)S(1)} %get-tuple-element.61), channel_id=1, source_target_pairs={{0,1},{1,0},{2,3},{3,2},{4,5},{5,4},{6,7},{7,6},{8,9},{9,8},{10,11... | collective-permute-start | bytes 417800 | tf_op jit(solution)/shard_map/ppermute | solution.py:325
  50.1 8.2 %collective-permute-start.16 = (bf16[3,136,128]{2,1,0:T(8,128)(2,1)S(1)}, bf16[3,136,128]{2,1,0:T(8,128)(2,1)S(1)}, u32[]{:S(2)}, u32[]{:S(2)}) collective-permute-start(bf16[3,136,128]{2,1,0:T(8,128)(2,1)S(1)} %pair_q.4.mine_ref), channel_id=1, source_target_pairs={{0,4},{1,5},{2,6},{3,7},{4,0},{5,1},{6,2},{7,3},{8,12},{9,13},{10,... | collective-permute-start | bytes 313352 | tf_op jit(solution)/shard_map/ppermute | solution.py:325
  58.3 9.5 %collective-permute-start.17 = (bf16[4,136,128]{2,1,0:T(8,128)(2,1)S(1)}, bf16[4,136,128]{2,1,0:T(8,128)(2,1)S(1)}, u32[]{:S(2)}, u32[]{:S(2)}) collective-permute-start(bf16[4,136,128]{2,1,0:T(8,128)(2,1)S(1)} %hop_q.4.mine_ref), channel_id=1, source_target_pairs={{0,2},{1,3},{2,0},{3,1},{4,6},{5,7},{6,4},{7,5},{8,10},{9,11},{10,... | collective-permute-start | bytes 417800 | tf_op jit(solution)/shard_map/ppermute | solution.py:325
  59.1 5.4 %collective-permute-start.13 = (bf16[2,136,128]{2,1,0:T(8,128)(2,1)S(1)}, bf16[2,136,128]{2,1,0:T(8,128)(2,1)S(1)}, u32[]{:S(2)}, u32[]{:S(2)}) collective-permute-start(bf16[2,136,128]{2,1,0:T(8,128)(2,1)S(1)} %pair_p.4.mine_ref), channel_id=1, source_target_pairs={{0,2},{1,3},{2,0},{3,1},{4,6},{5,7},{6,4},{7,5},{8,10},{9,11},{10,... | collective-permute-start | bytes 208904 | tf_op jit(solution)/shard_map/ppermute | solution.py:325
  64.5 6.1 %collective-permute-start.14 = (bf16[2,136,128]{2,1,0:T(8,128)(2,1)S(1)}, bf16[2,136,128]{2,1,0:T(8,128)(2,1)S(1)}, u32[]{:S(2)}, u32[]{:S(2)}) collective-permute-start(bf16[2,136,128]{2,1,0:T(8,128)(2,1)S(1)} %hop_p.4.mine_ref), channel_id=1, source_target_pairs={{0,4},{1,5},{2,6},{3,7},{4,0},{5,1},{6,2},{7,3},{8,12},{9,13},{10,... | collective-permute-start | bytes 208904 | tf_op jit(solution)/shard_map/ppermute | solution.py:325
  69.1 2.1 %collective-permute-start.19 = (bf16[2,128,128]{2,1,0:T(8,128)(2,1)S(1)}, bf16[2,128,128]{2,1,0:T(8,128)(2,1)S(1)}, u32[]{:S(2)}, u32[]{:S(2)}) collective-permute-start(bf16[2,128,128]{2,1,0:T(8,128)(2,1)S(1)} %get-tuple-element.67.q_ref), channel_id=1, source_target_pairs={{0,1},{1,0},{2,3},{3,2},{4,5},{5,4},{6,7},{7,6},{8,9},{9,8},{10,11... | collective-permute-start | bytes 196616 | tf_op jit(solution)/shard_map/ppermute | solution.py:325
  71.2 1.3 %collective-permute-start.18 = (bf16[2,128,128]{2,1,0:T(8,128)(2,1)S(1)}, bf16[2,128,128]{2,1,0:T(8,128)(2,1)S(1)}, u32[]{:S(2)}, u32[]{:S(2)}) collective-permute-start(bf16[2,128,128]{2,1,0:T(8,128)(2,1)S(1)} %get-tuple-element.65.p_ref), channel_id=1, source_target_pairs={{0,1},{1,0},{2,3},{3,2},{4,5},{5,4},{6,7},{7,6},{8,9},{9,8},{10,11... | collective-permute-start | bytes 196616 | tf_op jit(solution)/shard_map/ppermute | solution.py:325
  73.2 5.6 %collective-permute-start.22 = (bf16[512,128]{1,0:T(8,128)(2,1)S(1)}, bf16[512,128]{1,0:T(8,128)(2,1)S(1)}, u32[]{:S(2)}, u32[]{:S(2)}) collective-permute-start(bf16[512,128]{1,0:T(8,128)(2,1)S(1)} %get-tuple-element.70), channel_id=1, source_target_pairs={{0,16},{8,24},{16,0},{24,8},{1,17},{9,25},{17,1},{25,9},{2,18},{10... | collective-permute-start | bytes 393224 | tf_op jit(solution)/shard_map/ppermute | solution.py:325
  74.8 5.3 %collective-permute-start.20 = (bf16[512,128]{1,0:T(8,128)(2,1)S(1)}, bf16[512,128]{1,0:T(8,128)(2,1)S(1)}, u32[]{:S(2)}, u32[]{:S(2)}) collective-permute-start(bf16[512,128]{1,0:T(8,128)(2,1)S(1)} %get-tuple-element.69), channel_id=1, source_target_pairs={{0,8},{8,0},{16,24},{24,16},{1,9},{9,1},{17,25},{25,17},{2,10},{10... | collective-permute-start | bytes 393224 | tf_op jit(solution)/shard_map/ppermute | solution.py:325
  78.9 5.0 %collective-permute-start.23 = (bf16[512,128]{1,0:T(8,128)(2,1)S(1)}, bf16[512,128]{1,0:T(8,128)(2,1)S(1)}, u32[]{:S(2)}, u32[]{:S(2)}) collective-permute-start(bf16[512,128]{1,0:T(8,128)(2,1)S(1)} %add_convert_fusion.b_ref), channel_id=1, source_target_pairs={{0,8},{8,0},{16,24},{24,16},{1,9},{9,1},{17,25},{25,17},{2,10},{10... | collective-permute-start | bytes 393224 | tf_op jit(solution)/shard_map/ppermute | solution.py:325
  80.1 5.0 %copy-start.6 = (s32[1024]{0:T(1024)S(1)}, s32[1024]{0:T(1024)}, u32[]{:S(2)}) copy-start(s32[1024]{0:T(1024)} %param.8) | copy-start | bytes 12292
  80.1 5.0 %collective-permute-start.21 = (bf16[512,128]{1,0:T(8,128)(2,1)S(1)}, bf16[512,128]{1,0:T(8,128)(2,1)S(1)}, u32[]{:S(2)}, u32[]{:S(2)}) collective-permute-start(bf16[512,128]{1,0:T(8,128)(2,1)S(1)} %add_convert_fusion.1.a_ref), channel_id=1, source_target_pairs={{0,16},{8,24},{16,0},{24,8},{1,17},{9,25},{17,1},{25,9},{2,18},{10... | collective-permute-start | bytes 393224 | tf_op jit(solution)/shard_map/ppermute | solution.py:325
  86.9 1.4 %collective-permute-start.27 = (f32[2,136,128]{2,1,0:T(8,128)S(1)}, f32[2,136,128]{2,1,0:T(8,128)S(1)}, u32[]{:S(2)}, u32[]{:S(2)}) collective-permute-start(f32[2,136,128]{2,1,0:T(8,128)S(1)} %get-tuple-element.79), channel_id=1, source_target_pairs={{0,1},{1,0},{2,3},{3,2},{4,5},{5,4},{6,7},{7,6},{8,9},{9,8},{10,11... | collective-permute-start | bytes 417800 | tf_op jit(solution)/shard_map/ppermute | solution.py:325
  87.0 4.0 %collective-permute-start.24 = (f32[2,136,128]{2,1,0:T(8,128)S(1)}, f32[2,136,128]{2,1,0:T(8,128)S(1)}, u32[]{:S(2)}, u32[]{:S(2)}) collective-permute-start(f32[2,136,128]{2,1,0:T(8,128)S(1)} %get-tuple-element.74), channel_id=1, source_target_pairs={{0,1},{1,0},{2,3},{3,2},{4,5},{5,4},{6,7},{7,6},{8,9},{9,8},{10,11... | collective-permute-start | bytes 417800 | tf_op jit(solution)/shard_map/ppermute | solution.py:325
  88.4 5.3 %collective-permute-start.28 = (bf16[2,136,128]{2,1,0:T(8,128)(2,1)S(1)}, bf16[2,136,128]{2,1,0:T(8,128)(2,1)S(1)}, u32[]{:S(2)}, u32[]{:S(2)}) collective-permute-start(bf16[2,136,128]{2,1,0:T(8,128)(2,1)S(1)} %pair_q.5.mine_ref), channel_id=1, source_target_pairs={{0,4},{1,5},{2,6},{3,7},{4,0},{5,1},{6,2},{7,3},{8,12},{9,13},{10,... | collective-permute-start | bytes 208904 | tf_op jit(solution)/shard_map/ppermute | solution.py:325
  91.0 5.2 %collective-permute-start.25 = (bf16[2,136,128]{2,1,0:T(8,128)(2,1)S(1)}, bf16[2,136,128]{2,1,0:T(8,128)(2,1)S(1)}, u32[]{:S(2)}, u32[]{:S(2)}) collective-permute-start(bf16[2,136,128]{2,1,0:T(8,128)(2,1)S(1)} %pair_p.5.mine_ref), channel_id=1, source_target_pairs={{0,2},{1,3},{2,0},{3,1},{4,6},{5,7},{6,4},{7,5},{8,10},{9,11},{10,... | collective-permute-start | bytes 208904 | tf_op jit(solution)/shard_map/ppermute | solution.py:325
  93.7 5.7 %collective-permute-start.29 = (bf16[2,136,128]{2,1,0:T(8,128)(2,1)S(1)}, bf16[2,136,128]{2,1,0:T(8,128)(2,1)S(1)}, u32[]{:S(2)}, u32[]{:S(2)}) collective-permute-start(bf16[2,136,128]{2,1,0:T(8,128)(2,1)S(1)} %hop_q.5.mine_ref), channel_id=1, source_target_pairs={{0,2},{1,3},{2,0},{3,1},{4,6},{5,7},{6,4},{7,5},{8,10},{9,11},{10,... | collective-permute-start | bytes 208904 | tf_op jit(solution)/shard_map/ppermute | solution.py:325
  96.3 6.6 %collective-permute-start.26 = (bf16[2,136,128]{2,1,0:T(8,128)(2,1)S(1)}, bf16[2,136,128]{2,1,0:T(8,128)(2,1)S(1)}, u32[]{:S(2)}, u32[]{:S(2)}) collective-permute-start(bf16[2,136,128]{2,1,0:T(8,128)(2,1)S(1)} %hop_p.5.mine_ref), channel_id=1, source_target_pairs={{0,4},{1,5},{2,6},{3,7},{4,0},{5,1},{6,2},{7,3},{8,12},{9,13},{10,... | collective-permute-start | bytes 208904 | tf_op jit(solution)/shard_map/ppermute | solution.py:325
  100.0 3.6 %collective-permute-start.31 = (bf16[2,128,128]{2,1,0:T(8,128)(2,1)S(1)}, bf16[2,128,128]{2,1,0:T(8,128)(2,1)S(1)}, u32[]{:S(2)}, u32[]{:S(2)}) collective-permute-start(bf16[2,128,128]{2,1,0:T(8,128)(2,1)S(1)} %get-tuple-element.82.q_ref), channel_id=1, source_target_pairs={{0,1},{1,0},{2,3},{3,2},{4,5},{5,4},{6,7},{7,6},{8,9},{9,8},{10,11... | collective-permute-start | bytes 196616 | tf_op jit(solution)/shard_map/ppermute | solution.py:325
  103.5 1.3 %collective-permute-start.30 = (bf16[2,128,128]{2,1,0:T(8,128)(2,1)S(1)}, bf16[2,128,128]{2,1,0:T(8,128)(2,1)S(1)}, u32[]{:S(2)}, u32[]{:S(2)}) collective-permute-start(bf16[2,128,128]{2,1,0:T(8,128)(2,1)S(1)} %get-tuple-element.77.p_ref), channel_id=1, source_target_pairs={{0,1},{1,0},{2,3},{3,2},{4,5},{5,4},{6,7},{7,6},{8,9},{9,8},{10,11... | collective-permute-start | bytes 196616 | tf_op jit(solution)/shard_map/ppermute | solution.py:325
  105.5 8.4 %collective-permute-start.32 = (f32[512,128]{1,0:T(8,128)S(1)}, f32[512,128]{1,0:T(8,128)S(1)}, u32[]{:S(2)}, u32[]{:S(2)}) collective-permute-start(f32[512,128]{1,0:T(8,128)S(1)} %get-tuple-element.84), channel_id=1, source_target_pairs={{0,8},{8,0},{16,24},{24,16},{1,9},{9,1},{17,25},{25,17},{2,10},{10... | collective-permute-start | bytes 786440 | tf_op jit(solution)/shard_map/ppermute | solution.py:325
  106.5 8.5 %collective-permute-start.34 = (f32[512,128]{1,0:T(8,128)S(1)}, f32[512,128]{1,0:T(8,128)S(1)}, u32[]{:S(2)}, u32[]{:S(2)}) collective-permute-start(f32[512,128]{1,0:T(8,128)S(1)} %get-tuple-element.85), channel_id=1, source_target_pairs={{0,16},{8,24},{16,0},{24,8},{1,17},{9,25},{17,1},{25,9},{2,18},{10... | collective-permute-start | bytes 786440 | tf_op jit(solution)/shard_map/ppermute | solution.py:325
  114.0 7.6 %collective-permute-start.33 = (f32[512,128]{1,0:T(8,128)S(1)}, f32[512,128]{1,0:T(8,128)S(1)}, u32[]{:S(2)}, u32[]{:S(2)}) collective-permute-start(f32[512,128]{1,0:T(8,128)S(1)} %add.31), channel_id=1, source_target_pairs={{0,16},{8,24},{16,0},{24,8},{1,17},{9,25},{17,1},{25,9},{2,18},{10... | collective-permute-start | bytes 786440 | tf_op jit(solution)/shard_map/ppermute | solution.py:325
  115.1 7.3 %collective-permute-start.35 = (f32[512,128]{1,0:T(8,128)S(1)}, f32[512,128]{1,0:T(8,128)S(1)}, u32[]{:S(2)}, u32[]{:S(2)}) collective-permute-start(f32[512,128]{1,0:T(8,128)S(1)} %add.33), channel_id=1, source_target_pairs={{0,8},{8,0},{16,24},{24,16},{1,9},{9,1},{17,25},{25,17},{2,10},{10... | collective-permute-start | bytes 786440 | tf_op jit(solution)/shard_map/ppermute | solution.py:325

commit v4 on v0

v4 whole, which is shorter than its diff:
```python
import functools

import jax
import jax.numpy as jnp
from jax import lax
from jax.experimental import pallas as pl
from jax.experimental.pallas import tpu as pltpu
from jax.sharding import PartitionSpec as P

C = 128
BLOCK = 1024
STEPS = 3
HALF = BLOCK // 2
TILE = 128
NB = HALF // TILE
ROWS = C + 8

ridge = 0.002
lasso = 0.005

F32 = jnp.float32
BF16 = jnp.bfloat16


def vmem(n):
    return [pl.BlockSpec(memory_space=pltpu.VMEM)] * n


def smem(n):
    return [pl.BlockSpec(memory_space=pltpu.SMEM)] * n


def hbm(n):
    return [pl.BlockSpec(memory_space=pltpu.HBM)] * n


def call(body, outs, in_specs, name, flops=0, nbytes=0, **kw):
    f = pl.pallas_call(
        body,
        out_shape=outs,
        in_specs=in_specs,
        out_specs=jax.tree.map(lambda _: pl.BlockSpec(memory_space=pltpu.VMEM), outs),
        name=name,
        cost_estimate=pl.CostEstimate(flops=flops, bytes_accessed=nbytes, transcendentals=0),
        compiler_params=pltpu.CompilerParams(vmem_limit_bytes=16 << 20),
        **kw,
    )

    def run(*args):
        return f(
            *(
                x
                if spec.memory_space == pltpu.SMEM
                else pltpu.with_memory_space_constraint(x, spec.memory_space)
                for spec, x in zip(in_specs, args, strict=True)
            )
        )

    return run


def sds(shape, dtype):
    return pltpu.VMEM(shape, dtype)


def load_block(chosen, x_ref, buf, sems):
    copies = [
        pltpu.make_async_copy(
            x_ref.at[pl.ds(r * TILE, TILE), pl.ds(pl.multiple_of(chosen * BLOCK, BLOCK), BLOCK)],
            buf.at[pl.ds(r * TILE, TILE)],
            sems.at[r],
        )
        for r in range(buf.shape[0] // TILE)
    ]
    for copy in copies:
        copy.start()
    return copies


def mask_tile(r, chosen, core, live_ref, buf, out_ref):
    tiles = BLOCK // TILE
    here = pl.ds(r * TILE, TILE)
    for k in range(tiles):
        col = 2 * (k % NB) + (core if k < NB else 1 - core)
        live = live_ref[r, chosen * tiles + col].astype(F32)
        tile = buf[here, pl.ds(pl.multiple_of(col * TILE, TILE), TILE)]
        out_ref[here, k * TILE : (k + 1) * TILE] = (tile.astype(F32) * live).astype(BF16)


def prep_body(step, order_ref, live_ref, x_ref, out_ref, buf, sems):
    chosen, core = order_ref[0, step], lax.axis_index("ex") % 2
    copies = load_block(chosen, x_ref, buf, sems)
    for r, copy in enumerate(copies):
        copy.wait()
        mask_tile(r, chosen, core, live_ref, buf, out_ref)


def block_scratch(rows):
    return [pltpu.VMEM((rows, BLOCK), BF16), pltpu.SemaphoreType.DMA((rows // TILE,))]


def prep(order, tile_live, x_values, step):
    rows = x_values.shape[0]
    return call(
        functools.partial(prep_body, step),
        sds((rows, BLOCK), BF16),
        smem(2) + hbm(1),
        "prep",
        nbytes=4 * rows * BLOCK,
        scratch_shapes=block_scratch(rows),
    )(order, tile_live, x_values)


def prep_general(x_values, tile_live, chosen, core, own):
    rows = x_values.shape[0]
    tiles = BLOCK // TILE
    x = lax.dynamic_slice_in_dim(x_values, chosen * BLOCK, BLOCK, 1)
    live = lax.dynamic_slice_in_dim(tile_live, chosen * tiles, tiles, 1).astype(BF16)
    x = x.reshape(rows // TILE, TILE, tiles, TILE) * live[:, None, :, None]
    x = x.reshape(rows, HALF // own, 2, own)
    mine = lax.dynamic_index_in_dim(x, core, 2, keepdims=False)
    other = lax.dynamic_index_in_dim(x, 1 - core, 2, keepdims=False)
    return jnp.concatenate([mine.reshape(rows, HALF), other.reshape(rows, HALF)], axis=1)


def half_sums(res_t, spread_ref, x_ref, first, g_ref):
    rows = x_ref.shape[0]
    grad = jnp.dot(res_t, x_ref[:, first : first + HALF], preferred_element_type=F32)
    row = lax.broadcasted_iota(jnp.int32, (8, TILE), 0)
    for k in range(NB):
        lanes = slice(first + k * TILE, first + (k + 1) * TILE)
        acc = jnp.zeros((8, TILE), F32)
        for r in range(rows // TILE):
            here = slice(r * TILE, (r + 1) * TILE)
            x = x_ref[here, lanes].astype(F32)
            term = x * x * spread_ref[here, :]
            acc = acc + jnp.sum(term.reshape(TILE // 8, 8, TILE), axis=0)
        total = jnp.sum(acc, axis=0, keepdims=True)
        g_ref[k, 0:C, :] = grad[:, k * TILE : (k + 1) * TILE]
        g_ref[k, C:ROWS, :] = jnp.where(row == 0, total, 0.0)


def soft_rows(score, labels, here, res_ref, spread_ref):
    top = jnp.max(score, axis=0, keepdims=True)
    expo = jnp.exp(score - top)
    prob = expo / jnp.sum(expo, axis=0, keepdims=True)
    classes = lax.broadcasted_iota(jnp.int32, (C, TILE), 0)
    residual = prob - jnp.where(labels == classes, 1.0, 0.0)
    spread = (1.0 - jnp.sum(prob * prob, axis=0, keepdims=True)).astype(BF16).astype(F32)
    res_ref[:, here] = residual.astype(BF16)
    spread_ref[here, :] = jnp.broadcast_to(spread, (TILE, TILE)).T


def tiles_of(rows):
    return [(r, slice(r * TILE, (r + 1) * TILE)) for r in range(rows // TILE)]


def first_body(
    order_hbm, live_hbm, margins_hbm, lab_hbm, coef_hbm, x_hbm,
    x_ref, score_ref, res_ref, spread_ref, g_ref, first_ref, other_ref, *rest,
):
    same_refs = rest[: STEPS - 1]
    order, live, margins, labels, coef, small, buf, sems = rest[STEPS - 1 :]
    loads = [
        pltpu.make_async_copy(src, dst, small.at[i])
        for i, (src, dst) in enumerate(
            ((order_hbm, order), (live_hbm, live), (margins_hbm, margins), (lab_hbm, labels), (coef_hbm, coef))
        )
    ]
    for load in loads:
        load.start()
    loads[0].wait()
    chosen, core = order[0, 0], lax.axis_index("ex") % 2
    copies = load_block(chosen, x_hbm, buf, sems)
    for load in loads[1:]:
        load.wait()
    for r, here in tiles_of(margins.shape[0]):
        score = margins[here, :].astype(F32).T
        score_ref[:, here] = score
        soft_rows(score, labels[r : r + 1, :], here, res_ref, spread_ref)
    first_ref[...] = coef[chosen].T
    other_ref[...] = coef[1 - chosen].T
    for step, same_ref in enumerate(same_refs):
        same_ref[...] = jnp.full((8, TILE), (order[0, step + 1] == chosen).astype(F32))
    for r, copy in enumerate(copies):
        copy.wait()
        mask_tile(r, chosen, core, live, buf, x_ref)
    half_sums(res_ref[...], spread_ref, x_ref, HALF, g_ref)


def first_general_body(margins_ref, lab_ref, x_ref, score_ref, res_ref, spread_ref, g_ref):
    for r, here in tiles_of(margins_ref.shape[0]):
        score = margins_ref[here, :].astype(F32).T
        score_ref[:, here] = score
        soft_rows(score, lab_ref[r : r + 1, :], here, res_ref, spread_ref)
    half_sums(res_ref[...], spread_ref, x_ref, HALF, g_ref)


def next_body(before_ref, part_ref, got_ref, lab_ref, x_ref, score_ref, res_ref, spread_ref, g_ref):
    for r, here in tiles_of(before_ref.shape[1]):
        change = part_ref[:, here].astype(F32) + got_ref[:, here].astype(F32)
        score = before_ref[:, here] + change
        score_ref[:, here] = score
        soft_rows(score, lab_ref[r : r + 1, :], here, res_ref, spread_ref)
    half_sums(res_ref[...], spread_ref, x_ref, HALF, g_ref)


def own_body(res_ref, spread_ref, x_ref, g_ref):
    half_sums(res_ref[...], spread_ref, x_ref, 0, g_ref)


def encode(k, grad, curv, out_ref):
    out_ref[k, 0:C, :] = grad.astype(BF16)
    high = curv.astype(BF16).astype(F32)
    low = curv - high
    row = lax.broadcasted_iota(jnp.int32, (8, TILE), 0)
    tail = jnp.where(row == 0, high, jnp.where(row == 1, low, 0.0))
    out_ref[k, C:ROWS, :] = tail.astype(BF16)


def pair_body(own_ref, got_ref, out_ref):
    for k in range(NB):
        total = own_ref[k] + got_ref[k]
        encode(k, total[0:C], total[C : C + 1], out_ref)


def pair_with_body(own_ref, got_ref, coef_ref, out_ref):
    pair_body(own_ref, got_ref, out_ref)
    out_ref[NB, 0:C, :] = coef_ref[...].astype(BF16)
    out_ref[NB, C:ROWS, :] = jnp.zeros((ROWS - C, TILE), BF16)


def decode_sum(k, mine_ref, got_ref):
    total = mine_ref[k].astype(F32) + got_ref[k].astype(F32)
    return total[0:C], total[C : C + 1] + total[C + 1 : C + 2]


def hop_body(mine_ref, got_ref, out_ref):
    for k in range(NB):
        encode(k, *decode_sum(k, mine_ref, got_ref), out_ref)


def hop_with_body(mine_ref, got_ref, out_ref):
    hop_body(mine_ref, got_ref, out_ref)
    out_ref[NB] = mine_ref[NB]
    out_ref[NB + 1] = got_ref[NB]


def place_body(mine_ref, got_ref, coef_ref, out_ref):
    me = lax.axis_index("ex")
    place, first = me // 2, 1 + me % 2
    out_ref[place] = coef_ref[...]
    out_ref[jnp.bitwise_xor(place, first)] = mine_ref[NB + 1, 0:C, :].astype(F32)
    out_ref[jnp.bitwise_xor(place, 3 - first)] = got_ref[NB, 0:C, :].astype(F32)
    out_ref[jnp.bitwise_xor(place, 3)] = got_ref[NB + 1, 0:C, :].astype(F32)


def step_coef(count, k, mine_ref, got_ref, old):
    grad, curv = decode_sum(k, mine_ref, got_ref)
    inverse = 1.0 / (curv / count + ridge)
    shifted = old - grad * (inverse / count)
    limit = lasso * inverse
    return shifted - jnp.clip(shifted, -limit, limit)


def prox_first_body(count, mine_ref, got_ref, old_ref, new_ref, delta_ref):
    for k in range(NB):
        old = old_ref[k]
        new = step_coef(count, k, mine_ref, got_ref, old)
        new_ref[k] = new
        delta_ref[:, k * TILE : (k + 1) * TILE] = (new - old).astype(BF16)


def prox_body(count, same_ref, mine_ref, got_ref, old0_ref, old1_ref, new0_ref, new1_ref, delta_ref):
    same = jnp.broadcast_to(same_ref[0:1, :], (C, TILE)) > 0.5
    for k in range(NB):
        old0, old1 = old0_ref[k], old1_ref[k]
        old = jnp.where(same, old0, old1)
        new = step_coef(count, k, mine_ref, got_ref, old)
        new0_ref[k] = jnp.where(same, new, old0)
        new1_ref[k] = jnp.where(same, old1, new)
        delta_ref[:, k * TILE : (k + 1) * TILE] = (new - old).astype(BF16)


def coef_body(order_ref, first_ref, other_ref, out_ref):
    place = lax.axis_index("ex") // 2
    block = order_ref[0, 0]
    out_ref[block] = first_ref[place].T
    out_ref[1 - block] = other_ref[place].T


def contrib(x_ref, first, delta_ref):
    return lax.dot_general(
        x_ref[:, first : first + HALF], delta_ref[...],
        (((1,), (1,)), ((), ())), preferred_element_type=F32,
    )


def mine_body(x_ref, delta_ref, part_ref):
    part_ref[...] = contrib(x_ref, 0, delta_ref)


def change_first_body(x_ref, part_ref, delta_ref, total_ref, out_ref):
    total_ref[...] = part_ref[...] + contrib(x_ref, HALF, delta_ref)
    for _, here in tiles_of(x_ref.shape[0]):
        out_ref[:, here] = total_ref[here, :].T.astype(BF16)


def change_next_body(x_ref, part_ref, delta_ref, before_ref, total_ref, out_ref):
    part = part_ref[...] + contrib(x_ref, HALF, delta_ref)
    total_ref[...] = before_ref[...] + part
    for _, here in tiles_of(x_ref.shape[0]):
        out_ref[:, here] = part[here, :].T.astype(BF16)


def change_last_body(x_ref, part_ref, delta_ref, before_ref, out_ref):
    out_ref[...] = before_ref[...] + (part_ref[...] + contrib(x_ref, HALF, delta_ref))


def bits(n):
    return [1 << i for i in range(n.bit_length() - 1)]


def swap(x, move):
    n_feat, n_ex = lax.axis_size("feat"), lax.axis_size("ex")
    pairs = []
    for f in range(n_feat):
        for e in range(n_ex):
            to_f, to_e = move(f, e)
            pairs.append((f * n_ex + e, to_f * n_ex + to_e))
    return lax.ppermute(x, ("feat", "ex"), pairs)


def swap_core(x):
    return swap(x, lambda f, e: (f, e ^ 1))


def by_core(order, e, n):
    return order[n] if e % 2 == 0 else order[len(order) - 1 - n]


def add_as(x, y, dtype):
    return (x.astype(F32) + y.astype(F32)).astype(dtype)


def sum_over_feat(x):
    order = bits(lax.axis_size("feat"))
    for n in range(len(order)):
        got = swap(x, lambda f, e, n=n: (f ^ by_core(order, e, n), e))
        if n == len(order) - 1:
            return x, got
        x = add_as(x, got, x.dtype)


def gather_blocks(coef, order, z_bits):
    n_z = 1 << len(z_bits)
    far = jnp.swapaxes(coef, 1, 2)[:, None]
    for bit in z_bits:
        far = jnp.concatenate([far, swap(far, lambda f, e, bit=bit: (f, e ^ bit))], axis=1)
    place = lax.axis_index("ex") // 2
    far = jnp.take(far, jnp.bitwise_xor(jnp.arange(n_z), place), axis=1)
    old = far.transpose(0, 2, 1, 3).reshape(2, C, NB, TILE).transpose(0, 2, 1, 3)
    block = order[0, 0]
    return [lax.dynamic_index_in_dim(old, i, 0, keepdims=False) for i in (block, 1 - block)]


def own_blocks(olds, order, own):
    place = lax.axis_index("ex") // 2
    rows = []
    for old in olds:
        old = old.transpose(1, 0, 2).reshape(C, HALF)
        rows.append(lax.dynamic_slice_in_dim(old, place * own, own, 1))
    first = order[0, 0] == 0
    both = [jnp.where(first, rows[0], rows[1]), jnp.where(first, rows[1], rows[0])]
    return jnp.swapaxes(jnp.stack(both), 1, 2)


def local(x_values, tile_live, labels, margins, coef, order):
    rows = x_values.shape[0]
    n_ex = lax.axis_size("ex")
    count = float(rows * n_ex)
    own = coef.shape[1]
    core = lax.axis_index("ex") % 2
    aligned = own == TILE and n_ex == 2 * NB
    labels = labels.reshape(rows // TILE, TILE)
    order = order.reshape(1, STEPS)
    z_bits = [2 * b for b in bits(n_ex // 2)]

    x_shape = sds((rows, BLOCK), BF16)
    soft_shapes = (
        sds((C, rows), F32), sds((C, rows), BF16), sds((rows, TILE), F32), sds((NB, ROWS, TILE), F32),
    )
    g_shape = soft_shapes[-1]
    old_shape, delta_shape = sds((NB, C, TILE), F32), sds((C, HALF), BF16)
    total_shape, change_shape = sds((rows, C), F32), sds((C, rows), BF16)
    own_shape, same_shape = sds((C, TILE), F32), sds((8, TILE), F32)
    flops, nbytes = 2 * rows * HALF * C, 1 << 20

    def message(n):
        return sds((NB + n, ROWS, TILE), BF16)

    if aligned:
        x, score, res_t, spread, g_other, *rest = call(
            first_body,
            (x_shape,) + soft_shapes + (own_shape,) * 2 + (same_shape,) * (STEPS - 1),
            hbm(6), "soft_first", flops, nbytes,
            scratch_shapes=[
                pltpu.SMEM(order.shape, jnp.int32),
                pltpu.SMEM(tile_live.shape, jnp.int32),
                pltpu.VMEM(margins.shape, BF16),
                pltpu.VMEM(labels.shape, jnp.int32),
                pltpu.VMEM(coef.shape, F32),
                pltpu.SemaphoreType.DMA((5,)),
            ] + block_scratch(rows),
        )(order, tile_live, margins, labels, coef, x_values)
        blocks, same = rest[:2], rest[2:]
    else:
        x = prep_general(x_values, tile_live, order[0, 0], core, own)
        score, res_t, spread, g_other = call(
            first_general_body, soft_shapes, vmem(3), "soft_first", flops, nbytes
        )(margins, labels, x)
        blocks = gather_blocks(coef, order, z_bits)
        same = [
            jnp.full((8, TILE), (order[0, step] == order[0, 0]).astype(F32)) for step in range(1, STEPS)
        ]

    for step in range(STEPS):
        if step > 0:
            if aligned:
                x = prep(order, tile_live, x_values, step)
            else:
                x = prep_general(x_values, tile_live, order[0, step], core, own)
            score, res_t, spread, g_other = call(
                next_body, soft_shapes, vmem(5), "soft_next", flops, nbytes
            )(score, change, got, labels, x)
        got = swap_core(g_other)
        g_own = call(own_body, g_shape, vmem(3), "own", flops, nbytes)(res_t, spread, x)
        carry = aligned and step < 2
        if carry:
            m = call(pair_with_body, message(1), vmem(3), "pair")(g_own, got, blocks[step])
        else:
            m = call(pair_body, message(0), vmem(2), "pair")(g_own, got)
        for n in range(len(z_bits)):
            got = swap(m, lambda f, e, n=n: (f, e ^ by_core(z_bits, e, n)))
            if n < len(z_bits) - 1:
                body, extra = (hop_with_body, 2) if carry else (hop_body, 0)
                m = call(body, message(extra), vmem(2), "hop")(m, got)
        if step < 2:
            far = blocks[step]
            if aligned:
                far = call(place_body, old_shape, vmem(3), "place")(m, got, far)
        if step == 0:
            first, delta = call(
                functools.partial(prox_first_body, count), (old_shape, delta_shape), vmem(3), "prox"
            )(m, got, far)
        else:
            first, other, delta = call(
                functools.partial(prox_body, count), (old_shape, old_shape, delta_shape), vmem(5), "prox"
            )(same[step - 1], m, got, first, far if step == 1 else other)
        got = swap_core(delta)
        part = call(mine_body, total_shape, vmem(2), "mine", flops, nbytes)(x, delta)
        if step == 0:
            total, change = call(
                change_first_body, (total_shape, change_shape), vmem(3), "change", flops, nbytes
            )(x, part, got)
        elif step < STEPS - 1:
            total, change = call(
                change_next_body, (total_shape, change_shape), vmem(4), "change", flops, nbytes
            )(x, part, got, total)
        else:
            change = call(change_last_body, total_shape, vmem(4), "change", flops, nbytes)(
                x, part, got, total
            )
        change, got = sum_over_feat(change)
    score = margins.astype(F32) + (change + got)
    if aligned:
        coef = call(coef_body, sds(coef.shape, F32), smem(1) + vmem(2), "coef_out")(order, first, other)
    else:
        coef = own_blocks((first, other), order, own)
    return score, coef


def solution(mesh):
    return jax.shard_map(
        local,
        mesh=mesh,
        in_specs=(
            P("ex", "feat"),
            P("ex", "feat"),
            P("ex"),
            P("ex", None),
            P(None, ("feat", "ex"), None),
            P(None, "feat"),
        ),
        out_specs=(P("ex", None), P(None, ("feat", "ex"), None)),
        check_vma=False,
    )
```

time: 368 us -> 109 us (0.30)
  waiting for transfers between devices: 197 us -> 64.1 us
  blocking collectives: 96.3 us -> 0 us
  starting transfers between devices: 0.25 us -> 27.3 us
  between operations: 23.5 us -> 0.82 us
  other arithmetic: 21.1 us -> 1.08 us
  matrix products: 19.3 us -> 0 us
  Pallas kernels: 0 us -> 15.3 us
  local copies, waits for them, and re-layouts: 9.45 us -> 0.68 us
    psum x6 -> x0, waiting for transfers between devices: 197 us -> none  [the longest x3 99.7 us: local(): grad_sum, curv_sum = lax.psum((grad_part, curv_part), 'ex')]
    ppermute x0 -> x18, waiting for transfers between devices: none -> 64.1 us  [swap(): return lax.ppermute(x, ('feat', 'ex'), pairs)]
    psum x3 -> x0, blocking collectives: 50.6 us -> none  [local(): grad_sum, curv_sum = lax.psum((grad_part, curv_part), 'ex')]
    all_gather x3 -> x0, blocking collectives: 45.7 us -> none  [local(): old_block = lax.all_gather(old_rows, 'ex', axis=0, tiled=True)]
    ppermute x0 -> x18, starting transfers between devices: none -> 27.3 us  [swap(): return lax.ppermute(x, ('feat', 'ex'), pairs)]
    dot_general x9 -> x0, matrix products: 19.3 us -> none  [the longest x3 7.76 us: local(): contrib = jnp.dot(block_x, step_delta, preferred_element_type=jnp.float32)]
    pallas_call x0 -> x26, Pallas kernels: none -> 15.3 us  [run(): f(*(x if spec.memory_space == pltpu.SMEM else pltpu.with_memory_space_con...]
    reduce_sum x6 -> x0, other arithmetic: 5.63 us -> none  [the longest x3 3.1 us: soft_parts(): prob = expo / jnp.sum(expo, axis=1, keepdims=True)]
  transfers between devices with their start and end apart: 6 -> 18, of which waited for: 6 -> 18; matrix products, arithmetic and copies ran while one was open for 2% -> 1% of each run, Pallas kernels for 0% -> 7%
where the time goes in v4:
time: 109 us
  waiting for transfers between devices  64.1 us (59%)
  starting transfers between devices  27.3 us (25%)
  Pallas kernels  15.3 us (14%)
    ppermute x18, waiting for transfers between devices, swap(): return lax.ppermute(x, ('feat', 'ex'), pairs)  64.1 us
    ppermute x18, starting transfers between devices, swap(): return lax.ppermute(x, ('feat', 'ex'), pairs)  27.3 us
    pallas_call x26, Pallas kernels, run(): f(*(x if spec.memory_space == pltpu.SMEM else pltpu.with_memory_space_con...  15.3 us
  transfers between devices with their start and end apart: 18, of which 18 were waited for; matrix products, arithmetic and copies ran while one was open for 1% of the time, Pallas kernels for 7%

profile of v4, /device:TPU:0, one launch (start us, length us, event | category | flops | bytes accessed | tf_op | source)
XLA Modules:
  0.0 109.2 jit_solution(7005786920103753304)
XLA Ops:
  0.6 3.0 %soft_first.1 = (bf16[1024,1024]{1,0:T(8,128)(2,1)S(1)}, f32[128,1024]{1,0:T(8,128)S(1)}, bf16[128,1024]{1,0:T(8,128)(2,1)S(1)}, f32[1024,128]{1,0:T(8,128)S(1)}...) custom-call(s32[1,3]{1,0:T(1,128)} %bitcast.5, ...), custom_call_target="tpu_custom_call" | custom-call | flops 134217728 | bytes 1048576 | tf_op jit(solution)/shard_map/soft_first/pallas_call | solution.py:50
  3.6 0.5 collective-permute-start
  4.2 0.6 own.3.own_ref
  4.7 0.6 collective-permute-done.got_ref
  5.4 3.0 %collective-permute-start.1 = (bf16[5,136,128]{2,1,0:T(8,128)(2,1)S(1)}, bf16[5,136,128]{2,1,0:T(8,128)(2,1)S(1)}, u32[]{:S(2)}, u32[]{:S(2)}) collective-permute-start(bf16[5,136,128]{2,1,0:T(8,128)(2,1)S(1)} %pair.3.mine_ref), channel_id=1, source_target_pairs={{0,2},{1,5},{2,0},{3,7},{4,6},{5,1},{6,4},{7,3},{8,10},{9,13},{10,... | collective-permute-start | bytes 522248 | tf_op jit(solution)/shard_map/ppermute | solution.py:331
  8.4 4.9 %collective-permute-done.1.got_ref = bf16[5,136,128]{2,1,0:T(8,128)(2,1)S(1)} collective-permute-done((bf16[5,136,128]{2,1,0:T(8,128)(2,1)S(1)}, bf16[5,136,128]{2,1,0:T(8,128)(2,1)S(1)}, u32[]{:S(2)}, u32[]{:S(2)}) %collective-permute-start.1) | collective-permute-done | bytes 174112 | tf_op jit(solution)/shard_map/ppermute | solution.py:331
  13.3 2.6 %collective-permute-start.2 = (bf16[6,136,128]{2,1,0:T(8,128)(2,1)S(1)}, bf16[6,136,128]{2,1,0:T(8,128)(2,1)S(1)}, u32[]{:S(2)}, u32[]{:S(2)}) collective-permute-start(bf16[6,136,128]{2,1,0:T(8,128)(2,1)S(1)} %hop.3.mine_ref), channel_id=1, source_target_pairs={{0,4},{1,3},{2,6},{3,1},{4,0},{5,7},{6,2},{7,5},{8,12},{9,11},{10,... | collective-permute-start | bytes 626696 | tf_op jit(solution)/shard_map/ppermute | solution.py:331
  15.9 4.9 %collective-permute-done.2.got_ref = bf16[6,136,128]{2,1,0:T(8,128)(2,1)S(1)} collective-permute-done((bf16[6,136,128]{2,1,0:T(8,128)(2,1)S(1)}, bf16[6,136,128]{2,1,0:T(8,128)(2,1)S(1)}, u32[]{:S(2)}, u32[]{:S(2)}) %collective-permute-start.2) | collective-permute-done | bytes 208928 | tf_op jit(solution)/shard_map/ppermute | solution.py:331
  20.8 0.1 prox.3
  20.9 0.2 collective-permute-start.3
  21.1 0.4 mine.3.part_ref
  21.6 0.0 copy-start.1
  21.6 0.0 copy-start.2
  21.6 0.7 collective-permute-done.3.delta_ref
  22.3 0.5 change.3
  22.8 3.1 %collective-permute-start.4 = (bf16[128,1024]{1,0:T(8,128)(2,1)S(1)}, bf16[128,1024]{1,0:T(8,128)(2,1)S(1)}, u32[]{:S(2)}, u32[]{:S(2)}) collective-permute-start(bf16[128,1024]{1,0:T(8,128)(2,1)S(1)} %get-tuple-element.38), channel_id=1, source_target_pairs={{0,8},{1,17},{2,10},{3,19},{4,12},{5,21},{6,14},{7,23},{8,0},{9,25... | collective-permute-start | bytes 786440 | tf_op jit(solution)/shard_map/ppermute | solution.py:331
  25.9 4.4 %collective-permute-done.4 = bf16[128,1024]{1,0:T(8,128)(2,1)S(1)} collective-permute-done((bf16[128,1024]{1,0:T(8,128)(2,1)S(1)}, bf16[128,1024]{1,0:T(8,128)(2,1)S(1)}, u32[]{:S(2)}, u32[]{:S(2)}) %collective-permute-start.4) | collective-permute-done | bytes 262176 | tf_op jit(solution)/shard_map/ppermute | solution.py:331
  30.2 0.1 add_convert_fusion.1.part_ref
  30.3 0.0 copy-start
  30.3 2.1 %collective-permute-start.5 = (bf16[128,1024]{1,0:T(8,128)(2,1)S(1)}, bf16[128,1024]{1,0:T(8,128)(2,1)S(1)}, u32[]{:S(2)}, u32[]{:S(2)}) collective-permute-start(bf16[128,1024]{1,0:T(8,128)(2,1)S(1)} %add_convert_fusion.1.part_ref), channel_id=1, source_target_pairs={{0,16},{1,9},{2,18},{3,11},{4,20},{5,13},{6,22},{7,15},{8,24},{9,1... | collective-permute-start | bytes 786440 | tf_op jit(solution)/shard_map/ppermute | solution.py:331
  32.4 2.3 %prep.3.x_ref = bf16[1024,1024]{1,0:T(8,128)(2,1)S(1)} custom-call(s32[1,3]{1,0:T(1,128)S(1)} %bitcast.6, s32[8,16]{1,0:T(8,128)S(1)} %copy-done.1, bf16[1024,2048]{1,0:T(8,128)(2,1)} %x_ref.3), custom_call_target="tpu_custom_call" | custom-call | bytes 4194304 | tf_op jit(solution)/shard_map/prep/pallas_call | solution.py:50
  34.7 2.1 %collective-permute-done.5.got_ref = bf16[128,1024]{1,0:T(8,128)(2,1)S(1)} collective-permute-done((bf16[128,1024]{1,0:T(8,128)(2,1)S(1)}, bf16[128,1024]{1,0:T(8,128)(2,1)S(1)}, u32[]{:S(2)}, u32[]{:S(2)}) %collective-permute-start.5) | collective-permute-done | bytes 262176 | tf_op jit(solution)/shard_map/ppermute | solution.py:331
  36.8 0.8 soft_next.2
  37.6 0.1 collective-permute-start.6
  37.7 0.5 own.4.own_ref
  38.2 1.0 collective-permute-done.6.got_ref
  39.2 2.0 %collective-permute-start.7 = (bf16[5,136,128]{2,1,0:T(8,128)(2,1)S(1)}, bf16[5,136,128]{2,1,0:T(8,128)(2,1)S(1)}, u32[]{:S(2)}, u32[]{:S(2)}) collective-permute-start(bf16[5,136,128]{2,1,0:T(8,128)(2,1)S(1)} %pair.4.mine_ref), channel_id=1, source_target_pairs={{0,2},{1,5},{2,0},{3,7},{4,6},{5,1},{6,4},{7,3},{8,10},{9,13},{10,... | collective-permute-start | bytes 522248 | tf_op jit(solution)/shard_map/ppermute | solution.py:331
  41.3 5.3 %collective-permute-done.7.got_ref = bf16[5,136,128]{2,1,0:T(8,128)(2,1)S(1)} collective-permute-done((bf16[5,136,128]{2,1,0:T(8,128)(2,1)S(1)}, bf16[5,136,128]{2,1,0:T(8,128)(2,1)S(1)}, u32[]{:S(2)}, u32[]{:S(2)}) %collective-permute-start.7) | collective-permute-done | bytes 174112 | tf_op jit(solution)/shard_map/ppermute | solution.py:331
  46.6 2.5 %collective-permute-start.8 = (bf16[6,136,128]{2,1,0:T(8,128)(2,1)S(1)}, bf16[6,136,128]{2,1,0:T(8,128)(2,1)S(1)}, u32[]{:S(2)}, u32[]{:S(2)}) collective-permute-start(bf16[6,136,128]{2,1,0:T(8,128)(2,1)S(1)} %hop.4.mine_ref), channel_id=1, source_target_pairs={{0,4},{1,3},{2,6},{3,1},{4,0},{5,7},{6,2},{7,5},{8,12},{9,11},{10,... | collective-permute-start | bytes 626696 | tf_op jit(solution)/shard_map/ppermute | solution.py:331
  49.1 6.6 %collective-permute-done.8.got_ref = bf16[6,136,128]{2,1,0:T(8,128)(2,1)S(1)} collective-permute-done((bf16[6,136,128]{2,1,0:T(8,128)(2,1)S(1)}, bf16[6,136,128]{2,1,0:T(8,128)(2,1)S(1)}, u32[]{:S(2)}, u32[]{:S(2)}) %collective-permute-start.8) | collective-permute-done | bytes 208928 | tf_op jit(solution)/shard_map/ppermute | solution.py:331
  55.7 0.1 prox.4
  55.9 0.1 collective-permute-start.9
  56.0 0.4 mine.4.part_ref
  56.4 0.9 collective-permute-done.9.delta_ref
  57.3 0.5 change.4
  57.8 2.0 %collective-permute-start.10 = (bf16[128,1024]{1,0:T(8,128)(2,1)S(1)}, bf16[128,1024]{1,0:T(8,128)(2,1)S(1)}, u32[]{:S(2)}, u32[]{:S(2)}) collective-permute-start(bf16[128,1024]{1,0:T(8,128)(2,1)S(1)} %get-tuple-element.48), channel_id=1, source_target_pairs={{0,8},{1,17},{2,10},{3,19},{4,12},{5,21},{6,14},{7,23},{8,0},{9,25... | collective-permute-start | bytes 786440 | tf_op jit(solution)/shard_map/ppermute | solution.py:331
  59.8 4.4 %collective-permute-done.10 = bf16[128,1024]{1,0:T(8,128)(2,1)S(1)} collective-permute-done((bf16[128,1024]{1,0:T(8,128)(2,1)S(1)}, bf16[128,1024]{1,0:T(8,128)(2,1)S(1)}, u32[]{:S(2)}, u32[]{:S(2)}) %collective-permute-start.10) | collective-permute-done | bytes 262176 | tf_op jit(solution)/shard_map/ppermute | solution.py:331
  64.2 0.1 add_convert_fusion.part_ref
  64.3 2.0 %collective-permute-start.11 = (bf16[128,1024]{1,0:T(8,128)(2,1)S(1)}, bf16[128,1024]{1,0:T(8,128)(2,1)S(1)}, u32[]{:S(2)}, u32[]{:S(2)}) collective-permute-start(bf16[128,1024]{1,0:T(8,128)(2,1)S(1)} %add_convert_fusion.part_ref), channel_id=1, source_target_pairs={{0,16},{1,9},{2,18},{3,11},{4,20},{5,13},{6,22},{7,15},{8,24},{9,1... | collective-permute-start | bytes 786440 | tf_op jit(solution)/shard_map/ppermute | solution.py:331
  66.3 2.3 %prep.2.x_ref = bf16[1024,1024]{1,0:T(8,128)(2,1)S(1)} custom-call(s32[1,3]{1,0:T(1,128)S(1)} %bitcast.7, s32[8,16]{1,0:T(8,128)S(1)} %copy-done.1, bf16[1024,2048]{1,0:T(8,128)(2,1)} %x_ref.3), custom_call_target="tpu_custom_call" | custom-call | bytes 4194304 | tf_op jit(solution)/shard_map/prep/pallas_call | solution.py:50
  68.6 2.1 %collective-permute-done.11.got_ref = bf16[128,1024]{1,0:T(8,128)(2,1)S(1)} collective-permute-done((bf16[128,1024]{1,0:T(8,128)(2,1)S(1)}, bf16[128,1024]{1,0:T(8,128)(2,1)S(1)}, u32[]{:S(2)}, u32[]{:S(2)}) %collective-permute-start.11) | collective-permute-done | bytes 262176 | tf_op jit(solution)/shard_map/ppermute | solution.py:331
  70.8 1.2 %soft_next.3 = (f32[128,1024]{1,0:T(8,128)}, bf16[128,1024]{1,0:T(8,128)(2,1)S(1)}, f32[1024,128]{1,0:T(8,128)S(1)}, f32[4,136,128]{2,1,0:T(8,128)S(1)}) custom-call(f32[128,1024]{1,0:T(8,128)S(1)} %get-tuple-element.39.before_ref, bf16[128,1024]{1,0:T(8,128)(2,1)S(1)} %add_convert_fusion.part_ref, bf16[128,1024]{1,0:T(8,128)(2,1)S(1)} %collective-permute-done.11.got_ref, ...), custom_call_target="tpu_custom_call" | custom-call | flops 134217728 | bytes 1048576 | tf_op jit(solution)/shard_map/soft_next/pallas_call | solution.py:50
  72.0 0.0 collective-permute-start.12
  72.0 0.5 own.5.own_ref
  72.5 1.0 collective-permute-done.12.got_ref
  73.5 0.1 pair.5.mine_ref
  73.6 1.0 collective-permute-start.13
  74.6 5.6 %collective-permute-done.13.got_ref = bf16[4,136,128]{2,1,0:T(8,128)(2,1)S(1)} collective-permute-done((bf16[4,136,128]{2,1,0:T(8,128)(2,1)S(1)}, bf16[4,136,128]{2,1,0:T(8,128)(2,1)S(1)}, u32[]{:S(2)}, u32[]{:S(2)}) %collective-permute-start.13) | collective-permute-done | bytes 139296 | tf_op jit(solution)/shard_map/ppermute | solution.py:331
  80.2 1.9 %collective-permute-start.14 = (bf16[4,136,128]{2,1,0:T(8,128)(2,1)S(1)}, bf16[4,136,128]{2,1,0:T(8,128)(2,1)S(1)}, u32[]{:S(2)}, u32[]{:S(2)}) collective-permute-start(bf16[4,136,128]{2,1,0:T(8,128)(2,1)S(1)} %hop.5.mine_ref), channel_id=1, source_target_pairs={{0,4},{1,3},{2,6},{3,1},{4,0},{5,7},{6,2},{7,5},{8,12},{9,11},{10,... | collective-permute-start | bytes 417800 | tf_op jit(solution)/shard_map/ppermute | solution.py:331
  82.2 5.6 %collective-permute-done.14.got_ref = bf16[4,136,128]{2,1,0:T(8,128)(2,1)S(1)} collective-permute-done((bf16[4,136,128]{2,1,0:T(8,128)(2,1)S(1)}, bf16[4,136,128]{2,1,0:T(8,128)(2,1)S(1)}, u32[]{:S(2)}, u32[]{:S(2)}) %collective-permute-start.14) | collective-permute-done | bytes 139296 | tf_op jit(solution)/shard_map/ppermute | solution.py:331
  87.7 0.1 prox.5
  87.9 0.1 collective-permute-start.15
  88.0 0.4 mine.5.part_ref
  88.4 0.9 collective-permute-done.15.delta_ref
  89.3 0.5 change.5
  89.8 0.0 copy-start.3
  89.8 2.0 %collective-permute-start.16 = (f32[1024,128]{1,0:T(8,128)S(1)}, f32[1024,128]{1,0:T(8,128)S(1)}, u32[]{:S(2)}, u32[]{:S(2)}) collective-permute-start(f32[1024,128]{1,0:T(8,128)S(1)} %change.5), channel_id=1, source_target_pairs={{0,8},{1,17},{2,10},{3,19},{4,12},{5,21},{6,14},{7,23},{8,0},{9,25... | collective-permute-start | bytes 1572872 | tf_op jit(solution)/shard_map/ppermute | solution.py:331
  91.8 7.2 %collective-permute-done.16 = f32[1024,128]{1,0:T(8,128)S(1)} collective-permute-done((f32[1024,128]{1,0:T(8,128)S(1)}, f32[1024,128]{1,0:T(8,128)S(1)}, u32[]{:S(2)}, u32[]{:S(2)}) %collective-permute-start.16) | collective-permute-done | bytes 524320 | tf_op jit(solution)/shard_map/ppermute | solution.py:331
  99.0 0.1 add.17
  99.1 2.0 %collective-permute-start.17 = (f32[1024,128]{1,0:T(8,128)S(1)}, f32[1024,128]{1,0:T(8,128)S(1)}, u32[]{:S(2)}, u32[]{:S(2)}) collective-permute-start(f32[1024,128]{1,0:T(8,128)S(1)} %add.17), channel_id=1, source_target_pairs={{0,16},{1,9},{2,18},{3,11},{4,20},{5,13},{6,22},{7,15},{8,24},{9,1... | collective-permute-start | bytes 1572872 | tf_op jit(solution)/shard_map/ppermute | solution.py:331
  101.1 0.6 coef_out.1
  101.8 0.7 copy.8
  102.5 5.9 %collective-permute-done.17 = f32[1024,128]{1,0:T(8,128)S(1)} collective-permute-done((f32[1024,128]{1,0:T(8,128)S(1)}, f32[1024,128]{1,0:T(8,128)S(1)}, u32[]{:S(2)}, u32[]{:S(2)}) %collective-permute-start.17) | collective-permute-done | bytes 524320 | tf_op jit(solution)/shard_map/ppermute | solution.py:331
  108.4 0.9 add_add_fusion
  (11 shorter events, 0.3 us)
Async XLA Ops:
  3.6 1.7 %collective-permute-start = (f32[4,136,128]{2,1,0:T(8,128)S(1)}, f32[4,136,128]{2,1,0:T(8,128)S(1)}, u32[]{:S(2)}, u32[]{:S(2)}) collective-permute-start(f32[4,136,128]{2,1,0:T(8,128)S(1)} %get-tuple-element.35), channel_id=1, source_target_pairs={{0,1},{1,0},{2,3},{3,2},{4,5},{5,4},{6,7},{7,6},{8,9},{9,8},{10,11... | collective-permute-start | bytes 835592 | tf_op jit(solution)/shard_map/ppermute | solution.py:331
  5.4 7.9 %collective-permute-start.1 = (bf16[5,136,128]{2,1,0:T(8,128)(2,1)S(1)}, bf16[5,136,128]{2,1,0:T(8,128)(2,1)S(1)}, u32[]{:S(2)}, u32[]{:S(2)}) collective-permute-start(bf16[5,136,128]{2,1,0:T(8,128)(2,1)S(1)} %pair.3.mine_ref), channel_id=1, source_target_pairs={{0,2},{1,5},{2,0},{3,7},{4,6},{5,1},{6,4},{7,3},{8,10},{9,13},{10,... | collective-permute-start | bytes 522248 | tf_op jit(solution)/shard_map/ppermute | solution.py:331
  13.3 7.4 %collective-permute-start.2 = (bf16[6,136,128]{2,1,0:T(8,128)(2,1)S(1)}, bf16[6,136,128]{2,1,0:T(8,128)(2,1)S(1)}, u32[]{:S(2)}, u32[]{:S(2)}) collective-permute-start(bf16[6,136,128]{2,1,0:T(8,128)(2,1)S(1)} %hop.3.mine_ref), channel_id=1, source_target_pairs={{0,4},{1,3},{2,6},{3,1},{4,0},{5,7},{6,2},{7,5},{8,12},{9,11},{10,... | collective-permute-start | bytes 626696 | tf_op jit(solution)/shard_map/ppermute | solution.py:331
  20.9 1.4 %collective-permute-start.3 = (bf16[128,512]{1,0:T(8,128)(2,1)S(1)}, bf16[128,512]{1,0:T(8,128)(2,1)S(1)}, u32[]{:S(2)}, u32[]{:S(2)}) collective-permute-start(bf16[128,512]{1,0:T(8,128)(2,1)S(1)} %get-tuple-element.37.delta_ref), channel_id=1, source_target_pairs={{0,1},{1,0},{2,3},{3,2},{4,5},{5,4},{6,7},{7,6},{8,9},{9,8},{10,11... | collective-permute-start | bytes 393224 | tf_op jit(solution)/shard_map/ppermute | solution.py:331
  21.6 10.9 %copy-start.1 = (s32[8,16]{1,0:T(8,128)S(1)}, s32[8,16]{1,0:T(8,128)}, u32[]{:S(2)}) copy-start(s32[8,16]{1,0:T(8,128)} %live_ref.3) | copy-start | bytes 1540
  21.6 10.8 %copy-start.2 = (s32[3,1]{0,1:T(1,128)S(1)}, s32[3,1]{0,1:T(1,128)}, u32[]{:S(2)}) copy-start(s32[3,1]{0,1:T(1,128)} %param.11) | copy-start | bytes 40
  22.8 7.4 %collective-permute-start.4 = (bf16[128,1024]{1,0:T(8,128)(2,1)S(1)}, bf16[128,1024]{1,0:T(8,128)(2,1)S(1)}, u32[]{:S(2)}, u32[]{:S(2)}) collective-permute-start(bf16[128,1024]{1,0:T(8,128)(2,1)S(1)} %get-tuple-element.38), channel_id=1, source_target_pairs={{0,8},{1,17},{2,10},{3,19},{4,12},{5,21},{6,14},{7,23},{8,0},{9,25... | collective-permute-start | bytes 786440 | tf_op jit(solution)/shard_map/ppermute | solution.py:331
  30.3 6.5 %copy-start = (s32[1024]{0:T(1024)S(1)}, s32[1024]{0:T(1024)}, u32[]{:S(2)}) copy-start(s32[1024]{0:T(1024)} %param.8) | copy-start | bytes 12292
  30.3 6.5 %collective-permute-start.5 = (bf16[128,1024]{1,0:T(8,128)(2,1)S(1)}, bf16[128,1024]{1,0:T(8,128)(2,1)S(1)}, u32[]{:S(2)}, u32[]{:S(2)}) collective-permute-start(bf16[128,1024]{1,0:T(8,128)(2,1)S(1)} %add_convert_fusion.1.part_ref), channel_id=1, source_target_pairs={{0,16},{1,9},{2,18},{3,11},{4,20},{5,13},{6,22},{7,15},{8,24},{9,1... | collective-permute-start | bytes 786440 | tf_op jit(solution)/shard_map/ppermute | solution.py:331
  37.6 1.6 %collective-permute-start.6 = (f32[4,136,128]{2,1,0:T(8,128)S(1)}, f32[4,136,128]{2,1,0:T(8,128)S(1)}, u32[]{:S(2)}, u32[]{:S(2)}) collective-permute-start(f32[4,136,128]{2,1,0:T(8,128)S(1)} %get-tuple-element.43), channel_id=1, source_target_pairs={{0,1},{1,0},{2,3},{3,2},{4,5},{5,4},{6,7},{7,6},{8,9},{9,8},{10,11... | collective-permute-start | bytes 835592 | tf_op jit(solution)/shard_map/ppermute | solution.py:331
  39.2 7.4 %collective-permute-start.7 = (bf16[5,136,128]{2,1,0:T(8,128)(2,1)S(1)}, bf16[5,136,128]{2,1,0:T(8,128)(2,1)S(1)}, u32[]{:S(2)}, u32[]{:S(2)}) collective-permute-start(bf16[5,136,128]{2,1,0:T(8,128)(2,1)S(1)} %pair.4.mine_ref), channel_id=1, source_target_pairs={{0,2},{1,5},{2,0},{3,7},{4,6},{5,1},{6,4},{7,3},{8,10},{9,13},{10,... | collective-permute-start | bytes 522248 | tf_op jit(solution)/shard_map/ppermute | solution.py:331
  46.6 9.0 %collective-permute-start.8 = (bf16[6,136,128]{2,1,0:T(8,128)(2,1)S(1)}, bf16[6,136,128]{2,1,0:T(8,128)(2,1)S(1)}, u32[]{:S(2)}, u32[]{:S(2)}) collective-permute-start(bf16[6,136,128]{2,1,0:T(8,128)(2,1)S(1)} %hop.4.mine_ref), channel_id=1, source_target_pairs={{0,4},{1,3},{2,6},{3,1},{4,0},{5,7},{6,2},{7,5},{8,12},{9,11},{10,... | collective-permute-start | bytes 626696 | tf_op jit(solution)/shard_map/ppermute | solution.py:331
  55.9 1.4 %collective-permute-start.9 = (bf16[128,512]{1,0:T(8,128)(2,1)S(1)}, bf16[128,512]{1,0:T(8,128)(2,1)S(1)}, u32[]{:S(2)}, u32[]{:S(2)}) collective-permute-start(bf16[128,512]{1,0:T(8,128)(2,1)S(1)} %get-tuple-element.46.delta_ref), channel_id=1, source_target_pairs={{0,1},{1,0},{2,3},{3,2},{4,5},{5,4},{6,7},{7,6},{8,9},{9,8},{10,11... | collective-permute-start | bytes 393224 | tf_op jit(solution)/shard_map/ppermute | solution.py:331
  57.8 6.4 %collective-permute-start.10 = (bf16[128,1024]{1,0:T(8,128)(2,1)S(1)}, bf16[128,1024]{1,0:T(8,128)(2,1)S(1)}, u32[]{:S(2)}, u32[]{:S(2)}) collective-permute-start(bf16[128,1024]{1,0:T(8,128)(2,1)S(1)} %get-tuple-element.48), channel_id=1, source_target_pairs={{0,8},{1,17},{2,10},{3,19},{4,12},{5,21},{6,14},{7,23},{8,0},{9,25... | collective-permute-start | bytes 786440 | tf_op jit(solution)/shard_map/ppermute | solution.py:331
  64.3 6.4 %collective-permute-start.11 = (bf16[128,1024]{1,0:T(8,128)(2,1)S(1)}, bf16[128,1024]{1,0:T(8,128)(2,1)S(1)}, u32[]{:S(2)}, u32[]{:S(2)}) collective-permute-start(bf16[128,1024]{1,0:T(8,128)(2,1)S(1)} %add_convert_fusion.part_ref), channel_id=1, source_target_pairs={{0,16},{1,9},{2,18},{3,11},{4,20},{5,13},{6,22},{7,15},{8,24},{9,1... | collective-permute-start | bytes 786440 | tf_op jit(solution)/shard_map/ppermute | solution.py:331
  72.0 1.6 %collective-permute-start.12 = (f32[4,136,128]{2,1,0:T(8,128)S(1)}, f32[4,136,128]{2,1,0:T(8,128)S(1)}, u32[]{:S(2)}, u32[]{:S(2)}) collective-permute-start(f32[4,136,128]{2,1,0:T(8,128)S(1)} %get-tuple-element.51), channel_id=1, source_target_pairs={{0,1},{1,0},{2,3},{3,2},{4,5},{5,4},{6,7},{7,6},{8,9},{9,8},{10,11... | collective-permute-start | bytes 835592 | tf_op jit(solution)/shard_map/ppermute | solution.py:331
  73.6 6.6 %collective-permute-start.13 = (bf16[4,136,128]{2,1,0:T(8,128)(2,1)S(1)}, bf16[4,136,128]{2,1,0:T(8,128)(2,1)S(1)}, u32[]{:S(2)}, u32[]{:S(2)}) collective-permute-start(bf16[4,136,128]{2,1,0:T(8,128)(2,1)S(1)} %pair.5.mine_ref), channel_id=1, source_target_pairs={{0,2},{1,5},{2,0},{3,7},{4,6},{5,1},{6,4},{7,3},{8,10},{9,13},{10,... | collective-permute-start | bytes 417800 | tf_op jit(solution)/shard_map/ppermute | solution.py:331
  80.2 7.5 %collective-permute-start.14 = (bf16[4,136,128]{2,1,0:T(8,128)(2,1)S(1)}, bf16[4,136,128]{2,1,0:T(8,128)(2,1)S(1)}, u32[]{:S(2)}, u32[]{:S(2)}) collective-permute-start(bf16[4,136,128]{2,1,0:T(8,128)(2,1)S(1)} %hop.5.mine_ref), channel_id=1, source_target_pairs={{0,4},{1,3},{2,6},{3,1},{4,0},{5,7},{6,2},{7,5},{8,12},{9,11},{10,... | collective-permute-start | bytes 417800 | tf_op jit(solution)/shard_map/ppermute | solution.py:331
  87.9 1.4 %collective-permute-start.15 = (bf16[128,512]{1,0:T(8,128)(2,1)S(1)}, bf16[128,512]{1,0:T(8,128)(2,1)S(1)}, u32[]{:S(2)}, u32[]{:S(2)}) collective-permute-start(bf16[128,512]{1,0:T(8,128)(2,1)S(1)} %get-tuple-element.54.delta_ref), channel_id=1, source_target_pairs={{0,1},{1,0},{2,3},{3,2},{4,5},{5,4},{6,7},{7,6},{8,9},{9,8},{10,11... | collective-permute-start | bytes 393224 | tf_op jit(solution)/shard_map/ppermute | solution.py:331
  89.8 18.6 %copy-start.3 = (bf16[1024,128]{1,0:T(8,128)(2,1)S(1)}, bf16[1024,128]{1,0:T(8,128)(2,1)}, u32[]{:S(2)}) copy-start(bf16[1024,128]{1,0:T(8,128)(2,1)} %margins_hbm.1) | copy-start | bytes 786436
  89.8 9.2 %collective-permute-start.16 = (f32[1024,128]{1,0:T(8,128)S(1)}, f32[1024,128]{1,0:T(8,128)S(1)}, u32[]{:S(2)}, u32[]{:S(2)}) collective-permute-start(f32[1024,128]{1,0:T(8,128)S(1)} %change.5), channel_id=1, source_target_pairs={{0,8},{1,17},{2,10},{3,19},{4,12},{5,21},{6,14},{7,23},{8,0},{9,25... | collective-permute-start | bytes 1572872 | tf_op jit(solution)/shard_map/ppermute | solution.py:331
  99.1 9.2 %collective-permute-start.17 = (f32[1024,128]{1,0:T(8,128)S(1)}, f32[1024,128]{1,0:T(8,128)S(1)}, u32[]{:S(2)}, u32[]{:S(2)}) collective-permute-start(f32[1024,128]{1,0:T(8,128)S(1)} %add.17), channel_id=1, source_target_pairs={{0,16},{1,9},{2,18},{3,11},{4,20},{5,13},{6,22},{7,15},{8,24},{9,1... | collective-permute-start | bytes 1572872 | tf_op jit(solution)/shard_map/ppermute | solution.py:331

commit v5 on v4

--- a/solution.py
+++ b/solution.py
@@ -13,6 +13,7 @@
 HALF = BLOCK // 2
 TILE = 128
 NB = HALF // TILE
+PB = NB // 2
 ROWS = C + 8
 
 ridge = 0.002
@@ -196,13 +197,27 @@
     half_sums(res_ref[...], spread_ref, x_ref, HALF, g_ref)
 
 
-def next_body(before_ref, part_ref, got_ref, lab_ref, x_ref, score_ref, res_ref, spread_ref, g_ref):
-    for r, here in tiles_of(before_ref.shape[1]):
-        change = part_ref[:, here].astype(F32) + got_ref[:, here].astype(F32)
-        score = before_ref[:, here] + change
+def next_body(before_ref, a_ref, ra_ref, b_ref, rb_ref, lab_ref, x_ref, score_ref, res_ref, spread_ref, g_ref):
+    rows = before_ref.shape[1]
+    for r, here in tiles_of(rows):
+        score = before_ref[:, here] + change_tile(here, rows, a_ref, ra_ref, b_ref, rb_ref)
         score_ref[:, here] = score
         soft_rows(score, lab_ref[r : r + 1, :], here, res_ref, spread_ref)
     half_sums(res_ref[...], spread_ref, x_ref, HALF, g_ref)
+
+
+def last_body(before_ref, a_ref, ra_ref, b_ref, rb_ref, out_ref):
+    rows = before_ref.shape[1]
+    for _, here in tiles_of(rows):
+        score = before_ref[:, here] + change_tile(here, rows, a_ref, ra_ref, b_ref, rb_ref)
+        out_ref[here, :] = score.T
+
+
+def change_tile(here, rows, a_ref, ra_ref, b_ref, rb_ref):
+    if here.stop <= rows // 2:
+        return a_ref[:, here].astype(F32) + ra_ref[:, here].astype(F32)
+    at = slice(here.start - rows // 2, here.stop - rows // 2)
+    return b_ref[:, at].astype(F32) + rb_ref[:, at].astype(F32)
 
 
 def own_body(res_ref, spread_ref, x_ref, g_ref):
@@ -218,16 +233,16 @@
     out_ref[k, C:ROWS, :] = tail.astype(BF16)
 
 
-def pair_body(own_ref, got_ref, out_ref):
+def pair_body(own_ref, got_ref, p_ref, q_ref):
     for k in range(NB):
         total = own_ref[k] + got_ref[k]
-        encode(k, total[0:C], total[C : C + 1], out_ref)
-
-
-def pair_with_body(own_ref, got_ref, coef_ref, out_ref):
-    pair_body(own_ref, got_ref, out_ref)
-    out_ref[NB, 0:C, :] = coef_ref[...].astype(BF16)
-    out_ref[NB, C:ROWS, :] = jnp.zeros((ROWS - C, TILE), BF16)
+        encode(k % PB, total[0:C], total[C : C + 1], p_ref if k < PB else q_ref)
+
+
+def pair_with_body(own_ref, got_ref, coef_ref, p_ref, q_ref):
+    pair_body(own_ref, got_ref, p_ref, q_ref)
+    p_ref[PB, 0:C, :] = coef_ref[...].astype(BF16)
+    p_ref[PB, C:ROWS, :] = jnp.zeros((ROWS - C, TILE), BF16)
 
 
 def decode_sum(k, mine_ref, got_ref):
@@ -236,23 +251,22 @@
 
 
 def hop_body(mine_ref, got_ref, out_ref):
-    for k in range(NB):
+    for k in range(PB):
         encode(k, *decode_sum(k, mine_ref, got_ref), out_ref)
 
 
 def hop_with_body(mine_ref, got_ref, out_ref):
     hop_body(mine_ref, got_ref, out_ref)
-    out_ref[NB] = mine_ref[NB]
-    out_ref[NB + 1] = got_ref[NB]
+    out_ref[PB] = mine_ref[PB]
+    out_ref[PB + 1] = got_ref[PB]
 
 
 def place_body(mine_ref, got_ref, coef_ref, out_ref):
-    me = lax.axis_index("ex")
-    place, first = me // 2, 1 + me % 2
+    place = lax.axis_index("ex") // 2
     out_ref[place] = coef_ref[...]
-    out_ref[jnp.bitwise_xor(place, first)] = mine_ref[NB + 1, 0:C, :].astype(F32)
-    out_ref[jnp.bitwise_xor(place, 3 - first)] = got_ref[NB, 0:C, :].astype(F32)
-    out_ref[jnp.bitwise_xor(place, 3)] = got_ref[NB + 1, 0:C, :].astype(F32)
+    out_ref[jnp.bitwise_xor(place, 1)] = mine_ref[PB + 1, 0:C, :].astype(F32)
+    out_ref[jnp.bitwise_xor(place, 2)] = got_ref[PB, 0:C, :].astype(F32)
+    out_ref[jnp.bitwise_xor(place, 3)] = got_ref[PB + 1, 0:C, :].astype(F32)
 
 
 def step_coef(count, k, mine_ref, got_ref, old):
@@ -263,20 +277,22 @@
     return shifted - jnp.clip(shifted, -limit, limit)
 
 
-def prox_first_body(count, mine_ref, got_ref, old_ref, new_ref, delta_ref):
+def prox_first_body(count, p_ref, gp_ref, q_ref, gq_ref, old_ref, new_ref, delta_ref):
     for k in range(NB):
         old = old_ref[k]
-        new = step_coef(count, k, mine_ref, got_ref, old)
+        chunk = (p_ref, gp_ref) if k < PB else (q_ref, gq_ref)
+        new = step_coef(count, k % PB, *chunk, old)
         new_ref[k] = new
         delta_ref[:, k * TILE : (k + 1) * TILE] = (new - old).astype(BF16)
 
 
-def prox_body(count, same_ref, mine_ref, got_ref, old0_ref, old1_ref, new0_ref, new1_ref, delta_ref):
+def prox_body(count, same_ref, p_ref, gp_ref, q_ref, gq_ref, old0_ref, old1_ref, new0_ref, new1_ref, delta_ref):
     same = jnp.broadcast_to(same_ref[0:1, :], (C, TILE)) > 0.5
     for k in range(NB):
         old0, old1 = old0_ref[k], old1_ref[k]
         old = jnp.where(same, old0, old1)
-        new = step_coef(count, k, mine_ref, got_ref, old)
+        chunk = (p_ref, gp_ref) if k < PB else (q_ref, gq_ref)
+        new = step_coef(count, k % PB, *chunk, old)
         new0_ref[k] = jnp.where(same, new, old0)
         new1_ref[k] = jnp.where(same, old1, new)
         delta_ref[:, k * TILE : (k + 1) * TILE] = (new - old).astype(BF16)
@@ -300,21 +316,26 @@
     part_ref[...] = contrib(x_ref, 0, delta_ref)
 
 
-def change_first_body(x_ref, part_ref, delta_ref, total_ref, out_ref):
-    total_ref[...] = part_ref[...] + contrib(x_ref, HALF, delta_ref)
-    for _, here in tiles_of(x_ref.shape[0]):
-        out_ref[:, here] = total_ref[here, :].T.astype(BF16)
-
-
-def change_next_body(x_ref, part_ref, delta_ref, before_ref, total_ref, out_ref):
+def change_body(carried, x_ref, part_ref, delta_ref, *refs):
+    errors, (a_ref, b_ref, ea_ref, eb_ref) = refs[:carried], refs[carried:]
     part = part_ref[...] + contrib(x_ref, HALF, delta_ref)
-    total_ref[...] = before_ref[...] + part
-    for _, here in tiles_of(x_ref.shape[0]):
-        out_ref[:, here] = part[here, :].T.astype(BF16)
-
-
-def change_last_body(x_ref, part_ref, delta_ref, before_ref, out_ref):
-    out_ref[...] = before_ref[...] + (part_ref[...] + contrib(x_ref, HALF, delta_ref))
+    rows = x_ref.shape[0]
+    for _, here in tiles_of(rows):
+        low = here.stop <= rows // 2
+        at = here if low else slice(here.start - rows // 2, here.stop - rows // 2)
+        full = part[here, :].T
+        for e_ref in errors[0::2] if low else errors[1::2]:
+            full = full + e_ref[:, at]
+        sent = full.astype(BF16)
+        (a_ref if low else b_ref)[:, at] = sent
+        (ea_ref if low else eb_ref)[:, at] = full - sent.astype(F32)
+
+
+def meet_body(share, mine_ref, got_ref, out_ref, error_ref):
+    total = mine_ref[...].astype(F32) + got_ref[...].astype(F32)
+    sent = total.astype(BF16)
+    out_ref[...] = sent
+    error_ref[...] = share * (total - sent.astype(F32))
 
 
 def bits(n):
@@ -335,21 +356,20 @@
     return swap(x, lambda f, e: (f, e ^ 1))
 
 
-def by_core(order, e, n):
-    return order[n] if e % 2 == 0 else order[len(order) - 1 - n]
-
-
-def add_as(x, y, dtype):
-    return (x.astype(F32) + y.astype(F32)).astype(dtype)
-
-
-def sum_over_feat(x):
+def sum_over_feat(a, b):
     order = bits(lax.axis_size("feat"))
+    errors, pair = [], 1
     for n in range(len(order)):
-        got = swap(x, lambda f, e, n=n: (f ^ by_core(order, e, n), e))
+        got_a = swap(a, lambda f, e, n=n: (f ^ order[n], e))
+        got_b = swap(b, lambda f, e, n=n: (f ^ order[-1 - n], e))
         if n == len(order) - 1:
-            return x, got
-        x = add_as(x, got, x.dtype)
+            return (a, got_a, b, got_b), errors
+        pair *= 2
+        shapes = (sds(a.shape, BF16), sds(a.shape, F32))
+        meet = functools.partial(meet_body, 1.0 / pair)
+        a, ea = call(meet, shapes, vmem(2), "meet_a")(a, got_a)
+        b, eb = call(meet, shapes, vmem(2), "meet_b")(b, got_b)
+        errors += [ea, eb]
 
 
 def gather_blocks(coef, order, z_bits):
@@ -392,12 +412,12 @@
     )
     g_shape = soft_shapes[-1]
     old_shape, delta_shape = sds((NB, C, TILE), F32), sds((C, HALF), BF16)
-    total_shape, change_shape = sds((rows, C), F32), sds((C, rows), BF16)
+    part_shape, half = sds((rows, C), F32), (C, rows // 2)
     own_shape, same_shape = sds((C, TILE), F32), sds((8, TILE), F32)
     flops, nbytes = 2 * rows * HALF * C, 1 << 20
 
     def message(n):
-        return sds((NB + n, ROWS, TILE), BF16)
+        return sds((PB + n, ROWS, TILE), BF16)
 
     if aligned:
         x, score, res_t, spread, g_other, *rest = call(
@@ -424,6 +444,7 @@
             jnp.full((8, TILE), (order[0, step] == order[0, 0]).astype(F32)) for step in range(1, STEPS)
         ]
 
+    errors = []
     for step in range(STEPS):
         if step > 0:
             if aligned:
@@ -431,48 +452,45 @@
             else:
                 x = prep_general(x_values, tile_live, order[0, step], core, own)
             score, res_t, spread, g_other = call(
-                next_body, soft_shapes, vmem(5), "soft_next", flops, nbytes
-            )(score, change, got, labels, x)
+                next_body, soft_shapes, vmem(7), "soft_next", flops, nbytes
+            )(score, *halves, labels, x)
         got = swap_core(g_other)
         g_own = call(own_body, g_shape, vmem(3), "own", flops, nbytes)(res_t, spread, x)
         carry = aligned and step < 2
         if carry:
-            m = call(pair_with_body, message(1), vmem(3), "pair")(g_own, got, blocks[step])
+            p, q = call(pair_with_body, (message(1), message(0)), vmem(3), "pair")(g_own, got, blocks[step])
         else:
-            m = call(pair_body, message(0), vmem(2), "pair")(g_own, got)
-        for n in range(len(z_bits)):
-            got = swap(m, lambda f, e, n=n: (f, e ^ by_core(z_bits, e, n)))
+            p, q = call(pair_body, (message(0), message(0)), vmem(2), "pair")(g_own, got)
+        for n, bit in enumerate(z_bits):
+            got_p = swap(p, lambda f, e, bit=bit: (f, e ^ bit))
+            got_q = swap(q, lambda f, e, bit=bit: (f, e ^ bit))
             if n < len(z_bits) - 1:
                 body, extra = (hop_with_body, 2) if carry else (hop_body, 0)
-                m = call(body, message(extra), vmem(2), "hop")(m, got)
+                p = call(body, message(extra), vmem(2), "hop_p")(p, got_p)
+                q = call(hop_body, message(0), vmem(2), "hop_q")(q, got_q)
         if step < 2:
             far = blocks[step]
             if aligned:
-                far = call(place_body, old_shape, vmem(3), "place")(m, got, far)
+                far = call(place_body, old_shape, vmem(3), "place")(p, got_p, far)
+        sums = (p, got_p, q, got_q)
         if step == 0:
             first, delta = call(
-                functools.partial(prox_first_body, count), (old_shape, delta_shape), vmem(3), "prox"
-            )(m, got, far)
+                functools.partial(prox_first_body, count), (old_shape, delta_shape), vmem(5), "prox"
+            )(*sums, far)
         else:
             first, other, delta = call(
-                functools.partial(prox_body, count), (old_shape, old_shape, delta_shape), vmem(5), "prox"
-            )(same[step - 1], m, got, first, far if step == 1 else other)
+                functools.partial(prox_body, count), (old_shape, old_shape, delta_shape), vmem(7), "prox"
+            )(same[step - 1], *sums, first, far if step == 1 else other)
         got = swap_core(delta)
-        part = call(mine_body, total_shape, vmem(2), "mine", flops, nbytes)(x, delta)
-        if step == 0:
-            total, change = call(
-                change_first_body, (total_shape, change_shape), vmem(3), "change", flops, nbytes
-            )(x, part, got)
-        elif step < STEPS - 1:
-            total, change = call(
-                change_next_body, (total_shape, change_shape), vmem(4), "change", flops, nbytes
-            )(x, part, got, total)
-        else:
-            change = call(change_last_body, total_shape, vmem(4), "change", flops, nbytes)(
-                x, part, got, total
-            )
-        change, got = sum_over_feat(change)
-    score = margins.astype(F32) + (change + got)
+        part = call(mine_body, part_shape, vmem(2), "mine", flops, nbytes)(x, delta)
+        a, b, ea, eb = call(
+            functools.partial(change_body, len(errors)),
+            (sds(half, BF16), sds(half, BF16), sds(half, F32), sds(half, F32)),
+            vmem(3 + len(errors)), "change", flops, nbytes,
+        )(x, part, got, *errors)
+        halves, errors = sum_over_feat(a, b)
+        errors = [ea, eb] + errors
+    score = call(last_body, jax.ShapeDtypeStruct((rows, C), F32), vmem(5), "last")(score, *halves)
     if aligned:
         coef = call(coef_body, sds(coef.shape, F32), smem(1) + vmem(2), "coef_out")(order, first, other)
     else:

time: 109 us -> 105 us (0.963)
  waiting for transfers between devices: 64.1 us -> 51.1 us
  starting transfers between devices: 27.3 us -> 33.7 us
  Pallas kernels: 15.3 us -> 18.5 us
    ppermute x18 -> x30, waiting for transfers between devices: 64.1 us -> 51.1 us  [swap(): return lax.ppermute(x, ('feat', 'ex'), pairs)]
    ppermute x18 -> x30, starting transfers between devices: 27.3 us -> 33.7 us  [swap(): return lax.ppermute(x, ('feat', 'ex'), pairs)]
    pallas_call x26 -> x36, Pallas kernels: 15.3 us -> 18.5 us  [run(): f(*(x if spec.memory_space == pltpu.SMEM else pltpu.with_memory_space_con...]
  transfers between devices with their start and end apart: 18 -> 30, of which waited for: 18 -> 23; matrix products, arithmetic and copies ran while one was open for 1% -> 1% of each run, Pallas kernels for 7% -> 10%
where the time goes in v5:
time: 105 us
  waiting for transfers between devices  51.1 us (49%)
  starting transfers between devices  33.7 us (32%)
  Pallas kernels  18.5 us (18%)
    ppermute x30, waiting for transfers between devices, swap(): return lax.ppermute(x, ('feat', 'ex'), pairs)  51.1 us
    ppermute x30, starting transfers between devices, swap(): return lax.ppermute(x, ('feat', 'ex'), pairs)  33.7 us
    pallas_call x36, Pallas kernels, run(): f(*(x if spec.memory_space == pltpu.SMEM else pltpu.with_memory_space_con...  18.5 us
  transfers between devices with their start and end apart: 30, of which 23 were waited for; matrix products, arithmetic and copies ran while one was open for 1% of the time, Pallas kernels for 10%

profile of v5, /device:TPU:0, one launch (start us, length us, event | category | flops | bytes accessed | tf_op | source)
XLA Modules:
  0.0 104.8 jit_solution(12254970963943035684)
XLA Ops:
  0.6 3.0 %soft_first.1 = (bf16[1024,1024]{1,0:T(8,128)(2,1)S(1)}, f32[128,1024]{1,0:T(8,128)S(1)}, bf16[128,1024]{1,0:T(8,128)(2,1)S(1)}, f32[1024,128]{1,0:T(8,128)S(1)}...) custom-call(s32[1,3]{1,0:T(1,128)} %bitcast.5, ...), custom_call_target="tpu_custom_call" | custom-call | flops 134217728 | bytes 1048576 | tf_op jit(solution)/shard_map/soft_first/pallas_call | solution.py:51
  3.7 0.5 collective-permute-start
  4.2 0.6 own.3.own_ref
  4.7 0.6 collective-permute-done.got_ref
  5.4 3.0 %collective-permute-start.1 = (bf16[3,136,128]{2,1,0:T(8,128)(2,1)S(1)}, bf16[3,136,128]{2,1,0:T(8,128)(2,1)S(1)}, u32[]{:S(2)}, u32[]{:S(2)}) collective-permute-start(bf16[3,136,128]{2,1,0:T(8,128)(2,1)S(1)} %get-tuple-element.59.mine_ref), channel_id=1, source_target_pairs={{0,2},{1,3},{2,0},{3,1},{4,6},{5,7},{6,4},{7,5},{8,10},{9,11},{10,... | collective-permute-start | bytes 313352 | tf_op jit(solution)/shard_map/ppermute | solution.py:352
  8.5 3.6 %collective-permute-done.1.got_ref = bf16[3,136,128]{2,1,0:T(8,128)(2,1)S(1)} collective-permute-done((bf16[3,136,128]{2,1,0:T(8,128)(2,1)S(1)}, bf16[3,136,128]{2,1,0:T(8,128)(2,1)S(1)}, u32[]{:S(2)}, u32[]{:S(2)}) %collective-permute-start.1) | collective-permute-done | bytes 104480 | tf_op jit(solution)/shard_map/ppermute | solution.py:352
  12.1 3.1 %collective-permute-start.2 = (bf16[4,136,128]{2,1,0:T(8,128)(2,1)S(1)}, bf16[4,136,128]{2,1,0:T(8,128)(2,1)S(1)}, u32[]{:S(2)}, u32[]{:S(2)}) collective-permute-start(bf16[4,136,128]{2,1,0:T(8,128)(2,1)S(1)} %hop_p.3.mine_ref.p_ref), channel_id=1, source_target_pairs={{0,4},{1,5},{2,6},{3,7},{4,0},{5,1},{6,2},{7,3},{8,12},{9,13},{10,... | collective-permute-start | bytes 417800 | tf_op jit(solution)/shard_map/ppermute | solution.py:352
  15.3 0.7 collective-permute-start.4
  16.0 7.1 %collective-permute-done.2.got_ref.gp_ref = bf16[4,136,128]{2,1,0:T(8,128)(2,1)S(1)} collective-permute-done((bf16[4,136,128]{2,1,0:T(8,128)(2,1)S(1)}, bf16[4,136,128]{2,1,0:T(8,128)(2,1)S(1)}, u32[]{:S(2)}, u32[]{:S(2)}) %collective-permute-start.2) | collective-permute-done | bytes 139296 | tf_op jit(solution)/shard_map/ppermute | solution.py:352
  23.1 0.7 collective-permute-done.4.gq_ref
  24.0 0.4 mine.3.part_ref
  24.4 0.9 collective-permute-done.5.delta_ref
  25.3 0.5 change.3
  25.8 1.4 %collective-permute-start.8 = (bf16[128,512]{1,0:T(8,128)(2,1)S(1)}, bf16[128,512]{1,0:T(8,128)(2,1)S(1)}, u32[]{:S(2)}, u32[]{:S(2)}) collective-permute-start(bf16[128,512]{1,0:T(8,128)(2,1)S(1)} %get-tuple-element.64.mine_ref), channel_id=1, source_target_pairs={{0,16},{1,17},{2,18},{3,19},{4,20},{5,21},{6,22},{7,23},{8,24},{9,... | collective-permute-start | bytes 393224 | tf_op jit(solution)/shard_map/ppermute | solution.py:352
  27.3 1.5 %collective-permute-start.6 = (bf16[128,512]{1,0:T(8,128)(2,1)S(1)}, bf16[128,512]{1,0:T(8,128)(2,1)S(1)}, u32[]{:S(2)}, u32[]{:S(2)}) collective-permute-start(bf16[128,512]{1,0:T(8,128)(2,1)S(1)} %get-tuple-element.62.mine_ref), channel_id=1, source_target_pairs={{0,8},{1,9},{2,10},{3,11},{4,12},{5,13},{6,14},{7,15},{8,0},{9,1},... | collective-permute-start | bytes 393224 | tf_op jit(solution)/shard_map/ppermute | solution.py:352
  28.8 2.7 %collective-permute-done.8.got_ref = bf16[128,512]{1,0:T(8,128)(2,1)S(1)} collective-permute-done((bf16[128,512]{1,0:T(8,128)(2,1)S(1)}, bf16[128,512]{1,0:T(8,128)(2,1)S(1)}, u32[]{:S(2)}, u32[]{:S(2)}) %collective-permute-start.8) | collective-permute-done | bytes 131104 | tf_op jit(solution)/shard_map/ppermute | solution.py:352
  31.5 1.4 %collective-permute-start.9 = (bf16[128,512]{1,0:T(8,128)(2,1)S(1)}, bf16[128,512]{1,0:T(8,128)(2,1)S(1)}, u32[]{:S(2)}, u32[]{:S(2)}) collective-permute-start(bf16[128,512]{1,0:T(8,128)(2,1)S(1)} %get-tuple-element.65.b_ref), channel_id=1, source_target_pairs={{0,8},{1,9},{2,10},{3,11},{4,12},{5,13},{6,14},{7,15},{8,0},{9,1},... | collective-permute-start | bytes 393224 | tf_op jit(solution)/shard_map/ppermute | solution.py:352
  33.0 1.6 %collective-permute-start.7 = (bf16[128,512]{1,0:T(8,128)(2,1)S(1)}, bf16[128,512]{1,0:T(8,128)(2,1)S(1)}, u32[]{:S(2)}, u32[]{:S(2)}) collective-permute-start(bf16[128,512]{1,0:T(8,128)(2,1)S(1)} %get-tuple-element.63.a_ref), channel_id=1, source_target_pairs={{0,16},{1,17},{2,18},{3,19},{4,20},{5,21},{6,22},{7,23},{8,24},{9,... | collective-permute-start | bytes 393224 | tf_op jit(solution)/shard_map/ppermute | solution.py:352
  34.6 2.3 %prep.2.x_ref = bf16[1024,1024]{1,0:T(8,128)(2,1)S(1)} custom-call(s32[1,3]{1,0:T(1,128)S(1)} %bitcast.6, s32[8,16]{1,0:T(8,128)S(1)} %copy-done.1, bf16[1024,2048]{1,0:T(8,128)(2,1)} %x_ref.3), custom_call_target="tpu_custom_call" | custom-call | bytes 4194304 | tf_op jit(solution)/shard_map/prep/pallas_call | solution.py:51
  36.9 1.2 %collective-permute-done.7.ra_ref = bf16[128,512]{1,0:T(8,128)(2,1)S(1)} collective-permute-done((bf16[128,512]{1,0:T(8,128)(2,1)S(1)}, bf16[128,512]{1,0:T(8,128)(2,1)S(1)}, u32[]{:S(2)}, u32[]{:S(2)}) %collective-permute-start.7) | collective-permute-done | bytes 131104 | tf_op jit(solution)/shard_map/ppermute | solution.py:352
  38.0 0.8 soft_next.2
  38.9 0.5 own.4.own_ref
  39.5 1.0 collective-permute-done.10.got_ref
  40.5 0.7 collective-permute-start.11
  41.2 1.4 %collective-permute-start.13 = (bf16[2,136,128]{2,1,0:T(8,128)(2,1)S(1)}, bf16[2,136,128]{2,1,0:T(8,128)(2,1)S(1)}, u32[]{:S(2)}, u32[]{:S(2)}) collective-permute-start(bf16[2,136,128]{2,1,0:T(8,128)(2,1)S(1)} %get-tuple-element.73.mine_ref), channel_id=1, source_target_pairs={{0,2},{1,3},{2,0},{3,1},{4,6},{5,7},{6,4},{7,5},{8,10},{9,11},{10,... | collective-permute-start | bytes 208904 | tf_op jit(solution)/shard_map/ppermute | solution.py:352
  42.6 3.7 %collective-permute-done.11.got_ref = bf16[3,136,128]{2,1,0:T(8,128)(2,1)S(1)} collective-permute-done((bf16[3,136,128]{2,1,0:T(8,128)(2,1)S(1)}, bf16[3,136,128]{2,1,0:T(8,128)(2,1)S(1)}, u32[]{:S(2)}, u32[]{:S(2)}) %collective-permute-start.11) | collective-permute-done | bytes 104480 | tf_op jit(solution)/shard_map/ppermute | solution.py:352
  46.3 2.1 %collective-permute-start.12 = (bf16[4,136,128]{2,1,0:T(8,128)(2,1)S(1)}, bf16[4,136,128]{2,1,0:T(8,128)(2,1)S(1)}, u32[]{:S(2)}, u32[]{:S(2)}) collective-permute-start(bf16[4,136,128]{2,1,0:T(8,128)(2,1)S(1)} %hop_p.4.mine_ref.p_ref), channel_id=1, source_target_pairs={{0,4},{1,5},{2,6},{3,7},{4,0},{5,1},{6,2},{7,3},{8,12},{9,13},{10,... | collective-permute-start | bytes 417800 | tf_op jit(solution)/shard_map/ppermute | solution.py:352
  48.5 1.0 collective-permute-start.14
  49.5 7.2 %collective-permute-done.12.got_ref.gp_ref = bf16[4,136,128]{2,1,0:T(8,128)(2,1)S(1)} collective-permute-done((bf16[4,136,128]{2,1,0:T(8,128)(2,1)S(1)}, bf16[4,136,128]{2,1,0:T(8,128)(2,1)S(1)}, u32[]{:S(2)}, u32[]{:S(2)}) %collective-permute-start.12) | collective-permute-done | bytes 139296 | tf_op jit(solution)/shard_map/ppermute | solution.py:352
  56.7 0.7 collective-permute-done.14.gq_ref
  58.1 0.9 collective-permute-done.15.delta_ref
  59.0 0.5 change.4
  59.5 1.6 %collective-permute-start.18 = (bf16[128,512]{1,0:T(8,128)(2,1)S(1)}, bf16[128,512]{1,0:T(8,128)(2,1)S(1)}, u32[]{:S(2)}, u32[]{:S(2)}) collective-permute-start(bf16[128,512]{1,0:T(8,128)(2,1)S(1)} %get-tuple-element.82.mine_ref), channel_id=1, source_target_pairs={{0,16},{1,17},{2,18},{3,19},{4,20},{5,21},{6,22},{7,23},{8,24},{9,... | collective-permute-start | bytes 393224 | tf_op jit(solution)/shard_map/ppermute | solution.py:352
  61.1 0.5 collective-permute-start.16
  61.6 3.5 %collective-permute-done.18.got_ref = bf16[128,512]{1,0:T(8,128)(2,1)S(1)} collective-permute-done((bf16[128,512]{1,0:T(8,128)(2,1)S(1)}, bf16[128,512]{1,0:T(8,128)(2,1)S(1)}, u32[]{:S(2)}, u32[]{:S(2)}) %collective-permute-start.18) | collective-permute-done | bytes 131104 | tf_op jit(solution)/shard_map/ppermute | solution.py:352
  65.2 1.2 %collective-permute-start.19 = (bf16[128,512]{1,0:T(8,128)(2,1)S(1)}, bf16[128,512]{1,0:T(8,128)(2,1)S(1)}, u32[]{:S(2)}, u32[]{:S(2)}) collective-permute-start(bf16[128,512]{1,0:T(8,128)(2,1)S(1)} %get-tuple-element.83.b_ref), channel_id=1, source_target_pairs={{0,8},{1,9},{2,10},{3,11},{4,12},{5,13},{6,14},{7,15},{8,0},{9,1},... | collective-permute-start | bytes 393224 | tf_op jit(solution)/shard_map/ppermute | solution.py:352
  66.4 1.0 collective-permute-start.17
  67.4 2.3 %prep.3.x_ref = bf16[1024,1024]{1,0:T(8,128)(2,1)S(1)} custom-call(s32[1,3]{1,0:T(1,128)S(1)} %bitcast.7, s32[8,16]{1,0:T(8,128)S(1)} %copy-done.1, bf16[1024,2048]{1,0:T(8,128)(2,1)} %x_ref.3), custom_call_target="tpu_custom_call" | custom-call | bytes 4194304 | tf_op jit(solution)/shard_map/prep/pallas_call | solution.py:51
  69.7 0.5 collective-permute-done.19.rb_ref
  70.2 1.2 %collective-permute-done.17.ra_ref = bf16[128,512]{1,0:T(8,128)(2,1)S(1)} collective-permute-done((bf16[128,512]{1,0:T(8,128)(2,1)S(1)}, bf16[128,512]{1,0:T(8,128)(2,1)S(1)}, u32[]{:S(2)}, u32[]{:S(2)}) %collective-permute-start.17) | collective-permute-done | bytes 131104 | tf_op jit(solution)/shard_map/ppermute | solution.py:352
  71.4 0.8 soft_next.3
  72.3 0.5 own.5.own_ref
  72.9 1.0 collective-permute-done.20.got_ref
  73.9 0.7 collective-permute-start.23
  74.6 1.4 %collective-permute-start.21 = (bf16[2,136,128]{2,1,0:T(8,128)(2,1)S(1)}, bf16[2,136,128]{2,1,0:T(8,128)(2,1)S(1)}, u32[]{:S(2)}, u32[]{:S(2)}) collective-permute-start(bf16[2,136,128]{2,1,0:T(8,128)(2,1)S(1)} %get-tuple-element.89.mine_ref), channel_id=1, source_target_pairs={{0,2},{1,3},{2,0},{3,1},{4,6},{5,7},{6,4},{7,5},{8,10},{9,11},{10,... | collective-permute-start | bytes 208904 | tf_op jit(solution)/shard_map/ppermute | solution.py:352
  76.0 2.9 %collective-permute-done.23.got_ref = bf16[2,136,128]{2,1,0:T(8,128)(2,1)S(1)} collective-permute-done((bf16[2,136,128]{2,1,0:T(8,128)(2,1)S(1)}, bf16[2,136,128]{2,1,0:T(8,128)(2,1)S(1)}, u32[]{:S(2)}, u32[]{:S(2)}) %collective-permute-start.23) | collective-permute-done | bytes 69664 | tf_op jit(solution)/shard_map/ppermute | solution.py:352
  79.0 1.7 %collective-permute-start.24 = (bf16[2,136,128]{2,1,0:T(8,128)(2,1)S(1)}, bf16[2,136,128]{2,1,0:T(8,128)(2,1)S(1)}, u32[]{:S(2)}, u32[]{:S(2)}) collective-permute-start(bf16[2,136,128]{2,1,0:T(8,128)(2,1)S(1)} %hop_q.5.q_ref), channel_id=1, source_target_pairs={{0,4},{1,5},{2,6},{3,7},{4,0},{5,1},{6,2},{7,3},{8,12},{9,13},{10,... | collective-permute-start | bytes 208904 | tf_op jit(solution)/shard_map/ppermute | solution.py:352
  80.7 1.9 %collective-permute-start.22 = (bf16[2,136,128]{2,1,0:T(8,128)(2,1)S(1)}, bf16[2,136,128]{2,1,0:T(8,128)(2,1)S(1)}, u32[]{:S(2)}, u32[]{:S(2)}) collective-permute-start(bf16[2,136,128]{2,1,0:T(8,128)(2,1)S(1)} %hop_p.5.p_ref), channel_id=1, source_target_pairs={{0,4},{1,5},{2,6},{3,7},{4,0},{5,1},{6,2},{7,3},{8,12},{9,13},{10,... | collective-permute-start | bytes 208904 | tf_op jit(solution)/shard_map/ppermute | solution.py:352
  82.5 3.9 %collective-permute-done.24.gq_ref = bf16[2,136,128]{2,1,0:T(8,128)(2,1)S(1)} collective-permute-done((bf16[2,136,128]{2,1,0:T(8,128)(2,1)S(1)}, bf16[2,136,128]{2,1,0:T(8,128)(2,1)S(1)}, u32[]{:S(2)}, u32[]{:S(2)}) %collective-permute-start.24) | collective-permute-done | bytes 69664 | tf_op jit(solution)/shard_map/ppermute | solution.py:352
  86.4 1.5 %collective-permute-done.22.gp_ref = bf16[2,136,128]{2,1,0:T(8,128)(2,1)S(1)} collective-permute-done((bf16[2,136,128]{2,1,0:T(8,128)(2,1)S(1)}, bf16[2,136,128]{2,1,0:T(8,128)(2,1)S(1)}, u32[]{:S(2)}, u32[]{:S(2)}) %collective-permute-start.22) | collective-permute-done | bytes 69664 | tf_op jit(solution)/shard_map/ppermute | solution.py:352
  88.6 0.9 collective-permute-done.25.delta_ref
  89.6 1.2 %change.5 = (bf16[128,512]{1,0:T(8,128)(2,1)S(1)}, bf16[128,512]{1,0:T(8,128)(2,1)S(1)}, f32[128,512]{1,0:T(8,128)}, f32[128,512]{1,0:T(8,128)}) custom-call(bf16[1024,1024]{1,0:T(8,128)(2,1)S(1)} %prep.3.x_ref, f32[1024,128]{1,0:T(8,128)S(1)} %mine.5.part_ref, bf16[128,512]{1,0:T(8,128)(2,1)S(1)} %collective-permute-done.25.delta_ref, ...), custom_call_target="tpu_custom_call" | custom-call | flops 134217728 | bytes 1048576 | tf_op jit(solution)/shard_map/change/pallas_call | solution.py:51
  90.8 1.0 collective-permute-start.28
  91.7 1.5 %collective-permute-start.26 = (bf16[128,512]{1,0:T(8,128)(2,1)S(1)}, bf16[128,512]{1,0:T(8,128)(2,1)S(1)}, u32[]{:S(2)}, u32[]{:S(2)}) collective-permute-start(bf16[128,512]{1,0:T(8,128)(2,1)S(1)} %get-tuple-element.98.mine_ref), channel_id=1, source_target_pairs={{0,8},{1,9},{2,10},{3,11},{4,12},{5,13},{6,14},{7,15},{8,0},{9,1},... | collective-permute-start | bytes 393224 | tf_op jit(solution)/shard_map/ppermute | solution.py:352
  93.2 3.1 %collective-permute-done.28.got_ref = bf16[128,512]{1,0:T(8,128)(2,1)S(1)} collective-permute-done((bf16[128,512]{1,0:T(8,128)(2,1)S(1)}, bf16[128,512]{1,0:T(8,128)(2,1)S(1)}, u32[]{:S(2)}, u32[]{:S(2)}) %collective-permute-start.28) | collective-permute-done | bytes 131104 | tf_op jit(solution)/shard_map/ppermute | solution.py:352
  96.3 0.8 meet_b.5
  97.1 0.9 collective-permute-start.29
  98.0 0.8 meet_a.5
  98.8 1.5 %collective-permute-start.27 = (bf16[128,512]{1,0:T(8,128)(2,1)S(1)}, bf16[128,512]{1,0:T(8,128)(2,1)S(1)}, u32[]{:S(2)}, u32[]{:S(2)}) collective-permute-start(bf16[128,512]{1,0:T(8,128)(2,1)S(1)} %get-tuple-element.99.a_ref), channel_id=1, source_target_pairs={{0,16},{1,17},{2,18},{3,19},{4,20},{5,21},{6,22},{7,23},{8,24},{9,... | collective-permute-start | bytes 393224 | tf_op jit(solution)/shard_map/ppermute | solution.py:352
  100.3 0.6 coef_out.1
  101.0 0.7 copy.8
  101.6 0.4 collective-permute-done.29.rb_ref
  102.1 1.7 %collective-permute-done.27.ra_ref = bf16[128,512]{1,0:T(8,128)(2,1)S(1)} collective-permute-done((bf16[128,512]{1,0:T(8,128)(2,1)S(1)}, bf16[128,512]{1,0:T(8,128)(2,1)S(1)}, u32[]{:S(2)}, u32[]{:S(2)}) %collective-permute-start.27) | collective-permute-done | bytes 131104 | tf_op jit(solution)/shard_map/ppermute | solution.py:352
  103.8 1.0 last.1
  (39 shorter events, 2.3 us)
Async XLA Ops:
  3.7 1.7 %collective-permute-start = (f32[4,136,128]{2,1,0:T(8,128)S(1)}, f32[4,136,128]{2,1,0:T(8,128)S(1)}, u32[]{:S(2)}, u32[]{:S(2)}) collective-permute-start(f32[4,136,128]{2,1,0:T(8,128)S(1)} %get-tuple-element.57), channel_id=1, source_target_pairs={{0,1},{1,0},{2,3},{3,2},{4,5},{5,4},{6,7},{7,6},{8,9},{9,8},{10,11... | collective-permute-start | bytes 835592 | tf_op jit(solution)/shard_map/ppermute | solution.py:352
  5.4 6.7 %collective-permute-start.1 = (bf16[3,136,128]{2,1,0:T(8,128)(2,1)S(1)}, bf16[3,136,128]{2,1,0:T(8,128)(2,1)S(1)}, u32[]{:S(2)}, u32[]{:S(2)}) collective-permute-start(bf16[3,136,128]{2,1,0:T(8,128)(2,1)S(1)} %get-tuple-element.59.mine_ref), channel_id=1, source_target_pairs={{0,2},{1,3},{2,0},{3,1},{4,6},{5,7},{6,4},{7,5},{8,10},{9,11},{10,... | collective-permute-start | bytes 313352 | tf_op jit(solution)/shard_map/ppermute | solution.py:352
  8.4 6.8 %collective-permute-start.3 = (bf16[2,136,128]{2,1,0:T(8,128)(2,1)S(1)}, bf16[2,136,128]{2,1,0:T(8,128)(2,1)S(1)}, u32[]{:S(2)}, u32[]{:S(2)}) collective-permute-start(bf16[2,136,128]{2,1,0:T(8,128)(2,1)S(1)} %get-tuple-element.60.mine_ref), channel_id=1, source_target_pairs={{0,2},{1,3},{2,0},{3,1},{4,6},{5,7},{6,4},{7,5},{8,10},{9,11},{10,... | collective-permute-start | bytes 208904 | tf_op jit(solution)/shard_map/ppermute | solution.py:352
  12.1 10.9 %collective-permute-start.2 = (bf16[4,136,128]{2,1,0:T(8,128)(2,1)S(1)}, bf16[4,136,128]{2,1,0:T(8,128)(2,1)S(1)}, u32[]{:S(2)}, u32[]{:S(2)}) collective-permute-start(bf16[4,136,128]{2,1,0:T(8,128)(2,1)S(1)} %hop_p.3.mine_ref.p_ref), channel_id=1, source_target_pairs={{0,4},{1,5},{2,6},{3,7},{4,0},{5,1},{6,2},{7,3},{8,12},{9,13},{10,... | collective-permute-start | bytes 417800 | tf_op jit(solution)/shard_map/ppermute | solution.py:352
  15.3 8.5 %collective-permute-start.4 = (bf16[2,136,128]{2,1,0:T(8,128)(2,1)S(1)}, bf16[2,136,128]{2,1,0:T(8,128)(2,1)S(1)}, u32[]{:S(2)}, u32[]{:S(2)}) collective-permute-start(bf16[2,136,128]{2,1,0:T(8,128)(2,1)S(1)} %hop_q.3.q_ref), channel_id=1, source_target_pairs={{0,4},{1,5},{2,6},{3,7},{4,0},{5,1},{6,2},{7,3},{8,12},{9,13},{10,... | collective-permute-start | bytes 208904 | tf_op jit(solution)/shard_map/ppermute | solution.py:352
  23.9 1.4 %collective-permute-start.5 = (bf16[128,512]{1,0:T(8,128)(2,1)S(1)}, bf16[128,512]{1,0:T(8,128)(2,1)S(1)}, u32[]{:S(2)}, u32[]{:S(2)}) collective-permute-start(bf16[128,512]{1,0:T(8,128)(2,1)S(1)} %get-tuple-element.61.delta_ref), channel_id=1, source_target_pairs={{0,1},{1,0},{2,3},{3,2},{4,5},{5,4},{6,7},{7,6},{8,9},{9,8},{10,11... | collective-permute-start | bytes 393224 | tf_op jit(solution)/shard_map/ppermute | solution.py:352
  24.4 10.2 %copy-start.1 = (s32[8,16]{1,0:T(8,128)S(1)}, s32[8,16]{1,0:T(8,128)}, u32[]{:S(2)}) copy-start(s32[8,16]{1,0:T(8,128)} %live_ref.3) | copy-start | bytes 1540
  24.4 10.2 %copy-start.2 = (s32[3,1]{0,1:T(1,128)S(1)}, s32[3,1]{0,1:T(1,128)}, u32[]{:S(2)}) copy-start(s32[3,1]{0,1:T(1,128)} %param.11) | copy-start | bytes 40
  25.8 5.6 %collective-permute-start.8 = (bf16[128,512]{1,0:T(8,128)(2,1)S(1)}, bf16[128,512]{1,0:T(8,128)(2,1)S(1)}, u32[]{:S(2)}, u32[]{:S(2)}) collective-permute-start(bf16[128,512]{1,0:T(8,128)(2,1)S(1)} %get-tuple-element.64.mine_ref), channel_id=1, source_target_pairs={{0,16},{1,17},{2,18},{3,19},{4,20},{5,21},{6,22},{7,23},{8,24},{9,... | collective-permute-start | bytes 393224 | tf_op jit(solution)/shard_map/ppermute | solution.py:352
  27.3 5.6 %collective-permute-start.6 = (bf16[128,512]{1,0:T(8,128)(2,1)S(1)}, bf16[128,512]{1,0:T(8,128)(2,1)S(1)}, u32[]{:S(2)}, u32[]{:S(2)}) collective-permute-start(bf16[128,512]{1,0:T(8,128)(2,1)S(1)} %get-tuple-element.62.mine_ref), channel_id=1, source_target_pairs={{0,8},{1,9},{2,10},{3,11},{4,12},{5,13},{6,14},{7,15},{8,0},{9,1},... | collective-permute-start | bytes 393224 | tf_op jit(solution)/shard_map/ppermute | solution.py:352
  31.5 5.3 %collective-permute-start.9 = (bf16[128,512]{1,0:T(8,128)(2,1)S(1)}, bf16[128,512]{1,0:T(8,128)(2,1)S(1)}, u32[]{:S(2)}, u32[]{:S(2)}) collective-permute-start(bf16[128,512]{1,0:T(8,128)(2,1)S(1)} %get-tuple-element.65.b_ref), channel_id=1, source_target_pairs={{0,8},{1,9},{2,10},{3,11},{4,12},{5,13},{6,14},{7,15},{8,0},{9,1},... | collective-permute-start | bytes 393224 | tf_op jit(solution)/shard_map/ppermute | solution.py:352
  33.0 5.0 %copy-start = (s32[1024]{0:T(1024)S(1)}, s32[1024]{0:T(1024)}, u32[]{:S(2)}) copy-start(s32[1024]{0:T(1024)} %param.8) | copy-start | bytes 12292
  33.0 5.0 %collective-permute-start.7 = (bf16[128,512]{1,0:T(8,128)(2,1)S(1)}, bf16[128,512]{1,0:T(8,128)(2,1)S(1)}, u32[]{:S(2)}, u32[]{:S(2)}) collective-permute-start(bf16[128,512]{1,0:T(8,128)(2,1)S(1)} %get-tuple-element.63.a_ref), channel_id=1, source_target_pairs={{0,16},{1,17},{2,18},{3,19},{4,20},{5,21},{6,22},{7,23},{8,24},{9,... | collective-permute-start | bytes 393224 | tf_op jit(solution)/shard_map/ppermute | solution.py:352
  38.9 1.6 %collective-permute-start.10 = (f32[4,136,128]{2,1,0:T(8,128)S(1)}, f32[4,136,128]{2,1,0:T(8,128)S(1)}, u32[]{:S(2)}, u32[]{:S(2)}) collective-permute-start(f32[4,136,128]{2,1,0:T(8,128)S(1)} %get-tuple-element.70), channel_id=1, source_target_pairs={{0,1},{1,0},{2,3},{3,2},{4,5},{5,4},{6,7},{7,6},{8,9},{9,8},{10,11... | collective-permute-start | bytes 835592 | tf_op jit(solution)/shard_map/ppermute | solution.py:352
  40.5 5.8 %collective-permute-start.11 = (bf16[3,136,128]{2,1,0:T(8,128)(2,1)S(1)}, bf16[3,136,128]{2,1,0:T(8,128)(2,1)S(1)}, u32[]{:S(2)}, u32[]{:S(2)}) collective-permute-start(bf16[3,136,128]{2,1,0:T(8,128)(2,1)S(1)} %get-tuple-element.72.mine_ref), channel_id=1, source_target_pairs={{0,2},{1,3},{2,0},{3,1},{4,6},{5,7},{6,4},{7,5},{8,10},{9,11},{10,... | collective-permute-start | bytes 313352 | tf_op jit(solution)/shard_map/ppermute | solution.py:352
  41.2 7.2 %collective-permute-start.13 = (bf16[2,136,128]{2,1,0:T(8,128)(2,1)S(1)}, bf16[2,136,128]{2,1,0:T(8,128)(2,1)S(1)}, u32[]{:S(2)}, u32[]{:S(2)}) collective-permute-start(bf16[2,136,128]{2,1,0:T(8,128)(2,1)S(1)} %get-tuple-element.73.mine_ref), channel_id=1, source_target_pairs={{0,2},{1,3},{2,0},{3,1},{4,6},{5,7},{6,4},{7,5},{8,10},{9,11},{10,... | collective-permute-start | bytes 208904 | tf_op jit(solution)/shard_map/ppermute | solution.py:352
  46.3 10.3 %collective-permute-start.12 = (bf16[4,136,128]{2,1,0:T(8,128)(2,1)S(1)}, bf16[4,136,128]{2,1,0:T(8,128)(2,1)S(1)}, u32[]{:S(2)}, u32[]{:S(2)}) collective-permute-start(bf16[4,136,128]{2,1,0:T(8,128)(2,1)S(1)} %hop_p.4.mine_ref.p_ref), channel_id=1, source_target_pairs={{0,4},{1,5},{2,6},{3,7},{4,0},{5,1},{6,2},{7,3},{8,12},{9,13},{10,... | collective-permute-start | bytes 417800 | tf_op jit(solution)/shard_map/ppermute | solution.py:352
  48.5 8.9 %collective-permute-start.14 = (bf16[2,136,128]{2,1,0:T(8,128)(2,1)S(1)}, bf16[2,136,128]{2,1,0:T(8,128)(2,1)S(1)}, u32[]{:S(2)}, u32[]{:S(2)}) collective-permute-start(bf16[2,136,128]{2,1,0:T(8,128)(2,1)S(1)} %hop_q.4.q_ref), channel_id=1, source_target_pairs={{0,4},{1,5},{2,6},{3,7},{4,0},{5,1},{6,2},{7,3},{8,12},{9,13},{10,... | collective-permute-start | bytes 208904 | tf_op jit(solution)/shard_map/ppermute | solution.py:352
  57.6 1.4 %collective-permute-start.15 = (bf16[128,512]{1,0:T(8,128)(2,1)S(1)}, bf16[128,512]{1,0:T(8,128)(2,1)S(1)}, u32[]{:S(2)}, u32[]{:S(2)}) collective-permute-start(bf16[128,512]{1,0:T(8,128)(2,1)S(1)} %get-tuple-element.75.delta_ref), channel_id=1, source_target_pairs={{0,1},{1,0},{2,3},{3,2},{4,5},{5,4},{6,7},{7,6},{8,9},{9,8},{10,11... | collective-permute-start | bytes 393224 | tf_op jit(solution)/shard_map/ppermute | solution.py:352
  59.5 5.6 %collective-permute-start.18 = (bf16[128,512]{1,0:T(8,128)(2,1)S(1)}, bf16[128,512]{1,0:T(8,128)(2,1)S(1)}, u32[]{:S(2)}, u32[]{:S(2)}) collective-permute-start(bf16[128,512]{1,0:T(8,128)(2,1)S(1)} %get-tuple-element.82.mine_ref), channel_id=1, source_target_pairs={{0,16},{1,17},{2,18},{3,19},{4,20},{5,21},{6,22},{7,23},{8,24},{9,... | collective-permute-start | bytes 393224 | tf_op jit(solution)/shard_map/ppermute | solution.py:352
  61.1 5.3 %collective-permute-start.16 = (bf16[128,512]{1,0:T(8,128)(2,1)S(1)}, bf16[128,512]{1,0:T(8,128)(2,1)S(1)}, u32[]{:S(2)}, u32[]{:S(2)}) collective-permute-start(bf16[128,512]{1,0:T(8,128)(2,1)S(1)} %get-tuple-element.80.mine_ref), channel_id=1, source_target_pairs={{0,8},{1,9},{2,10},{3,11},{4,12},{5,13},{6,14},{7,15},{8,0},{9,1},... | collective-permute-start | bytes 393224 | tf_op jit(solution)/shard_map/ppermute | solution.py:352
  65.2 5.0 %collective-permute-start.19 = (bf16[128,512]{1,0:T(8,128)(2,1)S(1)}, bf16[128,512]{1,0:T(8,128)(2,1)S(1)}, u32[]{:S(2)}, u32[]{:S(2)}) collective-permute-start(bf16[128,512]{1,0:T(8,128)(2,1)S(1)} %get-tuple-element.83.b_ref), channel_id=1, source_target_pairs={{0,8},{1,9},{2,10},{3,11},{4,12},{5,13},{6,14},{7,15},{8,0},{9,1},... | collective-permute-start | bytes 393224 | tf_op jit(solution)/shard_map/ppermute | solution.py:352
  66.4 5.0 %collective-permute-start.17 = (bf16[128,512]{1,0:T(8,128)(2,1)S(1)}, bf16[128,512]{1,0:T(8,128)(2,1)S(1)}, u32[]{:S(2)}, u32[]{:S(2)}) collective-permute-start(bf16[128,512]{1,0:T(8,128)(2,1)S(1)} %get-tuple-element.81.a_ref), channel_id=1, source_target_pairs={{0,16},{1,17},{2,18},{3,19},{4,20},{5,21},{6,22},{7,23},{8,24},{9,... | collective-permute-start | bytes 393224 | tf_op jit(solution)/shard_map/ppermute | solution.py:352
  72.3 1.6 %collective-permute-start.20 = (f32[4,136,128]{2,1,0:T(8,128)S(1)}, f32[4,136,128]{2,1,0:T(8,128)S(1)}, u32[]{:S(2)}, u32[]{:S(2)}) collective-permute-start(f32[4,136,128]{2,1,0:T(8,128)S(1)} %get-tuple-element.88), channel_id=1, source_target_pairs={{0,1},{1,0},{2,3},{3,2},{4,5},{5,4},{6,7},{7,6},{8,9},{9,8},{10,11... | collective-permute-start | bytes 835592 | tf_op jit(solution)/shard_map/ppermute | solution.py:352
  73.9 5.0 %collective-permute-start.23 = (bf16[2,136,128]{2,1,0:T(8,128)(2,1)S(1)}, bf16[2,136,128]{2,1,0:T(8,128)(2,1)S(1)}, u32[]{:S(2)}, u32[]{:S(2)}) collective-permute-start(bf16[2,136,128]{2,1,0:T(8,128)(2,1)S(1)} %get-tuple-element.90.mine_ref), channel_id=1, source_target_pairs={{0,2},{1,3},{2,0},{3,1},{4,6},{5,7},{6,4},{7,5},{8,10},{9,11},{10,... | collective-permute-start | bytes 208904 | tf_op jit(solution)/shard_map/ppermute | solution.py:352
  74.6 6.0 %collective-permute-start.21 = (bf16[2,136,128]{2,1,0:T(8,128)(2,1)S(1)}, bf16[2,136,128]{2,1,0:T(8,128)(2,1)S(1)}, u32[]{:S(2)}, u32[]{:S(2)}) collective-permute-start(bf16[2,136,128]{2,1,0:T(8,128)(2,1)S(1)} %get-tuple-element.89.mine_ref), channel_id=1, source_target_pairs={{0,2},{1,3},{2,0},{3,1},{4,6},{5,7},{6,4},{7,5},{8,10},{9,11},{10,... | collective-permute-start | bytes 208904 | tf_op jit(solution)/shard_map/ppermute | solution.py:352
  79.0 7.5 %collective-permute-start.24 = (bf16[2,136,128]{2,1,0:T(8,128)(2,1)S(1)}, bf16[2,136,128]{2,1,0:T(8,128)(2,1)S(1)}, u32[]{:S(2)}, u32[]{:S(2)}) collective-permute-start(bf16[2,136,128]{2,1,0:T(8,128)(2,1)S(1)} %hop_q.5.q_ref), channel_id=1, source_target_pairs={{0,4},{1,5},{2,6},{3,7},{4,0},{5,1},{6,2},{7,3},{8,12},{9,13},{10,... | collective-permute-start | bytes 208904 | tf_op jit(solution)/shard_map/ppermute | solution.py:352
  80.7 7.3 %collective-permute-start.22 = (bf16[2,136,128]{2,1,0:T(8,128)(2,1)S(1)}, bf16[2,136,128]{2,1,0:T(8,128)(2,1)S(1)}, u32[]{:S(2)}, u32[]{:S(2)}) collective-permute-start(bf16[2,136,128]{2,1,0:T(8,128)(2,1)S(1)} %hop_p.5.p_ref), channel_id=1, source_target_pairs={{0,4},{1,5},{2,6},{3,7},{4,0},{5,1},{6,2},{7,3},{8,12},{9,13},{10,... | collective-permute-start | bytes 208904 | tf_op jit(solution)/shard_map/ppermute | solution.py:352
  88.1 1.4 %collective-permute-start.25 = (bf16[128,512]{1,0:T(8,128)(2,1)S(1)}, bf16[128,512]{1,0:T(8,128)(2,1)S(1)}, u32[]{:S(2)}, u32[]{:S(2)}) collective-permute-start(bf16[128,512]{1,0:T(8,128)(2,1)S(1)} %get-tuple-element.93.delta_ref), channel_id=1, source_target_pairs={{0,1},{1,0},{2,3},{3,2},{4,5},{5,4},{6,7},{7,6},{8,9},{9,8},{10,11... | collective-permute-start | bytes 393224 | tf_op jit(solution)/shard_map/ppermute | solution.py:352
  90.8 5.5 %collective-permute-start.28 = (bf16[128,512]{1,0:T(8,128)(2,1)S(1)}, bf16[128,512]{1,0:T(8,128)(2,1)S(1)}, u32[]{:S(2)}, u32[]{:S(2)}) collective-permute-start(bf16[128,512]{1,0:T(8,128)(2,1)S(1)} %get-tuple-element.100.mine_ref), channel_id=1, source_target_pairs={{0,16},{1,17},{2,18},{3,19},{4,20},{5,21},{6,22},{7,23},{8,24},{9,... | collective-permute-start | bytes 393224 | tf_op jit(solution)/shard_map/ppermute | solution.py:352
  91.7 6.3 %collective-permute-start.26 = (bf16[128,512]{1,0:T(8,128)(2,1)S(1)}, bf16[128,512]{1,0:T(8,128)(2,1)S(1)}, u32[]{:S(2)}, u32[]{:S(2)}) collective-permute-start(bf16[128,512]{1,0:T(8,128)(2,1)S(1)} %get-tuple-element.98.mine_ref), channel_id=1, source_target_pairs={{0,8},{1,9},{2,10},{3,11},{4,12},{5,13},{6,14},{7,15},{8,0},{9,1},... | collective-permute-start | bytes 393224 | tf_op jit(solution)/shard_map/ppermute | solution.py:352
  97.1 5.0 %collective-permute-start.29 = (bf16[128,512]{1,0:T(8,128)(2,1)S(1)}, bf16[128,512]{1,0:T(8,128)(2,1)S(1)}, u32[]{:S(2)}, u32[]{:S(2)}) collective-permute-start(bf16[128,512]{1,0:T(8,128)(2,1)S(1)} %get-tuple-element.101.b_ref), channel_id=1, source_target_pairs={{0,8},{1,9},{2,10},{3,11},{4,12},{5,13},{6,14},{7,15},{8,0},{9,1},... | collective-permute-start | bytes 393224 | tf_op jit(solution)/shard_map/ppermute | solution.py:352
  98.8 5.0 %collective-permute-start.27 = (bf16[128,512]{1,0:T(8,128)(2,1)S(1)}, bf16[128,512]{1,0:T(8,128)(2,1)S(1)}, u32[]{:S(2)}, u32[]{:S(2)}) collective-permute-start(bf16[128,512]{1,0:T(8,128)(2,1)S(1)} %get-tuple-element.99.a_ref), channel_id=1, source_target_pairs={{0,16},{1,17},{2,18},{3,19},{4,20},{5,21},{6,22},{7,23},{8,24},{9,... | collective-permute-start | bytes 393224 | tf_op jit(solution)/shard_map/ppermute | solution.py:352

commit v6 on v5

--- a/solution.py
+++ b/solution.py
@@ -158,7 +158,7 @@
 
 def first_body(
     order_hbm, live_hbm, margins_hbm, lab_hbm, coef_hbm, x_hbm,
-    x_ref, score_ref, res_ref, spread_ref, g_ref, first_ref, other_ref, *rest,
+    x_ref, score_ref, res_ref, spread_ref, g_ref, first_ref, other_ref, first_send, other_send, *rest,
 ):
     same_refs = rest[: STEPS - 1]
     order, live, margins, labels, coef, small, buf, sems = rest[STEPS - 1 :]
@@ -179,8 +179,10 @@
         score = margins[here, :].astype(F32).T
         score_ref[:, here] = score
         soft_rows(score, labels[r : r + 1, :], here, res_ref, spread_ref)
-    first_ref[...] = coef[chosen].T
-    other_ref[...] = coef[1 - chosen].T
+    for block, keep, send in ((chosen, first_ref, first_send), (1 - chosen, other_ref, other_send)):
+        rows = coef[block].T
+        keep[...] = rows
+        send[...] = rows.astype(BF16)
     for step, same_ref in enumerate(same_refs):
         same_ref[...] = jnp.full((8, TILE), (order[0, step + 1] == chosen).astype(F32))
     for r, copy in enumerate(copies):
@@ -239,10 +241,11 @@
         encode(k % PB, total[0:C], total[C : C + 1], p_ref if k < PB else q_ref)
 
 
-def pair_with_body(own_ref, got_ref, coef_ref, p_ref, q_ref):
+def pair_with_body(own_ref, got_ref, mine_ref, far_ref, p_ref, q_ref):
     pair_body(own_ref, got_ref, p_ref, q_ref)
-    p_ref[PB, 0:C, :] = coef_ref[...].astype(BF16)
-    p_ref[PB, C:ROWS, :] = jnp.zeros((ROWS - C, TILE), BF16)
+    for k, rows_ref in ((PB, mine_ref), (PB + 1, far_ref)):
+        q_ref[k, 0:C, :] = rows_ref[...]
+        q_ref[k, C:ROWS, :] = jnp.zeros((ROWS - C, TILE), BF16)
 
 
 def decode_sum(k, mine_ref, got_ref):
@@ -255,17 +258,11 @@
         encode(k, *decode_sum(k, mine_ref, got_ref), out_ref)
 
 
-def hop_with_body(mine_ref, got_ref, out_ref):
-    hop_body(mine_ref, got_ref, out_ref)
-    out_ref[PB] = mine_ref[PB]
-    out_ref[PB + 1] = got_ref[PB]
-
-
-def place_body(mine_ref, got_ref, coef_ref, out_ref):
+def place_body(got_ref, far_ref, coef_ref, out_ref):
     place = lax.axis_index("ex") // 2
     out_ref[place] = coef_ref[...]
-    out_ref[jnp.bitwise_xor(place, 1)] = mine_ref[PB + 1, 0:C, :].astype(F32)
-    out_ref[jnp.bitwise_xor(place, 2)] = got_ref[PB, 0:C, :].astype(F32)
+    out_ref[jnp.bitwise_xor(place, 1)] = got_ref[PB, 0:C, :].astype(F32)
+    out_ref[jnp.bitwise_xor(place, 2)] = far_ref[...].astype(F32)
     out_ref[jnp.bitwise_xor(place, 3)] = got_ref[PB + 1, 0:C, :].astype(F32)
 
 
@@ -317,7 +314,7 @@
 
 
 def change_body(carried, x_ref, part_ref, delta_ref, *refs):
-    errors, (a_ref, b_ref, ea_ref, eb_ref) = refs[:carried], refs[carried:]
+    errors, (a_ref, b_ref, *keep) = refs[:carried], refs[carried:]
     part = part_ref[...] + contrib(x_ref, HALF, delta_ref)
     rows = x_ref.shape[0]
     for _, here in tiles_of(rows):
@@ -328,14 +325,16 @@
             full = full + e_ref[:, at]
         sent = full.astype(BF16)
         (a_ref if low else b_ref)[:, at] = sent
-        (ea_ref if low else eb_ref)[:, at] = full - sent.astype(F32)
-
-
-def meet_body(share, mine_ref, got_ref, out_ref, error_ref):
+        if keep:
+            keep[0 if low else 1][:, at] = full - sent.astype(F32)
+
+
+def meet_body(share, mine_ref, got_ref, out_ref, *error_refs):
     total = mine_ref[...].astype(F32) + got_ref[...].astype(F32)
     sent = total.astype(BF16)
     out_ref[...] = sent
-    error_ref[...] = share * (total - sent.astype(F32))
+    for error_ref in error_refs:
+        error_ref[...] = share * (total - sent.astype(F32))
 
 
 def bits(n):
@@ -356,7 +355,7 @@
     return swap(x, lambda f, e: (f, e ^ 1))
 
 
-def sum_over_feat(a, b):
+def sum_over_feat(a, b, last):
     order = bits(lax.axis_size("feat"))
     errors, pair = [], 1
     for n in range(len(order)):
@@ -365,11 +364,11 @@
         if n == len(order) - 1:
             return (a, got_a, b, got_b), errors
         pair *= 2
-        shapes = (sds(a.shape, BF16), sds(a.shape, F32))
+        shapes = (sds(a.shape, BF16),) + (() if last else (sds(a.shape, F32),))
         meet = functools.partial(meet_body, 1.0 / pair)
-        a, ea = call(meet, shapes, vmem(2), "meet_a")(a, got_a)
-        b, eb = call(meet, shapes, vmem(2), "meet_b")(b, got_b)
-        errors += [ea, eb]
+        a, *ea = call(meet, shapes, vmem(2), "meet_a")(a, got_a)
+        b, *eb = call(meet, shapes, vmem(2), "meet_b")(b, got_b)
+        errors += ea + eb
 
 
 def gather_blocks(coef, order, z_bits):
@@ -413,7 +412,7 @@
     g_shape = soft_shapes[-1]
     old_shape, delta_shape = sds((NB, C, TILE), F32), sds((C, HALF), BF16)
     part_shape, half = sds((rows, C), F32), (C, rows // 2)
-    own_shape, same_shape = sds((C, TILE), F32), sds((8, TILE), F32)
+    own_shape, send_shape, same_shape = sds((C, TILE), F32), sds((C, TILE), BF16), sds((8, TILE), F32)
     flops, nbytes = 2 * rows * HALF * C, 1 << 20
 
     def message(n):
@@ -422,7 +421,7 @@
     if aligned:
         x, score, res_t, spread, g_other, *rest = call(
             first_body,
-            (x_shape,) + soft_shapes + (own_shape,) * 2 + (same_shape,) * (STEPS - 1),
+            (x_shape,) + soft_shapes + (own_shape,) * 2 + (send_shape,) * 2 + (same_shape,) * (STEPS - 1),
             hbm(6), "soft_first", flops, nbytes,
             scratch_shapes=[
                 pltpu.SMEM(order.shape, jnp.int32),
@@ -433,7 +432,9 @@
                 pltpu.SemaphoreType.DMA((5,)),
             ] + block_scratch(rows),
         )(order, tile_live, margins, labels, coef, x_values)
-        blocks, same = rest[:2], rest[2:]
+        blocks, sends, same = rest[:2], rest[2:4], rest[4:]
+        across = lambda rows: swap(rows, lambda f, e: (f, e ^ z_bits[-1]))
+        fars = [across(sends[0]), None]
     else:
         x = prep_general(x_values, tile_live, order[0, 0], core, own)
         score, res_t, spread, g_other = call(
@@ -447,10 +448,7 @@
     errors = []
     for step in range(STEPS):
         if step > 0:
-            if aligned:
-                x = prep(order, tile_live, x_values, step)
-            else:
-                x = prep_general(x_values, tile_live, order[0, step], core, own)
+            x = following
             score, res_t, spread, g_other = call(
                 next_body, soft_shapes, vmem(7), "soft_next", flops, nbytes
             )(score, *halves, labels, x)
@@ -458,38 +456,49 @@
         g_own = call(own_body, g_shape, vmem(3), "own", flops, nbytes)(res_t, spread, x)
         carry = aligned and step < 2
         if carry:
-            p, q = call(pair_with_body, (message(1), message(0)), vmem(3), "pair")(g_own, got, blocks[step])
+            p, q = call(pair_with_body, (message(0), message(2)), vmem(4), "pair")(
+                g_own, got, sends[step], fars[step]
+            )
         else:
             p, q = call(pair_body, (message(0), message(0)), vmem(2), "pair")(g_own, got)
         for n, bit in enumerate(z_bits):
             got_p = swap(p, lambda f, e, bit=bit: (f, e ^ bit))
             got_q = swap(q, lambda f, e, bit=bit: (f, e ^ bit))
+            if n == 0 and carry:
+                old = call(place_body, old_shape, vmem(3), "place")(got_q, fars[step], blocks[step])
+            elif n == 0 and step < 2:
+                old = blocks[step]
             if n < len(z_bits) - 1:
-                body, extra = (hop_with_body, 2) if carry else (hop_body, 0)
-                p = call(body, message(extra), vmem(2), "hop_p")(p, got_p)
+                p = call(hop_body, message(0), vmem(2), "hop_p")(p, got_p)
                 q = call(hop_body, message(0), vmem(2), "hop_q")(q, got_q)
-        if step < 2:
-            far = blocks[step]
-            if aligned:
-                far = call(place_body, old_shape, vmem(3), "place")(p, got_p, far)
         sums = (p, got_p, q, got_q)
+        if step < STEPS - 1 and aligned:
+            following = prep(order, tile_live, x_values, step + 1)
+            *sums, following = lax.optimization_barrier((*sums, following))
+        elif step < STEPS - 1:
+            following = prep_general(x_values, tile_live, order[0, step + 1], core, own)
         if step == 0:
             first, delta = call(
                 functools.partial(prox_first_body, count), (old_shape, delta_shape), vmem(5), "prox"
-            )(*sums, far)
+            )(*sums, old)
         else:
             first, other, delta = call(
                 functools.partial(prox_body, count), (old_shape, old_shape, delta_shape), vmem(7), "prox"
-            )(same[step - 1], *sums, first, far if step == 1 else other)
+            )(same[step - 1], *sums, first, old if step == 1 else other)
         got = swap_core(delta)
         part = call(mine_body, part_shape, vmem(2), "mine", flops, nbytes)(x, delta)
-        a, b, ea, eb = call(
-            functools.partial(change_body, len(errors)),
-            (sds(half, BF16), sds(half, BF16), sds(half, F32), sds(half, F32)),
-            vmem(3 + len(errors)), "change", flops, nbytes,
+        last = step == STEPS - 1
+        shapes = (sds(half, BF16),) * 2 + (() if last else (sds(half, F32),) * 2)
+        a, b, *kept = call(
+            functools.partial(change_body, len(errors)), shapes, vmem(3 + len(errors)), "change", flops, nbytes,
         )(x, part, got, *errors)
-        halves, errors = sum_over_feat(a, b)
-        errors = [ea, eb] + errors
+        if step == 0 and aligned:
+            a, b, send = lax.optimization_barrier((a, b, sends[1]))
+            fars[1] = across(send)
+        halves, errors = sum_over_feat(a, b, last)
+        if step == 0 and aligned:
+            *halves, fars[1] = lax.optimization_barrier((*halves, fars[1]))
+        errors = kept + errors
     score = call(last_body, jax.ShapeDtypeStruct((rows, C), F32), vmem(5), "last")(score, *halves)
     if aligned:
         coef = call(coef_body, sds(coef.shape, F32), smem(1) + vmem(2), "coef_out")(order, first, other)

time: 105 us -> 105 us (level)
  Pallas kernels: 18.5 us -> 16.3 us
  starting transfers between devices: 33.7 us -> 35.7 us
    pallas_call x36, Pallas kernels: 18.5 us -> 16.3 us  [run(): f(*(x if spec.memory_space == pltpu.SMEM else pltpu.with_memory_space_con...]
    ppermute x30 -> x32, starting transfers between devices: 33.7 us -> 35.7 us  [swap(): return lax.ppermute(x, ('feat', 'ex'), pairs)]
    ppermute x30 -> x32, waiting for transfers between devices: 51.1 us -> 51.1 us  [swap(): return lax.ppermute(x, ('feat', 'ex'), pairs)]
  transfers between devices with their start and end apart: 30 -> 32, of which waited for: 23 -> 23; matrix products, arithmetic and copies ran while one was open for 1% -> 1% of each run, Pallas kernels for 10% -> 8%
where the time goes in v6:
time: 105 us
  waiting for transfers between devices  51.1 us (49%)
  starting transfers between devices  35.7 us (34%)
  Pallas kernels  16.3 us (16%)
    ppermute x32, waiting for transfers between devices, swap(): return lax.ppermute(x, ('feat', 'ex'), pairs)  51.1 us
    ppermute x32, starting transfers between devices, swap(): return lax.ppermute(x, ('feat', 'ex'), pairs)  35.7 us
    pallas_call x36, Pallas kernels, run(): f(*(x if spec.memory_space == pltpu.SMEM else pltpu.with_memory_space_con...  16.3 us
  transfers between devices with their start and end apart: 32, of which 23 were waited for; matrix products, arithmetic and copies ran while one was open for 1% of the time, Pallas kernels for 8%

profile of v6, /device:TPU:0, one launch (start us, length us, event | category | flops | bytes accessed | tf_op | source)
XLA Modules:
  0.0 104.6 jit_solution(628155440083048158)
XLA Ops:
  0.6 3.0 %soft_first.1 = (bf16[1024,1024]{1,0:T(8,128)(2,1)S(1)}, f32[128,1024]{1,0:T(8,128)S(1)}, bf16[128,1024]{1,0:T(8,128)(2,1)S(1)}, f32[1024,128]{1,0:T(8,128)S(1)}...) custom-call(s32[1,3]{1,0:T(1,128)} %bitcast.5, ...), custom_call_target="tpu_custom_call" | custom-call | flops 134217728 | bytes 1048576 | tf_op jit(solution)/shard_map/soft_first/pallas_call | solution.py:51
  3.7 0.5 collective-permute-start
  4.2 3.7 %collective-permute-start.1 = (bf16[128,128]{1,0:T(8,128)(2,1)S(1)}, bf16[128,128]{1,0:T(8,128)(2,1)S(1)}, u32[]{:S(2)}, u32[]{:S(2)}) collective-permute-start(bf16[128,128]{1,0:T(8,128)(2,1)S(1)} %get-tuple-element.76.mine_ref), channel_id=1, source_target_pairs={{0,4},{1,5},{2,6},{3,7},{4,0},{5,1},{6,2},{7,3},{8,12},{9,13},{10,... | collective-permute-start | bytes 98312 | tf_op jit(solution)/shard_map/ppermute | solution.py:351
  7.8 0.6 own.3.own_ref
  8.4 1.4 %collective-permute-done.1.far_ref = bf16[128,128]{1,0:T(8,128)(2,1)S(1)} collective-permute-done((bf16[128,128]{1,0:T(8,128)(2,1)S(1)}, bf16[128,128]{1,0:T(8,128)(2,1)S(1)}, u32[]{:S(2)}, u32[]{:S(2)}) %collective-permute-start.1) | collective-permute-done | bytes 32800 | tf_op jit(solution)/shard_map/ppermute | solution.py:351
  9.9 1.9 %collective-permute-start.4 = (bf16[4,136,128]{2,1,0:T(8,128)(2,1)S(1)}, bf16[4,136,128]{2,1,0:T(8,128)(2,1)S(1)}, u32[]{:S(2)}, u32[]{:S(2)}) collective-permute-start(bf16[4,136,128]{2,1,0:T(8,128)(2,1)S(1)} %get-tuple-element.78.mine_ref), channel_id=1, source_target_pairs={{0,2},{1,3},{2,0},{3,1},{4,6},{5,7},{6,4},{7,5},{8,10},{9,11},{10,... | collective-permute-start | bytes 417800 | tf_op jit(solution)/shard_map/ppermute | solution.py:351
  11.7 0.2 collective-permute-start.2
  12.0 4.9 %collective-permute-done.2.got_ref = bf16[2,136,128]{2,1,0:T(8,128)(2,1)S(1)} collective-permute-done((bf16[2,136,128]{2,1,0:T(8,128)(2,1)S(1)}, bf16[2,136,128]{2,1,0:T(8,128)(2,1)S(1)}, u32[]{:S(2)}, u32[]{:S(2)}) %collective-permute-start.2) | collective-permute-done | bytes 69664 | tf_op jit(solution)/shard_map/ppermute | solution.py:351
  16.9 3.2 %collective-permute-start.3 = (bf16[2,136,128]{2,1,0:T(8,128)(2,1)S(1)}, bf16[2,136,128]{2,1,0:T(8,128)(2,1)S(1)}, u32[]{:S(2)}, u32[]{:S(2)}) collective-permute-start(bf16[2,136,128]{2,1,0:T(8,128)(2,1)S(1)} %hop_p.3.p_ref), channel_id=1, source_target_pairs={{0,4},{1,5},{2,6},{3,7},{4,0},{5,1},{6,2},{7,3},{8,12},{9,13},{10,... | collective-permute-start | bytes 208904 | tf_op jit(solution)/shard_map/ppermute | solution.py:351
  20.2 2.3 %prep.2.x_ref = bf16[1024,1024]{1,0:T(8,128)(2,1)S(1)} custom-call(s32[1,3]{1,0:T(1,128)S(1)} %bitcast.6, s32[8,16]{1,0:T(8,128)S(1)} %copy-done.1, bf16[1024,2048]{1,0:T(8,128)(2,1)} %x_ref.3), custom_call_target="tpu_custom_call" | custom-call | bytes 4194304 | tf_op jit(solution)/shard_map/prep/pallas_call | solution.py:51
  22.7 3.1 %collective-permute-done.5.gq_ref = bf16[2,136,128]{2,1,0:T(8,128)(2,1)S(1)} collective-permute-done((bf16[2,136,128]{2,1,0:T(8,128)(2,1)S(1)}, bf16[2,136,128]{2,1,0:T(8,128)(2,1)S(1)}, u32[]{:S(2)}, u32[]{:S(2)}) %collective-permute-start.5) | collective-permute-done | bytes 69664 | tf_op jit(solution)/shard_map/ppermute | solution.py:351
  26.0 0.4 mine.3.part_ref
  26.4 0.9 collective-permute-done.6.delta_ref
  27.3 0.5 change.3
  27.8 1.6 %collective-permute-start.7 = (bf16[128,512]{1,0:T(8,128)(2,1)S(1)}, bf16[128,512]{1,0:T(8,128)(2,1)S(1)}, u32[]{:S(2)}, u32[]{:S(2)}) collective-permute-start(bf16[128,512]{1,0:T(8,128)(2,1)S(1)} %get-tuple-element.88.mine_ref), channel_id=1, source_target_pairs={{0,8},{1,9},{2,10},{3,11},{4,12},{5,13},{6,14},{7,15},{8,0},{9,1},... | collective-permute-start | bytes 393224 | tf_op jit(solution)/shard_map/ppermute | solution.py:351
  29.4 1.5 %collective-permute-start.9 = (bf16[128,512]{1,0:T(8,128)(2,1)S(1)}, bf16[128,512]{1,0:T(8,128)(2,1)S(1)}, u32[]{:S(2)}, u32[]{:S(2)}) collective-permute-start(bf16[128,512]{1,0:T(8,128)(2,1)S(1)} %get-tuple-element.90.mine_ref), channel_id=1, source_target_pairs={{0,16},{1,17},{2,18},{3,19},{4,20},{5,21},{6,22},{7,23},{8,24},{9,... | collective-permute-start | bytes 393224 | tf_op jit(solution)/shard_map/ppermute | solution.py:351
  30.9 2.5 %collective-permute-done.7.got_ref = bf16[128,512]{1,0:T(8,128)(2,1)S(1)} collective-permute-done((bf16[128,512]{1,0:T(8,128)(2,1)S(1)}, bf16[128,512]{1,0:T(8,128)(2,1)S(1)}, u32[]{:S(2)}, u32[]{:S(2)}) %collective-permute-start.7) | collective-permute-done | bytes 131104 | tf_op jit(solution)/shard_map/ppermute | solution.py:351
  33.5 1.6 %collective-permute-start.8 = (bf16[128,512]{1,0:T(8,128)(2,1)S(1)}, bf16[128,512]{1,0:T(8,128)(2,1)S(1)}, u32[]{:S(2)}, u32[]{:S(2)}) collective-permute-start(bf16[128,512]{1,0:T(8,128)(2,1)S(1)} %get-tuple-element.93.a_ref), channel_id=1, source_target_pairs={{0,16},{1,17},{2,18},{3,19},{4,20},{5,21},{6,22},{7,23},{8,24},{9,... | collective-permute-start | bytes 393224 | tf_op jit(solution)/shard_map/ppermute | solution.py:351
  35.1 1.6 %collective-permute-start.10 = (bf16[128,512]{1,0:T(8,128)(2,1)S(1)}, bf16[128,512]{1,0:T(8,128)(2,1)S(1)}, u32[]{:S(2)}, u32[]{:S(2)}) collective-permute-start(bf16[128,512]{1,0:T(8,128)(2,1)S(1)} %get-tuple-element.95.b_ref), channel_id=1, source_target_pairs={{0,8},{1,9},{2,10},{3,11},{4,12},{5,13},{6,14},{7,15},{8,0},{9,1},... | collective-permute-start | bytes 393224 | tf_op jit(solution)/shard_map/ppermute | solution.py:351
  36.7 0.3 collective-permute-start.11
  37.0 4.5 %collective-permute-done.11.far_ref = bf16[128,128]{1,0:T(8,128)(2,1)S(1)} collective-permute-done((bf16[128,128]{1,0:T(8,128)(2,1)S(1)}, bf16[128,128]{1,0:T(8,128)(2,1)S(1)}, u32[]{:S(2)}, u32[]{:S(2)}) %collective-permute-start.11) | collective-permute-done | bytes 32800 | tf_op jit(solution)/shard_map/ppermute | solution.py:351
  41.5 0.8 soft_next.2
  42.4 0.5 own.4.own_ref
  42.9 1.0 collective-permute-done.12.got_ref
  44.0 1.8 %collective-permute-start.15 = (bf16[4,136,128]{2,1,0:T(8,128)(2,1)S(1)}, bf16[4,136,128]{2,1,0:T(8,128)(2,1)S(1)}, u32[]{:S(2)}, u32[]{:S(2)}) collective-permute-start(bf16[4,136,128]{2,1,0:T(8,128)(2,1)S(1)} %get-tuple-element.105.mine_ref), channel_id=1, source_target_pairs={{0,2},{1,3},{2,0},{3,1},{4,6},{5,7},{6,4},{7,5},{8,10},{9,11},{10,... | collective-permute-start | bytes 417800 | tf_op jit(solution)/shard_map/ppermute | solution.py:351
  45.8 0.3 collective-permute-start.13
  46.1 5.2 %collective-permute-done.13.got_ref = bf16[2,136,128]{2,1,0:T(8,128)(2,1)S(1)} collective-permute-done((bf16[2,136,128]{2,1,0:T(8,128)(2,1)S(1)}, bf16[2,136,128]{2,1,0:T(8,128)(2,1)S(1)}, u32[]{:S(2)}, u32[]{:S(2)}) %collective-permute-start.13) | collective-permute-done | bytes 69664 | tf_op jit(solution)/shard_map/ppermute | solution.py:351
  51.3 2.9 %collective-permute-start.14 = (bf16[2,136,128]{2,1,0:T(8,128)(2,1)S(1)}, bf16[2,136,128]{2,1,0:T(8,128)(2,1)S(1)}, u32[]{:S(2)}, u32[]{:S(2)}) collective-permute-start(bf16[2,136,128]{2,1,0:T(8,128)(2,1)S(1)} %hop_p.4.p_ref), channel_id=1, source_target_pairs={{0,4},{1,5},{2,6},{3,7},{4,0},{5,1},{6,2},{7,3},{8,12},{9,13},{10,... | collective-permute-start | bytes 208904 | tf_op jit(solution)/shard_map/ppermute | solution.py:351
  54.4 2.3 %prep.3.x_ref = bf16[1024,1024]{1,0:T(8,128)(2,1)S(1)} custom-call(s32[1,3]{1,0:T(1,128)S(1)} %bitcast.7, s32[8,16]{1,0:T(8,128)S(1)} %copy-done.1, bf16[1024,2048]{1,0:T(8,128)(2,1)} %x_ref.3), custom_call_target="tpu_custom_call" | custom-call | bytes 4194304 | tf_op jit(solution)/shard_map/prep/pallas_call | solution.py:51
  56.7 1.1 %collective-permute-done.14.gp_ref = bf16[2,136,128]{2,1,0:T(8,128)(2,1)S(1)} collective-permute-done((bf16[2,136,128]{2,1,0:T(8,128)(2,1)S(1)}, bf16[2,136,128]{2,1,0:T(8,128)(2,1)S(1)}, u32[]{:S(2)}, u32[]{:S(2)}) %collective-permute-start.14) | collective-permute-done | bytes 69664 | tf_op jit(solution)/shard_map/ppermute | solution.py:351
  57.8 2.2 %collective-permute-done.16.gq_ref = bf16[2,136,128]{2,1,0:T(8,128)(2,1)S(1)} collective-permute-done((bf16[2,136,128]{2,1,0:T(8,128)(2,1)S(1)}, bf16[2,136,128]{2,1,0:T(8,128)(2,1)S(1)}, u32[]{:S(2)}, u32[]{:S(2)}) %collective-permute-start.16) | collective-permute-done | bytes 69664 | tf_op jit(solution)/shard_map/ppermute | solution.py:351
  60.3 0.4 mine.4.part_ref
  60.7 0.9 collective-permute-done.17.delta_ref
  61.6 0.5 change.4
  62.2 0.6 collective-permute-start.18
  62.8 1.1 %collective-permute-start.20 = (bf16[128,512]{1,0:T(8,128)(2,1)S(1)}, bf16[128,512]{1,0:T(8,128)(2,1)S(1)}, u32[]{:S(2)}, u32[]{:S(2)}) collective-permute-start(bf16[128,512]{1,0:T(8,128)(2,1)S(1)} %get-tuple-element.119.mine_ref), channel_id=1, source_target_pairs={{0,16},{1,17},{2,18},{3,19},{4,20},{5,21},{6,22},{7,23},{8,24},{9,... | collective-permute-start | bytes 393224 | tf_op jit(solution)/shard_map/ppermute | solution.py:351
  63.8 3.9 %collective-permute-done.18.got_ref = bf16[128,512]{1,0:T(8,128)(2,1)S(1)} collective-permute-done((bf16[128,512]{1,0:T(8,128)(2,1)S(1)}, bf16[128,512]{1,0:T(8,128)(2,1)S(1)}, u32[]{:S(2)}, u32[]{:S(2)}) %collective-permute-start.18) | collective-permute-done | bytes 131104 | tf_op jit(solution)/shard_map/ppermute | solution.py:351
  67.8 0.6 collective-permute-start.19
  68.5 1.2 %collective-permute-start.21 = (bf16[128,512]{1,0:T(8,128)(2,1)S(1)}, bf16[128,512]{1,0:T(8,128)(2,1)S(1)}, u32[]{:S(2)}, u32[]{:S(2)}) collective-permute-start(bf16[128,512]{1,0:T(8,128)(2,1)S(1)} %get-tuple-element.120.b_ref), channel_id=1, source_target_pairs={{0,8},{1,9},{2,10},{3,11},{4,12},{5,13},{6,14},{7,15},{8,0},{9,1},... | collective-permute-start | bytes 393224 | tf_op jit(solution)/shard_map/ppermute | solution.py:351
  69.6 3.2 %collective-permute-done.19.ra_ref = bf16[128,512]{1,0:T(8,128)(2,1)S(1)} collective-permute-done((bf16[128,512]{1,0:T(8,128)(2,1)S(1)}, bf16[128,512]{1,0:T(8,128)(2,1)S(1)}, u32[]{:S(2)}, u32[]{:S(2)}) %collective-permute-start.19) | collective-permute-done | bytes 131104 | tf_op jit(solution)/shard_map/ppermute | solution.py:351
  72.9 0.6 collective-permute-done.21.rb_ref
  73.5 0.8 soft_next.3
  74.4 0.5 own.5.own_ref
  74.9 1.0 collective-permute-done.22.got_ref
  76.0 1.4 %collective-permute-start.23 = (bf16[2,136,128]{2,1,0:T(8,128)(2,1)S(1)}, bf16[2,136,128]{2,1,0:T(8,128)(2,1)S(1)}, u32[]{:S(2)}, u32[]{:S(2)}) collective-permute-start(bf16[2,136,128]{2,1,0:T(8,128)(2,1)S(1)} %get-tuple-element.127.mine_ref), channel_id=1, source_target_pairs={{0,2},{1,3},{2,0},{3,1},{4,6},{5,7},{6,4},{7,5},{8,10},{9,11},{10,... | collective-permute-start | bytes 208904 | tf_op jit(solution)/shard_map/ppermute | solution.py:351
  77.4 0.7 collective-permute-start.25
  78.1 2.8 %collective-permute-done.23.got_ref = bf16[2,136,128]{2,1,0:T(8,128)(2,1)S(1)} collective-permute-done((bf16[2,136,128]{2,1,0:T(8,128)(2,1)S(1)}, bf16[2,136,128]{2,1,0:T(8,128)(2,1)S(1)}, u32[]{:S(2)}, u32[]{:S(2)}) %collective-permute-start.23) | collective-permute-done | bytes 69664 | tf_op jit(solution)/shard_map/ppermute | solution.py:351
  80.9 2.4 %collective-permute-start.24 = (bf16[2,136,128]{2,1,0:T(8,128)(2,1)S(1)}, bf16[2,136,128]{2,1,0:T(8,128)(2,1)S(1)}, u32[]{:S(2)}, u32[]{:S(2)}) collective-permute-start(bf16[2,136,128]{2,1,0:T(8,128)(2,1)S(1)} %hop_p.5.p_ref), channel_id=1, source_target_pairs={{0,4},{1,5},{2,6},{3,7},{4,0},{5,1},{6,2},{7,3},{8,12},{9,13},{10,... | collective-permute-start | bytes 208904 | tf_op jit(solution)/shard_map/ppermute | solution.py:351
  83.4 1.9 %collective-permute-start.26 = (bf16[2,136,128]{2,1,0:T(8,128)(2,1)S(1)}, bf16[2,136,128]{2,1,0:T(8,128)(2,1)S(1)}, u32[]{:S(2)}, u32[]{:S(2)}) collective-permute-start(bf16[2,136,128]{2,1,0:T(8,128)(2,1)S(1)} %hop_q.5.q_ref), channel_id=1, source_target_pairs={{0,4},{1,5},{2,6},{3,7},{4,0},{5,1},{6,2},{7,3},{8,12},{9,13},{10,... | collective-permute-start | bytes 208904 | tf_op jit(solution)/shard_map/ppermute | solution.py:351
  85.2 1.0 collective-permute-done.24.gp_ref
  86.2 3.0 %collective-permute-done.26.gq_ref = bf16[2,136,128]{2,1,0:T(8,128)(2,1)S(1)} collective-permute-done((bf16[2,136,128]{2,1,0:T(8,128)(2,1)S(1)}, bf16[2,136,128]{2,1,0:T(8,128)(2,1)S(1)}, u32[]{:S(2)}, u32[]{:S(2)}) %collective-permute-start.26) | collective-permute-done | bytes 69664 | tf_op jit(solution)/shard_map/ppermute | solution.py:351
  89.5 0.4 mine.5.part_ref
  89.9 0.9 collective-permute-done.27.delta_ref
  90.8 0.5 change.5
  91.3 1.2 %collective-permute-start.28 = (bf16[128,512]{1,0:T(8,128)(2,1)S(1)}, bf16[128,512]{1,0:T(8,128)(2,1)S(1)}, u32[]{:S(2)}, u32[]{:S(2)}) collective-permute-start(bf16[128,512]{1,0:T(8,128)(2,1)S(1)} %get-tuple-element.136.mine_ref), channel_id=1, source_target_pairs={{0,8},{1,9},{2,10},{3,11},{4,12},{5,13},{6,14},{7,15},{8,0},{9,1},... | collective-permute-start | bytes 393224 | tf_op jit(solution)/shard_map/ppermute | solution.py:351
  92.5 1.0 collective-permute-start.30
  93.4 3.5 %collective-permute-done.28.got_ref = bf16[128,512]{1,0:T(8,128)(2,1)S(1)} collective-permute-done((bf16[128,512]{1,0:T(8,128)(2,1)S(1)}, bf16[128,512]{1,0:T(8,128)(2,1)S(1)}, u32[]{:S(2)}, u32[]{:S(2)}) %collective-permute-start.28) | collective-permute-done | bytes 131104 | tf_op jit(solution)/shard_map/ppermute | solution.py:351
  97.0 1.6 %collective-permute-start.29 = (bf16[128,512]{1,0:T(8,128)(2,1)S(1)}, bf16[128,512]{1,0:T(8,128)(2,1)S(1)}, u32[]{:S(2)}, u32[]{:S(2)}) collective-permute-start(bf16[128,512]{1,0:T(8,128)(2,1)S(1)} %meet_a.5.a_ref), channel_id=1, source_target_pairs={{0,16},{1,17},{2,18},{3,19},{4,20},{5,21},{6,22},{7,23},{8,24},{9,... | collective-permute-start | bytes 393224 | tf_op jit(solution)/shard_map/ppermute | solution.py:351
  98.6 0.6 collective-permute-start.31
  99.2 0.6 coef_out.1
  99.9 0.7 copy.8
  100.5 1.5 %collective-permute-done.29.ra_ref = bf16[128,512]{1,0:T(8,128)(2,1)S(1)} collective-permute-done((bf16[128,512]{1,0:T(8,128)(2,1)S(1)}, bf16[128,512]{1,0:T(8,128)(2,1)S(1)}, u32[]{:S(2)}, u32[]{:S(2)}) %collective-permute-start.29) | collective-permute-done | bytes 131104 | tf_op jit(solution)/shard_map/ppermute | solution.py:351
  102.0 1.6 %collective-permute-done.31.rb_ref = bf16[128,512]{1,0:T(8,128)(2,1)S(1)} collective-permute-done((bf16[128,512]{1,0:T(8,128)(2,1)S(1)}, bf16[128,512]{1,0:T(8,128)(2,1)S(1)}, u32[]{:S(2)}, u32[]{:S(2)}) %collective-permute-start.31) | collective-permute-done | bytes 131104 | tf_op jit(solution)/shard_map/ppermute | solution.py:351
  103.6 1.0 last.1
  (43 shorter events, 1.8 us)
Async XLA Ops:
  3.7 6.2 %collective-permute-start = (f32[4,136,128]{2,1,0:T(8,128)S(1)}, f32[4,136,128]{2,1,0:T(8,128)S(1)}, u32[]{:S(2)}, u32[]{:S(2)}) collective-permute-start(f32[4,136,128]{2,1,0:T(8,128)S(1)} %get-tuple-element.75), channel_id=1, source_target_pairs={{0,1},{1,0},{2,3},{3,2},{4,5},{5,4},{6,7},{7,6},{8,9},{9,8},{10,11... | collective-permute-start | bytes 835592 | tf_op jit(solution)/shard_map/ppermute | solution.py:351
  4.2 5.6 %collective-permute-start.1 = (bf16[128,128]{1,0:T(8,128)(2,1)S(1)}, bf16[128,128]{1,0:T(8,128)(2,1)S(1)}, u32[]{:S(2)}, u32[]{:S(2)}) collective-permute-start(bf16[128,128]{1,0:T(8,128)(2,1)S(1)} %get-tuple-element.76.mine_ref), channel_id=1, source_target_pairs={{0,4},{1,5},{2,6},{3,7},{4,0},{5,1},{6,2},{7,3},{8,12},{9,13},{10,... | collective-permute-start | bytes 98312 | tf_op jit(solution)/shard_map/ppermute | solution.py:351
  7.8 12.4 %copy-start.1 = (s32[8,16]{1,0:T(8,128)S(1)}, s32[8,16]{1,0:T(8,128)}, u32[]{:S(2)}) copy-start(s32[8,16]{1,0:T(8,128)} %live_ref.3) | copy-start | bytes 1540
  7.8 12.4 %copy-start.2 = (s32[3,1]{0,1:T(1,128)S(1)}, s32[3,1]{0,1:T(1,128)}, u32[]{:S(2)}) copy-start(s32[3,1]{0,1:T(1,128)} %param.11) | copy-start | bytes 40
  9.9 10.3 %collective-permute-start.4 = (bf16[4,136,128]{2,1,0:T(8,128)(2,1)S(1)}, bf16[4,136,128]{2,1,0:T(8,128)(2,1)S(1)}, u32[]{:S(2)}, u32[]{:S(2)}) collective-permute-start(bf16[4,136,128]{2,1,0:T(8,128)(2,1)S(1)} %get-tuple-element.78.mine_ref), channel_id=1, source_target_pairs={{0,2},{1,3},{2,0},{3,1},{4,6},{5,7},{6,4},{7,5},{8,10},{9,11},{10,... | collective-permute-start | bytes 417800 | tf_op jit(solution)/shard_map/ppermute | solution.py:351
  11.7 5.1 %collective-permute-start.2 = (bf16[2,136,128]{2,1,0:T(8,128)(2,1)S(1)}, bf16[2,136,128]{2,1,0:T(8,128)(2,1)S(1)}, u32[]{:S(2)}, u32[]{:S(2)}) collective-permute-start(bf16[2,136,128]{2,1,0:T(8,128)(2,1)S(1)} %get-tuple-element.77.mine_ref), channel_id=1, source_target_pairs={{0,2},{1,3},{2,0},{3,1},{4,6},{5,7},{6,4},{7,5},{8,10},{9,11},{10,... | collective-permute-start | bytes 208904 | tf_op jit(solution)/shard_map/ppermute | solution.py:351
  16.9 5.8 %collective-permute-start.3 = (bf16[2,136,128]{2,1,0:T(8,128)(2,1)S(1)}, bf16[2,136,128]{2,1,0:T(8,128)(2,1)S(1)}, u32[]{:S(2)}, u32[]{:S(2)}) collective-permute-start(bf16[2,136,128]{2,1,0:T(8,128)(2,1)S(1)} %hop_p.3.p_ref), channel_id=1, source_target_pairs={{0,4},{1,5},{2,6},{3,7},{4,0},{5,1},{6,2},{7,3},{8,12},{9,13},{10,... | collective-permute-start | bytes 208904 | tf_op jit(solution)/shard_map/ppermute | solution.py:351
  20.1 5.6 %collective-permute-start.5 = (bf16[2,136,128]{2,1,0:T(8,128)(2,1)S(1)}, bf16[2,136,128]{2,1,0:T(8,128)(2,1)S(1)}, u32[]{:S(2)}, u32[]{:S(2)}) collective-permute-start(bf16[2,136,128]{2,1,0:T(8,128)(2,1)S(1)} %hop_q.3.q_ref), channel_id=1, source_target_pairs={{0,4},{1,5},{2,6},{3,7},{4,0},{5,1},{6,2},{7,3},{8,12},{9,13},{10,... | collective-permute-start | bytes 208904 | tf_op jit(solution)/shard_map/ppermute | solution.py:351
  25.9 1.4 %collective-permute-start.6 = (bf16[128,512]{1,0:T(8,128)(2,1)S(1)}, bf16[128,512]{1,0:T(8,128)(2,1)S(1)}, u32[]{:S(2)}, u32[]{:S(2)}) collective-permute-start(bf16[128,512]{1,0:T(8,128)(2,1)S(1)} %get-tuple-element.84.delta_ref), channel_id=1, source_target_pairs={{0,1},{1,0},{2,3},{3,2},{4,5},{5,4},{6,7},{7,6},{8,9},{9,8},{10,11... | collective-permute-start | bytes 393224 | tf_op jit(solution)/shard_map/ppermute | solution.py:351
  26.4 15.1 %copy-start = (s32[1024]{0:T(1024)S(1)}, s32[1024]{0:T(1024)}, u32[]{:S(2)}) copy-start(s32[1024]{0:T(1024)} %param.8) | copy-start | bytes 12292
  27.8 5.6 %collective-permute-start.7 = (bf16[128,512]{1,0:T(8,128)(2,1)S(1)}, bf16[128,512]{1,0:T(8,128)(2,1)S(1)}, u32[]{:S(2)}, u32[]{:S(2)}) collective-permute-start(bf16[128,512]{1,0:T(8,128)(2,1)S(1)} %get-tuple-element.88.mine_ref), channel_id=1, source_target_pairs={{0,8},{1,9},{2,10},{3,11},{4,12},{5,13},{6,14},{7,15},{8,0},{9,1},... | collective-permute-start | bytes 393224 | tf_op jit(solution)/shard_map/ppermute | solution.py:351
  29.4 5.7 %collective-permute-start.9 = (bf16[128,512]{1,0:T(8,128)(2,1)S(1)}, bf16[128,512]{1,0:T(8,128)(2,1)S(1)}, u32[]{:S(2)}, u32[]{:S(2)}) collective-permute-start(bf16[128,512]{1,0:T(8,128)(2,1)S(1)} %get-tuple-element.90.mine_ref), channel_id=1, source_target_pairs={{0,16},{1,17},{2,18},{3,19},{4,20},{5,21},{6,22},{7,23},{8,24},{9,... | collective-permute-start | bytes 393224 | tf_op jit(solution)/shard_map/ppermute | solution.py:351
  33.5 8.0 %collective-permute-start.8 = (bf16[128,512]{1,0:T(8,128)(2,1)S(1)}, bf16[128,512]{1,0:T(8,128)(2,1)S(1)}, u32[]{:S(2)}, u32[]{:S(2)}) collective-permute-start(bf16[128,512]{1,0:T(8,128)(2,1)S(1)} %get-tuple-element.93.a_ref), channel_id=1, source_target_pairs={{0,16},{1,17},{2,18},{3,19},{4,20},{5,21},{6,22},{7,23},{8,24},{9,... | collective-permute-start | bytes 393224 | tf_op jit(solution)/shard_map/ppermute | solution.py:351
  35.1 6.4 %collective-permute-start.10 = (bf16[128,512]{1,0:T(8,128)(2,1)S(1)}, bf16[128,512]{1,0:T(8,128)(2,1)S(1)}, u32[]{:S(2)}, u32[]{:S(2)}) collective-permute-start(bf16[128,512]{1,0:T(8,128)(2,1)S(1)} %get-tuple-element.95.b_ref), channel_id=1, source_target_pairs={{0,8},{1,9},{2,10},{3,11},{4,12},{5,13},{6,14},{7,15},{8,0},{9,1},... | collective-permute-start | bytes 393224 | tf_op jit(solution)/shard_map/ppermute | solution.py:351
  36.7 4.8 %collective-permute-start.11 = (bf16[128,128]{1,0:T(8,128)(2,1)S(1)}, bf16[128,128]{1,0:T(8,128)(2,1)S(1)}, u32[]{:S(2)}, u32[]{:S(2)}) collective-permute-start(bf16[128,128]{1,0:T(8,128)(2,1)S(1)} %get-tuple-element.92.mine_ref), channel_id=1, source_target_pairs={{0,4},{1,5},{2,6},{3,7},{4,0},{5,1},{6,2},{7,3},{8,12},{9,13},{10,... | collective-permute-start | bytes 98312 | tf_op jit(solution)/shard_map/ppermute | solution.py:351
  42.3 1.6 %collective-permute-start.12 = (f32[4,136,128]{2,1,0:T(8,128)S(1)}, f32[4,136,128]{2,1,0:T(8,128)S(1)}, u32[]{:S(2)}, u32[]{:S(2)}) collective-permute-start(f32[4,136,128]{2,1,0:T(8,128)S(1)} %get-tuple-element.102), channel_id=1, source_target_pairs={{0,1},{1,0},{2,3},{3,2},{4,5},{5,4},{6,7},{7,6},{8,9},{9,8},{10,11... | collective-permute-start | bytes 835592 | tf_op jit(solution)/shard_map/ppermute | solution.py:351
  44.0 10.3 %collective-permute-start.15 = (bf16[4,136,128]{2,1,0:T(8,128)(2,1)S(1)}, bf16[4,136,128]{2,1,0:T(8,128)(2,1)S(1)}, u32[]{:S(2)}, u32[]{:S(2)}) collective-permute-start(bf16[4,136,128]{2,1,0:T(8,128)(2,1)S(1)} %get-tuple-element.105.mine_ref), channel_id=1, source_target_pairs={{0,2},{1,3},{2,0},{3,1},{4,6},{5,7},{6,4},{7,5},{8,10},{9,11},{10,... | collective-permute-start | bytes 417800 | tf_op jit(solution)/shard_map/ppermute | solution.py:351
  45.8 5.5 %collective-permute-start.13 = (bf16[2,136,128]{2,1,0:T(8,128)(2,1)S(1)}, bf16[2,136,128]{2,1,0:T(8,128)(2,1)S(1)}, u32[]{:S(2)}, u32[]{:S(2)}) collective-permute-start(bf16[2,136,128]{2,1,0:T(8,128)(2,1)S(1)} %get-tuple-element.104.mine_ref), channel_id=1, source_target_pairs={{0,2},{1,3},{2,0},{3,1},{4,6},{5,7},{6,4},{7,5},{8,10},{9,11},{10,... | collective-permute-start | bytes 208904 | tf_op jit(solution)/shard_map/ppermute | solution.py:351
  51.3 6.5 %collective-permute-start.14 = (bf16[2,136,128]{2,1,0:T(8,128)(2,1)S(1)}, bf16[2,136,128]{2,1,0:T(8,128)(2,1)S(1)}, u32[]{:S(2)}, u32[]{:S(2)}) collective-permute-start(bf16[2,136,128]{2,1,0:T(8,128)(2,1)S(1)} %hop_p.4.p_ref), channel_id=1, source_target_pairs={{0,4},{1,5},{2,6},{3,7},{4,0},{5,1},{6,2},{7,3},{8,12},{9,13},{10,... | collective-permute-start | bytes 208904 | tf_op jit(solution)/shard_map/ppermute | solution.py:351
  54.3 5.8 %collective-permute-start.16 = (bf16[2,136,128]{2,1,0:T(8,128)(2,1)S(1)}, bf16[2,136,128]{2,1,0:T(8,128)(2,1)S(1)}, u32[]{:S(2)}, u32[]{:S(2)}) collective-permute-start(bf16[2,136,128]{2,1,0:T(8,128)(2,1)S(1)} %hop_q.4.q_ref), channel_id=1, source_target_pairs={{0,4},{1,5},{2,6},{3,7},{4,0},{5,1},{6,2},{7,3},{8,12},{9,13},{10,... | collective-permute-start | bytes 208904 | tf_op jit(solution)/shard_map/ppermute | solution.py:351
  60.2 1.4 %collective-permute-start.17 = (bf16[128,512]{1,0:T(8,128)(2,1)S(1)}, bf16[128,512]{1,0:T(8,128)(2,1)S(1)}, u32[]{:S(2)}, u32[]{:S(2)}) collective-permute-start(bf16[128,512]{1,0:T(8,128)(2,1)S(1)} %get-tuple-element.112.delta_ref), channel_id=1, source_target_pairs={{0,1},{1,0},{2,3},{3,2},{4,5},{5,4},{6,7},{7,6},{8,9},{9,8},{10,11... | collective-permute-start | bytes 393224 | tf_op jit(solution)/shard_map/ppermute | solution.py:351
  62.2 5.6 %collective-permute-start.18 = (bf16[128,512]{1,0:T(8,128)(2,1)S(1)}, bf16[128,512]{1,0:T(8,128)(2,1)S(1)}, u32[]{:S(2)}, u32[]{:S(2)}) collective-permute-start(bf16[128,512]{1,0:T(8,128)(2,1)S(1)} %get-tuple-element.117.mine_ref), channel_id=1, source_target_pairs={{0,8},{1,9},{2,10},{3,11},{4,12},{5,13},{6,14},{7,15},{8,0},{9,1},... | collective-permute-start | bytes 393224 | tf_op jit(solution)/shard_map/ppermute | solution.py:351
  62.8 5.7 %collective-permute-start.20 = (bf16[128,512]{1,0:T(8,128)(2,1)S(1)}, bf16[128,512]{1,0:T(8,128)(2,1)S(1)}, u32[]{:S(2)}, u32[]{:S(2)}) collective-permute-start(bf16[128,512]{1,0:T(8,128)(2,1)S(1)} %get-tuple-element.119.mine_ref), channel_id=1, source_target_pairs={{0,16},{1,17},{2,18},{3,19},{4,20},{5,21},{6,22},{7,23},{8,24},{9,... | collective-permute-start | bytes 393224 | tf_op jit(solution)/shard_map/ppermute | solution.py:351
  67.8 5.0 %collective-permute-start.19 = (bf16[128,512]{1,0:T(8,128)(2,1)S(1)}, bf16[128,512]{1,0:T(8,128)(2,1)S(1)}, u32[]{:S(2)}, u32[]{:S(2)}) collective-permute-start(bf16[128,512]{1,0:T(8,128)(2,1)S(1)} %get-tuple-element.118.a_ref), channel_id=1, source_target_pairs={{0,16},{1,17},{2,18},{3,19},{4,20},{5,21},{6,22},{7,23},{8,24},{9,... | collective-permute-start | bytes 393224 | tf_op jit(solution)/shard_map/ppermute | solution.py:351
  68.5 5.0 %collective-permute-start.21 = (bf16[128,512]{1,0:T(8,128)(2,1)S(1)}, bf16[128,512]{1,0:T(8,128)(2,1)S(1)}, u32[]{:S(2)}, u32[]{:S(2)}) collective-permute-start(bf16[128,512]{1,0:T(8,128)(2,1)S(1)} %get-tuple-element.120.b_ref), channel_id=1, source_target_pairs={{0,8},{1,9},{2,10},{3,11},{4,12},{5,13},{6,14},{7,15},{8,0},{9,1},... | collective-permute-start | bytes 393224 | tf_op jit(solution)/shard_map/ppermute | solution.py:351
  74.3 1.6 %collective-permute-start.22 = (f32[4,136,128]{2,1,0:T(8,128)S(1)}, f32[4,136,128]{2,1,0:T(8,128)S(1)}, u32[]{:S(2)}, u32[]{:S(2)}) collective-permute-start(f32[4,136,128]{2,1,0:T(8,128)S(1)} %get-tuple-element.126), channel_id=1, source_target_pairs={{0,1},{1,0},{2,3},{3,2},{4,5},{5,4},{6,7},{7,6},{8,9},{9,8},{10,11... | collective-permute-start | bytes 835592 | tf_op jit(solution)/shard_map/ppermute | solution.py:351
  76.0 4.9 %collective-permute-start.23 = (bf16[2,136,128]{2,1,0:T(8,128)(2,1)S(1)}, bf16[2,136,128]{2,1,0:T(8,128)(2,1)S(1)}, u32[]{:S(2)}, u32[]{:S(2)}) collective-permute-start(bf16[2,136,128]{2,1,0:T(8,128)(2,1)S(1)} %get-tuple-element.127.mine_ref), channel_id=1, source_target_pairs={{0,2},{1,3},{2,0},{3,1},{4,6},{5,7},{6,4},{7,5},{8,10},{9,11},{10,... | collective-permute-start | bytes 208904 | tf_op jit(solution)/shard_map/ppermute | solution.py:351
  77.4 6.0 %collective-permute-start.25 = (bf16[2,136,128]{2,1,0:T(8,128)(2,1)S(1)}, bf16[2,136,128]{2,1,0:T(8,128)(2,1)S(1)}, u32[]{:S(2)}, u32[]{:S(2)}) collective-permute-start(bf16[2,136,128]{2,1,0:T(8,128)(2,1)S(1)} %get-tuple-element.128.mine_ref), channel_id=1, source_target_pairs={{0,2},{1,3},{2,0},{3,1},{4,6},{5,7},{6,4},{7,5},{8,10},{9,11},{10,... | collective-permute-start | bytes 208904 | tf_op jit(solution)/shard_map/ppermute | solution.py:351
  80.9 5.3 %collective-permute-start.24 = (bf16[2,136,128]{2,1,0:T(8,128)(2,1)S(1)}, bf16[2,136,128]{2,1,0:T(8,128)(2,1)S(1)}, u32[]{:S(2)}, u32[]{:S(2)}) collective-permute-start(bf16[2,136,128]{2,1,0:T(8,128)(2,1)S(1)} %hop_p.5.p_ref), channel_id=1, source_target_pairs={{0,4},{1,5},{2,6},{3,7},{4,0},{5,1},{6,2},{7,3},{8,12},{9,13},{10,... | collective-permute-start | bytes 208904 | tf_op jit(solution)/shard_map/ppermute | solution.py:351
  83.4 5.8 %collective-permute-start.26 = (bf16[2,136,128]{2,1,0:T(8,128)(2,1)S(1)}, bf16[2,136,128]{2,1,0:T(8,128)(2,1)S(1)}, u32[]{:S(2)}, u32[]{:S(2)}) collective-permute-start(bf16[2,136,128]{2,1,0:T(8,128)(2,1)S(1)} %hop_q.5.q_ref), channel_id=1, source_target_pairs={{0,4},{1,5},{2,6},{3,7},{4,0},{5,1},{6,2},{7,3},{8,12},{9,13},{10,... | collective-permute-start | bytes 208904 | tf_op jit(solution)/shard_map/ppermute | solution.py:351
  89.4 1.4 %collective-permute-start.27 = (bf16[128,512]{1,0:T(8,128)(2,1)S(1)}, bf16[128,512]{1,0:T(8,128)(2,1)S(1)}, u32[]{:S(2)}, u32[]{:S(2)}) collective-permute-start(bf16[128,512]{1,0:T(8,128)(2,1)S(1)} %get-tuple-element.131.delta_ref), channel_id=1, source_target_pairs={{0,1},{1,0},{2,3},{3,2},{4,5},{5,4},{6,7},{7,6},{8,9},{9,8},{10,11... | collective-permute-start | bytes 393224 | tf_op jit(solution)/shard_map/ppermute | solution.py:351
  91.3 5.6 %collective-permute-start.28 = (bf16[128,512]{1,0:T(8,128)(2,1)S(1)}, bf16[128,512]{1,0:T(8,128)(2,1)S(1)}, u32[]{:S(2)}, u32[]{:S(2)}) collective-permute-start(bf16[128,512]{1,0:T(8,128)(2,1)S(1)} %get-tuple-element.136.mine_ref), channel_id=1, source_target_pairs={{0,8},{1,9},{2,10},{3,11},{4,12},{5,13},{6,14},{7,15},{8,0},{9,1},... | collective-permute-start | bytes 393224 | tf_op jit(solution)/shard_map/ppermute | solution.py:351
  92.5 6.1 %collective-permute-start.30 = (bf16[128,512]{1,0:T(8,128)(2,1)S(1)}, bf16[128,512]{1,0:T(8,128)(2,1)S(1)}, u32[]{:S(2)}, u32[]{:S(2)}) collective-permute-start(bf16[128,512]{1,0:T(8,128)(2,1)S(1)} %get-tuple-element.137.mine_ref), channel_id=1, source_target_pairs={{0,16},{1,17},{2,18},{3,19},{4,20},{5,21},{6,22},{7,23},{8,24},{9,... | collective-permute-start | bytes 393224 | tf_op jit(solution)/shard_map/ppermute | solution.py:351
  97.0 5.0 %collective-permute-start.29 = (bf16[128,512]{1,0:T(8,128)(2,1)S(1)}, bf16[128,512]{1,0:T(8,128)(2,1)S(1)}, u32[]{:S(2)}, u32[]{:S(2)}) collective-permute-start(bf16[128,512]{1,0:T(8,128)(2,1)S(1)} %meet_a.5.a_ref), channel_id=1, source_target_pairs={{0,16},{1,17},{2,18},{3,19},{4,20},{5,21},{6,22},{7,23},{8,24},{9,... | collective-permute-start | bytes 393224 | tf_op jit(solution)/shard_map/ppermute | solution.py:351
  98.6 5.0 %collective-permute-start.31 = (bf16[128,512]{1,0:T(8,128)(2,1)S(1)}, bf16[128,512]{1,0:T(8,128)(2,1)S(1)}, u32[]{:S(2)}, u32[]{:S(2)}) collective-permute-start(bf16[128,512]{1,0:T(8,128)(2,1)S(1)} %meet_b.5.b_ref), channel_id=1, source_target_pairs={{0,8},{1,9},{2,10},{3,11},{4,12},{5,13},{6,14},{7,15},{8,0},{9,1},... | collective-permute-start | bytes 393224 | tf_op jit(solution)/shard_map/ppermute | solution.py:351

commit v7 on v6

--- a/solution.py
+++ b/solution.py
@@ -241,13 +241,6 @@
         encode(k % PB, total[0:C], total[C : C + 1], p_ref if k < PB else q_ref)
 
 
-def pair_with_body(own_ref, got_ref, mine_ref, far_ref, p_ref, q_ref):
-    pair_body(own_ref, got_ref, p_ref, q_ref)
-    for k, rows_ref in ((PB, mine_ref), (PB + 1, far_ref)):
-        q_ref[k, 0:C, :] = rows_ref[...]
-        q_ref[k, C:ROWS, :] = jnp.zeros((ROWS - C, TILE), BF16)
-
-
 def decode_sum(k, mine_ref, got_ref):
     total = mine_ref[k].astype(F32) + got_ref[k].astype(F32)
     return total[0:C], total[C : C + 1] + total[C + 1 : C + 2]
@@ -258,12 +251,12 @@
         encode(k, *decode_sum(k, mine_ref, got_ref), out_ref)
 
 
-def place_body(got_ref, far_ref, coef_ref, out_ref):
+def place_body(far_ref, near_ref, coef_ref, out_ref):
     place = lax.axis_index("ex") // 2
     out_ref[place] = coef_ref[...]
-    out_ref[jnp.bitwise_xor(place, 1)] = got_ref[PB, 0:C, :].astype(F32)
     out_ref[jnp.bitwise_xor(place, 2)] = far_ref[...].astype(F32)
-    out_ref[jnp.bitwise_xor(place, 3)] = got_ref[PB + 1, 0:C, :].astype(F32)
+    out_ref[jnp.bitwise_xor(place, 1)] = near_ref[0].astype(F32)
+    out_ref[jnp.bitwise_xor(place, 3)] = near_ref[1].astype(F32)
 
 
 def step_coef(count, k, mine_ref, got_ref, old):
@@ -415,8 +408,7 @@
     own_shape, send_shape, same_shape = sds((C, TILE), F32), sds((C, TILE), BF16), sds((8, TILE), F32)
     flops, nbytes = 2 * rows * HALF * C, 1 << 20
 
-    def message(n):
-        return sds((PB + n, ROWS, TILE), BF16)
+    message = sds((PB, ROWS, TILE), BF16)
 
     if aligned:
         x, score, res_t, spread, g_other, *rest = call(
@@ -433,8 +425,6 @@
             ] + block_scratch(rows),
         )(order, tile_live, margins, labels, coef, x_values)
         blocks, sends, same = rest[:2], rest[2:4], rest[4:]
-        across = lambda rows: swap(rows, lambda f, e: (f, e ^ z_bits[-1]))
-        fars = [across(sends[0]), None]
     else:
         x = prep_general(x_values, tile_live, order[0, 0], core, own)
         score, res_t, spread, g_other = call(
@@ -454,23 +444,23 @@
             )(score, *halves, labels, x)
         got = swap_core(g_other)
         g_own = call(own_body, g_shape, vmem(3), "own", flops, nbytes)(res_t, spread, x)
+        p, q = call(pair_body, (message, message), vmem(2), "pair")(g_own, got)
         carry = aligned and step < 2
         if carry:
-            p, q = call(pair_with_body, (message(0), message(2)), vmem(4), "pair")(
-                g_own, got, sends[step], fars[step]
-            )
-        else:
-            p, q = call(pair_body, (message(0), message(0)), vmem(2), "pair")(g_own, got)
+            p, q, send = lax.optimization_barrier((p, q, sends[step]))
         for n, bit in enumerate(z_bits):
             got_p = swap(p, lambda f, e, bit=bit: (f, e ^ bit))
             got_q = swap(q, lambda f, e, bit=bit: (f, e ^ bit))
-            if n == 0 and carry:
-                old = call(place_body, old_shape, vmem(3), "place")(got_q, fars[step], blocks[step])
-            elif n == 0 and step < 2:
-                old = blocks[step]
             if n < len(z_bits) - 1:
-                p = call(hop_body, message(0), vmem(2), "hop_p")(p, got_p)
-                q = call(hop_body, message(0), vmem(2), "hop_q")(q, got_q)
+                if carry:
+                    far = swap(send, lambda f, e: (f, e ^ z_bits[1]))
+                p = call(hop_body, message, vmem(2), "hop_p")(p, got_p)
+                q = call(hop_body, message, vmem(2), "hop_q")(q, got_q)
+        if carry:
+            near = swap(jnp.stack([send, far]), lambda f, e: (f, e ^ z_bits[0]))
+            old = call(place_body, old_shape, vmem(3), "place")(far, near, blocks[step])
+        elif step < 2:
+            old = blocks[step]
         sums = (p, got_p, q, got_q)
         if step < STEPS - 1 and aligned:
             following = prep(order, tile_live, x_values, step + 1)
@@ -492,12 +482,7 @@
         a, b, *kept = call(
             functools.partial(change_body, len(errors)), shapes, vmem(3 + len(errors)), "change", flops, nbytes,
         )(x, part, got, *errors)
-        if step == 0 and aligned:
-            a, b, send = lax.optimization_barrier((a, b, sends[1]))
-            fars[1] = across(send)
         halves, errors = sum_over_feat(a, b, last)
-        if step == 0 and aligned:
-            *halves, fars[1] = lax.optimization_barrier((*halves, fars[1]))
         errors = kept + errors
     score = call(last_body, jax.ShapeDtypeStruct((rows, C), F32), vmem(5), "last")(score, *halves)
     if aligned:

time: 105 us -> 96.9 us (0.923)
  waiting for transfers between devices: 51.1 us -> 36.1 us
  starting transfers between devices: 35.7 us -> 42.7 us
    ppermute x32 -> x34, waiting for transfers between devices: 51.1 us -> 36.1 us  [swap(): return lax.ppermute(x, ('feat', 'ex'), pairs)]
    ppermute x32 -> x34, starting transfers between devices: 35.7 us -> 42.7 us  [swap(): return lax.ppermute(x, ('feat', 'ex'), pairs)]
  transfers between devices with their start and end apart: 32 -> 34, of which waited for: 23 -> 21; matrix products, arithmetic and copies ran while one was open for 1% -> 1% of each run, Pallas kernels for 8% -> 9%
where the time goes in v7:
time: 96.9 us; the launch traced here: 96.7 us
  starting transfers between devices  42.7 us (44%)
  waiting for transfers between devices  36.1 us (37%)
  Pallas kernels  16.2 us (17%)
    ppermute x34, starting transfers between devices, swap(): return lax.ppermute(x, ('feat', 'ex'), pairs)  42.7 us
    ppermute x34, waiting for transfers between devices, swap(): return lax.ppermute(x, ('feat', 'ex'), pairs)  36.1 us
    pallas_call x36, Pallas kernels, run(): f(*(x if spec.memory_space == pltpu.SMEM else pltpu.with_memory_space_con...  16.2 us
  transfers between devices with their start and end apart: 34, of which 21 were waited for; matrix products, arithmetic and copies ran while one was open for 1% of the time, Pallas kernels for 9%

profile of v7, /device:TPU:0, one launch (start us, length us, event | category | flops | bytes accessed | tf_op | source)
XLA Modules:
  0.0 96.7 jit_solution(9989039389202655460)
XLA Ops:
  0.6 3.0 %soft_first.1 = (bf16[1024,1024]{1,0:T(8,128)(2,1)S(1)}, f32[128,1024]{1,0:T(8,128)S(1)}, bf16[128,1024]{1,0:T(8,128)(2,1)S(1)}, f32[1024,128]{1,0:T(8,128)S(1)}...) custom-call(s32[1,3]{1,0:T(1,128)} %bitcast.13, ...), custom_call_target="tpu_custom_call" | custom-call | flops 134217728 | bytes 1048576 | tf_op jit(solution)/shard_map/soft_first/pallas_call | solution.py:51
  3.7 0.5 collective-permute-start
  4.2 0.6 own.3.own_ref
  4.7 0.6 collective-permute-done.got_ref
  5.4 3.0 %collective-permute-start.1 = (bf16[2,136,128]{2,1,0:T(8,128)(2,1)S(1)}, bf16[2,136,128]{2,1,0:T(8,128)(2,1)S(1)}, u32[]{:S(2)}, u32[]{:S(2)}) collective-permute-start(bf16[2,136,128]{2,1,0:T(8,128)(2,1)S(1)} %get-tuple-element.77.mine_ref), channel_id=1, source_target_pairs={{0,2},{1,3},{2,0},{3,1},{4,6},{5,7},{6,4},{7,5},{8,10},{9,11},{10,... | collective-permute-start | bytes 208904 | tf_op jit(solution)/shard_map/ppermute | solution.py:344
  8.5 3.0 %collective-permute-start.5 = (bf16[128,128]{1,0:T(8,128)(2,1)S(1)}, bf16[128,128]{1,0:T(8,128)(2,1)S(1)}, u32[]{:S(2)}, u32[]{:S(2)}) collective-permute-start(bf16[128,128]{1,0:T(8,128)(2,1)S(1)} %get-tuple-element.83), channel_id=1, source_target_pairs={{0,4},{1,5},{2,6},{3,7},{4,0},{5,1},{6,2},{7,3},{8,12},{9,13},{10,... | collective-permute-start | bytes 98312 | tf_op jit(solution)/shard_map/ppermute | solution.py:344
  11.5 2.7 %collective-permute-start.2 = (bf16[2,136,128]{2,1,0:T(8,128)(2,1)S(1)}, bf16[2,136,128]{2,1,0:T(8,128)(2,1)S(1)}, u32[]{:S(2)}, u32[]{:S(2)}) collective-permute-start(bf16[2,136,128]{2,1,0:T(8,128)(2,1)S(1)} %hop_p.3.p_ref), channel_id=1, source_target_pairs={{0,4},{1,5},{2,6},{3,7},{4,0},{5,1},{6,2},{7,3},{8,12},{9,13},{10,... | collective-permute-start | bytes 208904 | tf_op jit(solution)/shard_map/ppermute | solution.py:344
  14.2 1.5 %collective-permute-start.4 = (bf16[2,136,128]{2,1,0:T(8,128)(2,1)S(1)}, bf16[2,136,128]{2,1,0:T(8,128)(2,1)S(1)}, u32[]{:S(2)}, u32[]{:S(2)}) collective-permute-start(bf16[2,136,128]{2,1,0:T(8,128)(2,1)S(1)} %hop_q.3.q_ref), channel_id=1, source_target_pairs={{0,4},{1,5},{2,6},{3,7},{4,0},{5,1},{6,2},{7,3},{8,12},{9,13},{10,... | collective-permute-start | bytes 208904 | tf_op jit(solution)/shard_map/ppermute | solution.py:344
  15.7 1.6 %collective-permute-start.6 = (bf16[2,128,128]{2,1,0:T(8,128)(2,1)S(1)}, bf16[2,128,128]{2,1,0:T(8,128)(2,1)S(1)}, u32[]{:S(2)}, u32[]{:S(2)}) collective-permute-start(bf16[2,128,128]{2,1,0:T(8,128)(2,1)S(1)} %pad_maximum_fusion), channel_id=1, source_target_pairs={{0,2},{1,3},{2,0},{3,1},{4,6},{5,7},{6,4},{7,5},{8,10},{9,11},{10,... | collective-permute-start | bytes 196616 | tf_op jit(solution)/shard_map/ppermute | solution.py:344
  17.2 2.3 %prep.2.x_ref = bf16[1024,1024]{1,0:T(8,128)(2,1)S(1)} custom-call(s32[1,3]{1,0:T(1,128)S(1)} %bitcast.14, s32[8,16]{1,0:T(8,128)S(1)} %copy-done.1, bf16[1024,2048]{1,0:T(8,128)(2,1)} %x_ref.3), custom_call_target="tpu_custom_call" | custom-call | bytes 4194304 | tf_op jit(solution)/shard_map/prep/pallas_call | solution.py:51
  19.5 1.2 %collective-permute-done.6.near_ref = bf16[2,128,128]{2,1,0:T(8,128)(2,1)S(1)} collective-permute-done((bf16[2,128,128]{2,1,0:T(8,128)(2,1)S(1)}, bf16[2,128,128]{2,1,0:T(8,128)(2,1)S(1)}, u32[]{:S(2)}, u32[]{:S(2)}) %collective-permute-start.6) | collective-permute-done | bytes 65568 | tf_op jit(solution)/shard_map/ppermute | solution.py:344
  20.9 0.4 mine.3.part_ref
  21.4 0.9 collective-permute-done.7.delta_ref
  22.3 0.5 change.3
  22.8 1.6 %collective-permute-start.8 = (bf16[128,512]{1,0:T(8,128)(2,1)S(1)}, bf16[128,512]{1,0:T(8,128)(2,1)S(1)}, u32[]{:S(2)}, u32[]{:S(2)}) collective-permute-start(bf16[128,512]{1,0:T(8,128)(2,1)S(1)} %get-tuple-element.86.mine_ref), channel_id=1, source_target_pairs={{0,8},{1,9},{2,10},{3,11},{4,12},{5,13},{6,14},{7,15},{8,0},{9,1},... | collective-permute-start | bytes 393224 | tf_op jit(solution)/shard_map/ppermute | solution.py:344
  24.3 1.5 %collective-permute-start.10 = (bf16[128,512]{1,0:T(8,128)(2,1)S(1)}, bf16[128,512]{1,0:T(8,128)(2,1)S(1)}, u32[]{:S(2)}, u32[]{:S(2)}) collective-permute-start(bf16[128,512]{1,0:T(8,128)(2,1)S(1)} %get-tuple-element.88.mine_ref), channel_id=1, source_target_pairs={{0,16},{1,17},{2,18},{3,19},{4,20},{5,21},{6,22},{7,23},{8,24},{9,... | collective-permute-start | bytes 393224 | tf_op jit(solution)/shard_map/ppermute | solution.py:344
  25.9 2.5 %collective-permute-done.8.got_ref = bf16[128,512]{1,0:T(8,128)(2,1)S(1)} collective-permute-done((bf16[128,512]{1,0:T(8,128)(2,1)S(1)}, bf16[128,512]{1,0:T(8,128)(2,1)S(1)}, u32[]{:S(2)}, u32[]{:S(2)}) %collective-permute-start.8) | collective-permute-done | bytes 131104 | tf_op jit(solution)/shard_map/ppermute | solution.py:344
  28.5 1.6 %collective-permute-start.9 = (bf16[128,512]{1,0:T(8,128)(2,1)S(1)}, bf16[128,512]{1,0:T(8,128)(2,1)S(1)}, u32[]{:S(2)}, u32[]{:S(2)}) collective-permute-start(bf16[128,512]{1,0:T(8,128)(2,1)S(1)} %get-tuple-element.87.a_ref), channel_id=1, source_target_pairs={{0,16},{1,17},{2,18},{3,19},{4,20},{5,21},{6,22},{7,23},{8,24},{9,... | collective-permute-start | bytes 393224 | tf_op jit(solution)/shard_map/ppermute | solution.py:344
  30.1 1.6 %collective-permute-start.11 = (bf16[128,512]{1,0:T(8,128)(2,1)S(1)}, bf16[128,512]{1,0:T(8,128)(2,1)S(1)}, u32[]{:S(2)}, u32[]{:S(2)}) collective-permute-start(bf16[128,512]{1,0:T(8,128)(2,1)S(1)} %get-tuple-element.89.b_ref), channel_id=1, source_target_pairs={{0,8},{1,9},{2,10},{3,11},{4,12},{5,13},{6,14},{7,15},{8,0},{9,1},... | collective-permute-start | bytes 393224 | tf_op jit(solution)/shard_map/ppermute | solution.py:344
  31.7 1.8 %collective-permute-done.9.ra_ref = bf16[128,512]{1,0:T(8,128)(2,1)S(1)} collective-permute-done((bf16[128,512]{1,0:T(8,128)(2,1)S(1)}, bf16[128,512]{1,0:T(8,128)(2,1)S(1)}, u32[]{:S(2)}, u32[]{:S(2)}) %collective-permute-start.9) | collective-permute-done | bytes 131104 | tf_op jit(solution)/shard_map/ppermute | solution.py:344
  33.5 1.7 %collective-permute-done.11.rb_ref = bf16[128,512]{1,0:T(8,128)(2,1)S(1)} collective-permute-done((bf16[128,512]{1,0:T(8,128)(2,1)S(1)}, bf16[128,512]{1,0:T(8,128)(2,1)S(1)}, u32[]{:S(2)}, u32[]{:S(2)}) %collective-permute-start.11) | collective-permute-done | bytes 131104 | tf_op jit(solution)/shard_map/ppermute | solution.py:344
  35.2 0.8 soft_next.2
  36.0 0.5 own.4.own_ref
  36.6 1.0 %collective-permute-done.12.got_ref = f32[4,136,128]{2,1,0:T(8,128)S(1)} collective-permute-done((f32[4,136,128]{2,1,0:T(8,128)S(1)}, f32[4,136,128]{2,1,0:T(8,128)S(1)}, u32[]{:S(2)}, u32[]{:S(2)}) %collective-permute-start.12) | collective-permute-done | bytes 278560 | tf_op jit(solution)/shard_map/ppermute | solution.py:344
  37.6 0.9 collective-permute-start.13
  38.5 1.2 %collective-permute-start.15 = (bf16[2,136,128]{2,1,0:T(8,128)(2,1)S(1)}, bf16[2,136,128]{2,1,0:T(8,128)(2,1)S(1)}, u32[]{:S(2)}, u32[]{:S(2)}) collective-permute-start(bf16[2,136,128]{2,1,0:T(8,128)(2,1)S(1)} %get-tuple-element.100.mine_ref), channel_id=1, source_target_pairs={{0,2},{1,3},{2,0},{3,1},{4,6},{5,7},{6,4},{7,5},{8,10},{9,11},{10,... | collective-permute-start | bytes 208904 | tf_op jit(solution)/shard_map/ppermute | solution.py:344
  39.7 2.1 %collective-permute-start.17 = (bf16[128,128]{1,0:T(8,128)(2,1)S(1)}, bf16[128,128]{1,0:T(8,128)(2,1)S(1)}, u32[]{:S(2)}, u32[]{:S(2)}) collective-permute-start(bf16[128,128]{1,0:T(8,128)(2,1)S(1)} %get-tuple-element.106), channel_id=1, source_target_pairs={{0,4},{1,5},{2,6},{3,7},{4,0},{5,1},{6,2},{7,3},{8,12},{9,13},{10,... | collective-permute-start | bytes 98312 | tf_op jit(solution)/shard_map/ppermute | solution.py:344
  41.8 0.8 collective-permute-done.13.got_ref
  42.7 1.7 %collective-permute-start.14 = (bf16[2,136,128]{2,1,0:T(8,128)(2,1)S(1)}, bf16[2,136,128]{2,1,0:T(8,128)(2,1)S(1)}, u32[]{:S(2)}, u32[]{:S(2)}) collective-permute-start(bf16[2,136,128]{2,1,0:T(8,128)(2,1)S(1)} %hop_p.4.p_ref), channel_id=1, source_target_pairs={{0,4},{1,5},{2,6},{3,7},{4,0},{5,1},{6,2},{7,3},{8,12},{9,13},{10,... | collective-permute-start | bytes 208904 | tf_op jit(solution)/shard_map/ppermute | solution.py:344
  44.4 1.8 %collective-permute-start.16 = (bf16[2,136,128]{2,1,0:T(8,128)(2,1)S(1)}, bf16[2,136,128]{2,1,0:T(8,128)(2,1)S(1)}, u32[]{:S(2)}, u32[]{:S(2)}) collective-permute-start(bf16[2,136,128]{2,1,0:T(8,128)(2,1)S(1)} %hop_q.4.q_ref), channel_id=1, source_target_pairs={{0,4},{1,5},{2,6},{3,7},{4,0},{5,1},{6,2},{7,3},{8,12},{9,13},{10,... | collective-permute-start | bytes 208904 | tf_op jit(solution)/shard_map/ppermute | solution.py:344
  46.2 1.8 %collective-permute-start.18 = (bf16[2,128,128]{2,1,0:T(8,128)(2,1)S(1)}, bf16[2,128,128]{2,1,0:T(8,128)(2,1)S(1)}, u32[]{:S(2)}, u32[]{:S(2)}) collective-permute-start(bf16[2,128,128]{2,1,0:T(8,128)(2,1)S(1)} %pad_maximum_fusion.1), channel_id=1, source_target_pairs={{0,2},{1,3},{2,0},{3,1},{4,6},{5,7},{6,4},{7,5},{8,10},{9,11},{10,... | collective-permute-start | bytes 196616 | tf_op jit(solution)/shard_map/ppermute | solution.py:344
  48.0 2.3 %prep.3.x_ref = bf16[1024,1024]{1,0:T(8,128)(2,1)S(1)} custom-call(s32[1,3]{1,0:T(1,128)S(1)} %bitcast.15, s32[8,16]{1,0:T(8,128)S(1)} %copy-done.1, bf16[1024,2048]{1,0:T(8,128)(2,1)} %x_ref.3), custom_call_target="tpu_custom_call" | custom-call | bytes 4194304 | tf_op jit(solution)/shard_map/prep/pallas_call | solution.py:51
  50.2 1.4 %collective-permute-done.18.near_ref = bf16[2,128,128]{2,1,0:T(8,128)(2,1)S(1)} collective-permute-done((bf16[2,128,128]{2,1,0:T(8,128)(2,1)S(1)}, bf16[2,128,128]{2,1,0:T(8,128)(2,1)S(1)}, u32[]{:S(2)}, u32[]{:S(2)}) %collective-permute-start.18) | collective-permute-done | bytes 65568 | tf_op jit(solution)/shard_map/ppermute | solution.py:344
  52.3 0.9 collective-permute-done.19.delta_ref
  53.3 0.5 change.4
  53.8 1.6 %collective-permute-start.20 = (bf16[128,512]{1,0:T(8,128)(2,1)S(1)}, bf16[128,512]{1,0:T(8,128)(2,1)S(1)}, u32[]{:S(2)}, u32[]{:S(2)}) collective-permute-start(bf16[128,512]{1,0:T(8,128)(2,1)S(1)} %get-tuple-element.113.mine_ref), channel_id=1, source_target_pairs={{0,8},{1,9},{2,10},{3,11},{4,12},{5,13},{6,14},{7,15},{8,0},{9,1},... | collective-permute-start | bytes 393224 | tf_op jit(solution)/shard_map/ppermute | solution.py:344
  55.3 0.5 collective-permute-start.22
  55.8 3.6 %collective-permute-done.20.got_ref = bf16[128,512]{1,0:T(8,128)(2,1)S(1)} collective-permute-done((bf16[128,512]{1,0:T(8,128)(2,1)S(1)}, bf16[128,512]{1,0:T(8,128)(2,1)S(1)}, u32[]{:S(2)}, u32[]{:S(2)}) %collective-permute-start.20) | collective-permute-done | bytes 131104 | tf_op jit(solution)/shard_map/ppermute | solution.py:344
  59.5 1.1 %collective-permute-start.21 = (bf16[128,512]{1,0:T(8,128)(2,1)S(1)}, bf16[128,512]{1,0:T(8,128)(2,1)S(1)}, u32[]{:S(2)}, u32[]{:S(2)}) collective-permute-start(bf16[128,512]{1,0:T(8,128)(2,1)S(1)} %get-tuple-element.114.a_ref), channel_id=1, source_target_pairs={{0,16},{1,17},{2,18},{3,19},{4,20},{5,21},{6,22},{7,23},{8,24},{9,... | collective-permute-start | bytes 393224 | tf_op jit(solution)/shard_map/ppermute | solution.py:344
  60.7 1.0 %collective-permute-start.23 = (bf16[128,512]{1,0:T(8,128)(2,1)S(1)}, bf16[128,512]{1,0:T(8,128)(2,1)S(1)}, u32[]{:S(2)}, u32[]{:S(2)}) collective-permute-start(bf16[128,512]{1,0:T(8,128)(2,1)S(1)} %get-tuple-element.116.b_ref), channel_id=1, source_target_pairs={{0,8},{1,9},{2,10},{3,11},{4,12},{5,13},{6,14},{7,15},{8,0},{9,1},... | collective-permute-start | bytes 393224 | tf_op jit(solution)/shard_map/ppermute | solution.py:344
  61.7 2.8 %collective-permute-done.21.ra_ref = bf16[128,512]{1,0:T(8,128)(2,1)S(1)} collective-permute-done((bf16[128,512]{1,0:T(8,128)(2,1)S(1)}, bf16[128,512]{1,0:T(8,128)(2,1)S(1)}, u32[]{:S(2)}, u32[]{:S(2)}) %collective-permute-start.21) | collective-permute-done | bytes 131104 | tf_op jit(solution)/shard_map/ppermute | solution.py:344
  64.5 1.2 %collective-permute-done.23.rb_ref = bf16[128,512]{1,0:T(8,128)(2,1)S(1)} collective-permute-done((bf16[128,512]{1,0:T(8,128)(2,1)S(1)}, bf16[128,512]{1,0:T(8,128)(2,1)S(1)}, u32[]{:S(2)}, u32[]{:S(2)}) %collective-permute-start.23) | collective-permute-done | bytes 131104 | tf_op jit(solution)/shard_map/ppermute | solution.py:344
  65.7 0.8 soft_next.3
  66.6 0.5 own.5.own_ref
  67.1 1.0 %collective-permute-done.24.got_ref = f32[4,136,128]{2,1,0:T(8,128)S(1)} collective-permute-done((f32[4,136,128]{2,1,0:T(8,128)S(1)}, f32[4,136,128]{2,1,0:T(8,128)S(1)}, u32[]{:S(2)}, u32[]{:S(2)}) %collective-permute-start.24) | collective-permute-done | bytes 278560 | tf_op jit(solution)/shard_map/ppermute | solution.py:344
  68.2 0.7 collective-permute-start.25
  68.8 1.4 %collective-permute-start.27 = (bf16[2,136,128]{2,1,0:T(8,128)(2,1)S(1)}, bf16[2,136,128]{2,1,0:T(8,128)(2,1)S(1)}, u32[]{:S(2)}, u32[]{:S(2)}) collective-permute-start(bf16[2,136,128]{2,1,0:T(8,128)(2,1)S(1)} %get-tuple-element.124.mine_ref), channel_id=1, source_target_pairs={{0,2},{1,3},{2,0},{3,1},{4,6},{5,7},{6,4},{7,5},{8,10},{9,11},{10,... | collective-permute-start | bytes 208904 | tf_op jit(solution)/shard_map/ppermute | solution.py:344
  70.3 2.9 %collective-permute-done.25.got_ref = bf16[2,136,128]{2,1,0:T(8,128)(2,1)S(1)} collective-permute-done((bf16[2,136,128]{2,1,0:T(8,128)(2,1)S(1)}, bf16[2,136,128]{2,1,0:T(8,128)(2,1)S(1)}, u32[]{:S(2)}, u32[]{:S(2)}) %collective-permute-start.25) | collective-permute-done | bytes 69664 | tf_op jit(solution)/shard_map/ppermute | solution.py:344
  73.2 1.3 %collective-permute-start.26 = (bf16[2,136,128]{2,1,0:T(8,128)(2,1)S(1)}, bf16[2,136,128]{2,1,0:T(8,128)(2,1)S(1)}, u32[]{:S(2)}, u32[]{:S(2)}) collective-permute-start(bf16[2,136,128]{2,1,0:T(8,128)(2,1)S(1)} %hop_p.5.p_ref), channel_id=1, source_target_pairs={{0,4},{1,5},{2,6},{3,7},{4,0},{5,1},{6,2},{7,3},{8,12},{9,13},{10,... | collective-permute-start | bytes 208904 | tf_op jit(solution)/shard_map/ppermute | solution.py:344
  74.5 1.9 %collective-permute-start.28 = (bf16[2,136,128]{2,1,0:T(8,128)(2,1)S(1)}, bf16[2,136,128]{2,1,0:T(8,128)(2,1)S(1)}, u32[]{:S(2)}, u32[]{:S(2)}) collective-permute-start(bf16[2,136,128]{2,1,0:T(8,128)(2,1)S(1)} %hop_q.5.q_ref), channel_id=1, source_target_pairs={{0,4},{1,5},{2,6},{3,7},{4,0},{5,1},{6,2},{7,3},{8,12},{9,13},{10,... | collective-permute-start | bytes 208904 | tf_op jit(solution)/shard_map/ppermute | solution.py:344
  76.4 4.0 %collective-permute-done.26.gp_ref = bf16[2,136,128]{2,1,0:T(8,128)(2,1)S(1)} collective-permute-done((bf16[2,136,128]{2,1,0:T(8,128)(2,1)S(1)}, bf16[2,136,128]{2,1,0:T(8,128)(2,1)S(1)}, u32[]{:S(2)}, u32[]{:S(2)}) %collective-permute-start.26) | collective-permute-done | bytes 69664 | tf_op jit(solution)/shard_map/ppermute | solution.py:344
  80.4 1.5 %collective-permute-done.28.gq_ref = bf16[2,136,128]{2,1,0:T(8,128)(2,1)S(1)} collective-permute-done((bf16[2,136,128]{2,1,0:T(8,128)(2,1)S(1)}, bf16[2,136,128]{2,1,0:T(8,128)(2,1)S(1)}, u32[]{:S(2)}, u32[]{:S(2)}) %collective-permute-start.28) | collective-permute-done | bytes 69664 | tf_op jit(solution)/shard_map/ppermute | solution.py:344
  82.5 0.9 collective-permute-done.29.delta_ref
  83.4 0.5 change.5
  84.0 1.0 %collective-permute-start.30 = (bf16[128,512]{1,0:T(8,128)(2,1)S(1)}, bf16[128,512]{1,0:T(8,128)(2,1)S(1)}, u32[]{:S(2)}, u32[]{:S(2)}) collective-permute-start(bf16[128,512]{1,0:T(8,128)(2,1)S(1)} %get-tuple-element.132.mine_ref), channel_id=1, source_target_pairs={{0,8},{1,9},{2,10},{3,11},{4,12},{5,13},{6,14},{7,15},{8,0},{9,1},... | collective-permute-start | bytes 393224 | tf_op jit(solution)/shard_map/ppermute | solution.py:344
  84.9 1.5 %collective-permute-start.32 = (bf16[128,512]{1,0:T(8,128)(2,1)S(1)}, bf16[128,512]{1,0:T(8,128)(2,1)S(1)}, u32[]{:S(2)}, u32[]{:S(2)}) collective-permute-start(bf16[128,512]{1,0:T(8,128)(2,1)S(1)} %get-tuple-element.133.mine_ref), channel_id=1, source_target_pairs={{0,16},{1,17},{2,18},{3,19},{4,20},{5,21},{6,22},{7,23},{8,24},{9,... | collective-permute-start | bytes 393224 | tf_op jit(solution)/shard_map/ppermute | solution.py:344
  86.5 3.1 %collective-permute-done.30.got_ref = bf16[128,512]{1,0:T(8,128)(2,1)S(1)} collective-permute-done((bf16[128,512]{1,0:T(8,128)(2,1)S(1)}, bf16[128,512]{1,0:T(8,128)(2,1)S(1)}, u32[]{:S(2)}, u32[]{:S(2)}) %collective-permute-start.30) | collective-permute-done | bytes 131104 | tf_op jit(solution)/shard_map/ppermute | solution.py:344
  89.6 1.0 %collective-permute-start.31 = (bf16[128,512]{1,0:T(8,128)(2,1)S(1)}, bf16[128,512]{1,0:T(8,128)(2,1)S(1)}, u32[]{:S(2)}, u32[]{:S(2)}) collective-permute-start(bf16[128,512]{1,0:T(8,128)(2,1)S(1)} %meet_a.5.a_ref), channel_id=1, source_target_pairs={{0,16},{1,17},{2,18},{3,19},{4,20},{5,21},{6,22},{7,23},{8,24},{9,... | collective-permute-start | bytes 393224 | tf_op jit(solution)/shard_map/ppermute | solution.py:344
  90.7 1.6 %collective-permute-start.33 = (bf16[128,512]{1,0:T(8,128)(2,1)S(1)}, bf16[128,512]{1,0:T(8,128)(2,1)S(1)}, u32[]{:S(2)}, u32[]{:S(2)}) collective-permute-start(bf16[128,512]{1,0:T(8,128)(2,1)S(1)} %meet_b.5.b_ref), channel_id=1, source_target_pairs={{0,8},{1,9},{2,10},{3,11},{4,12},{5,13},{6,14},{7,15},{8,0},{9,1},... | collective-permute-start | bytes 393224 | tf_op jit(solution)/shard_map/ppermute | solution.py:344
  92.2 0.6 coef_out.1
  92.9 0.7 copy.8
  93.5 1.1 %collective-permute-done.31.ra_ref = bf16[128,512]{1,0:T(8,128)(2,1)S(1)} collective-permute-done((bf16[128,512]{1,0:T(8,128)(2,1)S(1)}, bf16[128,512]{1,0:T(8,128)(2,1)S(1)}, u32[]{:S(2)}, u32[]{:S(2)}) %collective-permute-start.31) | collective-permute-done | bytes 131104 | tf_op jit(solution)/shard_map/ppermute | solution.py:344
  94.7 1.1 %collective-permute-done.33.rb_ref = bf16[128,512]{1,0:T(8,128)(2,1)S(1)} collective-permute-done((bf16[128,512]{1,0:T(8,128)(2,1)S(1)}, bf16[128,512]{1,0:T(8,128)(2,1)S(1)}, u32[]{:S(2)}, u32[]{:S(2)}) %collective-permute-start.33) | collective-permute-done | bytes 131104 | tf_op jit(solution)/shard_map/ppermute | solution.py:344
  95.7 1.0 %last.1 = f32[1024,128]{1,0:T(8,128)} custom-call(f32[128,1024]{1,0:T(8,128)S(1)} %get-tuple-element.118.before_ref, bf16[128,512]{1,0:T(8,128)(2,1)S(1)} %meet_a.5.a_ref, bf16[128,512]{1,0:T(8,128)(2,1)S(1)} %collective-permute-done.31.ra_ref, bf16[128,512]{1,0:T(8,128)(2,1)S(1)} %meet_b.5.b_ref, bf16[128,512]{1,0:T(8,128)(2,1)S(1)} %collective-permute-done.33.rb_ref), custom_call_target="tpu_custom_call" | custom-call | tf_op jit(solution)/shard_map/last/pallas_call | solution.py:51
  (49 shorter events, 2.5 us)
Async XLA Ops:
  3.7 1.7 %collective-permute-start = (f32[4,136,128]{2,1,0:T(8,128)S(1)}, f32[4,136,128]{2,1,0:T(8,128)S(1)}, u32[]{:S(2)}, u32[]{:S(2)}) collective-permute-start(f32[4,136,128]{2,1,0:T(8,128)S(1)} %get-tuple-element.73), channel_id=1, source_target_pairs={{0,1},{1,0},{2,3},{3,2},{4,5},{5,4},{6,7},{7,6},{8,9},{9,8},{10,11... | collective-permute-start | bytes 835592 | tf_op jit(solution)/shard_map/ppermute | solution.py:344
  4.2 13.1 %copy-start.1 = (s32[8,16]{1,0:T(8,128)S(1)}, s32[8,16]{1,0:T(8,128)}, u32[]{:S(2)}) copy-start(s32[8,16]{1,0:T(8,128)} %live_ref.3) | copy-start | bytes 1540
  4.2 13.1 %copy-start.2 = (s32[3,1]{0,1:T(1,128)S(1)}, s32[3,1]{0,1:T(1,128)}, u32[]{:S(2)}) copy-start(s32[3,1]{0,1:T(1,128)} %param.11) | copy-start | bytes 40
  5.4 6.1 %collective-permute-start.1 = (bf16[2,136,128]{2,1,0:T(8,128)(2,1)S(1)}, bf16[2,136,128]{2,1,0:T(8,128)(2,1)S(1)}, u32[]{:S(2)}, u32[]{:S(2)}) collective-permute-start(bf16[2,136,128]{2,1,0:T(8,128)(2,1)S(1)} %get-tuple-element.77.mine_ref), channel_id=1, source_target_pairs={{0,2},{1,3},{2,0},{3,1},{4,6},{5,7},{6,4},{7,5},{8,10},{9,11},{10,... | collective-permute-start | bytes 208904 | tf_op jit(solution)/shard_map/ppermute | solution.py:344
  8.4 5.8 %collective-permute-start.3 = (bf16[2,136,128]{2,1,0:T(8,128)(2,1)S(1)}, bf16[2,136,128]{2,1,0:T(8,128)(2,1)S(1)}, u32[]{:S(2)}, u32[]{:S(2)}) collective-permute-start(bf16[2,136,128]{2,1,0:T(8,128)(2,1)S(1)} %get-tuple-element.78.mine_ref), channel_id=1, source_target_pairs={{0,2},{1,3},{2,0},{3,1},{4,6},{5,7},{6,4},{7,5},{8,10},{9,11},{10,... | collective-permute-start | bytes 208904 | tf_op jit(solution)/shard_map/ppermute | solution.py:344
  8.5 7.2 %collective-permute-start.5 = (bf16[128,128]{1,0:T(8,128)(2,1)S(1)}, bf16[128,128]{1,0:T(8,128)(2,1)S(1)}, u32[]{:S(2)}, u32[]{:S(2)}) collective-permute-start(bf16[128,128]{1,0:T(8,128)(2,1)S(1)} %get-tuple-element.83), channel_id=1, source_target_pairs={{0,4},{1,5},{2,6},{3,7},{4,0},{5,1},{6,2},{7,3},{8,12},{9,13},{10,... | collective-permute-start | bytes 98312 | tf_op jit(solution)/shard_map/ppermute | solution.py:344
  11.5 9.3 %collective-permute-start.2 = (bf16[2,136,128]{2,1,0:T(8,128)(2,1)S(1)}, bf16[2,136,128]{2,1,0:T(8,128)(2,1)S(1)}, u32[]{:S(2)}, u32[]{:S(2)}) collective-permute-start(bf16[2,136,128]{2,1,0:T(8,128)(2,1)S(1)} %hop_p.3.p_ref), channel_id=1, source_target_pairs={{0,4},{1,5},{2,6},{3,7},{4,0},{5,1},{6,2},{7,3},{8,12},{9,13},{10,... | collective-permute-start | bytes 208904 | tf_op jit(solution)/shard_map/ppermute | solution.py:344
  14.2 6.5 %collective-permute-start.4 = (bf16[2,136,128]{2,1,0:T(8,128)(2,1)S(1)}, bf16[2,136,128]{2,1,0:T(8,128)(2,1)S(1)}, u32[]{:S(2)}, u32[]{:S(2)}) collective-permute-start(bf16[2,136,128]{2,1,0:T(8,128)(2,1)S(1)} %hop_q.3.q_ref), channel_id=1, source_target_pairs={{0,4},{1,5},{2,6},{3,7},{4,0},{5,1},{6,2},{7,3},{8,12},{9,13},{10,... | collective-permute-start | bytes 208904 | tf_op jit(solution)/shard_map/ppermute | solution.py:344
  15.7 5.0 %collective-permute-start.6 = (bf16[2,128,128]{2,1,0:T(8,128)(2,1)S(1)}, bf16[2,128,128]{2,1,0:T(8,128)(2,1)S(1)}, u32[]{:S(2)}, u32[]{:S(2)}) collective-permute-start(bf16[2,128,128]{2,1,0:T(8,128)(2,1)S(1)} %pad_maximum_fusion), channel_id=1, source_target_pairs={{0,2},{1,3},{2,0},{3,1},{4,6},{5,7},{6,4},{7,5},{8,10},{9,11},{10,... | collective-permute-start | bytes 196616 | tf_op jit(solution)/shard_map/ppermute | solution.py:344
  20.9 1.4 %collective-permute-start.7 = (bf16[128,512]{1,0:T(8,128)(2,1)S(1)}, bf16[128,512]{1,0:T(8,128)(2,1)S(1)}, u32[]{:S(2)}, u32[]{:S(2)}) collective-permute-start(bf16[128,512]{1,0:T(8,128)(2,1)S(1)} %get-tuple-element.85.delta_ref), channel_id=1, source_target_pairs={{0,1},{1,0},{2,3},{3,2},{4,5},{5,4},{6,7},{7,6},{8,9},{9,8},{10,11... | collective-permute-start | bytes 393224 | tf_op jit(solution)/shard_map/ppermute | solution.py:344
  21.4 13.8 %copy-start = (s32[1024]{0:T(1024)S(1)}, s32[1024]{0:T(1024)}, u32[]{:S(2)}) copy-start(s32[1024]{0:T(1024)} %param.8) | copy-start | bytes 12292
  22.8 5.6 %collective-permute-start.8 = (bf16[128,512]{1,0:T(8,128)(2,1)S(1)}, bf16[128,512]{1,0:T(8,128)(2,1)S(1)}, u32[]{:S(2)}, u32[]{:S(2)}) collective-permute-start(bf16[128,512]{1,0:T(8,128)(2,1)S(1)} %get-tuple-element.86.mine_ref), channel_id=1, source_target_pairs={{0,8},{1,9},{2,10},{3,11},{4,12},{5,13},{6,14},{7,15},{8,0},{9,1},... | collective-permute-start | bytes 393224 | tf_op jit(solution)/shard_map/ppermute | solution.py:344
  24.3 5.7 %collective-permute-start.10 = (bf16[128,512]{1,0:T(8,128)(2,1)S(1)}, bf16[128,512]{1,0:T(8,128)(2,1)S(1)}, u32[]{:S(2)}, u32[]{:S(2)}) collective-permute-start(bf16[128,512]{1,0:T(8,128)(2,1)S(1)} %get-tuple-element.88.mine_ref), channel_id=1, source_target_pairs={{0,16},{1,17},{2,18},{3,19},{4,20},{5,21},{6,22},{7,23},{8,24},{9,... | collective-permute-start | bytes 393224 | tf_op jit(solution)/shard_map/ppermute | solution.py:344
  28.5 5.0 %collective-permute-start.9 = (bf16[128,512]{1,0:T(8,128)(2,1)S(1)}, bf16[128,512]{1,0:T(8,128)(2,1)S(1)}, u32[]{:S(2)}, u32[]{:S(2)}) collective-permute-start(bf16[128,512]{1,0:T(8,128)(2,1)S(1)} %get-tuple-element.87.a_ref), channel_id=1, source_target_pairs={{0,16},{1,17},{2,18},{3,19},{4,20},{5,21},{6,22},{7,23},{8,24},{9,... | collective-permute-start | bytes 393224 | tf_op jit(solution)/shard_map/ppermute | solution.py:344
  30.1 5.0 %collective-permute-start.11 = (bf16[128,512]{1,0:T(8,128)(2,1)S(1)}, bf16[128,512]{1,0:T(8,128)(2,1)S(1)}, u32[]{:S(2)}, u32[]{:S(2)}) collective-permute-start(bf16[128,512]{1,0:T(8,128)(2,1)S(1)} %get-tuple-element.89.b_ref), channel_id=1, source_target_pairs={{0,8},{1,9},{2,10},{3,11},{4,12},{5,13},{6,14},{7,15},{8,0},{9,1},... | collective-permute-start | bytes 393224 | tf_op jit(solution)/shard_map/ppermute | solution.py:344
  36.0 1.6 %collective-permute-start.12 = (f32[4,136,128]{2,1,0:T(8,128)S(1)}, f32[4,136,128]{2,1,0:T(8,128)S(1)}, u32[]{:S(2)}, u32[]{:S(2)}) collective-permute-start(f32[4,136,128]{2,1,0:T(8,128)S(1)} %get-tuple-element.95), channel_id=1, source_target_pairs={{0,1},{1,0},{2,3},{3,2},{4,5},{5,4},{6,7},{7,6},{8,9},{9,8},{10,11... | collective-permute-start | bytes 835592 | tf_op jit(solution)/shard_map/ppermute | solution.py:344
  37.6 5.0 %collective-permute-start.13 = (bf16[2,136,128]{2,1,0:T(8,128)(2,1)S(1)}, bf16[2,136,128]{2,1,0:T(8,128)(2,1)S(1)}, u32[]{:S(2)}, u32[]{:S(2)}) collective-permute-start(bf16[2,136,128]{2,1,0:T(8,128)(2,1)S(1)} %get-tuple-element.99.mine_ref), channel_id=1, source_target_pairs={{0,2},{1,3},{2,0},{3,1},{4,6},{5,7},{6,4},{7,5},{8,10},{9,11},{10,... | collective-permute-start | bytes 208904 | tf_op jit(solution)/shard_map/ppermute | solution.py:344
  38.5 5.9 %collective-permute-start.15 = (bf16[2,136,128]{2,1,0:T(8,128)(2,1)S(1)}, bf16[2,136,128]{2,1,0:T(8,128)(2,1)S(1)}, u32[]{:S(2)}, u32[]{:S(2)}) collective-permute-start(bf16[2,136,128]{2,1,0:T(8,128)(2,1)S(1)} %get-tuple-element.100.mine_ref), channel_id=1, source_target_pairs={{0,2},{1,3},{2,0},{3,1},{4,6},{5,7},{6,4},{7,5},{8,10},{9,11},{10,... | collective-permute-start | bytes 208904 | tf_op jit(solution)/shard_map/ppermute | solution.py:344
  39.7 6.4 %collective-permute-start.17 = (bf16[128,128]{1,0:T(8,128)(2,1)S(1)}, bf16[128,128]{1,0:T(8,128)(2,1)S(1)}, u32[]{:S(2)}, u32[]{:S(2)}) collective-permute-start(bf16[128,128]{1,0:T(8,128)(2,1)S(1)} %get-tuple-element.106), channel_id=1, source_target_pairs={{0,4},{1,5},{2,6},{3,7},{4,0},{5,1},{6,2},{7,3},{8,12},{9,13},{10,... | collective-permute-start | bytes 98312 | tf_op jit(solution)/shard_map/ppermute | solution.py:344
  42.7 8.9 %collective-permute-start.14 = (bf16[2,136,128]{2,1,0:T(8,128)(2,1)S(1)}, bf16[2,136,128]{2,1,0:T(8,128)(2,1)S(1)}, u32[]{:S(2)}, u32[]{:S(2)}) collective-permute-start(bf16[2,136,128]{2,1,0:T(8,128)(2,1)S(1)} %hop_p.4.p_ref), channel_id=1, source_target_pairs={{0,4},{1,5},{2,6},{3,7},{4,0},{5,1},{6,2},{7,3},{8,12},{9,13},{10,... | collective-permute-start | bytes 208904 | tf_op jit(solution)/shard_map/ppermute | solution.py:344
  44.4 7.3 %collective-permute-start.16 = (bf16[2,136,128]{2,1,0:T(8,128)(2,1)S(1)}, bf16[2,136,128]{2,1,0:T(8,128)(2,1)S(1)}, u32[]{:S(2)}, u32[]{:S(2)}) collective-permute-start(bf16[2,136,128]{2,1,0:T(8,128)(2,1)S(1)} %hop_q.4.q_ref), channel_id=1, source_target_pairs={{0,4},{1,5},{2,6},{3,7},{4,0},{5,1},{6,2},{7,3},{8,12},{9,13},{10,... | collective-permute-start | bytes 208904 | tf_op jit(solution)/shard_map/ppermute | solution.py:344
  46.2 5.4 %collective-permute-start.18 = (bf16[2,128,128]{2,1,0:T(8,128)(2,1)S(1)}, bf16[2,128,128]{2,1,0:T(8,128)(2,1)S(1)}, u32[]{:S(2)}, u32[]{:S(2)}) collective-permute-start(bf16[2,128,128]{2,1,0:T(8,128)(2,1)S(1)} %pad_maximum_fusion.1), channel_id=1, source_target_pairs={{0,2},{1,3},{2,0},{3,1},{4,6},{5,7},{6,4},{7,5},{8,10},{9,11},{10,... | collective-permute-start | bytes 196616 | tf_op jit(solution)/shard_map/ppermute | solution.py:344
  51.8 1.4 %collective-permute-start.19 = (bf16[128,512]{1,0:T(8,128)(2,1)S(1)}, bf16[128,512]{1,0:T(8,128)(2,1)S(1)}, u32[]{:S(2)}, u32[]{:S(2)}) collective-permute-start(bf16[128,512]{1,0:T(8,128)(2,1)S(1)} %get-tuple-element.108.delta_ref), channel_id=1, source_target_pairs={{0,1},{1,0},{2,3},{3,2},{4,5},{5,4},{6,7},{7,6},{8,9},{9,8},{10,11... | collective-permute-start | bytes 393224 | tf_op jit(solution)/shard_map/ppermute | solution.py:344
  53.8 5.6 %collective-permute-start.20 = (bf16[128,512]{1,0:T(8,128)(2,1)S(1)}, bf16[128,512]{1,0:T(8,128)(2,1)S(1)}, u32[]{:S(2)}, u32[]{:S(2)}) collective-permute-start(bf16[128,512]{1,0:T(8,128)(2,1)S(1)} %get-tuple-element.113.mine_ref), channel_id=1, source_target_pairs={{0,8},{1,9},{2,10},{3,11},{4,12},{5,13},{6,14},{7,15},{8,0},{9,1},... | collective-permute-start | bytes 393224 | tf_op jit(solution)/shard_map/ppermute | solution.py:344
  55.3 5.3 %collective-permute-start.22 = (bf16[128,512]{1,0:T(8,128)(2,1)S(1)}, bf16[128,512]{1,0:T(8,128)(2,1)S(1)}, u32[]{:S(2)}, u32[]{:S(2)}) collective-permute-start(bf16[128,512]{1,0:T(8,128)(2,1)S(1)} %get-tuple-element.115.mine_ref), channel_id=1, source_target_pairs={{0,16},{1,17},{2,18},{3,19},{4,20},{5,21},{6,22},{7,23},{8,24},{9,... | collective-permute-start | bytes 393224 | tf_op jit(solution)/shard_map/ppermute | solution.py:344
  59.5 5.0 %collective-permute-start.21 = (bf16[128,512]{1,0:T(8,128)(2,1)S(1)}, bf16[128,512]{1,0:T(8,128)(2,1)S(1)}, u32[]{:S(2)}, u32[]{:S(2)}) collective-permute-start(bf16[128,512]{1,0:T(8,128)(2,1)S(1)} %get-tuple-element.114.a_ref), channel_id=1, source_target_pairs={{0,16},{1,17},{2,18},{3,19},{4,20},{5,21},{6,22},{7,23},{8,24},{9,... | collective-permute-start | bytes 393224 | tf_op jit(solution)/shard_map/ppermute | solution.py:344
  60.7 5.0 %collective-permute-start.23 = (bf16[128,512]{1,0:T(8,128)(2,1)S(1)}, bf16[128,512]{1,0:T(8,128)(2,1)S(1)}, u32[]{:S(2)}, u32[]{:S(2)}) collective-permute-start(bf16[128,512]{1,0:T(8,128)(2,1)S(1)} %get-tuple-element.116.b_ref), channel_id=1, source_target_pairs={{0,8},{1,9},{2,10},{3,11},{4,12},{5,13},{6,14},{7,15},{8,0},{9,1},... | collective-permute-start | bytes 393224 | tf_op jit(solution)/shard_map/ppermute | solution.py:344
  66.5 1.6 %collective-permute-start.24 = (f32[4,136,128]{2,1,0:T(8,128)S(1)}, f32[4,136,128]{2,1,0:T(8,128)S(1)}, u32[]{:S(2)}, u32[]{:S(2)}) collective-permute-start(f32[4,136,128]{2,1,0:T(8,128)S(1)} %get-tuple-element.122), channel_id=1, source_target_pairs={{0,1},{1,0},{2,3},{3,2},{4,5},{5,4},{6,7},{7,6},{8,9},{9,8},{10,11... | collective-permute-start | bytes 835592 | tf_op jit(solution)/shard_map/ppermute | solution.py:344
  68.2 5.0 %collective-permute-start.25 = (bf16[2,136,128]{2,1,0:T(8,128)(2,1)S(1)}, bf16[2,136,128]{2,1,0:T(8,128)(2,1)S(1)}, u32[]{:S(2)}, u32[]{:S(2)}) collective-permute-start(bf16[2,136,128]{2,1,0:T(8,128)(2,1)S(1)} %get-tuple-element.123.mine_ref), channel_id=1, source_target_pairs={{0,2},{1,3},{2,0},{3,1},{4,6},{5,7},{6,4},{7,5},{8,10},{9,11},{10,... | collective-permute-start | bytes 208904 | tf_op jit(solution)/shard_map/ppermute | solution.py:344
  68.8 5.7 %collective-permute-start.27 = (bf16[2,136,128]{2,1,0:T(8,128)(2,1)S(1)}, bf16[2,136,128]{2,1,0:T(8,128)(2,1)S(1)}, u32[]{:S(2)}, u32[]{:S(2)}) collective-permute-start(bf16[2,136,128]{2,1,0:T(8,128)(2,1)S(1)} %get-tuple-element.124.mine_ref), channel_id=1, source_target_pairs={{0,2},{1,3},{2,0},{3,1},{4,6},{5,7},{6,4},{7,5},{8,10},{9,11},{10,... | collective-permute-start | bytes 208904 | tf_op jit(solution)/shard_map/ppermute | solution.py:344
  73.2 7.2 %collective-permute-start.26 = (bf16[2,136,128]{2,1,0:T(8,128)(2,1)S(1)}, bf16[2,136,128]{2,1,0:T(8,128)(2,1)S(1)}, u32[]{:S(2)}, u32[]{:S(2)}) collective-permute-start(bf16[2,136,128]{2,1,0:T(8,128)(2,1)S(1)} %hop_p.5.p_ref), channel_id=1, source_target_pairs={{0,4},{1,5},{2,6},{3,7},{4,0},{5,1},{6,2},{7,3},{8,12},{9,13},{10,... | collective-permute-start | bytes 208904 | tf_op jit(solution)/shard_map/ppermute | solution.py:344
  74.5 7.3 %collective-permute-start.28 = (bf16[2,136,128]{2,1,0:T(8,128)(2,1)S(1)}, bf16[2,136,128]{2,1,0:T(8,128)(2,1)S(1)}, u32[]{:S(2)}, u32[]{:S(2)}) collective-permute-start(bf16[2,136,128]{2,1,0:T(8,128)(2,1)S(1)} %hop_q.5.q_ref), channel_id=1, source_target_pairs={{0,4},{1,5},{2,6},{3,7},{4,0},{5,1},{6,2},{7,3},{8,12},{9,13},{10,... | collective-permute-start | bytes 208904 | tf_op jit(solution)/shard_map/ppermute | solution.py:344
  82.0 1.4 %collective-permute-start.29 = (bf16[128,512]{1,0:T(8,128)(2,1)S(1)}, bf16[128,512]{1,0:T(8,128)(2,1)S(1)}, u32[]{:S(2)}, u32[]{:S(2)}) collective-permute-start(bf16[128,512]{1,0:T(8,128)(2,1)S(1)} %get-tuple-element.127.delta_ref), channel_id=1, source_target_pairs={{0,1},{1,0},{2,3},{3,2},{4,5},{5,4},{6,7},{7,6},{8,9},{9,8},{10,11... | collective-permute-start | bytes 393224 | tf_op jit(solution)/shard_map/ppermute | solution.py:344
  84.0 5.6 %collective-permute-start.30 = (bf16[128,512]{1,0:T(8,128)(2,1)S(1)}, bf16[128,512]{1,0:T(8,128)(2,1)S(1)}, u32[]{:S(2)}, u32[]{:S(2)}) collective-permute-start(bf16[128,512]{1,0:T(8,128)(2,1)S(1)} %get-tuple-element.132.mine_ref), channel_id=1, source_target_pairs={{0,8},{1,9},{2,10},{3,11},{4,12},{5,13},{6,14},{7,15},{8,0},{9,1},... | collective-permute-start | bytes 393224 | tf_op jit(solution)/shard_map/ppermute | solution.py:344
  84.9 5.7 %collective-permute-start.32 = (bf16[128,512]{1,0:T(8,128)(2,1)S(1)}, bf16[128,512]{1,0:T(8,128)(2,1)S(1)}, u32[]{:S(2)}, u32[]{:S(2)}) collective-permute-start(bf16[128,512]{1,0:T(8,128)(2,1)S(1)} %get-tuple-element.133.mine_ref), channel_id=1, source_target_pairs={{0,16},{1,17},{2,18},{3,19},{4,20},{5,21},{6,22},{7,23},{8,24},{9,... | collective-permute-start | bytes 393224 | tf_op jit(solution)/shard_map/ppermute | solution.py:344
  89.6 5.0 %collective-permute-start.31 = (bf16[128,512]{1,0:T(8,128)(2,1)S(1)}, bf16[128,512]{1,0:T(8,128)(2,1)S(1)}, u32[]{:S(2)}, u32[]{:S(2)}) collective-permute-start(bf16[128,512]{1,0:T(8,128)(2,1)S(1)} %meet_a.5.a_ref), channel_id=1, source_target_pairs={{0,16},{1,17},{2,18},{3,19},{4,20},{5,21},{6,22},{7,23},{8,24},{9,... | collective-permute-start | bytes 393224 | tf_op jit(solution)/shard_map/ppermute | solution.py:344
  90.7 5.0 %collective-permute-start.33 = (bf16[128,512]{1,0:T(8,128)(2,1)S(1)}, bf16[128,512]{1,0:T(8,128)(2,1)S(1)}, u32[]{:S(2)}, u32[]{:S(2)}) collective-permute-start(bf16[128,512]{1,0:T(8,128)(2,1)S(1)} %meet_b.5.b_ref), channel_id=1, source_target_pairs={{0,8},{1,9},{2,10},{3,11},{4,12},{5,13},{6,14},{7,15},{8,0},{9,1},... | collective-permute-start | bytes 393224 | tf_op jit(solution)/shard_map/ppermute | solution.py:344

commit v8 on v7

--- a/solution.py
+++ b/solution.py
@@ -124,21 +124,23 @@
     return jnp.concatenate([mine.reshape(rows, HALF), other.reshape(rows, HALF)], axis=1)
 
 
-def half_sums(res_t, spread_ref, x_ref, first, g_ref):
-    rows = x_ref.shape[0]
-    grad = jnp.dot(res_t, x_ref[:, first : first + HALF], preferred_element_type=F32)
+def half_sums(res_t, spread_ref, x_ref, start, first, g_ref, so_far=None):
+    rows = spread_ref.shape[0]
+    grad = jnp.dot(res_t, x_ref[start : start + rows, first : first + HALF], preferred_element_type=F32)
     row = lax.broadcasted_iota(jnp.int32, (8, TILE), 0)
     for k in range(NB):
         lanes = slice(first + k * TILE, first + (k + 1) * TILE)
         acc = jnp.zeros((8, TILE), F32)
-        for r in range(rows // TILE):
-            here = slice(r * TILE, (r + 1) * TILE)
-            x = x_ref[here, lanes].astype(F32)
+        for r, here in tiles_of(rows):
+            x = x_ref[start + r * TILE : start + (r + 1) * TILE, lanes].astype(F32)
             term = x * x * spread_ref[here, :]
             acc = acc + jnp.sum(term.reshape(TILE // 8, 8, TILE), axis=0)
-        total = jnp.sum(acc, axis=0, keepdims=True)
-        g_ref[k, 0:C, :] = grad[:, k * TILE : (k + 1) * TILE]
-        g_ref[k, C:ROWS, :] = jnp.where(row == 0, total, 0.0)
+        total = jnp.where(row == 0, jnp.sum(acc, axis=0, keepdims=True), 0.0)
+        here = grad[:, k * TILE : (k + 1) * TILE]
+        if so_far is not None:
+            here, total = here + so_far[k, 0:C, :], total + so_far[k, C:ROWS, :]
+        g_ref[k, 0:C, :] = here
+        g_ref[k, C:ROWS, :] = total
 
 
 def soft_rows(score, labels, here, res_ref, spread_ref):
@@ -156,9 +158,14 @@
     return [(r, slice(r * TILE, (r + 1) * TILE)) for r in range(rows // TILE)]
 
 
+def keep_score(score, r, low_ref, high_ref):
+    per = low_ref.shape[1] // TILE
+    (low_ref if r < per else high_ref)[:, r % per * TILE : (r % per + 1) * TILE] = score
+
+
 def first_body(
     order_hbm, live_hbm, margins_hbm, lab_hbm, coef_hbm, x_hbm,
-    x_ref, score_ref, res_ref, spread_ref, g_ref, first_ref, other_ref, first_send, other_send, *rest,
+    x_ref, low_ref, high_ref, res_ref, spread_ref, g_ref, first_ref, other_ref, first_send, other_send, *rest,
 ):
     same_refs = rest[: STEPS - 1]
     order, live, margins, labels, coef, small, buf, sems = rest[STEPS - 1 :]
@@ -177,7 +184,7 @@
         load.wait()
     for r, here in tiles_of(margins.shape[0]):
         score = margins[here, :].astype(F32).T
-        score_ref[:, here] = score
+        keep_score(score, r, low_ref, high_ref)
         soft_rows(score, labels[r : r + 1, :], here, res_ref, spread_ref)
     for block, keep, send in ((chosen, first_ref, first_send), (1 - chosen, other_ref, other_send)):
         rows = coef[block].T
@@ -188,42 +195,62 @@
     for r, copy in enumerate(copies):
         copy.wait()
         mask_tile(r, chosen, core, live, buf, x_ref)
-    half_sums(res_ref[...], spread_ref, x_ref, HALF, g_ref)
-
-
-def first_general_body(margins_ref, lab_ref, x_ref, score_ref, res_ref, spread_ref, g_ref):
+    half_sums(res_ref[...], spread_ref, x_ref, 0, HALF, g_ref)
+
+
+def first_general_body(margins_ref, lab_ref, x_ref, low_ref, high_ref, res_ref, spread_ref, g_ref):
     for r, here in tiles_of(margins_ref.shape[0]):
         score = margins_ref[here, :].astype(F32).T
+        keep_score(score, r, low_ref, high_ref)
+        soft_rows(score, lab_ref[r : r + 1, :], here, res_ref, spread_ref)
+    half_sums(res_ref[...], spread_ref, x_ref, 0, HALF, g_ref)
+
+
+def next_rows(start, before_ref, part_ref, got_ref, lab_ref, score_ref, res_ref, spread_ref):
+    for r, here in tiles_of(before_ref.shape[1]):
+        score = before_ref[:, here] + (part_ref[:, here].astype(F32) + got_ref[:, here].astype(F32))
         score_ref[:, here] = score
-        soft_rows(score, lab_ref[r : r + 1, :], here, res_ref, spread_ref)
-    half_sums(res_ref[...], spread_ref, x_ref, HALF, g_ref)
-
-
-def next_body(before_ref, a_ref, ra_ref, b_ref, rb_ref, lab_ref, x_ref, score_ref, res_ref, spread_ref, g_ref):
+        row = start // TILE + r
+        soft_rows(score, lab_ref[row : row + 1, :], here, res_ref, spread_ref)
+
+
+def next_low_body(before_ref, part_ref, got_ref, lab_ref, x_ref, score_ref, res_ref, spread_ref, g_ref, own_ref):
+    next_rows(0, before_ref, part_ref, got_ref, lab_ref, score_ref, res_ref, spread_ref)
+    half_sums(res_ref[...], spread_ref, x_ref, 0, HALF, g_ref)
+    half_sums(res_ref[...], spread_ref, x_ref, 0, 0, own_ref)
+
+
+def next_high_body(before_ref, part_ref, got_ref, lab_ref, x_ref, so_far, score_ref, res_ref, spread_ref, g_ref):
+    start = before_ref.shape[1]
+    next_rows(start, before_ref, part_ref, got_ref, lab_ref, score_ref, res_ref, spread_ref)
+    half_sums(res_ref[...], spread_ref, x_ref, start, HALF, g_ref, so_far)
+
+
+def last_low_body(before_ref, part_ref, got_ref, out_ref):
+    for _, here in tiles_of(before_ref.shape[1]):
+        score = before_ref[:, here] + (part_ref[:, here].astype(F32) + got_ref[:, here].astype(F32))
+        out_ref[here, :] = score.T
+
+
+def last_high_body(low_ref, before_ref, part_ref, got_ref, out_hbm, buf, sems):
     rows = before_ref.shape[1]
-    for r, here in tiles_of(rows):
-        score = before_ref[:, here] + change_tile(here, rows, a_ref, ra_ref, b_ref, rb_ref)
-        score_ref[:, here] = score
-        soft_rows(score, lab_ref[r : r + 1, :], here, res_ref, spread_ref)
-    half_sums(res_ref[...], spread_ref, x_ref, HALF, g_ref)
-
-
-def last_body(before_ref, a_ref, ra_ref, b_ref, rb_ref, out_ref):
-    rows = before_ref.shape[1]
-    for _, here in tiles_of(rows):
-        score = before_ref[:, here] + change_tile(here, rows, a_ref, ra_ref, b_ref, rb_ref)
-        out_ref[here, :] = score.T
-
-
-def change_tile(here, rows, a_ref, ra_ref, b_ref, rb_ref):
-    if here.stop <= rows // 2:
-        return a_ref[:, here].astype(F32) + ra_ref[:, here].astype(F32)
-    at = slice(here.start - rows // 2, here.stop - rows // 2)
-    return b_ref[:, at].astype(F32) + rb_ref[:, at].astype(F32)
+    copies = [
+        pltpu.make_async_copy(ref, out_hbm.at[pl.ds(i * rows, rows)], sems.at[i])
+        for i, ref in enumerate((low_ref, buf))
+    ]
+    copies[0].start()
+    last_low_body(before_ref, part_ref, got_ref, buf)
+    copies[1].start()
+    for copy in copies:
+        copy.wait()
 
 
 def own_body(res_ref, spread_ref, x_ref, g_ref):
-    half_sums(res_ref[...], spread_ref, x_ref, 0, g_ref)
+    half_sums(res_ref[...], spread_ref, x_ref, 0, 0, g_ref)
+
+
+def own_high_body(res_ref, spread_ref, x_ref, so_far, g_ref):
+    half_sums(res_ref[...], spread_ref, x_ref, spread_ref.shape[0], 0, g_ref, so_far)
 
 
 def encode(k, grad, curv, out_ref):
@@ -238,7 +265,7 @@
 def pair_body(own_ref, got_ref, p_ref, q_ref):
     for k in range(NB):
         total = own_ref[k] + got_ref[k]
-        encode(k % PB, total[0:C], total[C : C + 1], p_ref if k < PB else q_ref)
+        encode(k if k < PB else k - PB, total[0:C], total[C : C + 1], p_ref if k < PB else q_ref)
 
 
 def decode_sum(k, mine_ref, got_ref):
@@ -247,7 +274,7 @@
 
 
 def hop_body(mine_ref, got_ref, out_ref):
-    for k in range(PB):
+    for k in range(out_ref.shape[0]):
         encode(k, *decode_sum(k, mine_ref, got_ref), out_ref)
 
 
@@ -271,7 +298,7 @@
     for k in range(NB):
         old = old_ref[k]
         chunk = (p_ref, gp_ref) if k < PB else (q_ref, gq_ref)
-        new = step_coef(count, k % PB, *chunk, old)
+        new = step_coef(count, k if k < PB else k - PB, *chunk, old)
         new_ref[k] = new
         delta_ref[:, k * TILE : (k + 1) * TILE] = (new - old).astype(BF16)
 
@@ -282,7 +309,7 @@
         old0, old1 = old0_ref[k], old1_ref[k]
         old = jnp.where(same, old0, old1)
         chunk = (p_ref, gp_ref) if k < PB else (q_ref, gq_ref)
-        new = step_coef(count, k % PB, *chunk, old)
+        new = step_coef(count, k if k < PB else k - PB, *chunk, old)
         new0_ref[k] = jnp.where(same, new, old0)
         new1_ref[k] = jnp.where(same, old1, new)
         delta_ref[:, k * TILE : (k + 1) * TILE] = (new - old).astype(BF16)
@@ -400,18 +427,20 @@
 
     x_shape = sds((rows, BLOCK), BF16)
     soft_shapes = (
-        sds((C, rows), F32), sds((C, rows), BF16), sds((rows, TILE), F32), sds((NB, ROWS, TILE), F32),
+        sds((C, rows // 2), F32), sds((C, rows // 2), F32),
+        sds((C, rows), BF16), sds((rows, TILE), F32), sds((NB, ROWS, TILE), F32),
     )
     g_shape = soft_shapes[-1]
+    next_shapes = (soft_shapes[0], sds((C, rows // 2), BF16), sds((rows // 2, TILE), F32), g_shape)
     old_shape, delta_shape = sds((NB, C, TILE), F32), sds((C, HALF), BF16)
     part_shape, half = sds((rows, C), F32), (C, rows // 2)
     own_shape, send_shape, same_shape = sds((C, TILE), F32), sds((C, TILE), BF16), sds((8, TILE), F32)
     flops, nbytes = 2 * rows * HALF * C, 1 << 20
 
-    message = sds((PB, ROWS, TILE), BF16)
+    p_shape, q_shape = sds((PB, ROWS, TILE), BF16), sds((NB - PB, ROWS, TILE), BF16)
 
     if aligned:
-        x, score, res_t, spread, g_other, *rest = call(
+        x, low, high, res_t, spread, g_other, *rest = call(
             first_body,
             (x_shape,) + soft_shapes + (own_shape,) * 2 + (send_shape,) * 2 + (same_shape,) * (STEPS - 1),
             hbm(6), "soft_first", flops, nbytes,
@@ -427,7 +456,7 @@
         blocks, sends, same = rest[:2], rest[2:4], rest[4:]
     else:
         x = prep_general(x_values, tile_live, order[0, 0], core, own)
-        score, res_t, spread, g_other = call(
+        low, high, res_t, spread, g_other = call(
             first_general_body, soft_shapes, vmem(3), "soft_first", flops, nbytes
         )(margins, labels, x)
         blocks = gather_blocks(coef, order, z_bits)
@@ -439,12 +468,19 @@
     for step in range(STEPS):
         if step > 0:
             x = following
-            score, res_t, spread, g_other = call(
-                next_body, soft_shapes, vmem(7), "soft_next", flops, nbytes
-            )(score, *halves, labels, x)
-        got = swap_core(g_other)
-        g_own = call(own_body, g_shape, vmem(3), "own", flops, nbytes)(res_t, spread, x)
-        p, q = call(pair_body, (message, message), vmem(2), "pair")(g_own, got)
+            a, got_a, b, got_b = halves
+            low, _, _, g_other, g_own = call(
+                next_low_body, next_shapes + (g_shape,), vmem(5), "soft_low", flops, nbytes
+            )(low, a, got_a, labels, x)
+            high, res_t, spread, g_other = call(
+                next_high_body, next_shapes, vmem(6), "soft_high", flops // 2, nbytes
+            )(high, b, got_b, labels, x, g_other)
+            got = swap_core(g_other)
+            g_own = call(own_high_body, g_shape, vmem(4), "own", flops // 2, nbytes)(res_t, spread, x, g_own)
+        else:
+            got = swap_core(g_other)
+            g_own = call(own_body, g_shape, vmem(3), "own", flops, nbytes)(res_t, spread, x)
+        p, q = call(pair_body, (p_shape, q_shape), vmem(2), "pair")(g_own, got)
         carry = aligned and step < 2
         if carry:
             p, q, send = lax.optimization_barrier((p, q, sends[step]))
@@ -454,8 +490,8 @@
             if n < len(z_bits) - 1:
                 if carry:
                     far = swap(send, lambda f, e: (f, e ^ z_bits[1]))
-                p = call(hop_body, message, vmem(2), "hop_p")(p, got_p)
-                q = call(hop_body, message, vmem(2), "hop_q")(q, got_q)
+                p = call(hop_body, p_shape, vmem(2), "hop_p")(p, got_p)
+                q = call(hop_body, q_shape, vmem(2), "hop_q")(q, got_q)
         if carry:
             near = swap(jnp.stack([send, far]), lambda f, e: (f, e ^ z_bits[0]))
             old = call(place_body, old_shape, vmem(3), "place")(far, near, blocks[step])
@@ -484,7 +520,18 @@
         )(x, part, got, *errors)
         halves, errors = sum_over_feat(a, b, last)
         errors = kept + errors
-    score = call(last_body, jax.ShapeDtypeStruct((rows, C), F32), vmem(5), "last")(score, *halves)
+    a, got_a, b, got_b = halves
+    half = sds((rows // 2, C), F32)
+    low = call(last_low_body, half, vmem(3), "last_low", flops // 4, nbytes)(low, a, got_a)
+    score = pl.pallas_call(
+        last_high_body,
+        out_shape=jax.ShapeDtypeStruct((rows, C), F32),
+        in_specs=vmem(4),
+        out_specs=pl.BlockSpec(memory_space=pltpu.HBM),
+        scratch_shapes=[pltpu.VMEM(half.shape, F32), pltpu.SemaphoreType.DMA((2,))],
+        name="last_high",
+        compiler_params=pltpu.CompilerParams(vmem_limit_bytes=16 << 20),
+    )(*(pltpu.with_memory_space_constraint(v, pltpu.VMEM) for v in (low, high, b, got_b)))
     if aligned:
         coef = call(coef_body, sds(coef.shape, F32), smem(1) + vmem(2), "coef_out")(order, first, other)
     else:

time: 96.9 us -> 96.4 us (level)
  waiting for transfers between devices: 36.1 us -> 32.4 us
  starting transfers between devices: 42.7 us -> 44.6 us
  Pallas kernels: 16.2 us -> 17.7 us
    ppermute x34, waiting for transfers between devices: 36.1 us -> 32.4 us  [swap(): return lax.ppermute(x, ('feat', 'ex'), pairs)]
    ppermute x34, starting transfers between devices: 42.7 us -> 44.6 us  [swap(): return lax.ppermute(x, ('feat', 'ex'), pairs)]
    pallas_call x36 -> x38, Pallas kernels: 16.2 us -> 16.8 us  [run(): f(*(x if spec.memory_space == pltpu.SMEM else pltpu.with_memory_space_con...]
  transfers between devices with their start and end apart: 34 -> 34, of which waited for: 21 -> 20; matrix products, arithmetic and copies ran while one was open for 1% -> 1% of each run, Pallas kernels for 9% -> 11%
where the time goes in v8:
time: 96.4 us; the launch traced here: 96.2 us
  starting transfers between devices  44.6 us (46%)
  waiting for transfers between devices  32.4 us (34%)
  Pallas kernels  17.7 us (18%)
    ppermute x34, starting transfers between devices, swap(): return lax.ppermute(x, ('feat', 'ex'), pairs)  44.6 us
    ppermute x34, waiting for transfers between devices, swap(): return lax.ppermute(x, ('feat', 'ex'), pairs)  32.4 us
    pallas_call x38, Pallas kernels, run(): f(*(x if spec.memory_space == pltpu.SMEM else pltpu.with_memory_space_con...  16.8 us
  transfers between devices with their start and end apart: 34, of which 20 were waited for; matrix products, arithmetic and copies ran while one was open for 1% of the time, Pallas kernels for 11%

profile of v8, /device:TPU:0, one launch (start us, length us, event | category | flops | bytes accessed | tf_op | source)
XLA Modules:
  0.0 96.2 jit_solution(16858623193692741748)
XLA Ops:
  0.6 3.0 %soft_first.1 = (bf16[1024,1024]{1,0:T(8,128)(2,1)S(1)}, f32[128,512]{1,0:T(8,128)S(1)}, f32[128,512]{1,0:T(8,128)S(1)}, bf16[128,1024]{1,0:T(8,128)(2,1)S(1)}, ...) custom-call(s32[1,3]{1,0:T(1,128)} %bitcast.15, ...), custom_call_target="tpu_custom_call" | custom-call | flops 134217728 | bytes 1048576 | tf_op jit(solution)/shard_map/soft_first/pallas_call | solution.py:51
  3.6 0.5 collective-permute-start
  4.1 0.5 own.3.own_ref
  4.7 0.7 collective-permute-done.got_ref
  5.3 3.0 %collective-permute-start.1 = (bf16[2,136,128]{2,1,0:T(8,128)(2,1)S(1)}, bf16[2,136,128]{2,1,0:T(8,128)(2,1)S(1)}, u32[]{:S(2)}, u32[]{:S(2)}) collective-permute-start(bf16[2,136,128]{2,1,0:T(8,128)(2,1)S(1)} %get-tuple-element.84.mine_ref), channel_id=1, source_target_pairs={{0,2},{1,3},{2,0},{3,1},{4,6},{5,7},{6,4},{7,5},{8,10},{9,11},{10,... | collective-permute-start | bytes 208904 | tf_op jit(solution)/shard_map/ppermute | solution.py:371
  8.4 3.0 %collective-permute-start.5 = (bf16[128,128]{1,0:T(8,128)(2,1)S(1)}, bf16[128,128]{1,0:T(8,128)(2,1)S(1)}, u32[]{:S(2)}, u32[]{:S(2)}) collective-permute-start(bf16[128,128]{1,0:T(8,128)(2,1)S(1)} %get-tuple-element.90), channel_id=1, source_target_pairs={{0,4},{1,5},{2,6},{3,7},{4,0},{5,1},{6,2},{7,3},{8,12},{9,13},{10,... | collective-permute-start | bytes 98312 | tf_op jit(solution)/shard_map/ppermute | solution.py:371
  11.4 2.7 %collective-permute-start.2 = (bf16[2,136,128]{2,1,0:T(8,128)(2,1)S(1)}, bf16[2,136,128]{2,1,0:T(8,128)(2,1)S(1)}, u32[]{:S(2)}, u32[]{:S(2)}) collective-permute-start(bf16[2,136,128]{2,1,0:T(8,128)(2,1)S(1)} %hop_p.3.p_ref), channel_id=1, source_target_pairs={{0,4},{1,5},{2,6},{3,7},{4,0},{5,1},{6,2},{7,3},{8,12},{9,13},{10,... | collective-permute-start | bytes 208904 | tf_op jit(solution)/shard_map/ppermute | solution.py:371
  14.2 1.5 %collective-permute-start.4 = (bf16[2,136,128]{2,1,0:T(8,128)(2,1)S(1)}, bf16[2,136,128]{2,1,0:T(8,128)(2,1)S(1)}, u32[]{:S(2)}, u32[]{:S(2)}) collective-permute-start(bf16[2,136,128]{2,1,0:T(8,128)(2,1)S(1)} %hop_q.3.q_ref), channel_id=1, source_target_pairs={{0,4},{1,5},{2,6},{3,7},{4,0},{5,1},{6,2},{7,3},{8,12},{9,13},{10,... | collective-permute-start | bytes 208904 | tf_op jit(solution)/shard_map/ppermute | solution.py:371
  15.6 1.6 %collective-permute-start.6 = (bf16[2,128,128]{2,1,0:T(8,128)(2,1)S(1)}, bf16[2,128,128]{2,1,0:T(8,128)(2,1)S(1)}, u32[]{:S(2)}, u32[]{:S(2)}) collective-permute-start(bf16[2,128,128]{2,1,0:T(8,128)(2,1)S(1)} %pad_maximum_fusion), channel_id=1, source_target_pairs={{0,2},{1,3},{2,0},{3,1},{4,6},{5,7},{6,4},{7,5},{8,10},{9,11},{10,... | collective-permute-start | bytes 196616 | tf_op jit(solution)/shard_map/ppermute | solution.py:371
  17.2 2.3 %prep.2.x_ref = bf16[1024,1024]{1,0:T(8,128)(2,1)S(1)} custom-call(s32[1,3]{1,0:T(1,128)S(1)} %bitcast.16, s32[8,16]{1,0:T(8,128)S(1)} %copy-done.1, bf16[1024,2048]{1,0:T(8,128)(2,1)} %x_ref.3), custom_call_target="tpu_custom_call" | custom-call | bytes 4194304 | tf_op jit(solution)/shard_map/prep/pallas_call | solution.py:51
  19.4 1.2 %collective-permute-done.6.near_ref = bf16[2,128,128]{2,1,0:T(8,128)(2,1)S(1)} collective-permute-done((bf16[2,128,128]{2,1,0:T(8,128)(2,1)S(1)}, bf16[2,128,128]{2,1,0:T(8,128)(2,1)S(1)}, u32[]{:S(2)}, u32[]{:S(2)}) %collective-permute-start.6) | collective-permute-done | bytes 65568 | tf_op jit(solution)/shard_map/ppermute | solution.py:371
  20.9 0.4 mine.3.part_ref
  21.3 0.9 collective-permute-done.7.delta_ref
  22.2 0.5 change.3
  22.7 1.6 %collective-permute-start.8 = (bf16[128,512]{1,0:T(8,128)(2,1)S(1)}, bf16[128,512]{1,0:T(8,128)(2,1)S(1)}, u32[]{:S(2)}, u32[]{:S(2)}) collective-permute-start(bf16[128,512]{1,0:T(8,128)(2,1)S(1)} %get-tuple-element.93.mine_ref), channel_id=1, source_target_pairs={{0,8},{1,9},{2,10},{3,11},{4,12},{5,13},{6,14},{7,15},{8,0},{9,1},... | collective-permute-start | bytes 393224 | tf_op jit(solution)/shard_map/ppermute | solution.py:371
  24.3 1.5 %collective-permute-start.10 = (bf16[128,512]{1,0:T(8,128)(2,1)S(1)}, bf16[128,512]{1,0:T(8,128)(2,1)S(1)}, u32[]{:S(2)}, u32[]{:S(2)}) collective-permute-start(bf16[128,512]{1,0:T(8,128)(2,1)S(1)} %get-tuple-element.99.mine_ref), channel_id=1, source_target_pairs={{0,16},{1,17},{2,18},{3,19},{4,20},{5,21},{6,22},{7,23},{8,24},{9,... | collective-permute-start | bytes 393224 | tf_op jit(solution)/shard_map/ppermute | solution.py:371
  25.8 2.5 %collective-permute-done.8.got_ref = bf16[128,512]{1,0:T(8,128)(2,1)S(1)} collective-permute-done((bf16[128,512]{1,0:T(8,128)(2,1)S(1)}, bf16[128,512]{1,0:T(8,128)(2,1)S(1)}, u32[]{:S(2)}, u32[]{:S(2)}) %collective-permute-start.8) | collective-permute-done | bytes 131104 | tf_op jit(solution)/shard_map/ppermute | solution.py:371
  28.4 1.6 %collective-permute-start.9 = (bf16[128,512]{1,0:T(8,128)(2,1)S(1)}, bf16[128,512]{1,0:T(8,128)(2,1)S(1)}, u32[]{:S(2)}, u32[]{:S(2)}) collective-permute-start(bf16[128,512]{1,0:T(8,128)(2,1)S(1)} %get-tuple-element.94.part_ref), channel_id=1, source_target_pairs={{0,16},{1,17},{2,18},{3,19},{4,20},{5,21},{6,22},{7,23},{8,24},{9,... | collective-permute-start | bytes 393224 | tf_op jit(solution)/shard_map/ppermute | solution.py:371
  30.1 1.5 %collective-permute-start.11 = (bf16[128,512]{1,0:T(8,128)(2,1)S(1)}, bf16[128,512]{1,0:T(8,128)(2,1)S(1)}, u32[]{:S(2)}, u32[]{:S(2)}) collective-permute-start(bf16[128,512]{1,0:T(8,128)(2,1)S(1)} %get-tuple-element.100.part_ref), channel_id=1, source_target_pairs={{0,8},{1,9},{2,10},{3,11},{4,12},{5,13},{6,14},{7,15},{8,0},{9,1},... | collective-permute-start | bytes 393224 | tf_op jit(solution)/shard_map/ppermute | solution.py:371
  31.6 1.8 %collective-permute-done.9.got_ref = bf16[128,512]{1,0:T(8,128)(2,1)S(1)} collective-permute-done((bf16[128,512]{1,0:T(8,128)(2,1)S(1)}, bf16[128,512]{1,0:T(8,128)(2,1)S(1)}, u32[]{:S(2)}, u32[]{:S(2)}) %collective-permute-start.9) | collective-permute-done | bytes 131104 | tf_op jit(solution)/shard_map/ppermute | solution.py:371
  33.5 1.3 %soft_low.2 = (f32[128,512]{1,0:T(8,128)S(1)}, bf16[128,512]{1,0:T(8,128)(2,1)}, f32[512,128]{1,0:T(8,128)}, f32[4,136,128]{2,1,0:T(8,128)S(1)}, f32[4,136,128]{2,1,0:T(8,128)S(1)}) custom-call(f32[128,512]{1,0:T(8,128)S(1)} %get-tuple-element.76.before_ref, bf16[128,512]{1,0:T(8,128)(2,1)S(1)} %get-tuple-element.94.part_ref, ...), custom_call_target="tpu_custom_call" | custom-call | flops 134217728 | bytes 1048576 | tf_op jit(solution)/shard_map/soft_low/pallas_call | solution.py:51
  35.1 0.4 soft_high.2
  36.0 1.2 %collective-permute-done.12.got_ref = f32[4,136,128]{2,1,0:T(8,128)S(1)} collective-permute-done((f32[4,136,128]{2,1,0:T(8,128)S(1)}, f32[4,136,128]{2,1,0:T(8,128)S(1)}, u32[]{:S(2)}, u32[]{:S(2)}) %collective-permute-start.12) | collective-permute-done | bytes 278560 | tf_op jit(solution)/shard_map/ppermute | solution.py:371
  37.2 0.8 collective-permute-start.13
  38.1 1.2 %collective-permute-start.15 = (bf16[2,136,128]{2,1,0:T(8,128)(2,1)S(1)}, bf16[2,136,128]{2,1,0:T(8,128)(2,1)S(1)}, u32[]{:S(2)}, u32[]{:S(2)}) collective-permute-start(bf16[2,136,128]{2,1,0:T(8,128)(2,1)S(1)} %get-tuple-element.110.mine_ref), channel_id=1, source_target_pairs={{0,2},{1,3},{2,0},{3,1},{4,6},{5,7},{6,4},{7,5},{8,10},{9,11},{10,... | collective-permute-start | bytes 208904 | tf_op jit(solution)/shard_map/ppermute | solution.py:371
  39.3 2.1 %collective-permute-start.17 = (bf16[128,128]{1,0:T(8,128)(2,1)S(1)}, bf16[128,128]{1,0:T(8,128)(2,1)S(1)}, u32[]{:S(2)}, u32[]{:S(2)}) collective-permute-start(bf16[128,128]{1,0:T(8,128)(2,1)S(1)} %get-tuple-element.116), channel_id=1, source_target_pairs={{0,4},{1,5},{2,6},{3,7},{4,0},{5,1},{6,2},{7,3},{8,12},{9,13},{10,... | collective-permute-start | bytes 98312 | tf_op jit(solution)/shard_map/ppermute | solution.py:371
  41.4 0.8 collective-permute-done.13.got_ref
  42.3 1.7 %collective-permute-start.14 = (bf16[2,136,128]{2,1,0:T(8,128)(2,1)S(1)}, bf16[2,136,128]{2,1,0:T(8,128)(2,1)S(1)}, u32[]{:S(2)}, u32[]{:S(2)}) collective-permute-start(bf16[2,136,128]{2,1,0:T(8,128)(2,1)S(1)} %hop_p.4.p_ref), channel_id=1, source_target_pairs={{0,4},{1,5},{2,6},{3,7},{4,0},{5,1},{6,2},{7,3},{8,12},{9,13},{10,... | collective-permute-start | bytes 208904 | tf_op jit(solution)/shard_map/ppermute | solution.py:371
  44.0 1.8 %collective-permute-start.16 = (bf16[2,136,128]{2,1,0:T(8,128)(2,1)S(1)}, bf16[2,136,128]{2,1,0:T(8,128)(2,1)S(1)}, u32[]{:S(2)}, u32[]{:S(2)}) collective-permute-start(bf16[2,136,128]{2,1,0:T(8,128)(2,1)S(1)} %hop_q.4.q_ref), channel_id=1, source_target_pairs={{0,4},{1,5},{2,6},{3,7},{4,0},{5,1},{6,2},{7,3},{8,12},{9,13},{10,... | collective-permute-start | bytes 208904 | tf_op jit(solution)/shard_map/ppermute | solution.py:371
  45.8 1.8 %collective-permute-start.18 = (bf16[2,128,128]{2,1,0:T(8,128)(2,1)S(1)}, bf16[2,128,128]{2,1,0:T(8,128)(2,1)S(1)}, u32[]{:S(2)}, u32[]{:S(2)}) collective-permute-start(bf16[2,128,128]{2,1,0:T(8,128)(2,1)S(1)} %pad_maximum_fusion.1), channel_id=1, source_target_pairs={{0,2},{1,3},{2,0},{3,1},{4,6},{5,7},{6,4},{7,5},{8,10},{9,11},{10,... | collective-permute-start | bytes 196616 | tf_op jit(solution)/shard_map/ppermute | solution.py:371
  47.6 2.3 %prep.3.x_ref = bf16[1024,1024]{1,0:T(8,128)(2,1)S(1)} custom-call(s32[1,3]{1,0:T(1,128)S(1)} %bitcast.17, s32[8,16]{1,0:T(8,128)S(1)} %copy-done.1, bf16[1024,2048]{1,0:T(8,128)(2,1)} %x_ref.3), custom_call_target="tpu_custom_call" | custom-call | bytes 4194304 | tf_op jit(solution)/shard_map/prep/pallas_call | solution.py:51
  49.8 1.4 %collective-permute-done.18.near_ref = bf16[2,128,128]{2,1,0:T(8,128)(2,1)S(1)} collective-permute-done((bf16[2,128,128]{2,1,0:T(8,128)(2,1)S(1)}, bf16[2,128,128]{2,1,0:T(8,128)(2,1)S(1)}, u32[]{:S(2)}, u32[]{:S(2)}) %collective-permute-start.18) | collective-permute-done | bytes 65568 | tf_op jit(solution)/shard_map/ppermute | solution.py:371
  51.5 0.4 mine.4.part_ref
  52.0 0.9 collective-permute-done.19.delta_ref
  52.9 0.5 change.4
  53.4 1.5 %collective-permute-start.20 = (bf16[128,512]{1,0:T(8,128)(2,1)S(1)}, bf16[128,512]{1,0:T(8,128)(2,1)S(1)}, u32[]{:S(2)}, u32[]{:S(2)}) collective-permute-start(bf16[128,512]{1,0:T(8,128)(2,1)S(1)} %get-tuple-element.123.mine_ref), channel_id=1, source_target_pairs={{0,8},{1,9},{2,10},{3,11},{4,12},{5,13},{6,14},{7,15},{8,0},{9,1},... | collective-permute-start | bytes 393224 | tf_op jit(solution)/shard_map/ppermute | solution.py:371
  54.9 1.2 %collective-permute-start.22 = (bf16[128,512]{1,0:T(8,128)(2,1)S(1)}, bf16[128,512]{1,0:T(8,128)(2,1)S(1)}, u32[]{:S(2)}, u32[]{:S(2)}) collective-permute-start(bf16[128,512]{1,0:T(8,128)(2,1)S(1)} %get-tuple-element.129.mine_ref), channel_id=1, source_target_pairs={{0,16},{1,17},{2,18},{3,19},{4,20},{5,21},{6,22},{7,23},{8,24},{9,... | collective-permute-start | bytes 393224 | tf_op jit(solution)/shard_map/ppermute | solution.py:371
  56.1 2.9 %collective-permute-done.20.got_ref = bf16[128,512]{1,0:T(8,128)(2,1)S(1)} collective-permute-done((bf16[128,512]{1,0:T(8,128)(2,1)S(1)}, bf16[128,512]{1,0:T(8,128)(2,1)S(1)}, u32[]{:S(2)}, u32[]{:S(2)}) %collective-permute-start.20) | collective-permute-done | bytes 131104 | tf_op jit(solution)/shard_map/ppermute | solution.py:371
  59.1 1.3 %collective-permute-start.21 = (bf16[128,512]{1,0:T(8,128)(2,1)S(1)}, bf16[128,512]{1,0:T(8,128)(2,1)S(1)}, u32[]{:S(2)}, u32[]{:S(2)}) collective-permute-start(bf16[128,512]{1,0:T(8,128)(2,1)S(1)} %get-tuple-element.124.part_ref), channel_id=1, source_target_pairs={{0,16},{1,17},{2,18},{3,19},{4,20},{5,21},{6,22},{7,23},{8,24},{9,... | collective-permute-start | bytes 393224 | tf_op jit(solution)/shard_map/ppermute | solution.py:371
  60.4 1.5 %collective-permute-start.23 = (bf16[128,512]{1,0:T(8,128)(2,1)S(1)}, bf16[128,512]{1,0:T(8,128)(2,1)S(1)}, u32[]{:S(2)}, u32[]{:S(2)}) collective-permute-start(bf16[128,512]{1,0:T(8,128)(2,1)S(1)} %get-tuple-element.130.part_ref), channel_id=1, source_target_pairs={{0,8},{1,9},{2,10},{3,11},{4,12},{5,13},{6,14},{7,15},{8,0},{9,1},... | collective-permute-start | bytes 393224 | tf_op jit(solution)/shard_map/ppermute | solution.py:371
  61.9 2.2 %collective-permute-done.21.got_ref = bf16[128,512]{1,0:T(8,128)(2,1)S(1)} collective-permute-done((bf16[128,512]{1,0:T(8,128)(2,1)S(1)}, bf16[128,512]{1,0:T(8,128)(2,1)S(1)}, u32[]{:S(2)}, u32[]{:S(2)}) %collective-permute-start.21) | collective-permute-done | bytes 131104 | tf_op jit(solution)/shard_map/ppermute | solution.py:371
  64.1 1.3 %soft_low.3 = (f32[128,512]{1,0:T(8,128)S(1)}, bf16[128,512]{1,0:T(8,128)(2,1)}, f32[512,128]{1,0:T(8,128)}, f32[4,136,128]{2,1,0:T(8,128)S(1)}, f32[4,136,128]{2,1,0:T(8,128)S(1)}) custom-call(f32[128,512]{1,0:T(8,128)S(1)} %get-tuple-element.96.before_ref, bf16[128,512]{1,0:T(8,128)(2,1)S(1)} %get-tuple-element.124.part_ref, ...), custom_call_target="tpu_custom_call" | custom-call | flops 134217728 | bytes 1048576 | tf_op jit(solution)/shard_map/soft_low/pallas_call | solution.py:51
  65.4 0.4 soft_high.3
  66.3 1.2 %collective-permute-done.24.got_ref = f32[4,136,128]{2,1,0:T(8,128)S(1)} collective-permute-done((f32[4,136,128]{2,1,0:T(8,128)S(1)}, f32[4,136,128]{2,1,0:T(8,128)S(1)}, u32[]{:S(2)}, u32[]{:S(2)}) %collective-permute-start.24) | collective-permute-done | bytes 278560 | tf_op jit(solution)/shard_map/ppermute | solution.py:371
  67.6 0.7 collective-permute-start.25
  68.2 1.4 %collective-permute-start.27 = (bf16[2,136,128]{2,1,0:T(8,128)(2,1)S(1)}, bf16[2,136,128]{2,1,0:T(8,128)(2,1)S(1)}, u32[]{:S(2)}, u32[]{:S(2)}) collective-permute-start(bf16[2,136,128]{2,1,0:T(8,128)(2,1)S(1)} %get-tuple-element.137.mine_ref), channel_id=1, source_target_pairs={{0,2},{1,3},{2,0},{3,1},{4,6},{5,7},{6,4},{7,5},{8,10},{9,11},{10,... | collective-permute-start | bytes 208904 | tf_op jit(solution)/shard_map/ppermute | solution.py:371
  69.7 2.9 %collective-permute-done.25.got_ref = bf16[2,136,128]{2,1,0:T(8,128)(2,1)S(1)} collective-permute-done((bf16[2,136,128]{2,1,0:T(8,128)(2,1)S(1)}, bf16[2,136,128]{2,1,0:T(8,128)(2,1)S(1)}, u32[]{:S(2)}, u32[]{:S(2)}) %collective-permute-start.25) | collective-permute-done | bytes 69664 | tf_op jit(solution)/shard_map/ppermute | solution.py:371
  72.6 1.3 %collective-permute-start.26 = (bf16[2,136,128]{2,1,0:T(8,128)(2,1)S(1)}, bf16[2,136,128]{2,1,0:T(8,128)(2,1)S(1)}, u32[]{:S(2)}, u32[]{:S(2)}) collective-permute-start(bf16[2,136,128]{2,1,0:T(8,128)(2,1)S(1)} %hop_p.5.p_ref), channel_id=1, source_target_pairs={{0,4},{1,5},{2,6},{3,7},{4,0},{5,1},{6,2},{7,3},{8,12},{9,13},{10,... | collective-permute-start | bytes 208904 | tf_op jit(solution)/shard_map/ppermute | solution.py:371
  73.9 1.9 %collective-permute-start.28 = (bf16[2,136,128]{2,1,0:T(8,128)(2,1)S(1)}, bf16[2,136,128]{2,1,0:T(8,128)(2,1)S(1)}, u32[]{:S(2)}, u32[]{:S(2)}) collective-permute-start(bf16[2,136,128]{2,1,0:T(8,128)(2,1)S(1)} %hop_q.5.q_ref), channel_id=1, source_target_pairs={{0,4},{1,5},{2,6},{3,7},{4,0},{5,1},{6,2},{7,3},{8,12},{9,13},{10,... | collective-permute-start | bytes 208904 | tf_op jit(solution)/shard_map/ppermute | solution.py:371
  75.8 4.0 %collective-permute-done.26.gp_ref = bf16[2,136,128]{2,1,0:T(8,128)(2,1)S(1)} collective-permute-done((bf16[2,136,128]{2,1,0:T(8,128)(2,1)S(1)}, bf16[2,136,128]{2,1,0:T(8,128)(2,1)S(1)}, u32[]{:S(2)}, u32[]{:S(2)}) %collective-permute-start.26) | collective-permute-done | bytes 69664 | tf_op jit(solution)/shard_map/ppermute | solution.py:371
  79.8 1.5 %collective-permute-done.28.gq_ref = bf16[2,136,128]{2,1,0:T(8,128)(2,1)S(1)} collective-permute-done((bf16[2,136,128]{2,1,0:T(8,128)(2,1)S(1)}, bf16[2,136,128]{2,1,0:T(8,128)(2,1)S(1)}, u32[]{:S(2)}, u32[]{:S(2)}) %collective-permute-start.28) | collective-permute-done | bytes 69664 | tf_op jit(solution)/shard_map/ppermute | solution.py:371
  81.5 0.4 mine.5.part_ref
  81.9 0.9 collective-permute-done.29.delta_ref
  82.8 0.5 change.5
  83.3 1.6 %collective-permute-start.30 = (bf16[128,512]{1,0:T(8,128)(2,1)S(1)}, bf16[128,512]{1,0:T(8,128)(2,1)S(1)}, u32[]{:S(2)}, u32[]{:S(2)}) collective-permute-start(bf16[128,512]{1,0:T(8,128)(2,1)S(1)} %get-tuple-element.145.mine_ref), channel_id=1, source_target_pairs={{0,8},{1,9},{2,10},{3,11},{4,12},{5,13},{6,14},{7,15},{8,0},{9,1},... | collective-permute-start | bytes 393224 | tf_op jit(solution)/shard_map/ppermute | solution.py:371
  84.9 1.2 %collective-permute-start.32 = (bf16[128,512]{1,0:T(8,128)(2,1)S(1)}, bf16[128,512]{1,0:T(8,128)(2,1)S(1)}, u32[]{:S(2)}, u32[]{:S(2)}) collective-permute-start(bf16[128,512]{1,0:T(8,128)(2,1)S(1)} %get-tuple-element.147.mine_ref), channel_id=1, source_target_pairs={{0,16},{1,17},{2,18},{3,19},{4,20},{5,21},{6,22},{7,23},{8,24},{9,... | collective-permute-start | bytes 393224 | tf_op jit(solution)/shard_map/ppermute | solution.py:371
  86.1 2.9 %collective-permute-done.30.got_ref = bf16[128,512]{1,0:T(8,128)(2,1)S(1)} collective-permute-done((bf16[128,512]{1,0:T(8,128)(2,1)S(1)}, bf16[128,512]{1,0:T(8,128)(2,1)S(1)}, u32[]{:S(2)}, u32[]{:S(2)}) %collective-permute-start.30) | collective-permute-done | bytes 131104 | tf_op jit(solution)/shard_map/ppermute | solution.py:371
  89.0 1.3 %collective-permute-start.31 = (bf16[128,512]{1,0:T(8,128)(2,1)S(1)}, bf16[128,512]{1,0:T(8,128)(2,1)S(1)}, u32[]{:S(2)}, u32[]{:S(2)}) collective-permute-start(bf16[128,512]{1,0:T(8,128)(2,1)S(1)} %meet_a.5.part_ref), channel_id=1, source_target_pairs={{0,16},{1,17},{2,18},{3,19},{4,20},{5,21},{6,22},{7,23},{8,24},{9,... | collective-permute-start | bytes 393224 | tf_op jit(solution)/shard_map/ppermute | solution.py:371
  90.3 1.5 %collective-permute-start.33 = (bf16[128,512]{1,0:T(8,128)(2,1)S(1)}, bf16[128,512]{1,0:T(8,128)(2,1)S(1)}, u32[]{:S(2)}, u32[]{:S(2)}) collective-permute-start(bf16[128,512]{1,0:T(8,128)(2,1)S(1)} %meet_b.5.part_ref), channel_id=1, source_target_pairs={{0,8},{1,9},{2,10},{3,11},{4,12},{5,13},{6,14},{7,15},{8,0},{9,1},... | collective-permute-start | bytes 393224 | tf_op jit(solution)/shard_map/ppermute | solution.py:371
  91.9 0.6 coef_out.1
  92.5 0.7 copy.8
  93.2 0.9 collective-permute-done.31.got_ref
  94.2 1.2 %collective-permute-done.33.got_ref = bf16[128,512]{1,0:T(8,128)(2,1)S(1)} collective-permute-done((bf16[128,512]{1,0:T(8,128)(2,1)S(1)}, bf16[128,512]{1,0:T(8,128)(2,1)S(1)}, u32[]{:S(2)}, u32[]{:S(2)}) %collective-permute-start.33) | collective-permute-done | bytes 131104 | tf_op jit(solution)/shard_map/ppermute | solution.py:371
  95.3 0.9 last_high.1
  (52 shorter events, 2.7 us)
Async XLA Ops:
  3.6 1.7 %collective-permute-start = (f32[4,136,128]{2,1,0:T(8,128)S(1)}, f32[4,136,128]{2,1,0:T(8,128)S(1)}, u32[]{:S(2)}, u32[]{:S(2)}) collective-permute-start(f32[4,136,128]{2,1,0:T(8,128)S(1)} %get-tuple-element.80), channel_id=1, source_target_pairs={{0,1},{1,0},{2,3},{3,2},{4,5},{5,4},{6,7},{7,6},{8,9},{9,8},{10,11... | collective-permute-start | bytes 835592 | tf_op jit(solution)/shard_map/ppermute | solution.py:371
  4.1 13.1 %copy-start.1 = (s32[8,16]{1,0:T(8,128)S(1)}, s32[8,16]{1,0:T(8,128)}, u32[]{:S(2)}) copy-start(s32[8,16]{1,0:T(8,128)} %live_ref.3) | copy-start | bytes 1540
  4.1 13.1 %copy-start.2 = (s32[3,1]{0,1:T(1,128)S(1)}, s32[3,1]{0,1:T(1,128)}, u32[]{:S(2)}) copy-start(s32[3,1]{0,1:T(1,128)} %param.11) | copy-start | bytes 40
  5.3 6.1 %collective-permute-start.1 = (bf16[2,136,128]{2,1,0:T(8,128)(2,1)S(1)}, bf16[2,136,128]{2,1,0:T(8,128)(2,1)S(1)}, u32[]{:S(2)}, u32[]{:S(2)}) collective-permute-start(bf16[2,136,128]{2,1,0:T(8,128)(2,1)S(1)} %get-tuple-element.84.mine_ref), channel_id=1, source_target_pairs={{0,2},{1,3},{2,0},{3,1},{4,6},{5,7},{6,4},{7,5},{8,10},{9,11},{10,... | collective-permute-start | bytes 208904 | tf_op jit(solution)/shard_map/ppermute | solution.py:371
  8.3 5.8 %collective-permute-start.3 = (bf16[2,136,128]{2,1,0:T(8,128)(2,1)S(1)}, bf16[2,136,128]{2,1,0:T(8,128)(2,1)S(1)}, u32[]{:S(2)}, u32[]{:S(2)}) collective-permute-start(bf16[2,136,128]{2,1,0:T(8,128)(2,1)S(1)} %get-tuple-element.85.mine_ref), channel_id=1, source_target_pairs={{0,2},{1,3},{2,0},{3,1},{4,6},{5,7},{6,4},{7,5},{8,10},{9,11},{10,... | collective-permute-start | bytes 208904 | tf_op jit(solution)/shard_map/ppermute | solution.py:371
  8.4 7.2 %collective-permute-start.5 = (bf16[128,128]{1,0:T(8,128)(2,1)S(1)}, bf16[128,128]{1,0:T(8,128)(2,1)S(1)}, u32[]{:S(2)}, u32[]{:S(2)}) collective-permute-start(bf16[128,128]{1,0:T(8,128)(2,1)S(1)} %get-tuple-element.90), channel_id=1, source_target_pairs={{0,4},{1,5},{2,6},{3,7},{4,0},{5,1},{6,2},{7,3},{8,12},{9,13},{10,... | collective-permute-start | bytes 98312 | tf_op jit(solution)/shard_map/ppermute | solution.py:371
  11.4 9.3 %collective-permute-start.2 = (bf16[2,136,128]{2,1,0:T(8,128)(2,1)S(1)}, bf16[2,136,128]{2,1,0:T(8,128)(2,1)S(1)}, u32[]{:S(2)}, u32[]{:S(2)}) collective-permute-start(bf16[2,136,128]{2,1,0:T(8,128)(2,1)S(1)} %hop_p.3.p_ref), channel_id=1, source_target_pairs={{0,4},{1,5},{2,6},{3,7},{4,0},{5,1},{6,2},{7,3},{8,12},{9,13},{10,... | collective-permute-start | bytes 208904 | tf_op jit(solution)/shard_map/ppermute | solution.py:371
  14.2 6.5 %collective-permute-start.4 = (bf16[2,136,128]{2,1,0:T(8,128)(2,1)S(1)}, bf16[2,136,128]{2,1,0:T(8,128)(2,1)S(1)}, u32[]{:S(2)}, u32[]{:S(2)}) collective-permute-start(bf16[2,136,128]{2,1,0:T(8,128)(2,1)S(1)} %hop_q.3.q_ref), channel_id=1, source_target_pairs={{0,4},{1,5},{2,6},{3,7},{4,0},{5,1},{6,2},{7,3},{8,12},{9,13},{10,... | collective-permute-start | bytes 208904 | tf_op jit(solution)/shard_map/ppermute | solution.py:371
  15.6 5.0 %collective-permute-start.6 = (bf16[2,128,128]{2,1,0:T(8,128)(2,1)S(1)}, bf16[2,128,128]{2,1,0:T(8,128)(2,1)S(1)}, u32[]{:S(2)}, u32[]{:S(2)}) collective-permute-start(bf16[2,128,128]{2,1,0:T(8,128)(2,1)S(1)} %pad_maximum_fusion), channel_id=1, source_target_pairs={{0,2},{1,3},{2,0},{3,1},{4,6},{5,7},{6,4},{7,5},{8,10},{9,11},{10,... | collective-permute-start | bytes 196616 | tf_op jit(solution)/shard_map/ppermute | solution.py:371
  20.8 1.4 %collective-permute-start.7 = (bf16[128,512]{1,0:T(8,128)(2,1)S(1)}, bf16[128,512]{1,0:T(8,128)(2,1)S(1)}, u32[]{:S(2)}, u32[]{:S(2)}) collective-permute-start(bf16[128,512]{1,0:T(8,128)(2,1)S(1)} %get-tuple-element.92.delta_ref), channel_id=1, source_target_pairs={{0,1},{1,0},{2,3},{3,2},{4,5},{5,4},{6,7},{7,6},{8,9},{9,8},{10,11... | collective-permute-start | bytes 393224 | tf_op jit(solution)/shard_map/ppermute | solution.py:371
  21.3 12.1 %copy-start = (s32[1024]{0:T(1024)S(1)}, s32[1024]{0:T(1024)}, u32[]{:S(2)}) copy-start(s32[1024]{0:T(1024)} %param.8) | copy-start | bytes 12292
  22.7 5.6 %collective-permute-start.8 = (bf16[128,512]{1,0:T(8,128)(2,1)S(1)}, bf16[128,512]{1,0:T(8,128)(2,1)S(1)}, u32[]{:S(2)}, u32[]{:S(2)}) collective-permute-start(bf16[128,512]{1,0:T(8,128)(2,1)S(1)} %get-tuple-element.93.mine_ref), channel_id=1, source_target_pairs={{0,8},{1,9},{2,10},{3,11},{4,12},{5,13},{6,14},{7,15},{8,0},{9,1},... | collective-permute-start | bytes 393224 | tf_op jit(solution)/shard_map/ppermute | solution.py:371
  24.3 5.7 %collective-permute-start.10 = (bf16[128,512]{1,0:T(8,128)(2,1)S(1)}, bf16[128,512]{1,0:T(8,128)(2,1)S(1)}, u32[]{:S(2)}, u32[]{:S(2)}) collective-permute-start(bf16[128,512]{1,0:T(8,128)(2,1)S(1)} %get-tuple-element.99.mine_ref), channel_id=1, source_target_pairs={{0,16},{1,17},{2,18},{3,19},{4,20},{5,21},{6,22},{7,23},{8,24},{9,... | collective-permute-start | bytes 393224 | tf_op jit(solution)/shard_map/ppermute | solution.py:371
  28.4 5.0 %collective-permute-start.9 = (bf16[128,512]{1,0:T(8,128)(2,1)S(1)}, bf16[128,512]{1,0:T(8,128)(2,1)S(1)}, u32[]{:S(2)}, u32[]{:S(2)}) collective-permute-start(bf16[128,512]{1,0:T(8,128)(2,1)S(1)} %get-tuple-element.94.part_ref), channel_id=1, source_target_pairs={{0,16},{1,17},{2,18},{3,19},{4,20},{5,21},{6,22},{7,23},{8,24},{9,... | collective-permute-start | bytes 393224 | tf_op jit(solution)/shard_map/ppermute | solution.py:371
  30.1 5.0 %collective-permute-start.11 = (bf16[128,512]{1,0:T(8,128)(2,1)S(1)}, bf16[128,512]{1,0:T(8,128)(2,1)S(1)}, u32[]{:S(2)}, u32[]{:S(2)}) collective-permute-start(bf16[128,512]{1,0:T(8,128)(2,1)S(1)} %get-tuple-element.100.part_ref), channel_id=1, source_target_pairs={{0,8},{1,9},{2,10},{3,11},{4,12},{5,13},{6,14},{7,15},{8,0},{9,1},... | collective-permute-start | bytes 393224 | tf_op jit(solution)/shard_map/ppermute | solution.py:371
  35.6 1.6 %collective-permute-start.12 = (f32[4,136,128]{2,1,0:T(8,128)S(1)}, f32[4,136,128]{2,1,0:T(8,128)S(1)}, u32[]{:S(2)}, u32[]{:S(2)}) collective-permute-start(f32[4,136,128]{2,1,0:T(8,128)S(1)} %get-tuple-element.105), channel_id=1, source_target_pairs={{0,1},{1,0},{2,3},{3,2},{4,5},{5,4},{6,7},{7,6},{8,9},{9,8},{10,11... | collective-permute-start | bytes 835592 | tf_op jit(solution)/shard_map/ppermute | solution.py:371
  37.2 5.0 %collective-permute-start.13 = (bf16[2,136,128]{2,1,0:T(8,128)(2,1)S(1)}, bf16[2,136,128]{2,1,0:T(8,128)(2,1)S(1)}, u32[]{:S(2)}, u32[]{:S(2)}) collective-permute-start(bf16[2,136,128]{2,1,0:T(8,128)(2,1)S(1)} %get-tuple-element.109.mine_ref), channel_id=1, source_target_pairs={{0,2},{1,3},{2,0},{3,1},{4,6},{5,7},{6,4},{7,5},{8,10},{9,11},{10,... | collective-permute-start | bytes 208904 | tf_op jit(solution)/shard_map/ppermute | solution.py:371
  38.1 5.9 %collective-permute-start.15 = (bf16[2,136,128]{2,1,0:T(8,128)(2,1)S(1)}, bf16[2,136,128]{2,1,0:T(8,128)(2,1)S(1)}, u32[]{:S(2)}, u32[]{:S(2)}) collective-permute-start(bf16[2,136,128]{2,1,0:T(8,128)(2,1)S(1)} %get-tuple-element.110.mine_ref), channel_id=1, source_target_pairs={{0,2},{1,3},{2,0},{3,1},{4,6},{5,7},{6,4},{7,5},{8,10},{9,11},{10,... | collective-permute-start | bytes 208904 | tf_op jit(solution)/shard_map/ppermute | solution.py:371
  39.3 6.4 %collective-permute-start.17 = (bf16[128,128]{1,0:T(8,128)(2,1)S(1)}, bf16[128,128]{1,0:T(8,128)(2,1)S(1)}, u32[]{:S(2)}, u32[]{:S(2)}) collective-permute-start(bf16[128,128]{1,0:T(8,128)(2,1)S(1)} %get-tuple-element.116), channel_id=1, source_target_pairs={{0,4},{1,5},{2,6},{3,7},{4,0},{5,1},{6,2},{7,3},{8,12},{9,13},{10,... | collective-permute-start | bytes 98312 | tf_op jit(solution)/shard_map/ppermute | solution.py:371
  42.3 8.9 %collective-permute-start.14 = (bf16[2,136,128]{2,1,0:T(8,128)(2,1)S(1)}, bf16[2,136,128]{2,1,0:T(8,128)(2,1)S(1)}, u32[]{:S(2)}, u32[]{:S(2)}) collective-permute-start(bf16[2,136,128]{2,1,0:T(8,128)(2,1)S(1)} %hop_p.4.p_ref), channel_id=1, source_target_pairs={{0,4},{1,5},{2,6},{3,7},{4,0},{5,1},{6,2},{7,3},{8,12},{9,13},{10,... | collective-permute-start | bytes 208904 | tf_op jit(solution)/shard_map/ppermute | solution.py:371
  44.0 7.3 %collective-permute-start.16 = (bf16[2,136,128]{2,1,0:T(8,128)(2,1)S(1)}, bf16[2,136,128]{2,1,0:T(8,128)(2,1)S(1)}, u32[]{:S(2)}, u32[]{:S(2)}) collective-permute-start(bf16[2,136,128]{2,1,0:T(8,128)(2,1)S(1)} %hop_q.4.q_ref), channel_id=1, source_target_pairs={{0,4},{1,5},{2,6},{3,7},{4,0},{5,1},{6,2},{7,3},{8,12},{9,13},{10,... | collective-permute-start | bytes 208904 | tf_op jit(solution)/shard_map/ppermute | solution.py:371
  45.8 5.4 %collective-permute-start.18 = (bf16[2,128,128]{2,1,0:T(8,128)(2,1)S(1)}, bf16[2,128,128]{2,1,0:T(8,128)(2,1)S(1)}, u32[]{:S(2)}, u32[]{:S(2)}) collective-permute-start(bf16[2,128,128]{2,1,0:T(8,128)(2,1)S(1)} %pad_maximum_fusion.1), channel_id=1, source_target_pairs={{0,2},{1,3},{2,0},{3,1},{4,6},{5,7},{6,4},{7,5},{8,10},{9,11},{10,... | collective-permute-start | bytes 196616 | tf_op jit(solution)/shard_map/ppermute | solution.py:371
  51.5 1.4 %collective-permute-start.19 = (bf16[128,512]{1,0:T(8,128)(2,1)S(1)}, bf16[128,512]{1,0:T(8,128)(2,1)S(1)}, u32[]{:S(2)}, u32[]{:S(2)}) collective-permute-start(bf16[128,512]{1,0:T(8,128)(2,1)S(1)} %get-tuple-element.118.delta_ref), channel_id=1, source_target_pairs={{0,1},{1,0},{2,3},{3,2},{4,5},{5,4},{6,7},{7,6},{8,9},{9,8},{10,11... | collective-permute-start | bytes 393224 | tf_op jit(solution)/shard_map/ppermute | solution.py:371
  53.4 5.6 %collective-permute-start.20 = (bf16[128,512]{1,0:T(8,128)(2,1)S(1)}, bf16[128,512]{1,0:T(8,128)(2,1)S(1)}, u32[]{:S(2)}, u32[]{:S(2)}) collective-permute-start(bf16[128,512]{1,0:T(8,128)(2,1)S(1)} %get-tuple-element.123.mine_ref), channel_id=1, source_target_pairs={{0,8},{1,9},{2,10},{3,11},{4,12},{5,13},{6,14},{7,15},{8,0},{9,1},... | collective-permute-start | bytes 393224 | tf_op jit(solution)/shard_map/ppermute | solution.py:371
  54.9 5.4 %collective-permute-start.22 = (bf16[128,512]{1,0:T(8,128)(2,1)S(1)}, bf16[128,512]{1,0:T(8,128)(2,1)S(1)}, u32[]{:S(2)}, u32[]{:S(2)}) collective-permute-start(bf16[128,512]{1,0:T(8,128)(2,1)S(1)} %get-tuple-element.129.mine_ref), channel_id=1, source_target_pairs={{0,16},{1,17},{2,18},{3,19},{4,20},{5,21},{6,22},{7,23},{8,24},{9,... | collective-permute-start | bytes 393224 | tf_op jit(solution)/shard_map/ppermute | solution.py:371
  59.1 5.0 %collective-permute-start.21 = (bf16[128,512]{1,0:T(8,128)(2,1)S(1)}, bf16[128,512]{1,0:T(8,128)(2,1)S(1)}, u32[]{:S(2)}, u32[]{:S(2)}) collective-permute-start(bf16[128,512]{1,0:T(8,128)(2,1)S(1)} %get-tuple-element.124.part_ref), channel_id=1, source_target_pairs={{0,16},{1,17},{2,18},{3,19},{4,20},{5,21},{6,22},{7,23},{8,24},{9,... | collective-permute-start | bytes 393224 | tf_op jit(solution)/shard_map/ppermute | solution.py:371
  60.4 5.0 %collective-permute-start.23 = (bf16[128,512]{1,0:T(8,128)(2,1)S(1)}, bf16[128,512]{1,0:T(8,128)(2,1)S(1)}, u32[]{:S(2)}, u32[]{:S(2)}) collective-permute-start(bf16[128,512]{1,0:T(8,128)(2,1)S(1)} %get-tuple-element.130.part_ref), channel_id=1, source_target_pairs={{0,8},{1,9},{2,10},{3,11},{4,12},{5,13},{6,14},{7,15},{8,0},{9,1},... | collective-permute-start | bytes 393224 | tf_op jit(solution)/shard_map/ppermute | solution.py:371
  65.9 1.6 %collective-permute-start.24 = (f32[4,136,128]{2,1,0:T(8,128)S(1)}, f32[4,136,128]{2,1,0:T(8,128)S(1)}, u32[]{:S(2)}, u32[]{:S(2)}) collective-permute-start(f32[4,136,128]{2,1,0:T(8,128)S(1)} %get-tuple-element.135), channel_id=1, source_target_pairs={{0,1},{1,0},{2,3},{3,2},{4,5},{5,4},{6,7},{7,6},{8,9},{9,8},{10,11... | collective-permute-start | bytes 835592 | tf_op jit(solution)/shard_map/ppermute | solution.py:371
  67.6 5.0 %collective-permute-start.25 = (bf16[2,136,128]{2,1,0:T(8,128)(2,1)S(1)}, bf16[2,136,128]{2,1,0:T(8,128)(2,1)S(1)}, u32[]{:S(2)}, u32[]{:S(2)}) collective-permute-start(bf16[2,136,128]{2,1,0:T(8,128)(2,1)S(1)} %get-tuple-element.136.mine_ref), channel_id=1, source_target_pairs={{0,2},{1,3},{2,0},{3,1},{4,6},{5,7},{6,4},{7,5},{8,10},{9,11},{10,... | collective-permute-start | bytes 208904 | tf_op jit(solution)/shard_map/ppermute | solution.py:371
  68.2 5.7 %collective-permute-start.27 = (bf16[2,136,128]{2,1,0:T(8,128)(2,1)S(1)}, bf16[2,136,128]{2,1,0:T(8,128)(2,1)S(1)}, u32[]{:S(2)}, u32[]{:S(2)}) collective-permute-start(bf16[2,136,128]{2,1,0:T(8,128)(2,1)S(1)} %get-tuple-element.137.mine_ref), channel_id=1, source_target_pairs={{0,2},{1,3},{2,0},{3,1},{4,6},{5,7},{6,4},{7,5},{8,10},{9,11},{10,... | collective-permute-start | bytes 208904 | tf_op jit(solution)/shard_map/ppermute | solution.py:371
  72.6 7.1 %collective-permute-start.26 = (bf16[2,136,128]{2,1,0:T(8,128)(2,1)S(1)}, bf16[2,136,128]{2,1,0:T(8,128)(2,1)S(1)}, u32[]{:S(2)}, u32[]{:S(2)}) collective-permute-start(bf16[2,136,128]{2,1,0:T(8,128)(2,1)S(1)} %hop_p.5.p_ref), channel_id=1, source_target_pairs={{0,4},{1,5},{2,6},{3,7},{4,0},{5,1},{6,2},{7,3},{8,12},{9,13},{10,... | collective-permute-start | bytes 208904 | tf_op jit(solution)/shard_map/ppermute | solution.py:371
  73.9 7.3 %collective-permute-start.28 = (bf16[2,136,128]{2,1,0:T(8,128)(2,1)S(1)}, bf16[2,136,128]{2,1,0:T(8,128)(2,1)S(1)}, u32[]{:S(2)}, u32[]{:S(2)}) collective-permute-start(bf16[2,136,128]{2,1,0:T(8,128)(2,1)S(1)} %hop_q.5.q_ref), channel_id=1, source_target_pairs={{0,4},{1,5},{2,6},{3,7},{4,0},{5,1},{6,2},{7,3},{8,12},{9,13},{10,... | collective-permute-start | bytes 208904 | tf_op jit(solution)/shard_map/ppermute | solution.py:371
  81.4 1.4 %collective-permute-start.29 = (bf16[128,512]{1,0:T(8,128)(2,1)S(1)}, bf16[128,512]{1,0:T(8,128)(2,1)S(1)}, u32[]{:S(2)}, u32[]{:S(2)}) collective-permute-start(bf16[128,512]{1,0:T(8,128)(2,1)S(1)} %get-tuple-element.140.delta_ref), channel_id=1, source_target_pairs={{0,1},{1,0},{2,3},{3,2},{4,5},{5,4},{6,7},{7,6},{8,9},{9,8},{10,11... | collective-permute-start | bytes 393224 | tf_op jit(solution)/shard_map/ppermute | solution.py:371
  83.3 5.6 %collective-permute-start.30 = (bf16[128,512]{1,0:T(8,128)(2,1)S(1)}, bf16[128,512]{1,0:T(8,128)(2,1)S(1)}, u32[]{:S(2)}, u32[]{:S(2)}) collective-permute-start(bf16[128,512]{1,0:T(8,128)(2,1)S(1)} %get-tuple-element.145.mine_ref), channel_id=1, source_target_pairs={{0,8},{1,9},{2,10},{3,11},{4,12},{5,13},{6,14},{7,15},{8,0},{9,1},... | collective-permute-start | bytes 393224 | tf_op jit(solution)/shard_map/ppermute | solution.py:371
  84.9 5.4 %collective-permute-start.32 = (bf16[128,512]{1,0:T(8,128)(2,1)S(1)}, bf16[128,512]{1,0:T(8,128)(2,1)S(1)}, u32[]{:S(2)}, u32[]{:S(2)}) collective-permute-start(bf16[128,512]{1,0:T(8,128)(2,1)S(1)} %get-tuple-element.147.mine_ref), channel_id=1, source_target_pairs={{0,16},{1,17},{2,18},{3,19},{4,20},{5,21},{6,22},{7,23},{8,24},{9,... | collective-permute-start | bytes 393224 | tf_op jit(solution)/shard_map/ppermute | solution.py:371
  89.0 5.0 %collective-permute-start.31 = (bf16[128,512]{1,0:T(8,128)(2,1)S(1)}, bf16[128,512]{1,0:T(8,128)(2,1)S(1)}, u32[]{:S(2)}, u32[]{:S(2)}) collective-permute-start(bf16[128,512]{1,0:T(8,128)(2,1)S(1)} %meet_a.5.part_ref), channel_id=1, source_target_pairs={{0,16},{1,17},{2,18},{3,19},{4,20},{5,21},{6,22},{7,23},{8,24},{9,... | collective-permute-start | bytes 393224 | tf_op jit(solution)/shard_map/ppermute | solution.py:371
  90.3 5.0 %collective-permute-start.33 = (bf16[128,512]{1,0:T(8,128)(2,1)S(1)}, bf16[128,512]{1,0:T(8,128)(2,1)S(1)}, u32[]{:S(2)}, u32[]{:S(2)}) collective-permute-start(bf16[128,512]{1,0:T(8,128)(2,1)S(1)} %meet_b.5.part_ref), channel_id=1, source_target_pairs={{0,8},{1,9},{2,10},{3,11},{4,12},{5,13},{6,14},{7,15},{8,0},{9,1},... | collective-permute-start | bytes 393224 | tf_op jit(solution)/shard_map/ppermute | solution.py:371

commit v9 on v8

--- a/solution.py
+++ b/solution.py
@@ -14,7 +14,7 @@
 TILE = 128
 NB = HALF // TILE
 PB = NB // 2
-ROWS = C + 8
+TAIL = 8
 
 ridge = 0.002
 lasso = 0.005
@@ -124,10 +124,28 @@
     return jnp.concatenate([mine.reshape(rows, HALF), other.reshape(rows, HALF)], axis=1)
 
 
+def stack_rows(rows):
+    if len(rows) < TAIL:
+        rows = rows + [jnp.zeros((TAIL - len(rows), TILE), F32)]
+    return jnp.concatenate(rows, axis=0)
+
+
+def split_rows(curvs):
+    rows = []
+    for curv in curvs:
+        high = curv.astype(BF16).astype(F32)
+        rows += [high, curv - high]
+    return stack_rows(rows).astype(BF16)
+
+
+def block(k):
+    return slice(k * C, (k + 1) * C)
+
+
 def half_sums(res_t, spread_ref, x_ref, start, first, g_ref, so_far=None):
     rows = spread_ref.shape[0]
     grad = jnp.dot(res_t, x_ref[start : start + rows, first : first + HALF], preferred_element_type=F32)
-    row = lax.broadcasted_iota(jnp.int32, (8, TILE), 0)
+    curvs = []
     for k in range(NB):
         lanes = slice(first + k * TILE, first + (k + 1) * TILE)
         acc = jnp.zeros((8, TILE), F32)
@@ -135,12 +153,13 @@
             x = x_ref[start + r * TILE : start + (r + 1) * TILE, lanes].astype(F32)
             term = x * x * spread_ref[here, :]
             acc = acc + jnp.sum(term.reshape(TILE // 8, 8, TILE), axis=0)
-        total = jnp.where(row == 0, jnp.sum(acc, axis=0, keepdims=True), 0.0)
-        here = grad[:, k * TILE : (k + 1) * TILE]
+        curv = jnp.sum(acc, axis=0, keepdims=True)
+        part = grad[:, k * TILE : (k + 1) * TILE]
         if so_far is not None:
-            here, total = here + so_far[k, 0:C, :], total + so_far[k, C:ROWS, :]
-        g_ref[k, 0:C, :] = here
-        g_ref[k, C:ROWS, :] = total
+            part, curv = part + so_far[block(k), :], curv + so_far[NB * C + k : NB * C + k + 1, :]
+        g_ref[block(k), :] = part.astype(g_ref.dtype)
+        curvs.append(curv)
+    g_ref[NB * C : NB * C + TAIL, :] = split_rows(curvs) if g_ref.dtype == BF16 else stack_rows(curvs)
 
 
 def soft_rows(score, labels, here, res_ref, spread_ref):
@@ -214,7 +233,7 @@
         soft_rows(score, lab_ref[row : row + 1, :], here, res_ref, spread_ref)
 
 
-def next_low_body(before_ref, part_ref, got_ref, lab_ref, x_ref, score_ref, res_ref, spread_ref, g_ref, own_ref):
+def next_low_body(before_ref, part_ref, got_ref, lab_ref, x_ref, score_ref, g_ref, own_ref, res_ref, spread_ref):
     next_rows(0, before_ref, part_ref, got_ref, lab_ref, score_ref, res_ref, spread_ref)
     half_sums(res_ref[...], spread_ref, x_ref, 0, HALF, g_ref)
     half_sums(res_ref[...], spread_ref, x_ref, 0, 0, own_ref)
@@ -253,29 +272,33 @@
     half_sums(res_ref[...], spread_ref, x_ref, spread_ref.shape[0], 0, g_ref, so_far)
 
 
-def encode(k, grad, curv, out_ref):
-    out_ref[k, 0:C, :] = grad.astype(BF16)
-    high = curv.astype(BF16).astype(F32)
-    low = curv - high
-    row = lax.broadcasted_iota(jnp.int32, (8, TILE), 0)
-    tail = jnp.where(row == 0, high, jnp.where(row == 1, low, 0.0))
-    out_ref[k, C:ROWS, :] = tail.astype(BF16)
-
-
 def pair_body(own_ref, got_ref, p_ref, q_ref):
+    tail = got_ref[NB * C : NB * C + TAIL, :].astype(F32)
+    curvs = []
     for k in range(NB):
-        total = own_ref[k] + got_ref[k]
-        encode(k if k < PB else k - PB, total[0:C], total[C : C + 1], p_ref if k < PB else q_ref)
-
-
-def decode_sum(k, mine_ref, got_ref):
-    total = mine_ref[k].astype(F32) + got_ref[k].astype(F32)
-    return total[0:C], total[C : C + 1] + total[C + 1 : C + 2]
+        total = own_ref[block(k), :] + got_ref[block(k), :].astype(F32)
+        ref, j = (p_ref, k) if k < PB else (q_ref, k - PB)
+        ref[block(j), :] = total.astype(BF16)
+        curvs.append(own_ref[NB * C + k : NB * C + k + 1, :] + tail[2 * k : 2 * k + 1] + tail[2 * k + 1 : 2 * k + 2])
+    p_ref[PB * C : PB * C + TAIL, :] = split_rows(curvs[:PB])
+    q_ref[(NB - PB) * C : (NB - PB) * C + TAIL, :] = split_rows(curvs[PB:])
+
+
+def sum_of(mine_ref, got_ref, rows):
+    return mine_ref[rows, :].astype(F32) + got_ref[rows, :].astype(F32)
+
+
+def curvs_of(mine_ref, got_ref):
+    n = mine_ref.shape[0] // C
+    tail = sum_of(mine_ref, got_ref, slice(n * C, n * C + TAIL))
+    return [tail[2 * j : 2 * j + 1] + tail[2 * j + 1 : 2 * j + 2] for j in range(n)]
 
 
 def hop_body(mine_ref, got_ref, out_ref):
-    for k in range(out_ref.shape[0]):
-        encode(k, *decode_sum(k, mine_ref, got_ref), out_ref)
+    curvs = curvs_of(mine_ref, got_ref)
+    for j in range(len(curvs)):
+        out_ref[block(j), :] = sum_of(mine_ref, got_ref, block(j)).astype(BF16)
+    out_ref[len(curvs) * C : len(curvs) * C + TAIL, :] = split_rows(curvs)
 
 
 def place_body(far_ref, near_ref, coef_ref, out_ref):
@@ -286,8 +309,14 @@
     out_ref[jnp.bitwise_xor(place, 3)] = near_ref[1].astype(F32)
 
 
-def step_coef(count, k, mine_ref, got_ref, old):
-    grad, curv = decode_sum(k, mine_ref, got_ref)
+def totals(p_ref, gp_ref, q_ref, gq_ref):
+    both = []
+    for pair in ((p_ref, gp_ref), (q_ref, gq_ref)):
+        both += [(sum_of(*pair, block(j)), curv) for j, curv in enumerate(curvs_of(*pair))]
+    return both
+
+
+def step_coef(count, grad, curv, old):
     inverse = 1.0 / (curv / count + ridge)
     shifted = old - grad * (inverse / count)
     limit = lasso * inverse
@@ -295,21 +324,19 @@
 
 
 def prox_first_body(count, p_ref, gp_ref, q_ref, gq_ref, old_ref, new_ref, delta_ref):
-    for k in range(NB):
+    for k, (grad, curv) in enumerate(totals(p_ref, gp_ref, q_ref, gq_ref)):
         old = old_ref[k]
-        chunk = (p_ref, gp_ref) if k < PB else (q_ref, gq_ref)
-        new = step_coef(count, k if k < PB else k - PB, *chunk, old)
+        new = step_coef(count, grad, curv, old)
         new_ref[k] = new
         delta_ref[:, k * TILE : (k + 1) * TILE] = (new - old).astype(BF16)
 
 
 def prox_body(count, same_ref, p_ref, gp_ref, q_ref, gq_ref, old0_ref, old1_ref, new0_ref, new1_ref, delta_ref):
     same = jnp.broadcast_to(same_ref[0:1, :], (C, TILE)) > 0.5
-    for k in range(NB):
+    for k, (grad, curv) in enumerate(totals(p_ref, gp_ref, q_ref, gq_ref)):
         old0, old1 = old0_ref[k], old1_ref[k]
         old = jnp.where(same, old0, old1)
-        chunk = (p_ref, gp_ref) if k < PB else (q_ref, gq_ref)
-        new = step_coef(count, k if k < PB else k - PB, *chunk, old)
+        new = step_coef(count, grad, curv, old)
         new0_ref[k] = jnp.where(same, new, old0)
         new1_ref[k] = jnp.where(same, old1, new)
         delta_ref[:, k * TILE : (k + 1) * TILE] = (new - old).astype(BF16)
@@ -428,16 +455,17 @@
     x_shape = sds((rows, BLOCK), BF16)
     soft_shapes = (
         sds((C, rows // 2), F32), sds((C, rows // 2), F32),
-        sds((C, rows), BF16), sds((rows, TILE), F32), sds((NB, ROWS, TILE), F32),
+        sds((C, rows), BF16), sds((rows, TILE), F32), sds((NB * C + TAIL, TILE), BF16),
     )
-    g_shape = soft_shapes[-1]
-    next_shapes = (soft_shapes[0], sds((C, rows // 2), BF16), sds((rows // 2, TILE), F32), g_shape)
+    g_shape = sds((NB * C + TAIL, TILE), F32)
+    score_shape, g_sent_shape = soft_shapes[0], soft_shapes[-1]
+    rows_shapes = (sds((C, rows // 2), BF16), sds((rows // 2, TILE), F32))
     old_shape, delta_shape = sds((NB, C, TILE), F32), sds((C, HALF), BF16)
     part_shape, half = sds((rows, C), F32), (C, rows // 2)
     own_shape, send_shape, same_shape = sds((C, TILE), F32), sds((C, TILE), BF16), sds((8, TILE), F32)
     flops, nbytes = 2 * rows * HALF * C, 1 << 20
 
-    p_shape, q_shape = sds((PB, ROWS, TILE), BF16), sds((NB - PB, ROWS, TILE), BF16)
+    p_shape, q_shape = sds((PB * C + TAIL, TILE), BF16), sds(((NB - PB) * C + TAIL, TILE), BF16)
 
     if aligned:
         x, low, high, res_t, spread, g_other, *rest = call(
@@ -469,11 +497,12 @@
         if step > 0:
             x = following
             a, got_a, b, got_b = halves
-            low, _, _, g_other, g_own = call(
-                next_low_body, next_shapes + (g_shape,), vmem(5), "soft_low", flops, nbytes
+            low, g_other, g_own = call(
+                next_low_body, (score_shape, g_shape, g_shape), vmem(5), "soft_low", flops, nbytes,
+                scratch_shapes=list(rows_shapes),
             )(low, a, got_a, labels, x)
             high, res_t, spread, g_other = call(
-                next_high_body, next_shapes, vmem(6), "soft_high", flops // 2, nbytes
+                next_high_body, (score_shape, *rows_shapes, g_sent_shape), vmem(6), "soft_high", flops // 2, nbytes
             )(high, b, got_b, labels, x, g_other)
             got = swap_core(g_other)
             g_own = call(own_high_body, g_shape, vmem(4), "own", flops // 2, nbytes)(res_t, spread, x, g_own)

time: 96.4 us -> 94.9 us (0.984)
  starting transfers between devices: 44.6 us -> 42.8 us
  waiting for transfers between devices: 32.4 us -> 34 us
  Pallas kernels: 17.7 us -> 16.3 us
    ppermute x34, starting transfers between devices: 44.6 us -> 42.8 us  [swap(): return lax.ppermute(x, ('feat', 'ex'), pairs)]
    ppermute x34, waiting for transfers between devices: 32.4 us -> 34 us  [swap(): return lax.ppermute(x, ('feat', 'ex'), pairs)]
    pallas_call x38, Pallas kernels: 16.8 us -> 15.4 us  [run(): f(*(x if spec.memory_space == pltpu.SMEM else pltpu.with_memory_space_con...]
  transfers between devices with their start and end apart: 34 -> 34, of which waited for: 20 -> 21; matrix products, arithmetic and copies ran while one was open for 1% -> 1% of each run, Pallas kernels for 11% -> 10%
where the time goes in v9:
time: 94.9 us; the launch traced here: 94.7 us
  starting transfers between devices  42.8 us (45%)
  waiting for transfers between devices  34 us (36%)
  Pallas kernels  16.3 us (17%)
    ppermute x34, starting transfers between devices, swap(): return lax.ppermute(x, ('feat', 'ex'), pairs)  42.8 us
    ppermute x34, waiting for transfers between devices, swap(): return lax.ppermute(x, ('feat', 'ex'), pairs)  34 us
    pallas_call x38, Pallas kernels, run(): f(*(x if spec.memory_space == pltpu.SMEM else pltpu.with_memory_space_con...  15.4 us
  transfers between devices with their start and end apart: 34, of which 21 were waited for; matrix products, arithmetic and copies ran while one was open for 1% of the time, Pallas kernels for 10%

profile of v9, /device:TPU:0, one launch (start us, length us, event | category | flops | bytes accessed | tf_op | source)
XLA Modules:
  0.0 94.7 jit_solution(15788416354110856653)
XLA Ops:
  0.6 3.0 %soft_first.1 = (bf16[1024,1024]{1,0:T(8,128)(2,1)S(1)}, f32[128,512]{1,0:T(8,128)S(1)}, f32[128,512]{1,0:T(8,128)S(1)}, bf16[128,1024]{1,0:T(8,128)(2,1)S(1)}, ...) custom-call(s32[1,3]{1,0:T(1,128)} %bitcast.15, ...), custom_call_target="tpu_custom_call" | custom-call | flops 134217728 | bytes 1048576 | tf_op jit(solution)/shard_map/soft_first/pallas_call | solution.py:51
  3.6 0.5 collective-permute-start
  4.1 0.5 own.3.own_ref
  4.7 0.5 collective-permute-done.got_ref
  5.2 3.0 %collective-permute-start.1 = (bf16[264,128]{1,0:T(8,128)(2,1)S(1)}, bf16[264,128]{1,0:T(8,128)(2,1)S(1)}, u32[]{:S(2)}, u32[]{:S(2)}) collective-permute-start(bf16[264,128]{1,0:T(8,128)(2,1)S(1)} %get-tuple-element.84.mine_ref), channel_id=1, source_target_pairs={{0,2},{1,3},{2,0},{3,1},{4,6},{5,7},{6,4},{7,5},{8,10},{9,11},{10,... | collective-permute-start | bytes 202760 | tf_op jit(solution)/shard_map/ppermute | solution.py:398
  8.2 3.0 %collective-permute-start.5 = (bf16[128,128]{1,0:T(8,128)(2,1)S(1)}, bf16[128,128]{1,0:T(8,128)(2,1)S(1)}, u32[]{:S(2)}, u32[]{:S(2)}) collective-permute-start(bf16[128,128]{1,0:T(8,128)(2,1)S(1)} %get-tuple-element.90), channel_id=1, source_target_pairs={{0,4},{1,5},{2,6},{3,7},{4,0},{5,1},{6,2},{7,3},{8,12},{9,13},{10,... | collective-permute-start | bytes 98312 | tf_op jit(solution)/shard_map/ppermute | solution.py:398
  11.2 2.6 %collective-permute-start.2 = (bf16[264,128]{1,0:T(8,128)(2,1)S(1)}, bf16[264,128]{1,0:T(8,128)(2,1)S(1)}, u32[]{:S(2)}, u32[]{:S(2)}) collective-permute-start(bf16[264,128]{1,0:T(8,128)(2,1)S(1)} %hop_p.3.p_ref), channel_id=1, source_target_pairs={{0,4},{1,5},{2,6},{3,7},{4,0},{5,1},{6,2},{7,3},{8,12},{9,13},{10,... | collective-permute-start | bytes 202760 | tf_op jit(solution)/shard_map/ppermute | solution.py:398
  13.9 1.4 %collective-permute-start.4 = (bf16[264,128]{1,0:T(8,128)(2,1)S(1)}, bf16[264,128]{1,0:T(8,128)(2,1)S(1)}, u32[]{:S(2)}, u32[]{:S(2)}) collective-permute-start(bf16[264,128]{1,0:T(8,128)(2,1)S(1)} %hop_q.3.q_ref), channel_id=1, source_target_pairs={{0,4},{1,5},{2,6},{3,7},{4,0},{5,1},{6,2},{7,3},{8,12},{9,13},{10,... | collective-permute-start | bytes 202760 | tf_op jit(solution)/shard_map/ppermute | solution.py:398
  15.4 1.5 %collective-permute-start.6 = (bf16[2,128,128]{2,1,0:T(8,128)(2,1)S(1)}, bf16[2,128,128]{2,1,0:T(8,128)(2,1)S(1)}, u32[]{:S(2)}, u32[]{:S(2)}) collective-permute-start(bf16[2,128,128]{2,1,0:T(8,128)(2,1)S(1)} %pad_maximum_fusion), channel_id=1, source_target_pairs={{0,2},{1,3},{2,0},{3,1},{4,6},{5,7},{6,4},{7,5},{8,10},{9,11},{10,... | collective-permute-start | bytes 196616 | tf_op jit(solution)/shard_map/ppermute | solution.py:398
  16.9 2.3 %prep.2.x_ref = bf16[1024,1024]{1,0:T(8,128)(2,1)S(1)} custom-call(s32[1,3]{1,0:T(1,128)S(1)} %bitcast.16, s32[8,16]{1,0:T(8,128)S(1)} %copy-done.1, bf16[1024,2048]{1,0:T(8,128)(2,1)} %x_ref.3), custom_call_target="tpu_custom_call" | custom-call | bytes 4194304 | tf_op jit(solution)/shard_map/prep/pallas_call | solution.py:51
  19.2 1.1 %collective-permute-done.6.near_ref = bf16[2,128,128]{2,1,0:T(8,128)(2,1)S(1)} collective-permute-done((bf16[2,128,128]{2,1,0:T(8,128)(2,1)S(1)}, bf16[2,128,128]{2,1,0:T(8,128)(2,1)S(1)}, u32[]{:S(2)}, u32[]{:S(2)}) %collective-permute-start.6) | collective-permute-done | bytes 65568 | tf_op jit(solution)/shard_map/ppermute | solution.py:398
  20.9 0.9 collective-permute-done.7.delta_ref
  21.8 0.5 change.3
  22.3 1.6 %collective-permute-start.8 = (bf16[128,512]{1,0:T(8,128)(2,1)S(1)}, bf16[128,512]{1,0:T(8,128)(2,1)S(1)}, u32[]{:S(2)}, u32[]{:S(2)}) collective-permute-start(bf16[128,512]{1,0:T(8,128)(2,1)S(1)} %get-tuple-element.93.mine_ref), channel_id=1, source_target_pairs={{0,8},{1,9},{2,10},{3,11},{4,12},{5,13},{6,14},{7,15},{8,0},{9,1},... | collective-permute-start | bytes 393224 | tf_op jit(solution)/shard_map/ppermute | solution.py:398
  23.9 1.5 %collective-permute-start.10 = (bf16[128,512]{1,0:T(8,128)(2,1)S(1)}, bf16[128,512]{1,0:T(8,128)(2,1)S(1)}, u32[]{:S(2)}, u32[]{:S(2)}) collective-permute-start(bf16[128,512]{1,0:T(8,128)(2,1)S(1)} %get-tuple-element.99.mine_ref), channel_id=1, source_target_pairs={{0,16},{1,17},{2,18},{3,19},{4,20},{5,21},{6,22},{7,23},{8,24},{9,... | collective-permute-start | bytes 393224 | tf_op jit(solution)/shard_map/ppermute | solution.py:398
  25.4 2.5 %collective-permute-done.8.got_ref = bf16[128,512]{1,0:T(8,128)(2,1)S(1)} collective-permute-done((bf16[128,512]{1,0:T(8,128)(2,1)S(1)}, bf16[128,512]{1,0:T(8,128)(2,1)S(1)}, u32[]{:S(2)}, u32[]{:S(2)}) %collective-permute-start.8) | collective-permute-done | bytes 131104 | tf_op jit(solution)/shard_map/ppermute | solution.py:398
  28.0 1.6 %collective-permute-start.9 = (bf16[128,512]{1,0:T(8,128)(2,1)S(1)}, bf16[128,512]{1,0:T(8,128)(2,1)S(1)}, u32[]{:S(2)}, u32[]{:S(2)}) collective-permute-start(bf16[128,512]{1,0:T(8,128)(2,1)S(1)} %get-tuple-element.94.part_ref), channel_id=1, source_target_pairs={{0,16},{1,17},{2,18},{3,19},{4,20},{5,21},{6,22},{7,23},{8,24},{9,... | collective-permute-start | bytes 393224 | tf_op jit(solution)/shard_map/ppermute | solution.py:398
  29.7 1.6 %collective-permute-start.11 = (bf16[128,512]{1,0:T(8,128)(2,1)S(1)}, bf16[128,512]{1,0:T(8,128)(2,1)S(1)}, u32[]{:S(2)}, u32[]{:S(2)}) collective-permute-start(bf16[128,512]{1,0:T(8,128)(2,1)S(1)} %get-tuple-element.100.part_ref), channel_id=1, source_target_pairs={{0,8},{1,9},{2,10},{3,11},{4,12},{5,13},{6,14},{7,15},{8,0},{9,1},... | collective-permute-start | bytes 393224 | tf_op jit(solution)/shard_map/ppermute | solution.py:398
  31.2 1.8 %collective-permute-done.9.got_ref = bf16[128,512]{1,0:T(8,128)(2,1)S(1)} collective-permute-done((bf16[128,512]{1,0:T(8,128)(2,1)S(1)}, bf16[128,512]{1,0:T(8,128)(2,1)S(1)}, u32[]{:S(2)}, u32[]{:S(2)}) %collective-permute-start.9) | collective-permute-done | bytes 131104 | tf_op jit(solution)/shard_map/ppermute | solution.py:398
  33.1 0.6 soft_low.2
  33.7 1.0 %collective-permute-done.11.got_ref = bf16[128,512]{1,0:T(8,128)(2,1)S(1)} collective-permute-done((bf16[128,512]{1,0:T(8,128)(2,1)S(1)}, bf16[128,512]{1,0:T(8,128)(2,1)S(1)}, u32[]{:S(2)}, u32[]{:S(2)}) %collective-permute-start.11) | collective-permute-done | bytes 131104 | tf_op jit(solution)/shard_map/ppermute | solution.py:398
  34.7 0.4 soft_high.2
  35.6 1.0 %collective-permute-done.12.got_ref = bf16[520,128]{1,0:T(8,128)(2,1)S(1)} collective-permute-done((bf16[520,128]{1,0:T(8,128)(2,1)S(1)}, bf16[520,128]{1,0:T(8,128)(2,1)S(1)}, u32[]{:S(2)}, u32[]{:S(2)}) %collective-permute-start.12) | collective-permute-done | bytes 133152 | tf_op jit(solution)/shard_map/ppermute | solution.py:398
  36.6 1.0 %collective-permute-start.13 = (bf16[264,128]{1,0:T(8,128)(2,1)S(1)}, bf16[264,128]{1,0:T(8,128)(2,1)S(1)}, u32[]{:S(2)}, u32[]{:S(2)}) collective-permute-start(bf16[264,128]{1,0:T(8,128)(2,1)S(1)} %get-tuple-element.109.mine_ref), channel_id=1, source_target_pairs={{0,2},{1,3},{2,0},{3,1},{4,6},{5,7},{6,4},{7,5},{8,10},{9,11},{10,... | collective-permute-start | bytes 202760 | tf_op jit(solution)/shard_map/ppermute | solution.py:398
  37.6 1.1 %collective-permute-start.15 = (bf16[264,128]{1,0:T(8,128)(2,1)S(1)}, bf16[264,128]{1,0:T(8,128)(2,1)S(1)}, u32[]{:S(2)}, u32[]{:S(2)}) collective-permute-start(bf16[264,128]{1,0:T(8,128)(2,1)S(1)} %get-tuple-element.110.mine_ref), channel_id=1, source_target_pairs={{0,2},{1,3},{2,0},{3,1},{4,6},{5,7},{6,4},{7,5},{8,10},{9,11},{10,... | collective-permute-start | bytes 202760 | tf_op jit(solution)/shard_map/ppermute | solution.py:398
  38.7 2.1 %collective-permute-start.17 = (bf16[128,128]{1,0:T(8,128)(2,1)S(1)}, bf16[128,128]{1,0:T(8,128)(2,1)S(1)}, u32[]{:S(2)}, u32[]{:S(2)}) collective-permute-start(bf16[128,128]{1,0:T(8,128)(2,1)S(1)} %get-tuple-element.116), channel_id=1, source_target_pairs={{0,4},{1,5},{2,6},{3,7},{4,0},{5,1},{6,2},{7,3},{8,12},{9,13},{10,... | collective-permute-start | bytes 98312 | tf_op jit(solution)/shard_map/ppermute | solution.py:398
  40.8 0.8 collective-permute-done.13.got_ref
  41.6 1.7 %collective-permute-start.14 = (bf16[264,128]{1,0:T(8,128)(2,1)S(1)}, bf16[264,128]{1,0:T(8,128)(2,1)S(1)}, u32[]{:S(2)}, u32[]{:S(2)}) collective-permute-start(bf16[264,128]{1,0:T(8,128)(2,1)S(1)} %hop_p.4.p_ref), channel_id=1, source_target_pairs={{0,4},{1,5},{2,6},{3,7},{4,0},{5,1},{6,2},{7,3},{8,12},{9,13},{10,... | collective-permute-start | bytes 202760 | tf_op jit(solution)/shard_map/ppermute | solution.py:398
  43.3 1.8 %collective-permute-start.16 = (bf16[264,128]{1,0:T(8,128)(2,1)S(1)}, bf16[264,128]{1,0:T(8,128)(2,1)S(1)}, u32[]{:S(2)}, u32[]{:S(2)}) collective-permute-start(bf16[264,128]{1,0:T(8,128)(2,1)S(1)} %hop_q.4.q_ref), channel_id=1, source_target_pairs={{0,4},{1,5},{2,6},{3,7},{4,0},{5,1},{6,2},{7,3},{8,12},{9,13},{10,... | collective-permute-start | bytes 202760 | tf_op jit(solution)/shard_map/ppermute | solution.py:398
  45.2 1.8 %collective-permute-start.18 = (bf16[2,128,128]{2,1,0:T(8,128)(2,1)S(1)}, bf16[2,128,128]{2,1,0:T(8,128)(2,1)S(1)}, u32[]{:S(2)}, u32[]{:S(2)}) collective-permute-start(bf16[2,128,128]{2,1,0:T(8,128)(2,1)S(1)} %pad_maximum_fusion.1), channel_id=1, source_target_pairs={{0,2},{1,3},{2,0},{3,1},{4,6},{5,7},{6,4},{7,5},{8,10},{9,11},{10,... | collective-permute-start | bytes 196616 | tf_op jit(solution)/shard_map/ppermute | solution.py:398
  46.9 2.3 %prep.3.x_ref = bf16[1024,1024]{1,0:T(8,128)(2,1)S(1)} custom-call(s32[1,3]{1,0:T(1,128)S(1)} %bitcast.17, s32[8,16]{1,0:T(8,128)S(1)} %copy-done.1, bf16[1024,2048]{1,0:T(8,128)(2,1)} %x_ref.3), custom_call_target="tpu_custom_call" | custom-call | bytes 4194304 | tf_op jit(solution)/shard_map/prep/pallas_call | solution.py:51
  49.2 1.3 %collective-permute-done.18.near_ref = bf16[2,128,128]{2,1,0:T(8,128)(2,1)S(1)} collective-permute-done((bf16[2,128,128]{2,1,0:T(8,128)(2,1)S(1)}, bf16[2,128,128]{2,1,0:T(8,128)(2,1)S(1)}, u32[]{:S(2)}, u32[]{:S(2)}) %collective-permute-start.18) | collective-permute-done | bytes 65568 | tf_op jit(solution)/shard_map/ppermute | solution.py:398
  50.8 0.4 mine.4.part_ref
  51.2 0.9 collective-permute-done.19.delta_ref
  52.1 0.5 change.4
  52.6 1.6 %collective-permute-start.20 = (bf16[128,512]{1,0:T(8,128)(2,1)S(1)}, bf16[128,512]{1,0:T(8,128)(2,1)S(1)}, u32[]{:S(2)}, u32[]{:S(2)}) collective-permute-start(bf16[128,512]{1,0:T(8,128)(2,1)S(1)} %get-tuple-element.123.mine_ref), channel_id=1, source_target_pairs={{0,8},{1,9},{2,10},{3,11},{4,12},{5,13},{6,14},{7,15},{8,0},{9,1},... | collective-permute-start | bytes 393224 | tf_op jit(solution)/shard_map/ppermute | solution.py:398
  54.2 0.5 collective-permute-start.22
  54.7 3.5 %collective-permute-done.20.got_ref = bf16[128,512]{1,0:T(8,128)(2,1)S(1)} collective-permute-done((bf16[128,512]{1,0:T(8,128)(2,1)S(1)}, bf16[128,512]{1,0:T(8,128)(2,1)S(1)}, u32[]{:S(2)}, u32[]{:S(2)}) %collective-permute-start.20) | collective-permute-done | bytes 131104 | tf_op jit(solution)/shard_map/ppermute | solution.py:398
  58.3 1.2 %collective-permute-start.21 = (bf16[128,512]{1,0:T(8,128)(2,1)S(1)}, bf16[128,512]{1,0:T(8,128)(2,1)S(1)}, u32[]{:S(2)}, u32[]{:S(2)}) collective-permute-start(bf16[128,512]{1,0:T(8,128)(2,1)S(1)} %get-tuple-element.124.part_ref), channel_id=1, source_target_pairs={{0,16},{1,17},{2,18},{3,19},{4,20},{5,21},{6,22},{7,23},{8,24},{9,... | collective-permute-start | bytes 393224 | tf_op jit(solution)/shard_map/ppermute | solution.py:398
  59.5 1.0 %collective-permute-start.23 = (bf16[128,512]{1,0:T(8,128)(2,1)S(1)}, bf16[128,512]{1,0:T(8,128)(2,1)S(1)}, u32[]{:S(2)}, u32[]{:S(2)}) collective-permute-start(bf16[128,512]{1,0:T(8,128)(2,1)S(1)} %get-tuple-element.130.part_ref), channel_id=1, source_target_pairs={{0,8},{1,9},{2,10},{3,11},{4,12},{5,13},{6,14},{7,15},{8,0},{9,1},... | collective-permute-start | bytes 393224 | tf_op jit(solution)/shard_map/ppermute | solution.py:398
  60.5 2.8 %collective-permute-done.21.got_ref = bf16[128,512]{1,0:T(8,128)(2,1)S(1)} collective-permute-done((bf16[128,512]{1,0:T(8,128)(2,1)S(1)}, bf16[128,512]{1,0:T(8,128)(2,1)S(1)}, u32[]{:S(2)}, u32[]{:S(2)}) %collective-permute-start.21) | collective-permute-done | bytes 131104 | tf_op jit(solution)/shard_map/ppermute | solution.py:398
  63.3 0.6 soft_low.3
  64.0 0.6 collective-permute-done.23.got_ref
  64.6 0.4 soft_high.3
  65.4 1.0 %collective-permute-done.24.got_ref = bf16[520,128]{1,0:T(8,128)(2,1)S(1)} collective-permute-done((bf16[520,128]{1,0:T(8,128)(2,1)S(1)}, bf16[520,128]{1,0:T(8,128)(2,1)S(1)}, u32[]{:S(2)}, u32[]{:S(2)}) %collective-permute-start.24) | collective-permute-done | bytes 133152 | tf_op jit(solution)/shard_map/ppermute | solution.py:398
  66.5 0.8 collective-permute-start.25
  67.2 1.3 %collective-permute-start.27 = (bf16[264,128]{1,0:T(8,128)(2,1)S(1)}, bf16[264,128]{1,0:T(8,128)(2,1)S(1)}, u32[]{:S(2)}, u32[]{:S(2)}) collective-permute-start(bf16[264,128]{1,0:T(8,128)(2,1)S(1)} %get-tuple-element.137.mine_ref), channel_id=1, source_target_pairs={{0,2},{1,3},{2,0},{3,1},{4,6},{5,7},{6,4},{7,5},{8,10},{9,11},{10,... | collective-permute-start | bytes 202760 | tf_op jit(solution)/shard_map/ppermute | solution.py:398
  68.6 2.9 %collective-permute-done.25.got_ref = bf16[264,128]{1,0:T(8,128)(2,1)S(1)} collective-permute-done((bf16[264,128]{1,0:T(8,128)(2,1)S(1)}, bf16[264,128]{1,0:T(8,128)(2,1)S(1)}, u32[]{:S(2)}, u32[]{:S(2)}) %collective-permute-start.25) | collective-permute-done | bytes 67616 | tf_op jit(solution)/shard_map/ppermute | solution.py:398
  71.5 1.2 %collective-permute-start.26 = (bf16[264,128]{1,0:T(8,128)(2,1)S(1)}, bf16[264,128]{1,0:T(8,128)(2,1)S(1)}, u32[]{:S(2)}, u32[]{:S(2)}) collective-permute-start(bf16[264,128]{1,0:T(8,128)(2,1)S(1)} %hop_p.5.p_ref), channel_id=1, source_target_pairs={{0,4},{1,5},{2,6},{3,7},{4,0},{5,1},{6,2},{7,3},{8,12},{9,13},{10,... | collective-permute-start | bytes 202760 | tf_op jit(solution)/shard_map/ppermute | solution.py:398
  72.8 1.9 %collective-permute-start.28 = (bf16[264,128]{1,0:T(8,128)(2,1)S(1)}, bf16[264,128]{1,0:T(8,128)(2,1)S(1)}, u32[]{:S(2)}, u32[]{:S(2)}) collective-permute-start(bf16[264,128]{1,0:T(8,128)(2,1)S(1)} %hop_q.5.q_ref), channel_id=1, source_target_pairs={{0,4},{1,5},{2,6},{3,7},{4,0},{5,1},{6,2},{7,3},{8,12},{9,13},{10,... | collective-permute-start | bytes 202760 | tf_op jit(solution)/shard_map/ppermute | solution.py:398
  74.7 3.9 %collective-permute-done.26.gp_ref = bf16[264,128]{1,0:T(8,128)(2,1)S(1)} collective-permute-done((bf16[264,128]{1,0:T(8,128)(2,1)S(1)}, bf16[264,128]{1,0:T(8,128)(2,1)S(1)}, u32[]{:S(2)}, u32[]{:S(2)}) %collective-permute-start.26) | collective-permute-done | bytes 67616 | tf_op jit(solution)/shard_map/ppermute | solution.py:398
  78.6 1.4 %collective-permute-done.28.gq_ref = bf16[264,128]{1,0:T(8,128)(2,1)S(1)} collective-permute-done((bf16[264,128]{1,0:T(8,128)(2,1)S(1)}, bf16[264,128]{1,0:T(8,128)(2,1)S(1)}, u32[]{:S(2)}, u32[]{:S(2)}) %collective-permute-start.28) | collective-permute-done | bytes 67616 | tf_op jit(solution)/shard_map/ppermute | solution.py:398
  80.7 0.9 collective-permute-done.29.delta_ref
  81.6 0.5 change.5
  82.1 1.0 %collective-permute-start.30 = (bf16[128,512]{1,0:T(8,128)(2,1)S(1)}, bf16[128,512]{1,0:T(8,128)(2,1)S(1)}, u32[]{:S(2)}, u32[]{:S(2)}) collective-permute-start(bf16[128,512]{1,0:T(8,128)(2,1)S(1)} %get-tuple-element.145.mine_ref), channel_id=1, source_target_pairs={{0,8},{1,9},{2,10},{3,11},{4,12},{5,13},{6,14},{7,15},{8,0},{9,1},... | collective-permute-start | bytes 393224 | tf_op jit(solution)/shard_map/ppermute | solution.py:398
  83.1 1.5 %collective-permute-start.32 = (bf16[128,512]{1,0:T(8,128)(2,1)S(1)}, bf16[128,512]{1,0:T(8,128)(2,1)S(1)}, u32[]{:S(2)}, u32[]{:S(2)}) collective-permute-start(bf16[128,512]{1,0:T(8,128)(2,1)S(1)} %get-tuple-element.147.mine_ref), channel_id=1, source_target_pairs={{0,16},{1,17},{2,18},{3,19},{4,20},{5,21},{6,22},{7,23},{8,24},{9,... | collective-permute-start | bytes 393224 | tf_op jit(solution)/shard_map/ppermute | solution.py:398
  84.6 3.1 %collective-permute-done.30.got_ref = bf16[128,512]{1,0:T(8,128)(2,1)S(1)} collective-permute-done((bf16[128,512]{1,0:T(8,128)(2,1)S(1)}, bf16[128,512]{1,0:T(8,128)(2,1)S(1)}, u32[]{:S(2)}, u32[]{:S(2)}) %collective-permute-start.30) | collective-permute-done | bytes 131104 | tf_op jit(solution)/shard_map/ppermute | solution.py:398
  87.7 1.0 %collective-permute-start.31 = (bf16[128,512]{1,0:T(8,128)(2,1)S(1)}, bf16[128,512]{1,0:T(8,128)(2,1)S(1)}, u32[]{:S(2)}, u32[]{:S(2)}) collective-permute-start(bf16[128,512]{1,0:T(8,128)(2,1)S(1)} %meet_a.5.part_ref), channel_id=1, source_target_pairs={{0,16},{1,17},{2,18},{3,19},{4,20},{5,21},{6,22},{7,23},{8,24},{9,... | collective-permute-start | bytes 393224 | tf_op jit(solution)/shard_map/ppermute | solution.py:398
  88.8 1.6 %collective-permute-start.33 = (bf16[128,512]{1,0:T(8,128)(2,1)S(1)}, bf16[128,512]{1,0:T(8,128)(2,1)S(1)}, u32[]{:S(2)}, u32[]{:S(2)}) collective-permute-start(bf16[128,512]{1,0:T(8,128)(2,1)S(1)} %meet_b.5.part_ref), channel_id=1, source_target_pairs={{0,8},{1,9},{2,10},{3,11},{4,12},{5,13},{6,14},{7,15},{8,0},{9,1},... | collective-permute-start | bytes 393224 | tf_op jit(solution)/shard_map/ppermute | solution.py:398
  90.3 0.6 coef_out.1
  91.0 0.7 copy.8
  91.7 1.1 %collective-permute-done.31.got_ref = bf16[128,512]{1,0:T(8,128)(2,1)S(1)} collective-permute-done((bf16[128,512]{1,0:T(8,128)(2,1)S(1)}, bf16[128,512]{1,0:T(8,128)(2,1)S(1)}, u32[]{:S(2)}, u32[]{:S(2)}) %collective-permute-start.31) | collective-permute-done | bytes 131104 | tf_op jit(solution)/shard_map/ppermute | solution.py:398
  92.9 0.9 collective-permute-done.33.got_ref
  93.8 0.9 last_high.1
  (52 shorter events, 3.2 us)
Async XLA Ops:
  3.6 13.3 %copy-start.1 = (s32[8,16]{1,0:T(8,128)S(1)}, s32[8,16]{1,0:T(8,128)}, u32[]{:S(2)}) copy-start(s32[8,16]{1,0:T(8,128)} %live_ref.3) | copy-start | bytes 1540
  3.6 13.3 %copy-start.2 = (s32[3,1]{0,1:T(1,128)S(1)}, s32[3,1]{0,1:T(1,128)}, u32[]{:S(2)}) copy-start(s32[3,1]{0,1:T(1,128)} %param.11) | copy-start | bytes 40
  3.6 1.5 %collective-permute-start = (bf16[520,128]{1,0:T(8,128)(2,1)S(1)}, bf16[520,128]{1,0:T(8,128)(2,1)S(1)}, u32[]{:S(2)}, u32[]{:S(2)}) collective-permute-start(bf16[520,128]{1,0:T(8,128)(2,1)S(1)} %get-tuple-element.80), channel_id=1, source_target_pairs={{0,1},{1,0},{2,3},{3,2},{4,5},{5,4},{6,7},{7,6},{8,9},{9,8},{10,11... | collective-permute-start | bytes 399368 | tf_op jit(solution)/shard_map/ppermute | solution.py:398
  5.2 6.0 %collective-permute-start.1 = (bf16[264,128]{1,0:T(8,128)(2,1)S(1)}, bf16[264,128]{1,0:T(8,128)(2,1)S(1)}, u32[]{:S(2)}, u32[]{:S(2)}) collective-permute-start(bf16[264,128]{1,0:T(8,128)(2,1)S(1)} %get-tuple-element.84.mine_ref), channel_id=1, source_target_pairs={{0,2},{1,3},{2,0},{3,1},{4,6},{5,7},{6,4},{7,5},{8,10},{9,11},{10,... | collective-permute-start | bytes 202760 | tf_op jit(solution)/shard_map/ppermute | solution.py:398
  8.2 5.7 %collective-permute-start.3 = (bf16[264,128]{1,0:T(8,128)(2,1)S(1)}, bf16[264,128]{1,0:T(8,128)(2,1)S(1)}, u32[]{:S(2)}, u32[]{:S(2)}) collective-permute-start(bf16[264,128]{1,0:T(8,128)(2,1)S(1)} %get-tuple-element.85.mine_ref), channel_id=1, source_target_pairs={{0,2},{1,3},{2,0},{3,1},{4,6},{5,7},{6,4},{7,5},{8,10},{9,11},{10,... | collective-permute-start | bytes 202760 | tf_op jit(solution)/shard_map/ppermute | solution.py:398
  8.2 7.1 %collective-permute-start.5 = (bf16[128,128]{1,0:T(8,128)(2,1)S(1)}, bf16[128,128]{1,0:T(8,128)(2,1)S(1)}, u32[]{:S(2)}, u32[]{:S(2)}) collective-permute-start(bf16[128,128]{1,0:T(8,128)(2,1)S(1)} %get-tuple-element.90), channel_id=1, source_target_pairs={{0,4},{1,5},{2,6},{3,7},{4,0},{5,1},{6,2},{7,3},{8,12},{9,13},{10,... | collective-permute-start | bytes 98312 | tf_op jit(solution)/shard_map/ppermute | solution.py:398
  11.2 9.1 %collective-permute-start.2 = (bf16[264,128]{1,0:T(8,128)(2,1)S(1)}, bf16[264,128]{1,0:T(8,128)(2,1)S(1)}, u32[]{:S(2)}, u32[]{:S(2)}) collective-permute-start(bf16[264,128]{1,0:T(8,128)(2,1)S(1)} %hop_p.3.p_ref), channel_id=1, source_target_pairs={{0,4},{1,5},{2,6},{3,7},{4,0},{5,1},{6,2},{7,3},{8,12},{9,13},{10,... | collective-permute-start | bytes 202760 | tf_op jit(solution)/shard_map/ppermute | solution.py:398
  13.9 6.4 %collective-permute-start.4 = (bf16[264,128]{1,0:T(8,128)(2,1)S(1)}, bf16[264,128]{1,0:T(8,128)(2,1)S(1)}, u32[]{:S(2)}, u32[]{:S(2)}) collective-permute-start(bf16[264,128]{1,0:T(8,128)(2,1)S(1)} %hop_q.3.q_ref), channel_id=1, source_target_pairs={{0,4},{1,5},{2,6},{3,7},{4,0},{5,1},{6,2},{7,3},{8,12},{9,13},{10,... | collective-permute-start | bytes 202760 | tf_op jit(solution)/shard_map/ppermute | solution.py:398
  15.4 4.9 %collective-permute-start.6 = (bf16[2,128,128]{2,1,0:T(8,128)(2,1)S(1)}, bf16[2,128,128]{2,1,0:T(8,128)(2,1)S(1)}, u32[]{:S(2)}, u32[]{:S(2)}) collective-permute-start(bf16[2,128,128]{2,1,0:T(8,128)(2,1)S(1)} %pad_maximum_fusion), channel_id=1, source_target_pairs={{0,2},{1,3},{2,0},{3,1},{4,6},{5,7},{6,4},{7,5},{8,10},{9,11},{10,... | collective-permute-start | bytes 196616 | tf_op jit(solution)/shard_map/ppermute | solution.py:398
  20.4 1.4 %collective-permute-start.7 = (bf16[128,512]{1,0:T(8,128)(2,1)S(1)}, bf16[128,512]{1,0:T(8,128)(2,1)S(1)}, u32[]{:S(2)}, u32[]{:S(2)}) collective-permute-start(bf16[128,512]{1,0:T(8,128)(2,1)S(1)} %get-tuple-element.92.delta_ref), channel_id=1, source_target_pairs={{0,1},{1,0},{2,3},{3,2},{4,5},{5,4},{6,7},{7,6},{8,9},{9,8},{10,11... | collective-permute-start | bytes 393224 | tf_op jit(solution)/shard_map/ppermute | solution.py:398
  20.9 12.1 %copy-start = (s32[1024]{0:T(1024)S(1)}, s32[1024]{0:T(1024)}, u32[]{:S(2)}) copy-start(s32[1024]{0:T(1024)} %param.8) | copy-start | bytes 12292
  22.3 5.6 %collective-permute-start.8 = (bf16[128,512]{1,0:T(8,128)(2,1)S(1)}, bf16[128,512]{1,0:T(8,128)(2,1)S(1)}, u32[]{:S(2)}, u32[]{:S(2)}) collective-permute-start(bf16[128,512]{1,0:T(8,128)(2,1)S(1)} %get-tuple-element.93.mine_ref), channel_id=1, source_target_pairs={{0,8},{1,9},{2,10},{3,11},{4,12},{5,13},{6,14},{7,15},{8,0},{9,1},... | collective-permute-start | bytes 393224 | tf_op jit(solution)/shard_map/ppermute | solution.py:398
  23.9 5.7 %collective-permute-start.10 = (bf16[128,512]{1,0:T(8,128)(2,1)S(1)}, bf16[128,512]{1,0:T(8,128)(2,1)S(1)}, u32[]{:S(2)}, u32[]{:S(2)}) collective-permute-start(bf16[128,512]{1,0:T(8,128)(2,1)S(1)} %get-tuple-element.99.mine_ref), channel_id=1, source_target_pairs={{0,16},{1,17},{2,18},{3,19},{4,20},{5,21},{6,22},{7,23},{8,24},{9,... | collective-permute-start | bytes 393224 | tf_op jit(solution)/shard_map/ppermute | solution.py:398
  28.0 5.0 %collective-permute-start.9 = (bf16[128,512]{1,0:T(8,128)(2,1)S(1)}, bf16[128,512]{1,0:T(8,128)(2,1)S(1)}, u32[]{:S(2)}, u32[]{:S(2)}) collective-permute-start(bf16[128,512]{1,0:T(8,128)(2,1)S(1)} %get-tuple-element.94.part_ref), channel_id=1, source_target_pairs={{0,16},{1,17},{2,18},{3,19},{4,20},{5,21},{6,22},{7,23},{8,24},{9,... | collective-permute-start | bytes 393224 | tf_op jit(solution)/shard_map/ppermute | solution.py:398
  29.7 5.0 %collective-permute-start.11 = (bf16[128,512]{1,0:T(8,128)(2,1)S(1)}, bf16[128,512]{1,0:T(8,128)(2,1)S(1)}, u32[]{:S(2)}, u32[]{:S(2)}) collective-permute-start(bf16[128,512]{1,0:T(8,128)(2,1)S(1)} %get-tuple-element.100.part_ref), channel_id=1, source_target_pairs={{0,8},{1,9},{2,10},{3,11},{4,12},{5,13},{6,14},{7,15},{8,0},{9,1},... | collective-permute-start | bytes 393224 | tf_op jit(solution)/shard_map/ppermute | solution.py:398
  35.2 1.4 %collective-permute-start.12 = (bf16[520,128]{1,0:T(8,128)(2,1)S(1)}, bf16[520,128]{1,0:T(8,128)(2,1)S(1)}, u32[]{:S(2)}, u32[]{:S(2)}) collective-permute-start(bf16[520,128]{1,0:T(8,128)(2,1)S(1)} %get-tuple-element.105), channel_id=1, source_target_pairs={{0,1},{1,0},{2,3},{3,2},{4,5},{5,4},{6,7},{7,6},{8,9},{9,8},{10,11... | collective-permute-start | bytes 399368 | tf_op jit(solution)/shard_map/ppermute | solution.py:398
  36.6 5.0 %collective-permute-start.13 = (bf16[264,128]{1,0:T(8,128)(2,1)S(1)}, bf16[264,128]{1,0:T(8,128)(2,1)S(1)}, u32[]{:S(2)}, u32[]{:S(2)}) collective-permute-start(bf16[264,128]{1,0:T(8,128)(2,1)S(1)} %get-tuple-element.109.mine_ref), channel_id=1, source_target_pairs={{0,2},{1,3},{2,0},{3,1},{4,6},{5,7},{6,4},{7,5},{8,10},{9,11},{10,... | collective-permute-start | bytes 202760 | tf_op jit(solution)/shard_map/ppermute | solution.py:398
  37.6 5.7 %collective-permute-start.15 = (bf16[264,128]{1,0:T(8,128)(2,1)S(1)}, bf16[264,128]{1,0:T(8,128)(2,1)S(1)}, u32[]{:S(2)}, u32[]{:S(2)}) collective-permute-start(bf16[264,128]{1,0:T(8,128)(2,1)S(1)} %get-tuple-element.110.mine_ref), channel_id=1, source_target_pairs={{0,2},{1,3},{2,0},{3,1},{4,6},{5,7},{6,4},{7,5},{8,10},{9,11},{10,... | collective-permute-start | bytes 202760 | tf_op jit(solution)/shard_map/ppermute | solution.py:398
  38.7 6.4 %collective-permute-start.17 = (bf16[128,128]{1,0:T(8,128)(2,1)S(1)}, bf16[128,128]{1,0:T(8,128)(2,1)S(1)}, u32[]{:S(2)}, u32[]{:S(2)}) collective-permute-start(bf16[128,128]{1,0:T(8,128)(2,1)S(1)} %get-tuple-element.116), channel_id=1, source_target_pairs={{0,4},{1,5},{2,6},{3,7},{4,0},{5,1},{6,2},{7,3},{8,12},{9,13},{10,... | collective-permute-start | bytes 98312 | tf_op jit(solution)/shard_map/ppermute | solution.py:398
  41.6 8.9 %collective-permute-start.14 = (bf16[264,128]{1,0:T(8,128)(2,1)S(1)}, bf16[264,128]{1,0:T(8,128)(2,1)S(1)}, u32[]{:S(2)}, u32[]{:S(2)}) collective-permute-start(bf16[264,128]{1,0:T(8,128)(2,1)S(1)} %hop_p.4.p_ref), channel_id=1, source_target_pairs={{0,4},{1,5},{2,6},{3,7},{4,0},{5,1},{6,2},{7,3},{8,12},{9,13},{10,... | collective-permute-start | bytes 202760 | tf_op jit(solution)/shard_map/ppermute | solution.py:398
  43.3 7.2 %collective-permute-start.16 = (bf16[264,128]{1,0:T(8,128)(2,1)S(1)}, bf16[264,128]{1,0:T(8,128)(2,1)S(1)}, u32[]{:S(2)}, u32[]{:S(2)}) collective-permute-start(bf16[264,128]{1,0:T(8,128)(2,1)S(1)} %hop_q.4.q_ref), channel_id=1, source_target_pairs={{0,4},{1,5},{2,6},{3,7},{4,0},{5,1},{6,2},{7,3},{8,12},{9,13},{10,... | collective-permute-start | bytes 202760 | tf_op jit(solution)/shard_map/ppermute | solution.py:398
  45.2 5.3 %collective-permute-start.18 = (bf16[2,128,128]{2,1,0:T(8,128)(2,1)S(1)}, bf16[2,128,128]{2,1,0:T(8,128)(2,1)S(1)}, u32[]{:S(2)}, u32[]{:S(2)}) collective-permute-start(bf16[2,128,128]{2,1,0:T(8,128)(2,1)S(1)} %pad_maximum_fusion.1), channel_id=1, source_target_pairs={{0,2},{1,3},{2,0},{3,1},{4,6},{5,7},{6,4},{7,5},{8,10},{9,11},{10,... | collective-permute-start | bytes 196616 | tf_op jit(solution)/shard_map/ppermute | solution.py:398
  50.7 1.4 %collective-permute-start.19 = (bf16[128,512]{1,0:T(8,128)(2,1)S(1)}, bf16[128,512]{1,0:T(8,128)(2,1)S(1)}, u32[]{:S(2)}, u32[]{:S(2)}) collective-permute-start(bf16[128,512]{1,0:T(8,128)(2,1)S(1)} %get-tuple-element.118.delta_ref), channel_id=1, source_target_pairs={{0,1},{1,0},{2,3},{3,2},{4,5},{5,4},{6,7},{7,6},{8,9},{9,8},{10,11... | collective-permute-start | bytes 393224 | tf_op jit(solution)/shard_map/ppermute | solution.py:398
  52.6 5.6 %collective-permute-start.20 = (bf16[128,512]{1,0:T(8,128)(2,1)S(1)}, bf16[128,512]{1,0:T(8,128)(2,1)S(1)}, u32[]{:S(2)}, u32[]{:S(2)}) collective-permute-start(bf16[128,512]{1,0:T(8,128)(2,1)S(1)} %get-tuple-element.123.mine_ref), channel_id=1, source_target_pairs={{0,8},{1,9},{2,10},{3,11},{4,12},{5,13},{6,14},{7,15},{8,0},{9,1},... | collective-permute-start | bytes 393224 | tf_op jit(solution)/shard_map/ppermute | solution.py:398
  54.2 5.3 %collective-permute-start.22 = (bf16[128,512]{1,0:T(8,128)(2,1)S(1)}, bf16[128,512]{1,0:T(8,128)(2,1)S(1)}, u32[]{:S(2)}, u32[]{:S(2)}) collective-permute-start(bf16[128,512]{1,0:T(8,128)(2,1)S(1)} %get-tuple-element.129.mine_ref), channel_id=1, source_target_pairs={{0,16},{1,17},{2,18},{3,19},{4,20},{5,21},{6,22},{7,23},{8,24},{9,... | collective-permute-start | bytes 393224 | tf_op jit(solution)/shard_map/ppermute | solution.py:398
  58.3 5.0 %collective-permute-start.21 = (bf16[128,512]{1,0:T(8,128)(2,1)S(1)}, bf16[128,512]{1,0:T(8,128)(2,1)S(1)}, u32[]{:S(2)}, u32[]{:S(2)}) collective-permute-start(bf16[128,512]{1,0:T(8,128)(2,1)S(1)} %get-tuple-element.124.part_ref), channel_id=1, source_target_pairs={{0,16},{1,17},{2,18},{3,19},{4,20},{5,21},{6,22},{7,23},{8,24},{9,... | collective-permute-start | bytes 393224 | tf_op jit(solution)/shard_map/ppermute | solution.py:398
  59.5 5.0 %collective-permute-start.23 = (bf16[128,512]{1,0:T(8,128)(2,1)S(1)}, bf16[128,512]{1,0:T(8,128)(2,1)S(1)}, u32[]{:S(2)}, u32[]{:S(2)}) collective-permute-start(bf16[128,512]{1,0:T(8,128)(2,1)S(1)} %get-tuple-element.130.part_ref), channel_id=1, source_target_pairs={{0,8},{1,9},{2,10},{3,11},{4,12},{5,13},{6,14},{7,15},{8,0},{9,1},... | collective-permute-start | bytes 393224 | tf_op jit(solution)/shard_map/ppermute | solution.py:398
  65.0 1.4 %collective-permute-start.24 = (bf16[520,128]{1,0:T(8,128)(2,1)S(1)}, bf16[520,128]{1,0:T(8,128)(2,1)S(1)}, u32[]{:S(2)}, u32[]{:S(2)}) collective-permute-start(bf16[520,128]{1,0:T(8,128)(2,1)S(1)} %get-tuple-element.135), channel_id=1, source_target_pairs={{0,1},{1,0},{2,3},{3,2},{4,5},{5,4},{6,7},{7,6},{8,9},{9,8},{10,11... | collective-permute-start | bytes 399368 | tf_op jit(solution)/shard_map/ppermute | solution.py:398
  66.5 5.0 %collective-permute-start.25 = (bf16[264,128]{1,0:T(8,128)(2,1)S(1)}, bf16[264,128]{1,0:T(8,128)(2,1)S(1)}, u32[]{:S(2)}, u32[]{:S(2)}) collective-permute-start(bf16[264,128]{1,0:T(8,128)(2,1)S(1)} %get-tuple-element.136.mine_ref), channel_id=1, source_target_pairs={{0,2},{1,3},{2,0},{3,1},{4,6},{5,7},{6,4},{7,5},{8,10},{9,11},{10,... | collective-permute-start | bytes 202760 | tf_op jit(solution)/shard_map/ppermute | solution.py:398
  67.2 5.5 %collective-permute-start.27 = (bf16[264,128]{1,0:T(8,128)(2,1)S(1)}, bf16[264,128]{1,0:T(8,128)(2,1)S(1)}, u32[]{:S(2)}, u32[]{:S(2)}) collective-permute-start(bf16[264,128]{1,0:T(8,128)(2,1)S(1)} %get-tuple-element.137.mine_ref), channel_id=1, source_target_pairs={{0,2},{1,3},{2,0},{3,1},{4,6},{5,7},{6,4},{7,5},{8,10},{9,11},{10,... | collective-permute-start | bytes 202760 | tf_op jit(solution)/shard_map/ppermute | solution.py:398
  71.5 7.1 %collective-permute-start.26 = (bf16[264,128]{1,0:T(8,128)(2,1)S(1)}, bf16[264,128]{1,0:T(8,128)(2,1)S(1)}, u32[]{:S(2)}, u32[]{:S(2)}) collective-permute-start(bf16[264,128]{1,0:T(8,128)(2,1)S(1)} %hop_p.5.p_ref), channel_id=1, source_target_pairs={{0,4},{1,5},{2,6},{3,7},{4,0},{5,1},{6,2},{7,3},{8,12},{9,13},{10,... | collective-permute-start | bytes 202760 | tf_op jit(solution)/shard_map/ppermute | solution.py:398
  72.8 7.3 %collective-permute-start.28 = (bf16[264,128]{1,0:T(8,128)(2,1)S(1)}, bf16[264,128]{1,0:T(8,128)(2,1)S(1)}, u32[]{:S(2)}, u32[]{:S(2)}) collective-permute-start(bf16[264,128]{1,0:T(8,128)(2,1)S(1)} %hop_q.5.q_ref), channel_id=1, source_target_pairs={{0,4},{1,5},{2,6},{3,7},{4,0},{5,1},{6,2},{7,3},{8,12},{9,13},{10,... | collective-permute-start | bytes 202760 | tf_op jit(solution)/shard_map/ppermute | solution.py:398
  80.2 1.4 %collective-permute-start.29 = (bf16[128,512]{1,0:T(8,128)(2,1)S(1)}, bf16[128,512]{1,0:T(8,128)(2,1)S(1)}, u32[]{:S(2)}, u32[]{:S(2)}) collective-permute-start(bf16[128,512]{1,0:T(8,128)(2,1)S(1)} %get-tuple-element.140.delta_ref), channel_id=1, source_target_pairs={{0,1},{1,0},{2,3},{3,2},{4,5},{5,4},{6,7},{7,6},{8,9},{9,8},{10,11... | collective-permute-start | bytes 393224 | tf_op jit(solution)/shard_map/ppermute | solution.py:398
  82.1 5.6 %collective-permute-start.30 = (bf16[128,512]{1,0:T(8,128)(2,1)S(1)}, bf16[128,512]{1,0:T(8,128)(2,1)S(1)}, u32[]{:S(2)}, u32[]{:S(2)}) collective-permute-start(bf16[128,512]{1,0:T(8,128)(2,1)S(1)} %get-tuple-element.145.mine_ref), channel_id=1, source_target_pairs={{0,8},{1,9},{2,10},{3,11},{4,12},{5,13},{6,14},{7,15},{8,0},{9,1},... | collective-permute-start | bytes 393224 | tf_op jit(solution)/shard_map/ppermute | solution.py:398
  83.1 5.7 %collective-permute-start.32 = (bf16[128,512]{1,0:T(8,128)(2,1)S(1)}, bf16[128,512]{1,0:T(8,128)(2,1)S(1)}, u32[]{:S(2)}, u32[]{:S(2)}) collective-permute-start(bf16[128,512]{1,0:T(8,128)(2,1)S(1)} %get-tuple-element.147.mine_ref), channel_id=1, source_target_pairs={{0,16},{1,17},{2,18},{3,19},{4,20},{5,21},{6,22},{7,23},{8,24},{9,... | collective-permute-start | bytes 393224 | tf_op jit(solution)/shard_map/ppermute | solution.py:398
  87.7 5.0 %collective-permute-start.31 = (bf16[128,512]{1,0:T(8,128)(2,1)S(1)}, bf16[128,512]{1,0:T(8,128)(2,1)S(1)}, u32[]{:S(2)}, u32[]{:S(2)}) collective-permute-start(bf16[128,512]{1,0:T(8,128)(2,1)S(1)} %meet_a.5.part_ref), channel_id=1, source_target_pairs={{0,16},{1,17},{2,18},{3,19},{4,20},{5,21},{6,22},{7,23},{8,24},{9,... | collective-permute-start | bytes 393224 | tf_op jit(solution)/shard_map/ppermute | solution.py:398
  88.8 5.0 %collective-permute-start.33 = (bf16[128,512]{1,0:T(8,128)(2,1)S(1)}, bf16[128,512]{1,0:T(8,128)(2,1)S(1)}, u32[]{:S(2)}, u32[]{:S(2)}) collective-permute-start(bf16[128,512]{1,0:T(8,128)(2,1)S(1)} %meet_b.5.part_ref), channel_id=1, source_target_pairs={{0,8},{1,9},{2,10},{3,11},{4,12},{5,13},{6,14},{7,15},{8,0},{9,1},... | collective-permute-start | bytes 393224 | tf_op jit(solution)/shard_map/ppermute | solution.py:398

commit v10 on v9

--- a/solution.py
+++ b/solution.py
@@ -360,20 +360,21 @@
     part_ref[...] = contrib(x_ref, 0, delta_ref)
 
 
-def change_body(carried, x_ref, part_ref, delta_ref, *refs):
-    errors, (a_ref, b_ref, *keep) = refs[:carried], refs[carried:]
-    part = part_ref[...] + contrib(x_ref, HALF, delta_ref)
-    rows = x_ref.shape[0]
+def change_body(carried, start, x_ref, part_ref, delta_ref, *refs):
+    errors, (out_ref, *keep) = refs[:carried], refs[carried:]
+    rows = out_ref.shape[1]
+    part = part_ref[start : start + rows, :] + lax.dot_general(
+        x_ref[start : start + rows, HALF:], delta_ref[...],
+        (((1,), (1,)), ((), ())), preferred_element_type=F32,
+    )
     for _, here in tiles_of(rows):
-        low = here.stop <= rows // 2
-        at = here if low else slice(here.start - rows // 2, here.stop - rows // 2)
         full = part[here, :].T
-        for e_ref in errors[0::2] if low else errors[1::2]:
-            full = full + e_ref[:, at]
+        for e_ref in errors:
+            full = full + e_ref[:, here]
         sent = full.astype(BF16)
-        (a_ref if low else b_ref)[:, at] = sent
-        if keep:
-            keep[0 if low else 1][:, at] = full - sent.astype(F32)
+        out_ref[:, here] = sent
+        for e_ref in keep:
+            e_ref[:, here] = full - sent.astype(F32)
 
 
 def meet_body(share, mine_ref, got_ref, out_ref, *error_refs):
@@ -543,10 +544,17 @@
         got = swap_core(delta)
         part = call(mine_body, part_shape, vmem(2), "mine", flops, nbytes)(x, delta)
         last = step == STEPS - 1
-        shapes = (sds(half, BF16),) * 2 + (() if last else (sds(half, F32),) * 2)
-        a, b, *kept = call(
-            functools.partial(change_body, len(errors)), shapes, vmem(3 + len(errors)), "change", flops, nbytes,
-        )(x, part, got, *errors)
+        shapes = (sds(half, BF16),) + (() if last else (sds(half, F32),))
+        sent, kept = [], []
+        for at in range(2):
+            mine = errors[at::2]
+            change, *error = call(
+                functools.partial(change_body, len(mine), at * (rows // 2)), shapes, vmem(3 + len(mine)),
+                "change", flops // 2, nbytes,
+            )(x, part, got, *mine)
+            sent.append(change)
+            kept += error
+        a, b = sent
         halves, errors = sum_over_feat(a, b, last)
         errors = kept + errors
     a, got_a, b, got_b = halves

time: 94.9 us -> 94.7 us (level)
    pallas_call x38 -> x41, Pallas kernels: 15.4 us -> 16.3 us  [run(): f(*(x if spec.memory_space == pltpu.SMEM else pltpu.with_memory_space_con...]
  transfers between devices with their start and end apart: 34 -> 34, of which waited for: 21 -> 21; matrix products, arithmetic and copies ran while one was open for 1% -> 1% of each run, Pallas kernels for 10% -> 11%
where the time goes in v10:
time: 94.7 us; the launch traced here: 94.4 us
  starting transfers between devices  42.2 us (45%)
  waiting for transfers between devices  33.5 us (35%)
  Pallas kernels  17.1 us (18%)
    ppermute x34, starting transfers between devices, swap(): return lax.ppermute(x, ('feat', 'ex'), pairs)  42.2 us
    ppermute x34, waiting for transfers between devices, swap(): return lax.ppermute(x, ('feat', 'ex'), pairs)  33.5 us
    pallas_call x41, Pallas kernels, run(): f(*(x if spec.memory_space == pltpu.SMEM else pltpu.with_memory_space_con...  16.3 us
  transfers between devices with their start and end apart: 34, of which 21 were waited for; matrix products, arithmetic and copies ran while one was open for 1% of the time, Pallas kernels for 11%

profile of v10, /device:TPU:0, one launch (start us, length us, event | category | flops | bytes accessed | tf_op | source)
XLA Modules:
  0.0 94.4 jit_solution(1996895944136716078)
XLA Ops:
  0.6 3.0 %soft_first.1 = (bf16[1024,1024]{1,0:T(8,128)(2,1)S(1)}, f32[128,512]{1,0:T(8,128)S(1)}, f32[128,512]{1,0:T(8,128)S(1)}, bf16[128,1024]{1,0:T(8,128)(2,1)S(1)}, ...) custom-call(s32[1,3]{1,0:T(1,128)} %bitcast.15, ...), custom_call_target="tpu_custom_call" | custom-call | flops 134217728 | bytes 1048576 | tf_op jit(solution)/shard_map/soft_first/pallas_call | solution.py:51
  3.7 0.5 collective-permute-start
  4.2 0.6 own.3.own_ref
  4.8 0.4 collective-permute-done.got_ref
  5.2 3.0 %collective-permute-start.3 = (bf16[264,128]{1,0:T(8,128)(2,1)S(1)}, bf16[264,128]{1,0:T(8,128)(2,1)S(1)}, u32[]{:S(2)}, u32[]{:S(2)}) collective-permute-start(bf16[264,128]{1,0:T(8,128)(2,1)S(1)} %get-tuple-element.83.mine_ref), channel_id=1, source_target_pairs={{0,2},{1,3},{2,0},{3,1},{4,6},{5,7},{6,4},{7,5},{8,10},{9,11},{10,... | collective-permute-start | bytes 202760 | tf_op jit(solution)/shard_map/ppermute | solution.py:399
  8.3 3.0 %collective-permute-start.5 = (bf16[128,128]{1,0:T(8,128)(2,1)S(1)}, bf16[128,128]{1,0:T(8,128)(2,1)S(1)}, u32[]{:S(2)}, u32[]{:S(2)}) collective-permute-start(bf16[128,128]{1,0:T(8,128)(2,1)S(1)} %get-tuple-element.88), channel_id=1, source_target_pairs={{0,4},{1,5},{2,6},{3,7},{4,0},{5,1},{6,2},{7,3},{8,12},{9,13},{10,... | collective-permute-start | bytes 98312 | tf_op jit(solution)/shard_map/ppermute | solution.py:399
  11.3 2.6 %collective-permute-start.4 = (bf16[264,128]{1,0:T(8,128)(2,1)S(1)}, bf16[264,128]{1,0:T(8,128)(2,1)S(1)}, u32[]{:S(2)}, u32[]{:S(2)}) collective-permute-start(bf16[264,128]{1,0:T(8,128)(2,1)S(1)} %hop_q.3.q_ref), channel_id=1, source_target_pairs={{0,4},{1,5},{2,6},{3,7},{4,0},{5,1},{6,2},{7,3},{8,12},{9,13},{10,... | collective-permute-start | bytes 202760 | tf_op jit(solution)/shard_map/ppermute | solution.py:399
  14.0 1.4 %collective-permute-start.2 = (bf16[264,128]{1,0:T(8,128)(2,1)S(1)}, bf16[264,128]{1,0:T(8,128)(2,1)S(1)}, u32[]{:S(2)}, u32[]{:S(2)}) collective-permute-start(bf16[264,128]{1,0:T(8,128)(2,1)S(1)} %hop_p.3.p_ref), channel_id=1, source_target_pairs={{0,4},{1,5},{2,6},{3,7},{4,0},{5,1},{6,2},{7,3},{8,12},{9,13},{10,... | collective-permute-start | bytes 202760 | tf_op jit(solution)/shard_map/ppermute | solution.py:399
  15.4 1.5 %collective-permute-start.6 = (bf16[2,128,128]{2,1,0:T(8,128)(2,1)S(1)}, bf16[2,128,128]{2,1,0:T(8,128)(2,1)S(1)}, u32[]{:S(2)}, u32[]{:S(2)}) collective-permute-start(bf16[2,128,128]{2,1,0:T(8,128)(2,1)S(1)} %pad_maximum_fusion), channel_id=1, source_target_pairs={{0,2},{1,3},{2,0},{3,1},{4,6},{5,7},{6,4},{7,5},{8,10},{9,11},{10,... | collective-permute-start | bytes 196616 | tf_op jit(solution)/shard_map/ppermute | solution.py:399
  17.0 2.3 %prep.2.x_ref = bf16[1024,1024]{1,0:T(8,128)(2,1)S(1)} custom-call(s32[1,3]{1,0:T(1,128)S(1)} %bitcast.16, s32[8,16]{1,0:T(8,128)S(1)} %copy-done.1, bf16[1024,2048]{1,0:T(8,128)(2,1)} %x_ref.3), custom_call_target="tpu_custom_call" | custom-call | bytes 4194304 | tf_op jit(solution)/shard_map/prep/pallas_call | solution.py:51
  19.2 1.1 %collective-permute-done.6.near_ref = bf16[2,128,128]{2,1,0:T(8,128)(2,1)S(1)} collective-permute-done((bf16[2,128,128]{2,1,0:T(8,128)(2,1)S(1)}, bf16[2,128,128]{2,1,0:T(8,128)(2,1)S(1)}, u32[]{:S(2)}, u32[]{:S(2)}) %collective-permute-start.6) | collective-permute-done | bytes 65568 | tf_op jit(solution)/shard_map/ppermute | solution.py:399
  20.6 0.4 mine.3.part_ref
  21.0 0.9 collective-permute-done.7.delta_ref
  22.3 1.6 %collective-permute-start.8 = (bf16[128,512]{1,0:T(8,128)(2,1)S(1)}, bf16[128,512]{1,0:T(8,128)(2,1)S(1)}, u32[]{:S(2)}, u32[]{:S(2)}) collective-permute-start(bf16[128,512]{1,0:T(8,128)(2,1)S(1)} %get-tuple-element.91.mine_ref), channel_id=1, source_target_pairs={{0,8},{1,9},{2,10},{3,11},{4,12},{5,13},{6,14},{7,15},{8,0},{9,1},... | collective-permute-start | bytes 393224 | tf_op jit(solution)/shard_map/ppermute | solution.py:399
  24.2 1.6 %collective-permute-start.10 = (bf16[128,512]{1,0:T(8,128)(2,1)S(1)}, bf16[128,512]{1,0:T(8,128)(2,1)S(1)}, u32[]{:S(2)}, u32[]{:S(2)}) collective-permute-start(bf16[128,512]{1,0:T(8,128)(2,1)S(1)} %get-tuple-element.97.mine_ref), channel_id=1, source_target_pairs={{0,16},{1,17},{2,18},{3,19},{4,20},{5,21},{6,22},{7,23},{8,24},{9,... | collective-permute-start | bytes 393224 | tf_op jit(solution)/shard_map/ppermute | solution.py:399
  25.8 2.1 %collective-permute-done.8.got_ref = bf16[128,512]{1,0:T(8,128)(2,1)S(1)} collective-permute-done((bf16[128,512]{1,0:T(8,128)(2,1)S(1)}, bf16[128,512]{1,0:T(8,128)(2,1)S(1)}, u32[]{:S(2)}, u32[]{:S(2)}) %collective-permute-start.8) | collective-permute-done | bytes 131104 | tf_op jit(solution)/shard_map/ppermute | solution.py:399
  28.0 1.6 %collective-permute-start.9 = (bf16[128,512]{1,0:T(8,128)(2,1)S(1)}, bf16[128,512]{1,0:T(8,128)(2,1)S(1)}, u32[]{:S(2)}, u32[]{:S(2)}) collective-permute-start(bf16[128,512]{1,0:T(8,128)(2,1)S(1)} %get-tuple-element.92.part_ref), channel_id=1, source_target_pairs={{0,16},{1,17},{2,18},{3,19},{4,20},{5,21},{6,22},{7,23},{8,24},{9,... | collective-permute-start | bytes 393224 | tf_op jit(solution)/shard_map/ppermute | solution.py:399
  29.6 1.6 %collective-permute-start.11 = (bf16[128,512]{1,0:T(8,128)(2,1)S(1)}, bf16[128,512]{1,0:T(8,128)(2,1)S(1)}, u32[]{:S(2)}, u32[]{:S(2)}) collective-permute-start(bf16[128,512]{1,0:T(8,128)(2,1)S(1)} %get-tuple-element.98.part_ref), channel_id=1, source_target_pairs={{0,8},{1,9},{2,10},{3,11},{4,12},{5,13},{6,14},{7,15},{8,0},{9,1},... | collective-permute-start | bytes 393224 | tf_op jit(solution)/shard_map/ppermute | solution.py:399
  31.2 1.8 %collective-permute-done.9.got_ref = bf16[128,512]{1,0:T(8,128)(2,1)S(1)} collective-permute-done((bf16[128,512]{1,0:T(8,128)(2,1)S(1)}, bf16[128,512]{1,0:T(8,128)(2,1)S(1)}, u32[]{:S(2)}, u32[]{:S(2)}) %collective-permute-start.9) | collective-permute-done | bytes 131104 | tf_op jit(solution)/shard_map/ppermute | solution.py:399
  33.0 0.6 soft_low.2
  33.7 1.0 %collective-permute-done.11.got_ref = bf16[128,512]{1,0:T(8,128)(2,1)S(1)} collective-permute-done((bf16[128,512]{1,0:T(8,128)(2,1)S(1)}, bf16[128,512]{1,0:T(8,128)(2,1)S(1)}, u32[]{:S(2)}, u32[]{:S(2)}) %collective-permute-start.11) | collective-permute-done | bytes 131104 | tf_op jit(solution)/shard_map/ppermute | solution.py:399
  34.7 0.5 soft_high.2
  35.5 1.0 %collective-permute-done.12.got_ref = bf16[520,128]{1,0:T(8,128)(2,1)S(1)} collective-permute-done((bf16[520,128]{1,0:T(8,128)(2,1)S(1)}, bf16[520,128]{1,0:T(8,128)(2,1)S(1)}, u32[]{:S(2)}, u32[]{:S(2)}) %collective-permute-start.12) | collective-permute-done | bytes 133152 | tf_op jit(solution)/shard_map/ppermute | solution.py:399
  36.6 1.0 %collective-permute-start.15 = (bf16[264,128]{1,0:T(8,128)(2,1)S(1)}, bf16[264,128]{1,0:T(8,128)(2,1)S(1)}, u32[]{:S(2)}, u32[]{:S(2)}) collective-permute-start(bf16[264,128]{1,0:T(8,128)(2,1)S(1)} %get-tuple-element.108.mine_ref), channel_id=1, source_target_pairs={{0,2},{1,3},{2,0},{3,1},{4,6},{5,7},{6,4},{7,5},{8,10},{9,11},{10,... | collective-permute-start | bytes 202760 | tf_op jit(solution)/shard_map/ppermute | solution.py:399
  37.6 1.1 %collective-permute-start.13 = (bf16[264,128]{1,0:T(8,128)(2,1)S(1)}, bf16[264,128]{1,0:T(8,128)(2,1)S(1)}, u32[]{:S(2)}, u32[]{:S(2)}) collective-permute-start(bf16[264,128]{1,0:T(8,128)(2,1)S(1)} %get-tuple-element.107.mine_ref), channel_id=1, source_target_pairs={{0,2},{1,3},{2,0},{3,1},{4,6},{5,7},{6,4},{7,5},{8,10},{9,11},{10,... | collective-permute-start | bytes 202760 | tf_op jit(solution)/shard_map/ppermute | solution.py:399
  38.7 2.1 %collective-permute-start.17 = (bf16[128,128]{1,0:T(8,128)(2,1)S(1)}, bf16[128,128]{1,0:T(8,128)(2,1)S(1)}, u32[]{:S(2)}, u32[]{:S(2)}) collective-permute-start(bf16[128,128]{1,0:T(8,128)(2,1)S(1)} %get-tuple-element.114), channel_id=1, source_target_pairs={{0,4},{1,5},{2,6},{3,7},{4,0},{5,1},{6,2},{7,3},{8,12},{9,13},{10,... | collective-permute-start | bytes 98312 | tf_op jit(solution)/shard_map/ppermute | solution.py:399
  40.8 0.8 collective-permute-done.15.got_ref
  41.6 1.7 %collective-permute-start.16 = (bf16[264,128]{1,0:T(8,128)(2,1)S(1)}, bf16[264,128]{1,0:T(8,128)(2,1)S(1)}, u32[]{:S(2)}, u32[]{:S(2)}) collective-permute-start(bf16[264,128]{1,0:T(8,128)(2,1)S(1)} %hop_q.4.q_ref), channel_id=1, source_target_pairs={{0,4},{1,5},{2,6},{3,7},{4,0},{5,1},{6,2},{7,3},{8,12},{9,13},{10,... | collective-permute-start | bytes 202760 | tf_op jit(solution)/shard_map/ppermute | solution.py:399
  43.3 1.8 %collective-permute-start.14 = (bf16[264,128]{1,0:T(8,128)(2,1)S(1)}, bf16[264,128]{1,0:T(8,128)(2,1)S(1)}, u32[]{:S(2)}, u32[]{:S(2)}) collective-permute-start(bf16[264,128]{1,0:T(8,128)(2,1)S(1)} %hop_p.4.p_ref), channel_id=1, source_target_pairs={{0,4},{1,5},{2,6},{3,7},{4,0},{5,1},{6,2},{7,3},{8,12},{9,13},{10,... | collective-permute-start | bytes 202760 | tf_op jit(solution)/shard_map/ppermute | solution.py:399
  45.1 1.8 %collective-permute-start.18 = (bf16[2,128,128]{2,1,0:T(8,128)(2,1)S(1)}, bf16[2,128,128]{2,1,0:T(8,128)(2,1)S(1)}, u32[]{:S(2)}, u32[]{:S(2)}) collective-permute-start(bf16[2,128,128]{2,1,0:T(8,128)(2,1)S(1)} %pad_maximum_fusion.1), channel_id=1, source_target_pairs={{0,2},{1,3},{2,0},{3,1},{4,6},{5,7},{6,4},{7,5},{8,10},{9,11},{10,... | collective-permute-start | bytes 196616 | tf_op jit(solution)/shard_map/ppermute | solution.py:399
  46.9 2.3 %prep.3.x_ref = bf16[1024,1024]{1,0:T(8,128)(2,1)S(1)} custom-call(s32[1,3]{1,0:T(1,128)S(1)} %bitcast.17, s32[8,16]{1,0:T(8,128)S(1)} %copy-done.1, bf16[1024,2048]{1,0:T(8,128)(2,1)} %x_ref.3), custom_call_target="tpu_custom_call" | custom-call | bytes 4194304 | tf_op jit(solution)/shard_map/prep/pallas_call | solution.py:51
  49.1 1.3 %collective-permute-done.18.near_ref = bf16[2,128,128]{2,1,0:T(8,128)(2,1)S(1)} collective-permute-done((bf16[2,128,128]{2,1,0:T(8,128)(2,1)S(1)}, bf16[2,128,128]{2,1,0:T(8,128)(2,1)S(1)}, u32[]{:S(2)}, u32[]{:S(2)}) %collective-permute-start.18) | collective-permute-done | bytes 65568 | tf_op jit(solution)/shard_map/ppermute | solution.py:399
  50.7 0.4 mine.4.part_ref
  51.2 0.9 collective-permute-done.19.delta_ref
  52.4 1.6 %collective-permute-start.20 = (bf16[128,512]{1,0:T(8,128)(2,1)S(1)}, bf16[128,512]{1,0:T(8,128)(2,1)S(1)}, u32[]{:S(2)}, u32[]{:S(2)}) collective-permute-start(bf16[128,512]{1,0:T(8,128)(2,1)S(1)} %get-tuple-element.119.mine_ref), channel_id=1, source_target_pairs={{0,8},{1,9},{2,10},{3,11},{4,12},{5,13},{6,14},{7,15},{8,0},{9,1},... | collective-permute-start | bytes 393224 | tf_op jit(solution)/shard_map/ppermute | solution.py:399
  54.0 0.4 change.9
  54.4 0.6 collective-permute-start.22
  55.0 3.1 %collective-permute-done.20.got_ref = bf16[128,512]{1,0:T(8,128)(2,1)S(1)} collective-permute-done((bf16[128,512]{1,0:T(8,128)(2,1)S(1)}, bf16[128,512]{1,0:T(8,128)(2,1)S(1)}, u32[]{:S(2)}, u32[]{:S(2)}) %collective-permute-start.20) | collective-permute-done | bytes 131104 | tf_op jit(solution)/shard_map/ppermute | solution.py:399
  58.1 1.6 %collective-permute-start.21 = (bf16[128,512]{1,0:T(8,128)(2,1)S(1)}, bf16[128,512]{1,0:T(8,128)(2,1)S(1)}, u32[]{:S(2)}, u32[]{:S(2)}) collective-permute-start(bf16[128,512]{1,0:T(8,128)(2,1)S(1)} %get-tuple-element.120.part_ref), channel_id=1, source_target_pairs={{0,16},{1,17},{2,18},{3,19},{4,20},{5,21},{6,22},{7,23},{8,24},{9,... | collective-permute-start | bytes 393224 | tf_op jit(solution)/shard_map/ppermute | solution.py:399
  59.8 0.6 collective-permute-start.23
  60.4 2.8 %collective-permute-done.21.got_ref = bf16[128,512]{1,0:T(8,128)(2,1)S(1)} collective-permute-done((bf16[128,512]{1,0:T(8,128)(2,1)S(1)}, bf16[128,512]{1,0:T(8,128)(2,1)S(1)}, u32[]{:S(2)}, u32[]{:S(2)}) %collective-permute-start.21) | collective-permute-done | bytes 131104 | tf_op jit(solution)/shard_map/ppermute | solution.py:399
  63.1 0.7 soft_low.3
  63.8 1.0 %collective-permute-done.23.got_ref = bf16[128,512]{1,0:T(8,128)(2,1)S(1)} collective-permute-done((bf16[128,512]{1,0:T(8,128)(2,1)S(1)}, bf16[128,512]{1,0:T(8,128)(2,1)S(1)}, u32[]{:S(2)}, u32[]{:S(2)}) %collective-permute-start.23) | collective-permute-done | bytes 131104 | tf_op jit(solution)/shard_map/ppermute | solution.py:399
  64.8 0.5 soft_high.3
  65.7 1.0 %collective-permute-done.24.got_ref = bf16[520,128]{1,0:T(8,128)(2,1)S(1)} collective-permute-done((bf16[520,128]{1,0:T(8,128)(2,1)S(1)}, bf16[520,128]{1,0:T(8,128)(2,1)S(1)}, u32[]{:S(2)}, u32[]{:S(2)}) %collective-permute-start.24) | collective-permute-done | bytes 133152 | tf_op jit(solution)/shard_map/ppermute | solution.py:399
  66.7 0.8 collective-permute-start.27
  67.5 1.3 %collective-permute-start.25 = (bf16[264,128]{1,0:T(8,128)(2,1)S(1)}, bf16[264,128]{1,0:T(8,128)(2,1)S(1)}, u32[]{:S(2)}, u32[]{:S(2)}) collective-permute-start(bf16[264,128]{1,0:T(8,128)(2,1)S(1)} %get-tuple-element.134.mine_ref), channel_id=1, source_target_pairs={{0,2},{1,3},{2,0},{3,1},{4,6},{5,7},{6,4},{7,5},{8,10},{9,11},{10,... | collective-permute-start | bytes 202760 | tf_op jit(solution)/shard_map/ppermute | solution.py:399
  68.8 2.9 %collective-permute-done.27.got_ref = bf16[264,128]{1,0:T(8,128)(2,1)S(1)} collective-permute-done((bf16[264,128]{1,0:T(8,128)(2,1)S(1)}, bf16[264,128]{1,0:T(8,128)(2,1)S(1)}, u32[]{:S(2)}, u32[]{:S(2)}) %collective-permute-start.27) | collective-permute-done | bytes 67616 | tf_op jit(solution)/shard_map/ppermute | solution.py:399
  71.7 1.2 %collective-permute-start.28 = (bf16[264,128]{1,0:T(8,128)(2,1)S(1)}, bf16[264,128]{1,0:T(8,128)(2,1)S(1)}, u32[]{:S(2)}, u32[]{:S(2)}) collective-permute-start(bf16[264,128]{1,0:T(8,128)(2,1)S(1)} %hop_q.5.q_ref), channel_id=1, source_target_pairs={{0,4},{1,5},{2,6},{3,7},{4,0},{5,1},{6,2},{7,3},{8,12},{9,13},{10,... | collective-permute-start | bytes 202760 | tf_op jit(solution)/shard_map/ppermute | solution.py:399
  73.0 1.9 %collective-permute-start.26 = (bf16[264,128]{1,0:T(8,128)(2,1)S(1)}, bf16[264,128]{1,0:T(8,128)(2,1)S(1)}, u32[]{:S(2)}, u32[]{:S(2)}) collective-permute-start(bf16[264,128]{1,0:T(8,128)(2,1)S(1)} %hop_p.5.p_ref), channel_id=1, source_target_pairs={{0,4},{1,5},{2,6},{3,7},{4,0},{5,1},{6,2},{7,3},{8,12},{9,13},{10,... | collective-permute-start | bytes 202760 | tf_op jit(solution)/shard_map/ppermute | solution.py:399
  74.9 3.9 %collective-permute-done.28.gq_ref = bf16[264,128]{1,0:T(8,128)(2,1)S(1)} collective-permute-done((bf16[264,128]{1,0:T(8,128)(2,1)S(1)}, bf16[264,128]{1,0:T(8,128)(2,1)S(1)}, u32[]{:S(2)}, u32[]{:S(2)}) %collective-permute-start.28) | collective-permute-done | bytes 67616 | tf_op jit(solution)/shard_map/ppermute | solution.py:399
  78.8 1.4 %collective-permute-done.26.gp_ref = bf16[264,128]{1,0:T(8,128)(2,1)S(1)} collective-permute-done((bf16[264,128]{1,0:T(8,128)(2,1)S(1)}, bf16[264,128]{1,0:T(8,128)(2,1)S(1)}, u32[]{:S(2)}, u32[]{:S(2)}) %collective-permute-start.26) | collective-permute-done | bytes 67616 | tf_op jit(solution)/shard_map/ppermute | solution.py:399
  80.5 0.4 mine.5.part_ref
  80.9 0.9 collective-permute-done.29.delta_ref
  82.2 0.6 collective-permute-start.30
  83.2 1.6 %collective-permute-start.32 = (bf16[128,512]{1,0:T(8,128)(2,1)S(1)}, bf16[128,512]{1,0:T(8,128)(2,1)S(1)}, u32[]{:S(2)}, u32[]{:S(2)}) collective-permute-start(bf16[128,512]{1,0:T(8,128)(2,1)S(1)} %change.11.mine_ref), channel_id=1, source_target_pairs={{0,16},{1,17},{2,18},{3,19},{4,20},{5,21},{6,22},{7,23},{8,24},{9,... | collective-permute-start | bytes 393224 | tf_op jit(solution)/shard_map/ppermute | solution.py:399
  84.7 3.1 %collective-permute-done.30.got_ref = bf16[128,512]{1,0:T(8,128)(2,1)S(1)} collective-permute-done((bf16[128,512]{1,0:T(8,128)(2,1)S(1)}, bf16[128,512]{1,0:T(8,128)(2,1)S(1)}, u32[]{:S(2)}, u32[]{:S(2)}) %collective-permute-start.30) | collective-permute-done | bytes 131104 | tf_op jit(solution)/shard_map/ppermute | solution.py:399
  87.8 0.6 collective-permute-start.31
  88.5 1.5 %collective-permute-start.33 = (bf16[128,512]{1,0:T(8,128)(2,1)S(1)}, bf16[128,512]{1,0:T(8,128)(2,1)S(1)}, u32[]{:S(2)}, u32[]{:S(2)}) collective-permute-start(bf16[128,512]{1,0:T(8,128)(2,1)S(1)} %meet_b.5.part_ref), channel_id=1, source_target_pairs={{0,8},{1,9},{2,10},{3,11},{4,12},{5,13},{6,14},{7,15},{8,0},{9,1},... | collective-permute-start | bytes 393224 | tf_op jit(solution)/shard_map/ppermute | solution.py:399
  90.1 0.6 coef_out.1
  90.7 0.7 copy.8
  91.4 1.5 %collective-permute-done.31.got_ref = bf16[128,512]{1,0:T(8,128)(2,1)S(1)} collective-permute-done((bf16[128,512]{1,0:T(8,128)(2,1)S(1)}, bf16[128,512]{1,0:T(8,128)(2,1)S(1)}, u32[]{:S(2)}, u32[]{:S(2)}) %collective-permute-start.31) | collective-permute-done | bytes 131104 | tf_op jit(solution)/shard_map/ppermute | solution.py:399
  93.0 0.6 collective-permute-done.33.got_ref
  93.6 0.9 last_high.1
  (55 shorter events, 4.2 us)
Async XLA Ops:
  3.7 13.3 %copy-start.1 = (s32[8,16]{1,0:T(8,128)S(1)}, s32[8,16]{1,0:T(8,128)}, u32[]{:S(2)}) copy-start(s32[8,16]{1,0:T(8,128)} %live_ref.3) | copy-start | bytes 1540
  3.7 13.3 %copy-start.2 = (s32[3,1]{0,1:T(1,128)S(1)}, s32[3,1]{0,1:T(1,128)}, u32[]{:S(2)}) copy-start(s32[3,1]{0,1:T(1,128)} %param.11) | copy-start | bytes 40
  3.7 1.5 %collective-permute-start = (bf16[520,128]{1,0:T(8,128)(2,1)S(1)}, bf16[520,128]{1,0:T(8,128)(2,1)S(1)}, u32[]{:S(2)}, u32[]{:S(2)}) collective-permute-start(bf16[520,128]{1,0:T(8,128)(2,1)S(1)} %get-tuple-element.78), channel_id=1, source_target_pairs={{0,1},{1,0},{2,3},{3,2},{4,5},{5,4},{6,7},{7,6},{8,9},{9,8},{10,11... | collective-permute-start | bytes 399368 | tf_op jit(solution)/shard_map/ppermute | solution.py:399
  5.2 6.0 %collective-permute-start.3 = (bf16[264,128]{1,0:T(8,128)(2,1)S(1)}, bf16[264,128]{1,0:T(8,128)(2,1)S(1)}, u32[]{:S(2)}, u32[]{:S(2)}) collective-permute-start(bf16[264,128]{1,0:T(8,128)(2,1)S(1)} %get-tuple-element.83.mine_ref), channel_id=1, source_target_pairs={{0,2},{1,3},{2,0},{3,1},{4,6},{5,7},{6,4},{7,5},{8,10},{9,11},{10,... | collective-permute-start | bytes 202760 | tf_op jit(solution)/shard_map/ppermute | solution.py:399
  8.2 5.7 %collective-permute-start.1 = (bf16[264,128]{1,0:T(8,128)(2,1)S(1)}, bf16[264,128]{1,0:T(8,128)(2,1)S(1)}, u32[]{:S(2)}, u32[]{:S(2)}) collective-permute-start(bf16[264,128]{1,0:T(8,128)(2,1)S(1)} %get-tuple-element.82.mine_ref), channel_id=1, source_target_pairs={{0,2},{1,3},{2,0},{3,1},{4,6},{5,7},{6,4},{7,5},{8,10},{9,11},{10,... | collective-permute-start | bytes 202760 | tf_op jit(solution)/shard_map/ppermute | solution.py:399
  8.3 7.1 %collective-permute-start.5 = (bf16[128,128]{1,0:T(8,128)(2,1)S(1)}, bf16[128,128]{1,0:T(8,128)(2,1)S(1)}, u32[]{:S(2)}, u32[]{:S(2)}) collective-permute-start(bf16[128,128]{1,0:T(8,128)(2,1)S(1)} %get-tuple-element.88), channel_id=1, source_target_pairs={{0,4},{1,5},{2,6},{3,7},{4,0},{5,1},{6,2},{7,3},{8,12},{9,13},{10,... | collective-permute-start | bytes 98312 | tf_op jit(solution)/shard_map/ppermute | solution.py:399
  11.3 9.1 %collective-permute-start.4 = (bf16[264,128]{1,0:T(8,128)(2,1)S(1)}, bf16[264,128]{1,0:T(8,128)(2,1)S(1)}, u32[]{:S(2)}, u32[]{:S(2)}) collective-permute-start(bf16[264,128]{1,0:T(8,128)(2,1)S(1)} %hop_q.3.q_ref), channel_id=1, source_target_pairs={{0,4},{1,5},{2,6},{3,7},{4,0},{5,1},{6,2},{7,3},{8,12},{9,13},{10,... | collective-permute-start | bytes 202760 | tf_op jit(solution)/shard_map/ppermute | solution.py:399
  14.0 6.4 %collective-permute-start.2 = (bf16[264,128]{1,0:T(8,128)(2,1)S(1)}, bf16[264,128]{1,0:T(8,128)(2,1)S(1)}, u32[]{:S(2)}, u32[]{:S(2)}) collective-permute-start(bf16[264,128]{1,0:T(8,128)(2,1)S(1)} %hop_p.3.p_ref), channel_id=1, source_target_pairs={{0,4},{1,5},{2,6},{3,7},{4,0},{5,1},{6,2},{7,3},{8,12},{9,13},{10,... | collective-permute-start | bytes 202760 | tf_op jit(solution)/shard_map/ppermute | solution.py:399
  15.4 4.9 %collective-permute-start.6 = (bf16[2,128,128]{2,1,0:T(8,128)(2,1)S(1)}, bf16[2,128,128]{2,1,0:T(8,128)(2,1)S(1)}, u32[]{:S(2)}, u32[]{:S(2)}) collective-permute-start(bf16[2,128,128]{2,1,0:T(8,128)(2,1)S(1)} %pad_maximum_fusion), channel_id=1, source_target_pairs={{0,2},{1,3},{2,0},{3,1},{4,6},{5,7},{6,4},{7,5},{8,10},{9,11},{10,... | collective-permute-start | bytes 196616 | tf_op jit(solution)/shard_map/ppermute | solution.py:399
  20.5 1.4 %collective-permute-start.7 = (bf16[128,512]{1,0:T(8,128)(2,1)S(1)}, bf16[128,512]{1,0:T(8,128)(2,1)S(1)}, u32[]{:S(2)}, u32[]{:S(2)}) collective-permute-start(bf16[128,512]{1,0:T(8,128)(2,1)S(1)} %get-tuple-element.90.delta_ref), channel_id=1, source_target_pairs={{0,1},{1,0},{2,3},{3,2},{4,5},{5,4},{6,7},{7,6},{8,9},{9,8},{10,11... | collective-permute-start | bytes 393224 | tf_op jit(solution)/shard_map/ppermute | solution.py:399
  22.3 10.7 %copy-start = (s32[1024]{0:T(1024)S(1)}, s32[1024]{0:T(1024)}, u32[]{:S(2)}) copy-start(s32[1024]{0:T(1024)} %param.8) | copy-start | bytes 12292
  22.3 5.6 %collective-permute-start.8 = (bf16[128,512]{1,0:T(8,128)(2,1)S(1)}, bf16[128,512]{1,0:T(8,128)(2,1)S(1)}, u32[]{:S(2)}, u32[]{:S(2)}) collective-permute-start(bf16[128,512]{1,0:T(8,128)(2,1)S(1)} %get-tuple-element.91.mine_ref), channel_id=1, source_target_pairs={{0,8},{1,9},{2,10},{3,11},{4,12},{5,13},{6,14},{7,15},{8,0},{9,1},... | collective-permute-start | bytes 393224 | tf_op jit(solution)/shard_map/ppermute | solution.py:399
  24.2 5.3 %collective-permute-start.10 = (bf16[128,512]{1,0:T(8,128)(2,1)S(1)}, bf16[128,512]{1,0:T(8,128)(2,1)S(1)}, u32[]{:S(2)}, u32[]{:S(2)}) collective-permute-start(bf16[128,512]{1,0:T(8,128)(2,1)S(1)} %get-tuple-element.97.mine_ref), channel_id=1, source_target_pairs={{0,16},{1,17},{2,18},{3,19},{4,20},{5,21},{6,22},{7,23},{8,24},{9,... | collective-permute-start | bytes 393224 | tf_op jit(solution)/shard_map/ppermute | solution.py:399
  28.0 5.0 %collective-permute-start.9 = (bf16[128,512]{1,0:T(8,128)(2,1)S(1)}, bf16[128,512]{1,0:T(8,128)(2,1)S(1)}, u32[]{:S(2)}, u32[]{:S(2)}) collective-permute-start(bf16[128,512]{1,0:T(8,128)(2,1)S(1)} %get-tuple-element.92.part_ref), channel_id=1, source_target_pairs={{0,16},{1,17},{2,18},{3,19},{4,20},{5,21},{6,22},{7,23},{8,24},{9,... | collective-permute-start | bytes 393224 | tf_op jit(solution)/shard_map/ppermute | solution.py:399
  29.6 5.0 %collective-permute-start.11 = (bf16[128,512]{1,0:T(8,128)(2,1)S(1)}, bf16[128,512]{1,0:T(8,128)(2,1)S(1)}, u32[]{:S(2)}, u32[]{:S(2)}) collective-permute-start(bf16[128,512]{1,0:T(8,128)(2,1)S(1)} %get-tuple-element.98.part_ref), channel_id=1, source_target_pairs={{0,8},{1,9},{2,10},{3,11},{4,12},{5,13},{6,14},{7,15},{8,0},{9,1},... | collective-permute-start | bytes 393224 | tf_op jit(solution)/shard_map/ppermute | solution.py:399
  35.1 1.4 %collective-permute-start.12 = (bf16[520,128]{1,0:T(8,128)(2,1)S(1)}, bf16[520,128]{1,0:T(8,128)(2,1)S(1)}, u32[]{:S(2)}, u32[]{:S(2)}) collective-permute-start(bf16[520,128]{1,0:T(8,128)(2,1)S(1)} %get-tuple-element.103), channel_id=1, source_target_pairs={{0,1},{1,0},{2,3},{3,2},{4,5},{5,4},{6,7},{7,6},{8,9},{9,8},{10,11... | collective-permute-start | bytes 399368 | tf_op jit(solution)/shard_map/ppermute | solution.py:399
  36.6 5.0 %collective-permute-start.15 = (bf16[264,128]{1,0:T(8,128)(2,1)S(1)}, bf16[264,128]{1,0:T(8,128)(2,1)S(1)}, u32[]{:S(2)}, u32[]{:S(2)}) collective-permute-start(bf16[264,128]{1,0:T(8,128)(2,1)S(1)} %get-tuple-element.108.mine_ref), channel_id=1, source_target_pairs={{0,2},{1,3},{2,0},{3,1},{4,6},{5,7},{6,4},{7,5},{8,10},{9,11},{10,... | collective-permute-start | bytes 202760 | tf_op jit(solution)/shard_map/ppermute | solution.py:399
  37.6 5.7 %collective-permute-start.13 = (bf16[264,128]{1,0:T(8,128)(2,1)S(1)}, bf16[264,128]{1,0:T(8,128)(2,1)S(1)}, u32[]{:S(2)}, u32[]{:S(2)}) collective-permute-start(bf16[264,128]{1,0:T(8,128)(2,1)S(1)} %get-tuple-element.107.mine_ref), channel_id=1, source_target_pairs={{0,2},{1,3},{2,0},{3,1},{4,6},{5,7},{6,4},{7,5},{8,10},{9,11},{10,... | collective-permute-start | bytes 202760 | tf_op jit(solution)/shard_map/ppermute | solution.py:399
  38.7 6.4 %collective-permute-start.17 = (bf16[128,128]{1,0:T(8,128)(2,1)S(1)}, bf16[128,128]{1,0:T(8,128)(2,1)S(1)}, u32[]{:S(2)}, u32[]{:S(2)}) collective-permute-start(bf16[128,128]{1,0:T(8,128)(2,1)S(1)} %get-tuple-element.114), channel_id=1, source_target_pairs={{0,4},{1,5},{2,6},{3,7},{4,0},{5,1},{6,2},{7,3},{8,12},{9,13},{10,... | collective-permute-start | bytes 98312 | tf_op jit(solution)/shard_map/ppermute | solution.py:399
  41.6 8.9 %collective-permute-start.16 = (bf16[264,128]{1,0:T(8,128)(2,1)S(1)}, bf16[264,128]{1,0:T(8,128)(2,1)S(1)}, u32[]{:S(2)}, u32[]{:S(2)}) collective-permute-start(bf16[264,128]{1,0:T(8,128)(2,1)S(1)} %hop_q.4.q_ref), channel_id=1, source_target_pairs={{0,4},{1,5},{2,6},{3,7},{4,0},{5,1},{6,2},{7,3},{8,12},{9,13},{10,... | collective-permute-start | bytes 202760 | tf_op jit(solution)/shard_map/ppermute | solution.py:399
  43.3 7.2 %collective-permute-start.14 = (bf16[264,128]{1,0:T(8,128)(2,1)S(1)}, bf16[264,128]{1,0:T(8,128)(2,1)S(1)}, u32[]{:S(2)}, u32[]{:S(2)}) collective-permute-start(bf16[264,128]{1,0:T(8,128)(2,1)S(1)} %hop_p.4.p_ref), channel_id=1, source_target_pairs={{0,4},{1,5},{2,6},{3,7},{4,0},{5,1},{6,2},{7,3},{8,12},{9,13},{10,... | collective-permute-start | bytes 202760 | tf_op jit(solution)/shard_map/ppermute | solution.py:399
  45.1 5.3 %collective-permute-start.18 = (bf16[2,128,128]{2,1,0:T(8,128)(2,1)S(1)}, bf16[2,128,128]{2,1,0:T(8,128)(2,1)S(1)}, u32[]{:S(2)}, u32[]{:S(2)}) collective-permute-start(bf16[2,128,128]{2,1,0:T(8,128)(2,1)S(1)} %pad_maximum_fusion.1), channel_id=1, source_target_pairs={{0,2},{1,3},{2,0},{3,1},{4,6},{5,7},{6,4},{7,5},{8,10},{9,11},{10,... | collective-permute-start | bytes 196616 | tf_op jit(solution)/shard_map/ppermute | solution.py:399
  50.6 1.4 %collective-permute-start.19 = (bf16[128,512]{1,0:T(8,128)(2,1)S(1)}, bf16[128,512]{1,0:T(8,128)(2,1)S(1)}, u32[]{:S(2)}, u32[]{:S(2)}) collective-permute-start(bf16[128,512]{1,0:T(8,128)(2,1)S(1)} %get-tuple-element.116.delta_ref), channel_id=1, source_target_pairs={{0,1},{1,0},{2,3},{3,2},{4,5},{5,4},{6,7},{7,6},{8,9},{9,8},{10,11... | collective-permute-start | bytes 393224 | tf_op jit(solution)/shard_map/ppermute | solution.py:399
  52.4 5.6 %collective-permute-start.20 = (bf16[128,512]{1,0:T(8,128)(2,1)S(1)}, bf16[128,512]{1,0:T(8,128)(2,1)S(1)}, u32[]{:S(2)}, u32[]{:S(2)}) collective-permute-start(bf16[128,512]{1,0:T(8,128)(2,1)S(1)} %get-tuple-element.119.mine_ref), channel_id=1, source_target_pairs={{0,8},{1,9},{2,10},{3,11},{4,12},{5,13},{6,14},{7,15},{8,0},{9,1},... | collective-permute-start | bytes 393224 | tf_op jit(solution)/shard_map/ppermute | solution.py:399
  54.4 5.3 %collective-permute-start.22 = (bf16[128,512]{1,0:T(8,128)(2,1)S(1)}, bf16[128,512]{1,0:T(8,128)(2,1)S(1)}, u32[]{:S(2)}, u32[]{:S(2)}) collective-permute-start(bf16[128,512]{1,0:T(8,128)(2,1)S(1)} %get-tuple-element.127.mine_ref), channel_id=1, source_target_pairs={{0,16},{1,17},{2,18},{3,19},{4,20},{5,21},{6,22},{7,23},{8,24},{9,... | collective-permute-start | bytes 393224 | tf_op jit(solution)/shard_map/ppermute | solution.py:399
  58.1 5.0 %collective-permute-start.21 = (bf16[128,512]{1,0:T(8,128)(2,1)S(1)}, bf16[128,512]{1,0:T(8,128)(2,1)S(1)}, u32[]{:S(2)}, u32[]{:S(2)}) collective-permute-start(bf16[128,512]{1,0:T(8,128)(2,1)S(1)} %get-tuple-element.120.part_ref), channel_id=1, source_target_pairs={{0,16},{1,17},{2,18},{3,19},{4,20},{5,21},{6,22},{7,23},{8,24},{9,... | collective-permute-start | bytes 393224 | tf_op jit(solution)/shard_map/ppermute | solution.py:399
  59.8 5.0 %collective-permute-start.23 = (bf16[128,512]{1,0:T(8,128)(2,1)S(1)}, bf16[128,512]{1,0:T(8,128)(2,1)S(1)}, u32[]{:S(2)}, u32[]{:S(2)}) collective-permute-start(bf16[128,512]{1,0:T(8,128)(2,1)S(1)} %get-tuple-element.128.part_ref), channel_id=1, source_target_pairs={{0,8},{1,9},{2,10},{3,11},{4,12},{5,13},{6,14},{7,15},{8,0},{9,1},... | collective-permute-start | bytes 393224 | tf_op jit(solution)/shard_map/ppermute | solution.py:399
  65.3 1.4 %collective-permute-start.24 = (bf16[520,128]{1,0:T(8,128)(2,1)S(1)}, bf16[520,128]{1,0:T(8,128)(2,1)S(1)}, u32[]{:S(2)}, u32[]{:S(2)}) collective-permute-start(bf16[520,128]{1,0:T(8,128)(2,1)S(1)} %get-tuple-element.133), channel_id=1, source_target_pairs={{0,1},{1,0},{2,3},{3,2},{4,5},{5,4},{6,7},{7,6},{8,9},{9,8},{10,11... | collective-permute-start | bytes 399368 | tf_op jit(solution)/shard_map/ppermute | solution.py:399
  66.7 5.0 %collective-permute-start.27 = (bf16[264,128]{1,0:T(8,128)(2,1)S(1)}, bf16[264,128]{1,0:T(8,128)(2,1)S(1)}, u32[]{:S(2)}, u32[]{:S(2)}) collective-permute-start(bf16[264,128]{1,0:T(8,128)(2,1)S(1)} %get-tuple-element.135.mine_ref), channel_id=1, source_target_pairs={{0,2},{1,3},{2,0},{3,1},{4,6},{5,7},{6,4},{7,5},{8,10},{9,11},{10,... | collective-permute-start | bytes 202760 | tf_op jit(solution)/shard_map/ppermute | solution.py:399
  67.5 5.5 %collective-permute-start.25 = (bf16[264,128]{1,0:T(8,128)(2,1)S(1)}, bf16[264,128]{1,0:T(8,128)(2,1)S(1)}, u32[]{:S(2)}, u32[]{:S(2)}) collective-permute-start(bf16[264,128]{1,0:T(8,128)(2,1)S(1)} %get-tuple-element.134.mine_ref), channel_id=1, source_target_pairs={{0,2},{1,3},{2,0},{3,1},{4,6},{5,7},{6,4},{7,5},{8,10},{9,11},{10,... | collective-permute-start | bytes 202760 | tf_op jit(solution)/shard_map/ppermute | solution.py:399
  71.7 7.1 %collective-permute-start.28 = (bf16[264,128]{1,0:T(8,128)(2,1)S(1)}, bf16[264,128]{1,0:T(8,128)(2,1)S(1)}, u32[]{:S(2)}, u32[]{:S(2)}) collective-permute-start(bf16[264,128]{1,0:T(8,128)(2,1)S(1)} %hop_q.5.q_ref), channel_id=1, source_target_pairs={{0,4},{1,5},{2,6},{3,7},{4,0},{5,1},{6,2},{7,3},{8,12},{9,13},{10,... | collective-permute-start | bytes 202760 | tf_op jit(solution)/shard_map/ppermute | solution.py:399
  73.0 7.3 %collective-permute-start.26 = (bf16[264,128]{1,0:T(8,128)(2,1)S(1)}, bf16[264,128]{1,0:T(8,128)(2,1)S(1)}, u32[]{:S(2)}, u32[]{:S(2)}) collective-permute-start(bf16[264,128]{1,0:T(8,128)(2,1)S(1)} %hop_p.5.p_ref), channel_id=1, source_target_pairs={{0,4},{1,5},{2,6},{3,7},{4,0},{5,1},{6,2},{7,3},{8,12},{9,13},{10,... | collective-permute-start | bytes 202760 | tf_op jit(solution)/shard_map/ppermute | solution.py:399
  80.4 1.4 %collective-permute-start.29 = (bf16[128,512]{1,0:T(8,128)(2,1)S(1)}, bf16[128,512]{1,0:T(8,128)(2,1)S(1)}, u32[]{:S(2)}, u32[]{:S(2)}) collective-permute-start(bf16[128,512]{1,0:T(8,128)(2,1)S(1)} %get-tuple-element.138.delta_ref), channel_id=1, source_target_pairs={{0,1},{1,0},{2,3},{3,2},{4,5},{5,4},{6,7},{7,6},{8,9},{9,8},{10,11... | collective-permute-start | bytes 393224 | tf_op jit(solution)/shard_map/ppermute | solution.py:399
  82.2 5.6 %collective-permute-start.30 = (bf16[128,512]{1,0:T(8,128)(2,1)S(1)}, bf16[128,512]{1,0:T(8,128)(2,1)S(1)}, u32[]{:S(2)}, u32[]{:S(2)}) collective-permute-start(bf16[128,512]{1,0:T(8,128)(2,1)S(1)} %change.10.mine_ref), channel_id=1, source_target_pairs={{0,8},{1,9},{2,10},{3,11},{4,12},{5,13},{6,14},{7,15},{8,0},{9,1},... | collective-permute-start | bytes 393224 | tf_op jit(solution)/shard_map/ppermute | solution.py:399
  83.2 5.3 %collective-permute-start.32 = (bf16[128,512]{1,0:T(8,128)(2,1)S(1)}, bf16[128,512]{1,0:T(8,128)(2,1)S(1)}, u32[]{:S(2)}, u32[]{:S(2)}) collective-permute-start(bf16[128,512]{1,0:T(8,128)(2,1)S(1)} %change.11.mine_ref), channel_id=1, source_target_pairs={{0,16},{1,17},{2,18},{3,19},{4,20},{5,21},{6,22},{7,23},{8,24},{9,... | collective-permute-start | bytes 393224 | tf_op jit(solution)/shard_map/ppermute | solution.py:399
  87.8 5.0 %collective-permute-start.31 = (bf16[128,512]{1,0:T(8,128)(2,1)S(1)}, bf16[128,512]{1,0:T(8,128)(2,1)S(1)}, u32[]{:S(2)}, u32[]{:S(2)}) collective-permute-start(bf16[128,512]{1,0:T(8,128)(2,1)S(1)} %meet_a.5.part_ref), channel_id=1, source_target_pairs={{0,16},{1,17},{2,18},{3,19},{4,20},{5,21},{6,22},{7,23},{8,24},{9,... | collective-permute-start | bytes 393224 | tf_op jit(solution)/shard_map/ppermute | solution.py:399
  88.5 5.0 %collective-permute-start.33 = (bf16[128,512]{1,0:T(8,128)(2,1)S(1)}, bf16[128,512]{1,0:T(8,128)(2,1)S(1)}, u32[]{:S(2)}, u32[]{:S(2)}) collective-permute-start(bf16[128,512]{1,0:T(8,128)(2,1)S(1)} %meet_b.5.part_ref), channel_id=1, source_target_pairs={{0,8},{1,9},{2,10},{3,11},{4,12},{5,13},{6,14},{7,15},{8,0},{9,1},... | collective-permute-start | bytes 393224 | tf_op jit(solution)/shard_map/ppermute | solution.py:399

commit v11 on v10

--- a/solution.py
+++ b/solution.py
@@ -78,13 +78,13 @@
     return copies
 
 
-def mask_tile(r, chosen, core, live_ref, buf, out_ref):
+def mask_tile(r, chosen, core, live_ref, buf, out_ref, begin=0):
     tiles = BLOCK // TILE
     here = pl.ds(r * TILE, TILE)
     for k in range(tiles):
         col = 2 * (k % NB) + (core if k < NB else 1 - core)
         live = live_ref[r, chosen * tiles + col].astype(F32)
-        tile = buf[here, pl.ds(pl.multiple_of(col * TILE, TILE), TILE)]
+        tile = buf[here, pl.ds(pl.multiple_of(begin + col * TILE, TILE), TILE)]
         out_ref[here, k * TILE : (k + 1) * TILE] = (tile.astype(F32) * live).astype(BF16)
 
 
@@ -196,11 +196,17 @@
     ]
     for load in loads:
         load.start()
-    loads[0].wait()
+    copies = [
+        pltpu.make_async_copy(
+            x_hbm.at[pl.ds(r * TILE, TILE)], buf.at[pl.ds(r * TILE, TILE)], sems.at[r]
+        )
+        for r in range(buf.shape[0] // TILE)
+    ]
+    for copy in copies:
+        copy.start()
+    for load in loads:
+        load.wait()
     chosen, core = order[0, 0], lax.axis_index("ex") % 2
-    copies = load_block(chosen, x_hbm, buf, sems)
-    for load in loads[1:]:
-        load.wait()
     for r, here in tiles_of(margins.shape[0]):
         score = margins[here, :].astype(F32).T
         keep_score(score, r, low_ref, high_ref)
@@ -213,7 +219,7 @@
         same_ref[...] = jnp.full((8, TILE), (order[0, step + 1] == chosen).astype(F32))
     for r, copy in enumerate(copies):
         copy.wait()
-        mask_tile(r, chosen, core, live, buf, x_ref)
+        mask_tile(r, chosen, core, live, buf, x_ref, chosen * BLOCK)
     half_sums(res_ref[...], spread_ref, x_ref, 0, HALF, g_ref)
 
 
@@ -480,7 +486,9 @@
                 pltpu.VMEM(labels.shape, jnp.int32),
                 pltpu.VMEM(coef.shape, F32),
                 pltpu.SemaphoreType.DMA((5,)),
-            ] + block_scratch(rows),
+                pltpu.VMEM(x_values.shape, BF16),
+                pltpu.SemaphoreType.DMA((rows // TILE,)),
+            ],
         )(order, tile_live, margins, labels, coef, x_values)
         blocks, sends, same = rest[:2], rest[2:4], rest[4:]
     else:

time: 94.7 us -> 95.6 us (level)
  Pallas kernels: 17.1 us -> 18.1 us
    pallas_call x41, Pallas kernels: 16.3 us -> 17.2 us  [run(): f(*(x if spec.memory_space == pltpu.SMEM else pltpu.with_memory_space_con...]
where the time goes in v11:
time: 95.6 us; the launch traced here: 95.4 us
  starting transfers between devices  42.1 us (44%)
  waiting for transfers between devices  33.5 us (35%)
  Pallas kernels  18.1 us (19%)
    ppermute x34, starting transfers between devices, swap(): return lax.ppermute(x, ('feat', 'ex'), pairs)  42.1 us
    ppermute x34, waiting for transfers between devices, swap(): return lax.ppermute(x, ('feat', 'ex'), pairs)  33.5 us
    pallas_call x41, Pallas kernels, run(): f(*(x if spec.memory_space == pltpu.SMEM else pltpu.with_memory_space_con...  17.2 us
  transfers between devices with their start and end apart: 34, of which 21 were waited for; matrix products, arithmetic and copies ran while one was open for 1% of the time, Pallas kernels for 11%

profile of v11, /device:TPU:0, one launch (start us, length us, event | category | flops | bytes accessed | tf_op | source)
XLA Modules:
  0.0 95.4 jit_solution(3273745769622879130)
XLA Ops:
  0.6 4.0 %soft_first.1 = (bf16[1024,1024]{1,0:T(8,128)(2,1)S(1)}, f32[128,512]{1,0:T(8,128)S(1)}, f32[128,512]{1,0:T(8,128)S(1)}, bf16[128,1024]{1,0:T(8,128)(2,1)S(1)}, ...) custom-call(s32[1,3]{1,0:T(1,128)} %bitcast.15, ...), custom_call_target="tpu_custom_call" | custom-call | flops 134217728 | bytes 1048576 | tf_op jit(solution)/shard_map/soft_first/pallas_call | solution.py:51
  4.6 0.5 collective-permute-start
  5.2 0.6 own.3.own_ref
  5.7 0.4 collective-permute-done.got_ref
  6.2 3.0 %collective-permute-start.3 = (bf16[264,128]{1,0:T(8,128)(2,1)S(1)}, bf16[264,128]{1,0:T(8,128)(2,1)S(1)}, u32[]{:S(2)}, u32[]{:S(2)}) collective-permute-start(bf16[264,128]{1,0:T(8,128)(2,1)S(1)} %get-tuple-element.83.mine_ref), channel_id=1, source_target_pairs={{0,2},{1,3},{2,0},{3,1},{4,6},{5,7},{6,4},{7,5},{8,10},{9,11},{10,... | collective-permute-start | bytes 202760 | tf_op jit(solution)/shard_map/ppermute | solution.py:405
  9.3 3.0 %collective-permute-start.5 = (bf16[128,128]{1,0:T(8,128)(2,1)S(1)}, bf16[128,128]{1,0:T(8,128)(2,1)S(1)}, u32[]{:S(2)}, u32[]{:S(2)}) collective-permute-start(bf16[128,128]{1,0:T(8,128)(2,1)S(1)} %get-tuple-element.88), channel_id=1, source_target_pairs={{0,4},{1,5},{2,6},{3,7},{4,0},{5,1},{6,2},{7,3},{8,12},{9,13},{10,... | collective-permute-start | bytes 98312 | tf_op jit(solution)/shard_map/ppermute | solution.py:405
  12.3 2.6 %collective-permute-start.4 = (bf16[264,128]{1,0:T(8,128)(2,1)S(1)}, bf16[264,128]{1,0:T(8,128)(2,1)S(1)}, u32[]{:S(2)}, u32[]{:S(2)}) collective-permute-start(bf16[264,128]{1,0:T(8,128)(2,1)S(1)} %hop_q.3.q_ref), channel_id=1, source_target_pairs={{0,4},{1,5},{2,6},{3,7},{4,0},{5,1},{6,2},{7,3},{8,12},{9,13},{10,... | collective-permute-start | bytes 202760 | tf_op jit(solution)/shard_map/ppermute | solution.py:405
  14.9 1.4 %collective-permute-start.2 = (bf16[264,128]{1,0:T(8,128)(2,1)S(1)}, bf16[264,128]{1,0:T(8,128)(2,1)S(1)}, u32[]{:S(2)}, u32[]{:S(2)}) collective-permute-start(bf16[264,128]{1,0:T(8,128)(2,1)S(1)} %hop_p.3.p_ref), channel_id=1, source_target_pairs={{0,4},{1,5},{2,6},{3,7},{4,0},{5,1},{6,2},{7,3},{8,12},{9,13},{10,... | collective-permute-start | bytes 202760 | tf_op jit(solution)/shard_map/ppermute | solution.py:405
  16.4 1.5 %collective-permute-start.6 = (bf16[2,128,128]{2,1,0:T(8,128)(2,1)S(1)}, bf16[2,128,128]{2,1,0:T(8,128)(2,1)S(1)}, u32[]{:S(2)}, u32[]{:S(2)}) collective-permute-start(bf16[2,128,128]{2,1,0:T(8,128)(2,1)S(1)} %pad_maximum_fusion), channel_id=1, source_target_pairs={{0,2},{1,3},{2,0},{3,1},{4,6},{5,7},{6,4},{7,5},{8,10},{9,11},{10,... | collective-permute-start | bytes 196616 | tf_op jit(solution)/shard_map/ppermute | solution.py:405
  18.0 2.3 %prep.2.x_ref = bf16[1024,1024]{1,0:T(8,128)(2,1)S(1)} custom-call(s32[1,3]{1,0:T(1,128)S(1)} %bitcast.16, s32[8,16]{1,0:T(8,128)S(1)} %copy-done.1, bf16[1024,2048]{1,0:T(8,128)(2,1)} %x_ref.3), custom_call_target="tpu_custom_call" | custom-call | bytes 4194304 | tf_op jit(solution)/shard_map/prep/pallas_call | solution.py:51
  20.2 1.1 %collective-permute-done.6.near_ref = bf16[2,128,128]{2,1,0:T(8,128)(2,1)S(1)} collective-permute-done((bf16[2,128,128]{2,1,0:T(8,128)(2,1)S(1)}, bf16[2,128,128]{2,1,0:T(8,128)(2,1)S(1)}, u32[]{:S(2)}, u32[]{:S(2)}) %collective-permute-start.6) | collective-permute-done | bytes 65568 | tf_op jit(solution)/shard_map/ppermute | solution.py:405
  21.5 0.4 mine.3.part_ref
  22.0 0.9 collective-permute-done.7.delta_ref
  23.3 1.6 %collective-permute-start.8 = (bf16[128,512]{1,0:T(8,128)(2,1)S(1)}, bf16[128,512]{1,0:T(8,128)(2,1)S(1)}, u32[]{:S(2)}, u32[]{:S(2)}) collective-permute-start(bf16[128,512]{1,0:T(8,128)(2,1)S(1)} %get-tuple-element.91.mine_ref), channel_id=1, source_target_pairs={{0,8},{1,9},{2,10},{3,11},{4,12},{5,13},{6,14},{7,15},{8,0},{9,1},... | collective-permute-start | bytes 393224 | tf_op jit(solution)/shard_map/ppermute | solution.py:405
  25.2 1.6 %collective-permute-start.10 = (bf16[128,512]{1,0:T(8,128)(2,1)S(1)}, bf16[128,512]{1,0:T(8,128)(2,1)S(1)}, u32[]{:S(2)}, u32[]{:S(2)}) collective-permute-start(bf16[128,512]{1,0:T(8,128)(2,1)S(1)} %get-tuple-element.97.mine_ref), channel_id=1, source_target_pairs={{0,16},{1,17},{2,18},{3,19},{4,20},{5,21},{6,22},{7,23},{8,24},{9,... | collective-permute-start | bytes 393224 | tf_op jit(solution)/shard_map/ppermute | solution.py:405
  26.8 2.1 %collective-permute-done.8.got_ref = bf16[128,512]{1,0:T(8,128)(2,1)S(1)} collective-permute-done((bf16[128,512]{1,0:T(8,128)(2,1)S(1)}, bf16[128,512]{1,0:T(8,128)(2,1)S(1)}, u32[]{:S(2)}, u32[]{:S(2)}) %collective-permute-start.8) | collective-permute-done | bytes 131104 | tf_op jit(solution)/shard_map/ppermute | solution.py:405
  28.9 1.6 %collective-permute-start.9 = (bf16[128,512]{1,0:T(8,128)(2,1)S(1)}, bf16[128,512]{1,0:T(8,128)(2,1)S(1)}, u32[]{:S(2)}, u32[]{:S(2)}) collective-permute-start(bf16[128,512]{1,0:T(8,128)(2,1)S(1)} %get-tuple-element.92.part_ref), channel_id=1, source_target_pairs={{0,16},{1,17},{2,18},{3,19},{4,20},{5,21},{6,22},{7,23},{8,24},{9,... | collective-permute-start | bytes 393224 | tf_op jit(solution)/shard_map/ppermute | solution.py:405
  30.6 1.6 %collective-permute-start.11 = (bf16[128,512]{1,0:T(8,128)(2,1)S(1)}, bf16[128,512]{1,0:T(8,128)(2,1)S(1)}, u32[]{:S(2)}, u32[]{:S(2)}) collective-permute-start(bf16[128,512]{1,0:T(8,128)(2,1)S(1)} %get-tuple-element.98.part_ref), channel_id=1, source_target_pairs={{0,8},{1,9},{2,10},{3,11},{4,12},{5,13},{6,14},{7,15},{8,0},{9,1},... | collective-permute-start | bytes 393224 | tf_op jit(solution)/shard_map/ppermute | solution.py:405
  32.2 1.8 %collective-permute-done.9.got_ref = bf16[128,512]{1,0:T(8,128)(2,1)S(1)} collective-permute-done((bf16[128,512]{1,0:T(8,128)(2,1)S(1)}, bf16[128,512]{1,0:T(8,128)(2,1)S(1)}, u32[]{:S(2)}, u32[]{:S(2)}) %collective-permute-start.9) | collective-permute-done | bytes 131104 | tf_op jit(solution)/shard_map/ppermute | solution.py:405
  34.0 0.6 soft_low.2
  34.6 1.0 %collective-permute-done.11.got_ref = bf16[128,512]{1,0:T(8,128)(2,1)S(1)} collective-permute-done((bf16[128,512]{1,0:T(8,128)(2,1)S(1)}, bf16[128,512]{1,0:T(8,128)(2,1)S(1)}, u32[]{:S(2)}, u32[]{:S(2)}) %collective-permute-start.11) | collective-permute-done | bytes 131104 | tf_op jit(solution)/shard_map/ppermute | solution.py:405
  35.6 0.5 soft_high.2
  36.5 1.0 %collective-permute-done.12.got_ref = bf16[520,128]{1,0:T(8,128)(2,1)S(1)} collective-permute-done((bf16[520,128]{1,0:T(8,128)(2,1)S(1)}, bf16[520,128]{1,0:T(8,128)(2,1)S(1)}, u32[]{:S(2)}, u32[]{:S(2)}) %collective-permute-start.12) | collective-permute-done | bytes 133152 | tf_op jit(solution)/shard_map/ppermute | solution.py:405
  37.6 1.0 %collective-permute-start.15 = (bf16[264,128]{1,0:T(8,128)(2,1)S(1)}, bf16[264,128]{1,0:T(8,128)(2,1)S(1)}, u32[]{:S(2)}, u32[]{:S(2)}) collective-permute-start(bf16[264,128]{1,0:T(8,128)(2,1)S(1)} %get-tuple-element.108.mine_ref), channel_id=1, source_target_pairs={{0,2},{1,3},{2,0},{3,1},{4,6},{5,7},{6,4},{7,5},{8,10},{9,11},{10,... | collective-permute-start | bytes 202760 | tf_op jit(solution)/shard_map/ppermute | solution.py:405
  38.5 1.1 %collective-permute-start.13 = (bf16[264,128]{1,0:T(8,128)(2,1)S(1)}, bf16[264,128]{1,0:T(8,128)(2,1)S(1)}, u32[]{:S(2)}, u32[]{:S(2)}) collective-permute-start(bf16[264,128]{1,0:T(8,128)(2,1)S(1)} %get-tuple-element.107.mine_ref), channel_id=1, source_target_pairs={{0,2},{1,3},{2,0},{3,1},{4,6},{5,7},{6,4},{7,5},{8,10},{9,11},{10,... | collective-permute-start | bytes 202760 | tf_op jit(solution)/shard_map/ppermute | solution.py:405
  39.7 2.1 %collective-permute-start.17 = (bf16[128,128]{1,0:T(8,128)(2,1)S(1)}, bf16[128,128]{1,0:T(8,128)(2,1)S(1)}, u32[]{:S(2)}, u32[]{:S(2)}) collective-permute-start(bf16[128,128]{1,0:T(8,128)(2,1)S(1)} %get-tuple-element.114), channel_id=1, source_target_pairs={{0,4},{1,5},{2,6},{3,7},{4,0},{5,1},{6,2},{7,3},{8,12},{9,13},{10,... | collective-permute-start | bytes 98312 | tf_op jit(solution)/shard_map/ppermute | solution.py:405
  41.8 0.8 collective-permute-done.15.got_ref
  42.6 1.7 %collective-permute-start.16 = (bf16[264,128]{1,0:T(8,128)(2,1)S(1)}, bf16[264,128]{1,0:T(8,128)(2,1)S(1)}, u32[]{:S(2)}, u32[]{:S(2)}) collective-permute-start(bf16[264,128]{1,0:T(8,128)(2,1)S(1)} %hop_q.4.q_ref), channel_id=1, source_target_pairs={{0,4},{1,5},{2,6},{3,7},{4,0},{5,1},{6,2},{7,3},{8,12},{9,13},{10,... | collective-permute-start | bytes 202760 | tf_op jit(solution)/shard_map/ppermute | solution.py:405
  44.3 1.8 %collective-permute-start.14 = (bf16[264,128]{1,0:T(8,128)(2,1)S(1)}, bf16[264,128]{1,0:T(8,128)(2,1)S(1)}, u32[]{:S(2)}, u32[]{:S(2)}) collective-permute-start(bf16[264,128]{1,0:T(8,128)(2,1)S(1)} %hop_p.4.p_ref), channel_id=1, source_target_pairs={{0,4},{1,5},{2,6},{3,7},{4,0},{5,1},{6,2},{7,3},{8,12},{9,13},{10,... | collective-permute-start | bytes 202760 | tf_op jit(solution)/shard_map/ppermute | solution.py:405
  46.1 1.8 %collective-permute-start.18 = (bf16[2,128,128]{2,1,0:T(8,128)(2,1)S(1)}, bf16[2,128,128]{2,1,0:T(8,128)(2,1)S(1)}, u32[]{:S(2)}, u32[]{:S(2)}) collective-permute-start(bf16[2,128,128]{2,1,0:T(8,128)(2,1)S(1)} %pad_maximum_fusion.1), channel_id=1, source_target_pairs={{0,2},{1,3},{2,0},{3,1},{4,6},{5,7},{6,4},{7,5},{8,10},{9,11},{10,... | collective-permute-start | bytes 196616 | tf_op jit(solution)/shard_map/ppermute | solution.py:405
  47.8 2.3 %prep.3.x_ref = bf16[1024,1024]{1,0:T(8,128)(2,1)S(1)} custom-call(s32[1,3]{1,0:T(1,128)S(1)} %bitcast.17, s32[8,16]{1,0:T(8,128)S(1)} %copy-done.1, bf16[1024,2048]{1,0:T(8,128)(2,1)} %x_ref.3), custom_call_target="tpu_custom_call" | custom-call | bytes 4194304 | tf_op jit(solution)/shard_map/prep/pallas_call | solution.py:51
  50.1 1.3 %collective-permute-done.18.near_ref = bf16[2,128,128]{2,1,0:T(8,128)(2,1)S(1)} collective-permute-done((bf16[2,128,128]{2,1,0:T(8,128)(2,1)S(1)}, bf16[2,128,128]{2,1,0:T(8,128)(2,1)S(1)}, u32[]{:S(2)}, u32[]{:S(2)}) %collective-permute-start.18) | collective-permute-done | bytes 65568 | tf_op jit(solution)/shard_map/ppermute | solution.py:405
  51.7 0.4 mine.4.part_ref
  52.1 0.9 collective-permute-done.19.delta_ref
  53.0 0.4 change.8
  53.4 1.5 %collective-permute-start.20 = (bf16[128,512]{1,0:T(8,128)(2,1)S(1)}, bf16[128,512]{1,0:T(8,128)(2,1)S(1)}, u32[]{:S(2)}, u32[]{:S(2)}) collective-permute-start(bf16[128,512]{1,0:T(8,128)(2,1)S(1)} %get-tuple-element.119.mine_ref), channel_id=1, source_target_pairs={{0,8},{1,9},{2,10},{3,11},{4,12},{5,13},{6,14},{7,15},{8,0},{9,1},... | collective-permute-start | bytes 393224 | tf_op jit(solution)/shard_map/ppermute | solution.py:405
  55.3 0.6 collective-permute-start.22
  56.0 3.1 %collective-permute-done.20.got_ref = bf16[128,512]{1,0:T(8,128)(2,1)S(1)} collective-permute-done((bf16[128,512]{1,0:T(8,128)(2,1)S(1)}, bf16[128,512]{1,0:T(8,128)(2,1)S(1)}, u32[]{:S(2)}, u32[]{:S(2)}) %collective-permute-start.20) | collective-permute-done | bytes 131104 | tf_op jit(solution)/shard_map/ppermute | solution.py:405
  59.1 1.6 %collective-permute-start.21 = (bf16[128,512]{1,0:T(8,128)(2,1)S(1)}, bf16[128,512]{1,0:T(8,128)(2,1)S(1)}, u32[]{:S(2)}, u32[]{:S(2)}) collective-permute-start(bf16[128,512]{1,0:T(8,128)(2,1)S(1)} %get-tuple-element.120.part_ref), channel_id=1, source_target_pairs={{0,16},{1,17},{2,18},{3,19},{4,20},{5,21},{6,22},{7,23},{8,24},{9,... | collective-permute-start | bytes 393224 | tf_op jit(solution)/shard_map/ppermute | solution.py:405
  60.7 0.6 collective-permute-start.23
  61.3 2.8 %collective-permute-done.21.got_ref = bf16[128,512]{1,0:T(8,128)(2,1)S(1)} collective-permute-done((bf16[128,512]{1,0:T(8,128)(2,1)S(1)}, bf16[128,512]{1,0:T(8,128)(2,1)S(1)}, u32[]{:S(2)}, u32[]{:S(2)}) %collective-permute-start.21) | collective-permute-done | bytes 131104 | tf_op jit(solution)/shard_map/ppermute | solution.py:405
  64.1 0.7 soft_low.3
  64.8 1.0 %collective-permute-done.23.got_ref = bf16[128,512]{1,0:T(8,128)(2,1)S(1)} collective-permute-done((bf16[128,512]{1,0:T(8,128)(2,1)S(1)}, bf16[128,512]{1,0:T(8,128)(2,1)S(1)}, u32[]{:S(2)}, u32[]{:S(2)}) %collective-permute-start.23) | collective-permute-done | bytes 131104 | tf_op jit(solution)/shard_map/ppermute | solution.py:405
  65.8 0.5 soft_high.3
  66.6 1.0 %collective-permute-done.24.got_ref = bf16[520,128]{1,0:T(8,128)(2,1)S(1)} collective-permute-done((bf16[520,128]{1,0:T(8,128)(2,1)S(1)}, bf16[520,128]{1,0:T(8,128)(2,1)S(1)}, u32[]{:S(2)}, u32[]{:S(2)}) %collective-permute-start.24) | collective-permute-done | bytes 133152 | tf_op jit(solution)/shard_map/ppermute | solution.py:405
  67.7 0.8 collective-permute-start.27
  68.5 1.3 %collective-permute-start.25 = (bf16[264,128]{1,0:T(8,128)(2,1)S(1)}, bf16[264,128]{1,0:T(8,128)(2,1)S(1)}, u32[]{:S(2)}, u32[]{:S(2)}) collective-permute-start(bf16[264,128]{1,0:T(8,128)(2,1)S(1)} %get-tuple-element.134.mine_ref), channel_id=1, source_target_pairs={{0,2},{1,3},{2,0},{3,1},{4,6},{5,7},{6,4},{7,5},{8,10},{9,11},{10,... | collective-permute-start | bytes 202760 | tf_op jit(solution)/shard_map/ppermute | solution.py:405
  69.8 2.9 %collective-permute-done.27.got_ref = bf16[264,128]{1,0:T(8,128)(2,1)S(1)} collective-permute-done((bf16[264,128]{1,0:T(8,128)(2,1)S(1)}, bf16[264,128]{1,0:T(8,128)(2,1)S(1)}, u32[]{:S(2)}, u32[]{:S(2)}) %collective-permute-start.27) | collective-permute-done | bytes 67616 | tf_op jit(solution)/shard_map/ppermute | solution.py:405
  72.7 1.2 %collective-permute-start.28 = (bf16[264,128]{1,0:T(8,128)(2,1)S(1)}, bf16[264,128]{1,0:T(8,128)(2,1)S(1)}, u32[]{:S(2)}, u32[]{:S(2)}) collective-permute-start(bf16[264,128]{1,0:T(8,128)(2,1)S(1)} %hop_q.5.q_ref), channel_id=1, source_target_pairs={{0,4},{1,5},{2,6},{3,7},{4,0},{5,1},{6,2},{7,3},{8,12},{9,13},{10,... | collective-permute-start | bytes 202760 | tf_op jit(solution)/shard_map/ppermute | solution.py:405
  74.0 1.9 %collective-permute-start.26 = (bf16[264,128]{1,0:T(8,128)(2,1)S(1)}, bf16[264,128]{1,0:T(8,128)(2,1)S(1)}, u32[]{:S(2)}, u32[]{:S(2)}) collective-permute-start(bf16[264,128]{1,0:T(8,128)(2,1)S(1)} %hop_p.5.p_ref), channel_id=1, source_target_pairs={{0,4},{1,5},{2,6},{3,7},{4,0},{5,1},{6,2},{7,3},{8,12},{9,13},{10,... | collective-permute-start | bytes 202760 | tf_op jit(solution)/shard_map/ppermute | solution.py:405
  75.9 3.9 %collective-permute-done.28.gq_ref = bf16[264,128]{1,0:T(8,128)(2,1)S(1)} collective-permute-done((bf16[264,128]{1,0:T(8,128)(2,1)S(1)}, bf16[264,128]{1,0:T(8,128)(2,1)S(1)}, u32[]{:S(2)}, u32[]{:S(2)}) %collective-permute-start.28) | collective-permute-done | bytes 67616 | tf_op jit(solution)/shard_map/ppermute | solution.py:405
  79.8 1.4 %collective-permute-done.26.gp_ref = bf16[264,128]{1,0:T(8,128)(2,1)S(1)} collective-permute-done((bf16[264,128]{1,0:T(8,128)(2,1)S(1)}, bf16[264,128]{1,0:T(8,128)(2,1)S(1)}, u32[]{:S(2)}, u32[]{:S(2)}) %collective-permute-start.26) | collective-permute-done | bytes 67616 | tf_op jit(solution)/shard_map/ppermute | solution.py:405
  81.5 0.4 mine.5.part_ref
  81.9 0.9 collective-permute-done.29.delta_ref
  83.2 0.6 collective-permute-start.30
  84.1 1.6 %collective-permute-start.32 = (bf16[128,512]{1,0:T(8,128)(2,1)S(1)}, bf16[128,512]{1,0:T(8,128)(2,1)S(1)}, u32[]{:S(2)}, u32[]{:S(2)}) collective-permute-start(bf16[128,512]{1,0:T(8,128)(2,1)S(1)} %change.11.mine_ref), channel_id=1, source_target_pairs={{0,16},{1,17},{2,18},{3,19},{4,20},{5,21},{6,22},{7,23},{8,24},{9,... | collective-permute-start | bytes 393224 | tf_op jit(solution)/shard_map/ppermute | solution.py:405
  85.7 3.1 %collective-permute-done.30.got_ref = bf16[128,512]{1,0:T(8,128)(2,1)S(1)} collective-permute-done((bf16[128,512]{1,0:T(8,128)(2,1)S(1)}, bf16[128,512]{1,0:T(8,128)(2,1)S(1)}, u32[]{:S(2)}, u32[]{:S(2)}) %collective-permute-start.30) | collective-permute-done | bytes 131104 | tf_op jit(solution)/shard_map/ppermute | solution.py:405
  88.8 0.6 collective-permute-start.31
  89.5 1.6 %collective-permute-start.33 = (bf16[128,512]{1,0:T(8,128)(2,1)S(1)}, bf16[128,512]{1,0:T(8,128)(2,1)S(1)}, u32[]{:S(2)}, u32[]{:S(2)}) collective-permute-start(bf16[128,512]{1,0:T(8,128)(2,1)S(1)} %meet_b.5.part_ref), channel_id=1, source_target_pairs={{0,8},{1,9},{2,10},{3,11},{4,12},{5,13},{6,14},{7,15},{8,0},{9,1},... | collective-permute-start | bytes 393224 | tf_op jit(solution)/shard_map/ppermute | solution.py:405
  91.0 0.6 coef_out.1
  91.7 0.7 copy.8
  92.4 1.5 %collective-permute-done.31.got_ref = bf16[128,512]{1,0:T(8,128)(2,1)S(1)} collective-permute-done((bf16[128,512]{1,0:T(8,128)(2,1)S(1)}, bf16[128,512]{1,0:T(8,128)(2,1)S(1)}, u32[]{:S(2)}, u32[]{:S(2)}) %collective-permute-start.31) | collective-permute-done | bytes 131104 | tf_op jit(solution)/shard_map/ppermute | solution.py:405
  94.0 0.5 collective-permute-done.33.got_ref
  94.5 0.9 last_high.1
  (55 shorter events, 4.2 us)
Async XLA Ops:
  4.6 13.3 %copy-start.1 = (s32[8,16]{1,0:T(8,128)S(1)}, s32[8,16]{1,0:T(8,128)}, u32[]{:S(2)}) copy-start(s32[8,16]{1,0:T(8,128)} %live_ref.3) | copy-start | bytes 1540
  4.6 13.3 %copy-start.2 = (s32[3,1]{0,1:T(1,128)S(1)}, s32[3,1]{0,1:T(1,128)}, u32[]{:S(2)}) copy-start(s32[3,1]{0,1:T(1,128)} %param.11) | copy-start | bytes 40
  4.6 1.5 %collective-permute-start = (bf16[520,128]{1,0:T(8,128)(2,1)S(1)}, bf16[520,128]{1,0:T(8,128)(2,1)S(1)}, u32[]{:S(2)}, u32[]{:S(2)}) collective-permute-start(bf16[520,128]{1,0:T(8,128)(2,1)S(1)} %get-tuple-element.78), channel_id=1, source_target_pairs={{0,1},{1,0},{2,3},{3,2},{4,5},{5,4},{6,7},{7,6},{8,9},{9,8},{10,11... | collective-permute-start | bytes 399368 | tf_op jit(solution)/shard_map/ppermute | solution.py:405
  6.2 6.0 %collective-permute-start.3 = (bf16[264,128]{1,0:T(8,128)(2,1)S(1)}, bf16[264,128]{1,0:T(8,128)(2,1)S(1)}, u32[]{:S(2)}, u32[]{:S(2)}) collective-permute-start(bf16[264,128]{1,0:T(8,128)(2,1)S(1)} %get-tuple-element.83.mine_ref), channel_id=1, source_target_pairs={{0,2},{1,3},{2,0},{3,1},{4,6},{5,7},{6,4},{7,5},{8,10},{9,11},{10,... | collective-permute-start | bytes 202760 | tf_op jit(solution)/shard_map/ppermute | solution.py:405
  9.2 5.7 %collective-permute-start.1 = (bf16[264,128]{1,0:T(8,128)(2,1)S(1)}, bf16[264,128]{1,0:T(8,128)(2,1)S(1)}, u32[]{:S(2)}, u32[]{:S(2)}) collective-permute-start(bf16[264,128]{1,0:T(8,128)(2,1)S(1)} %get-tuple-element.82.mine_ref), channel_id=1, source_target_pairs={{0,2},{1,3},{2,0},{3,1},{4,6},{5,7},{6,4},{7,5},{8,10},{9,11},{10,... | collective-permute-start | bytes 202760 | tf_op jit(solution)/shard_map/ppermute | solution.py:405
  9.3 7.1 %collective-permute-start.5 = (bf16[128,128]{1,0:T(8,128)(2,1)S(1)}, bf16[128,128]{1,0:T(8,128)(2,1)S(1)}, u32[]{:S(2)}, u32[]{:S(2)}) collective-permute-start(bf16[128,128]{1,0:T(8,128)(2,1)S(1)} %get-tuple-element.88), channel_id=1, source_target_pairs={{0,4},{1,5},{2,6},{3,7},{4,0},{5,1},{6,2},{7,3},{8,12},{9,13},{10,... | collective-permute-start | bytes 98312 | tf_op jit(solution)/shard_map/ppermute | solution.py:405
  12.3 9.1 %collective-permute-start.4 = (bf16[264,128]{1,0:T(8,128)(2,1)S(1)}, bf16[264,128]{1,0:T(8,128)(2,1)S(1)}, u32[]{:S(2)}, u32[]{:S(2)}) collective-permute-start(bf16[264,128]{1,0:T(8,128)(2,1)S(1)} %hop_q.3.q_ref), channel_id=1, source_target_pairs={{0,4},{1,5},{2,6},{3,7},{4,0},{5,1},{6,2},{7,3},{8,12},{9,13},{10,... | collective-permute-start | bytes 202760 | tf_op jit(solution)/shard_map/ppermute | solution.py:405
  14.9 6.4 %collective-permute-start.2 = (bf16[264,128]{1,0:T(8,128)(2,1)S(1)}, bf16[264,128]{1,0:T(8,128)(2,1)S(1)}, u32[]{:S(2)}, u32[]{:S(2)}) collective-permute-start(bf16[264,128]{1,0:T(8,128)(2,1)S(1)} %hop_p.3.p_ref), channel_id=1, source_target_pairs={{0,4},{1,5},{2,6},{3,7},{4,0},{5,1},{6,2},{7,3},{8,12},{9,13},{10,... | collective-permute-start | bytes 202760 | tf_op jit(solution)/shard_map/ppermute | solution.py:405
  16.4 4.9 %collective-permute-start.6 = (bf16[2,128,128]{2,1,0:T(8,128)(2,1)S(1)}, bf16[2,128,128]{2,1,0:T(8,128)(2,1)S(1)}, u32[]{:S(2)}, u32[]{:S(2)}) collective-permute-start(bf16[2,128,128]{2,1,0:T(8,128)(2,1)S(1)} %pad_maximum_fusion), channel_id=1, source_target_pairs={{0,2},{1,3},{2,0},{3,1},{4,6},{5,7},{6,4},{7,5},{8,10},{9,11},{10,... | collective-permute-start | bytes 196616 | tf_op jit(solution)/shard_map/ppermute | solution.py:405
  21.5 1.4 %collective-permute-start.7 = (bf16[128,512]{1,0:T(8,128)(2,1)S(1)}, bf16[128,512]{1,0:T(8,128)(2,1)S(1)}, u32[]{:S(2)}, u32[]{:S(2)}) collective-permute-start(bf16[128,512]{1,0:T(8,128)(2,1)S(1)} %get-tuple-element.90.delta_ref), channel_id=1, source_target_pairs={{0,1},{1,0},{2,3},{3,2},{4,5},{5,4},{6,7},{7,6},{8,9},{9,8},{10,11... | collective-permute-start | bytes 393224 | tf_op jit(solution)/shard_map/ppermute | solution.py:405
  23.3 10.7 %copy-start = (s32[1024]{0:T(1024)S(1)}, s32[1024]{0:T(1024)}, u32[]{:S(2)}) copy-start(s32[1024]{0:T(1024)} %param.8) | copy-start | bytes 12292
  23.3 5.6 %collective-permute-start.8 = (bf16[128,512]{1,0:T(8,128)(2,1)S(1)}, bf16[128,512]{1,0:T(8,128)(2,1)S(1)}, u32[]{:S(2)}, u32[]{:S(2)}) collective-permute-start(bf16[128,512]{1,0:T(8,128)(2,1)S(1)} %get-tuple-element.91.mine_ref), channel_id=1, source_target_pairs={{0,8},{1,9},{2,10},{3,11},{4,12},{5,13},{6,14},{7,15},{8,0},{9,1},... | collective-permute-start | bytes 393224 | tf_op jit(solution)/shard_map/ppermute | solution.py:405
  25.2 5.3 %collective-permute-start.10 = (bf16[128,512]{1,0:T(8,128)(2,1)S(1)}, bf16[128,512]{1,0:T(8,128)(2,1)S(1)}, u32[]{:S(2)}, u32[]{:S(2)}) collective-permute-start(bf16[128,512]{1,0:T(8,128)(2,1)S(1)} %get-tuple-element.97.mine_ref), channel_id=1, source_target_pairs={{0,16},{1,17},{2,18},{3,19},{4,20},{5,21},{6,22},{7,23},{8,24},{9,... | collective-permute-start | bytes 393224 | tf_op jit(solution)/shard_map/ppermute | solution.py:405
  28.9 5.0 %collective-permute-start.9 = (bf16[128,512]{1,0:T(8,128)(2,1)S(1)}, bf16[128,512]{1,0:T(8,128)(2,1)S(1)}, u32[]{:S(2)}, u32[]{:S(2)}) collective-permute-start(bf16[128,512]{1,0:T(8,128)(2,1)S(1)} %get-tuple-element.92.part_ref), channel_id=1, source_target_pairs={{0,16},{1,17},{2,18},{3,19},{4,20},{5,21},{6,22},{7,23},{8,24},{9,... | collective-permute-start | bytes 393224 | tf_op jit(solution)/shard_map/ppermute | solution.py:405
  30.6 5.0 %collective-permute-start.11 = (bf16[128,512]{1,0:T(8,128)(2,1)S(1)}, bf16[128,512]{1,0:T(8,128)(2,1)S(1)}, u32[]{:S(2)}, u32[]{:S(2)}) collective-permute-start(bf16[128,512]{1,0:T(8,128)(2,1)S(1)} %get-tuple-element.98.part_ref), channel_id=1, source_target_pairs={{0,8},{1,9},{2,10},{3,11},{4,12},{5,13},{6,14},{7,15},{8,0},{9,1},... | collective-permute-start | bytes 393224 | tf_op jit(solution)/shard_map/ppermute | solution.py:405
  36.1 1.4 %collective-permute-start.12 = (bf16[520,128]{1,0:T(8,128)(2,1)S(1)}, bf16[520,128]{1,0:T(8,128)(2,1)S(1)}, u32[]{:S(2)}, u32[]{:S(2)}) collective-permute-start(bf16[520,128]{1,0:T(8,128)(2,1)S(1)} %get-tuple-element.103), channel_id=1, source_target_pairs={{0,1},{1,0},{2,3},{3,2},{4,5},{5,4},{6,7},{7,6},{8,9},{9,8},{10,11... | collective-permute-start | bytes 399368 | tf_op jit(solution)/shard_map/ppermute | solution.py:405
  37.6 5.0 %collective-permute-start.15 = (bf16[264,128]{1,0:T(8,128)(2,1)S(1)}, bf16[264,128]{1,0:T(8,128)(2,1)S(1)}, u32[]{:S(2)}, u32[]{:S(2)}) collective-permute-start(bf16[264,128]{1,0:T(8,128)(2,1)S(1)} %get-tuple-element.108.mine_ref), channel_id=1, source_target_pairs={{0,2},{1,3},{2,0},{3,1},{4,6},{5,7},{6,4},{7,5},{8,10},{9,11},{10,... | collective-permute-start | bytes 202760 | tf_op jit(solution)/shard_map/ppermute | solution.py:405
  38.5 5.7 %collective-permute-start.13 = (bf16[264,128]{1,0:T(8,128)(2,1)S(1)}, bf16[264,128]{1,0:T(8,128)(2,1)S(1)}, u32[]{:S(2)}, u32[]{:S(2)}) collective-permute-start(bf16[264,128]{1,0:T(8,128)(2,1)S(1)} %get-tuple-element.107.mine_ref), channel_id=1, source_target_pairs={{0,2},{1,3},{2,0},{3,1},{4,6},{5,7},{6,4},{7,5},{8,10},{9,11},{10,... | collective-permute-start | bytes 202760 | tf_op jit(solution)/shard_map/ppermute | solution.py:405
  39.7 6.4 %collective-permute-start.17 = (bf16[128,128]{1,0:T(8,128)(2,1)S(1)}, bf16[128,128]{1,0:T(8,128)(2,1)S(1)}, u32[]{:S(2)}, u32[]{:S(2)}) collective-permute-start(bf16[128,128]{1,0:T(8,128)(2,1)S(1)} %get-tuple-element.114), channel_id=1, source_target_pairs={{0,4},{1,5},{2,6},{3,7},{4,0},{5,1},{6,2},{7,3},{8,12},{9,13},{10,... | collective-permute-start | bytes 98312 | tf_op jit(solution)/shard_map/ppermute | solution.py:405
  42.6 8.9 %collective-permute-start.16 = (bf16[264,128]{1,0:T(8,128)(2,1)S(1)}, bf16[264,128]{1,0:T(8,128)(2,1)S(1)}, u32[]{:S(2)}, u32[]{:S(2)}) collective-permute-start(bf16[264,128]{1,0:T(8,128)(2,1)S(1)} %hop_q.4.q_ref), channel_id=1, source_target_pairs={{0,4},{1,5},{2,6},{3,7},{4,0},{5,1},{6,2},{7,3},{8,12},{9,13},{10,... | collective-permute-start | bytes 202760 | tf_op jit(solution)/shard_map/ppermute | solution.py:405
  44.3 7.2 %collective-permute-start.14 = (bf16[264,128]{1,0:T(8,128)(2,1)S(1)}, bf16[264,128]{1,0:T(8,128)(2,1)S(1)}, u32[]{:S(2)}, u32[]{:S(2)}) collective-permute-start(bf16[264,128]{1,0:T(8,128)(2,1)S(1)} %hop_p.4.p_ref), channel_id=1, source_target_pairs={{0,4},{1,5},{2,6},{3,7},{4,0},{5,1},{6,2},{7,3},{8,12},{9,13},{10,... | collective-permute-start | bytes 202760 | tf_op jit(solution)/shard_map/ppermute | solution.py:405
  46.1 5.3 %collective-permute-start.18 = (bf16[2,128,128]{2,1,0:T(8,128)(2,1)S(1)}, bf16[2,128,128]{2,1,0:T(8,128)(2,1)S(1)}, u32[]{:S(2)}, u32[]{:S(2)}) collective-permute-start(bf16[2,128,128]{2,1,0:T(8,128)(2,1)S(1)} %pad_maximum_fusion.1), channel_id=1, source_target_pairs={{0,2},{1,3},{2,0},{3,1},{4,6},{5,7},{6,4},{7,5},{8,10},{9,11},{10,... | collective-permute-start | bytes 196616 | tf_op jit(solution)/shard_map/ppermute | solution.py:405
  51.6 1.4 %collective-permute-start.19 = (bf16[128,512]{1,0:T(8,128)(2,1)S(1)}, bf16[128,512]{1,0:T(8,128)(2,1)S(1)}, u32[]{:S(2)}, u32[]{:S(2)}) collective-permute-start(bf16[128,512]{1,0:T(8,128)(2,1)S(1)} %get-tuple-element.116.delta_ref), channel_id=1, source_target_pairs={{0,1},{1,0},{2,3},{3,2},{4,5},{5,4},{6,7},{7,6},{8,9},{9,8},{10,11... | collective-permute-start | bytes 393224 | tf_op jit(solution)/shard_map/ppermute | solution.py:405
  53.4 5.6 %collective-permute-start.20 = (bf16[128,512]{1,0:T(8,128)(2,1)S(1)}, bf16[128,512]{1,0:T(8,128)(2,1)S(1)}, u32[]{:S(2)}, u32[]{:S(2)}) collective-permute-start(bf16[128,512]{1,0:T(8,128)(2,1)S(1)} %get-tuple-element.119.mine_ref), channel_id=1, source_target_pairs={{0,8},{1,9},{2,10},{3,11},{4,12},{5,13},{6,14},{7,15},{8,0},{9,1},... | collective-permute-start | bytes 393224 | tf_op jit(solution)/shard_map/ppermute | solution.py:405
  55.3 5.3 %collective-permute-start.22 = (bf16[128,512]{1,0:T(8,128)(2,1)S(1)}, bf16[128,512]{1,0:T(8,128)(2,1)S(1)}, u32[]{:S(2)}, u32[]{:S(2)}) collective-permute-start(bf16[128,512]{1,0:T(8,128)(2,1)S(1)} %get-tuple-element.127.mine_ref), channel_id=1, source_target_pairs={{0,16},{1,17},{2,18},{3,19},{4,20},{5,21},{6,22},{7,23},{8,24},{9,... | collective-permute-start | bytes 393224 | tf_op jit(solution)/shard_map/ppermute | solution.py:405
  59.1 5.0 %collective-permute-start.21 = (bf16[128,512]{1,0:T(8,128)(2,1)S(1)}, bf16[128,512]{1,0:T(8,128)(2,1)S(1)}, u32[]{:S(2)}, u32[]{:S(2)}) collective-permute-start(bf16[128,512]{1,0:T(8,128)(2,1)S(1)} %get-tuple-element.120.part_ref), channel_id=1, source_target_pairs={{0,16},{1,17},{2,18},{3,19},{4,20},{5,21},{6,22},{7,23},{8,24},{9,... | collective-permute-start | bytes 393224 | tf_op jit(solution)/shard_map/ppermute | solution.py:405
  60.7 5.0 %collective-permute-start.23 = (bf16[128,512]{1,0:T(8,128)(2,1)S(1)}, bf16[128,512]{1,0:T(8,128)(2,1)S(1)}, u32[]{:S(2)}, u32[]{:S(2)}) collective-permute-start(bf16[128,512]{1,0:T(8,128)(2,1)S(1)} %get-tuple-element.128.part_ref), channel_id=1, source_target_pairs={{0,8},{1,9},{2,10},{3,11},{4,12},{5,13},{6,14},{7,15},{8,0},{9,1},... | collective-permute-start | bytes 393224 | tf_op jit(solution)/shard_map/ppermute | solution.py:405
  66.2 1.4 %collective-permute-start.24 = (bf16[520,128]{1,0:T(8,128)(2,1)S(1)}, bf16[520,128]{1,0:T(8,128)(2,1)S(1)}, u32[]{:S(2)}, u32[]{:S(2)}) collective-permute-start(bf16[520,128]{1,0:T(8,128)(2,1)S(1)} %get-tuple-element.133), channel_id=1, source_target_pairs={{0,1},{1,0},{2,3},{3,2},{4,5},{5,4},{6,7},{7,6},{8,9},{9,8},{10,11... | collective-permute-start | bytes 399368 | tf_op jit(solution)/shard_map/ppermute | solution.py:405
  67.7 5.0 %collective-permute-start.27 = (bf16[264,128]{1,0:T(8,128)(2,1)S(1)}, bf16[264,128]{1,0:T(8,128)(2,1)S(1)}, u32[]{:S(2)}, u32[]{:S(2)}) collective-permute-start(bf16[264,128]{1,0:T(8,128)(2,1)S(1)} %get-tuple-element.135.mine_ref), channel_id=1, source_target_pairs={{0,2},{1,3},{2,0},{3,1},{4,6},{5,7},{6,4},{7,5},{8,10},{9,11},{10,... | collective-permute-start | bytes 202760 | tf_op jit(solution)/shard_map/ppermute | solution.py:405
  68.5 5.5 %collective-permute-start.25 = (bf16[264,128]{1,0:T(8,128)(2,1)S(1)}, bf16[264,128]{1,0:T(8,128)(2,1)S(1)}, u32[]{:S(2)}, u32[]{:S(2)}) collective-permute-start(bf16[264,128]{1,0:T(8,128)(2,1)S(1)} %get-tuple-element.134.mine_ref), channel_id=1, source_target_pairs={{0,2},{1,3},{2,0},{3,1},{4,6},{5,7},{6,4},{7,5},{8,10},{9,11},{10,... | collective-permute-start | bytes 202760 | tf_op jit(solution)/shard_map/ppermute | solution.py:405
  72.7 7.1 %collective-permute-start.28 = (bf16[264,128]{1,0:T(8,128)(2,1)S(1)}, bf16[264,128]{1,0:T(8,128)(2,1)S(1)}, u32[]{:S(2)}, u32[]{:S(2)}) collective-permute-start(bf16[264,128]{1,0:T(8,128)(2,1)S(1)} %hop_q.5.q_ref), channel_id=1, source_target_pairs={{0,4},{1,5},{2,6},{3,7},{4,0},{5,1},{6,2},{7,3},{8,12},{9,13},{10,... | collective-permute-start | bytes 202760 | tf_op jit(solution)/shard_map/ppermute | solution.py:405
  74.0 7.3 %collective-permute-start.26 = (bf16[264,128]{1,0:T(8,128)(2,1)S(1)}, bf16[264,128]{1,0:T(8,128)(2,1)S(1)}, u32[]{:S(2)}, u32[]{:S(2)}) collective-permute-start(bf16[264,128]{1,0:T(8,128)(2,1)S(1)} %hop_p.5.p_ref), channel_id=1, source_target_pairs={{0,4},{1,5},{2,6},{3,7},{4,0},{5,1},{6,2},{7,3},{8,12},{9,13},{10,... | collective-permute-start | bytes 202760 | tf_op jit(solution)/shard_map/ppermute | solution.py:405
  81.4 1.4 %collective-permute-start.29 = (bf16[128,512]{1,0:T(8,128)(2,1)S(1)}, bf16[128,512]{1,0:T(8,128)(2,1)S(1)}, u32[]{:S(2)}, u32[]{:S(2)}) collective-permute-start(bf16[128,512]{1,0:T(8,128)(2,1)S(1)} %get-tuple-element.138.delta_ref), channel_id=1, source_target_pairs={{0,1},{1,0},{2,3},{3,2},{4,5},{5,4},{6,7},{7,6},{8,9},{9,8},{10,11... | collective-permute-start | bytes 393224 | tf_op jit(solution)/shard_map/ppermute | solution.py:405
  83.2 5.6 %collective-permute-start.30 = (bf16[128,512]{1,0:T(8,128)(2,1)S(1)}, bf16[128,512]{1,0:T(8,128)(2,1)S(1)}, u32[]{:S(2)}, u32[]{:S(2)}) collective-permute-start(bf16[128,512]{1,0:T(8,128)(2,1)S(1)} %change.10.mine_ref), channel_id=1, source_target_pairs={{0,8},{1,9},{2,10},{3,11},{4,12},{5,13},{6,14},{7,15},{8,0},{9,1},... | collective-permute-start | bytes 393224 | tf_op jit(solution)/shard_map/ppermute | solution.py:405
  84.1 5.3 %collective-permute-start.32 = (bf16[128,512]{1,0:T(8,128)(2,1)S(1)}, bf16[128,512]{1,0:T(8,128)(2,1)S(1)}, u32[]{:S(2)}, u32[]{:S(2)}) collective-permute-start(bf16[128,512]{1,0:T(8,128)(2,1)S(1)} %change.11.mine_ref), channel_id=1, source_target_pairs={{0,16},{1,17},{2,18},{3,19},{4,20},{5,21},{6,22},{7,23},{8,24},{9,... | collective-permute-start | bytes 393224 | tf_op jit(solution)/shard_map/ppermute | solution.py:405
  88.8 5.0 %collective-permute-start.31 = (bf16[128,512]{1,0:T(8,128)(2,1)S(1)}, bf16[128,512]{1,0:T(8,128)(2,1)S(1)}, u32[]{:S(2)}, u32[]{:S(2)}) collective-permute-start(bf16[128,512]{1,0:T(8,128)(2,1)S(1)} %meet_a.5.part_ref), channel_id=1, source_target_pairs={{0,16},{1,17},{2,18},{3,19},{4,20},{5,21},{6,22},{7,23},{8,24},{9,... | collective-permute-start | bytes 393224 | tf_op jit(solution)/shard_map/ppermute | solution.py:405
  89.5 5.0 %collective-permute-start.33 = (bf16[128,512]{1,0:T(8,128)(2,1)S(1)}, bf16[128,512]{1,0:T(8,128)(2,1)S(1)}, u32[]{:S(2)}, u32[]{:S(2)}) collective-permute-start(bf16[128,512]{1,0:T(8,128)(2,1)S(1)} %meet_b.5.part_ref), channel_id=1, source_target_pairs={{0,8},{1,9},{2,10},{3,11},{4,12},{5,13},{6,14},{7,15},{8,0},{9,1},... | collective-permute-start | bytes 393224 | tf_op jit(solution)/shard_map/ppermute | solution.py:405
